TPU v7x, 32 devices: a whole 2x2x4 slice. The times are simulated.
32 devices in a mesh: rows: 4 (over z), tp: 8 (over y, x, core).
Axes of the slice: x: 2, y: 2, z: 4, core: 2. Of those that a mesh axis runs over, the one named last changes fastest.
Arguments:
- tokens: bfloat16 [8, 2048, 2048], P('rows', 'tp'), may hold values from -120 to 120, as said below
- segment_ids: int32 [8, 2048], P('rows'), may hold values from 0 to 3, as said below
- positions: int32 [8, 2048], P('rows'), may hold values from 0 to 1023, as said below
- norm_gain: bfloat16 [2048], replicated, may hold values from 0.5 to 1.5
- norm_shift: bfloat16 [2048], replicated, may hold values from -1.5 to 1.5
- query_key_value_weight: bfloat16 [2048, 3, 2048], P(None, None, 'tp'), may hold values from -1 to 1, as said below
- b_qkv: bfloat16 [3, 2048], P(None, 'tp'), may hold values from -1.5 to 1.5
- dense_weight: bfloat16 [2048, 2048], P('tp'), may hold values from -1 to 1
- b_dense: bfloat16 [2048], replicated, may hold values from -1.5 to 1.5
- inward_weight: bfloat16 [2048, 8192], P(None, 'tp'), may hold values from -1 to 1, as said below
- b_in: bfloat16 [8192], P('tp'), may hold values from -1.5 to 1.5
- outward_weight: bfloat16 [8192, 2048], P('tp'), may hold values from -0.0625 to 0.0625
- b_out: bfloat16 [2048], replicated, may hold values from -1.5 to 1.5
- cotangent: bfloat16 [8, 2048, 2048], P('rows', 'tp'), may hold values from -6 to 6
Outputs:
- layer_out: bfloat16 [8, 2048, 2048], P('rows', 'tp')
- input_grad: bfloat16 [8, 2048, 2048], P('rows', 'tp')
- gain_grad: float32 [2048], P('tp')
- shift_grad: float32 [2048], P('tp')
- qkv_weight_grad: float32 [2048, 3, 2048], P(None, None, 'tp')
- qkv_bias_grad: float32 [3, 2048], P(None, 'tp')
- dense_weight_grad: float32 [2048, 2048], P('tp')
- dense_bias_grad: float32 [2048], P('tp')
- in_weight_grad: float32 [2048, 8192], P(None, 'tp')
- in_bias_grad: float32 [8192], P('tp')
- out_weight_grad: float32 [8192, 2048], P('tp')
- out_bias_grad: float32 [2048], P('tp')
- rms_values: float32 [4], replicated
Inputs may be any that keep to these rules, and one draw needn't show every extreme that they name: `segment_ids`: within each row the ids start at 0 and rise by one at each of 3 document starts; the first document of every row holds exactly 1024 tokens, the others fewer. `positions`: A token's position is the number of earlier tokens of its row with its segment id. `tokens`: Real-valued activations. `query_key_value_weight`: Real-valued weights. `inward_weight`: Real-valued weights.
All inputs are finite; a program needn't handle non-finite values.
Results may differ from a plain program's by a relative error of at most 0.0086.
Values may be sent and summed in bfloat16 or wider, within the bound.
No kernel may reach another device: no remote copies, remote signals or barrier semaphores. Data moves between devices by JAX's collectives and lax.ppermute only.
A program may use at most 384 MiB of HBM per device.

v0:
```python
import jax
import jax.numpy as jnp
from jax import lax
from jax.sharding import PartitionSpec as P

HD = 64
ROT = 32


epsilon = 1e-05
big_negative = -1e30
rope_base = 10000.0


def normalize(values, norm_gain, norm_shift):
    center = values - jnp.mean(values, axis=-1, keepdims=True)
    spread = jnp.mean(center * center, axis=-1, keepdims=True)
    return center * lax.rsqrt(spread + epsilon) * norm_gain + norm_shift


def gelu_tanh(hidden):
    return jax.nn.gelu(hidden, approximate=True)


def rope_tables(positions, rot_dims):
    half_rot = rot_dims // 2
    frequency = rope_base ** (-2.0 * jnp.arange(half_rot, dtype=jnp.float32) / rot_dims)
    angles = positions.astype(jnp.float32)[..., None] * frequency
    return (jnp.cos(angles)[..., None, :], jnp.sin(angles)[..., None, :])


def rotate(field_in, cosine_table, sine_table):
    half_rot = cosine_table.shape[-1]
    first_part = field_in[..., :half_rot]
    second = field_in[..., half_rot : 2 * half_rot]
    return jnp.concatenate(
        [
            first_part * cosine_table - second * sine_table,
            second * cosine_table + first_part * sine_table,
            field_in[..., 2 * half_rot :],
        ],
        axis=-1,
    )


def allowed_pairs(segment_ids, offset, block_rows):
    length = segment_ids.shape[1]
    query_ids = lax.dynamic_slice_in_dim(segment_ids, offset, block_rows, 1)
    same_doc = query_ids[:, :, None] == segment_ids[:, None, :]
    causal = (offset + jnp.arange(block_rows, dtype=jnp.int32))[:, None] >= jnp.arange(
        length, dtype=jnp.int32
    )[None, :]
    return (same_doc & causal[None])[:, None]


def share_normed(normed_low):
    return lax.all_gather(normed_low, "tp", axis=1, tiled=True)


def body(
    tokens,
    segment_ids,
    positions,
    norm_gain,
    norm_shift,
    query_key_value_weight,
    b_qkv,
    dense_weight,
    b_dense,
    inward_weight,
    b_in,
    outward_weight,
    b_out,
    cotangent,
):
    values = tokens.astype(jnp.float32)
    normed_local, norm_pull = jax.vjp(
        normalize, values, norm_gain.astype(jnp.float32), norm_shift.astype(jnp.float32)
    )
    normed_low = normed_local.astype(jnp.bfloat16)
    collected_rows = share_normed(normed_low)
    seqs, length, width = collected_rows.shape
    local_cols = query_key_value_weight.shape[2]
    head_dim = HD
    heads_here = local_cols // head_dim
    split_shape = (seqs, length, heads_here, head_dim)
    scale = head_dim ** (-0.5)
    qkv = jnp.einsum(
        "xue,egb->xugb", collected_rows, query_key_value_weight, preferred_element_type=jnp.float32
    ) + b_qkv.astype(jnp.float32)
    cosine_table, sine_table = rope_tables(positions, ROT)
    queries = rotate(qkv[:, :, 0].reshape(split_shape), cosine_table, sine_table).astype(
        jnp.bfloat16
    )
    keys_low = rotate(qkv[:, :, 1].reshape(split_shape), cosine_table, sine_table).astype(
        jnp.bfloat16
    )
    values_low = qkv[:, :, 2].reshape(split_shape).astype(jnp.bfloat16)
    block_rows = min(512, length)
    block_count = length // block_rows
    block_ids = jnp.arange(block_count, dtype=jnp.int32)

    def forward_block(carried, block_index):
        offset = block_index * block_rows
        query_block = lax.dynamic_slice_in_dim(queries, offset, block_rows, 1)
        raw_scores = (
            jnp.einsum("sqhe,skhe->shqk", query_block, keys_low, preferred_element_type=jnp.float32)
            * scale
        )
        scores = jnp.where(allowed_pairs(segment_ids, offset, block_rows), raw_scores, big_negative)
        row_max = jnp.max(scores, axis=-1, keepdims=True)
        expd = jnp.exp(scores - row_max)
        row_total = jnp.sum(expd, axis=-1, keepdims=True)
        soft_low = (expd / row_total).astype(jnp.bfloat16)
        attended_block = jnp.einsum(
            "shqk,skhe->sqhe", soft_low, values_low, preferred_element_type=jnp.float32
        )
        return (carried, (attended_block.astype(jnp.bfloat16), row_max + jnp.log(row_total)))

    unused, (attended_pieces, log_sums) = lax.scan(forward_block, None, block_ids)
    attended_reduced = jnp.moveaxis(attended_pieces, 0, 1).reshape(seqs, length, local_cols)
    hidden = jnp.einsum(
        "ezg,gq->ezq", collected_rows, inward_weight, preferred_element_type=jnp.float32
    ) + b_in.astype(jnp.float32)
    activated, gelu_pull = jax.vjp(gelu_tanh, hidden)
    activation_reduced = activated.astype(jnp.bfloat16)
    attention_part = jnp.einsum(
        "xpu,uw->xpw", attended_reduced, dense_weight, preferred_element_type=jnp.float32
    )
    perceptron_branch = jnp.einsum(
        "xpu,uw->xpw", activation_reduced, outward_weight, preferred_element_type=jnp.float32
    )
    attention_tok, mlp_tok = (
        lax.psum_scatter(attention_part, "tp", scatter_dimension=1, tiled=True),
        lax.psum_scatter(perceptron_branch, "tp", scatter_dimension=1, tiled=True),
    )
    attention = attention_tok + b_dense.astype(jnp.float32)
    mlp = mlp_tok + b_out.astype(jnp.float32)
    layer_sum = values + attention + mlp
    layer_out = layer_sum.astype(jnp.bfloat16)
    local_squares = jnp.stack(
        [
            jnp.sum(values * values),
            jnp.sum(attention * attention),
            jnp.sum(mlp * mlp),
            jnp.sum(layer_sum * layer_sum),
        ]
    )
    total_squares = lax.psum(local_squares, ("rows", "tp"))
    elements = seqs * lax.axis_size("rows") * length * width
    rms_values = jnp.sqrt(total_squares / elements)
    collected_backward = share_normed(normed_low)
    cotangent_full = lax.all_gather(cotangent, "tp", axis=1, tiled=True)
    bias_width = width // lax.axis_size("tp")
    bias_cols = lax.dynamic_slice_in_dim(
        cotangent_full, lax.axis_index("tp") * bias_width, bias_width, 2
    )
    out_bias_grad = jnp.sum(bias_cols.astype(jnp.float32), axis=(0, 1))
    activation_gradient = jnp.einsum(
        "rmu,xu->rmx", cotangent_full, outward_weight, preferred_element_type=jnp.float32
    )
    out_weight_grad = jnp.einsum(
        "yaw,yak->wk", activation_reduced, cotangent_full, preferred_element_type=jnp.float32
    )
    hidden_gradient = gelu_pull(activation_gradient)[0].astype(jnp.bfloat16)
    in_weight_grad = jnp.einsum(
        "evj,evu->ju", collected_backward, hidden_gradient, preferred_element_type=jnp.float32
    )
    in_bias_grad = jnp.sum(hidden_gradient.astype(jnp.float32), axis=(0, 1))
    perceptron_backward = jnp.einsum(
        "inj,rj->inr", hidden_gradient, inward_weight, preferred_element_type=jnp.float32
    )
    attended_grad = jnp.einsum(
        "rmu,xu->rmx", cotangent_full, dense_weight, preferred_element_type=jnp.float32
    )
    attended_grad = attended_grad.astype(jnp.bfloat16).reshape(split_shape)
    dense_weight_grad = jnp.einsum(
        "yaw,yak->wk", attended_reduced, cotangent_full, preferred_element_type=jnp.float32
    )

    def backward_block(carried, block_index):
        key_grad, value_grad = carried
        offset = block_index * block_rows
        query_block = lax.dynamic_slice_in_dim(queries, offset, block_rows, 1)
        grad_block = lax.dynamic_slice_in_dim(attended_grad, offset, block_rows, 1)
        raw_scores = (
            jnp.einsum("sqhe,skhe->shqk", query_block, keys_low, preferred_element_type=jnp.float32)
            * scale
        )
        scores = jnp.where(allowed_pairs(segment_ids, offset, block_rows), raw_scores, big_negative)
        soft_weights = jnp.exp(scores - log_sums[block_index])
        soft_low = soft_weights.astype(jnp.bfloat16)
        prob_grad = jnp.einsum(
            "sqhe,skhe->shqk", grad_block, values_low, preferred_element_type=jnp.float32
        )
        inner_sum = jnp.sum(soft_weights * prob_grad, axis=-1, keepdims=True)
        score_grad = (soft_weights * (prob_grad - inner_sum)).astype(jnp.bfloat16)
        query_grad = (
            jnp.einsum("shqk,skhe->sqhe", score_grad, keys_low, preferred_element_type=jnp.float32)
            * scale
        )
        key_grad = (
            key_grad
            + jnp.einsum(
                "shqk,sqhe->skhe", score_grad, query_block, preferred_element_type=jnp.float32
            )
            * scale
        )
        value_grad = value_grad + jnp.einsum(
            "shqk,sqhe->skhe", soft_low, grad_block, preferred_element_type=jnp.float32
        )
        return ((key_grad, value_grad), query_grad)

    zero_grad = jnp.zeros(split_shape, jnp.float32)
    (key_grad, value_grad), query_pieces = lax.scan(
        backward_block, (zero_grad, zero_grad), block_ids
    )
    query_grad = jnp.moveaxis(query_pieces, 0, 1).reshape(split_shape)
    query_back = rotate(query_grad, cosine_table, -sine_table).reshape(seqs, length, local_cols)
    key_back = rotate(key_grad, cosine_table, -sine_table).reshape(seqs, length, local_cols)
    query_key_value_gradient = jnp.stack(
        [query_back, key_back, value_grad.reshape(seqs, length, local_cols)], axis=2
    ).astype(jnp.bfloat16)
    qkv_weight_grad = jnp.einsum(
        "kxa,kxuh->auh",
        collected_backward,
        query_key_value_gradient,
        preferred_element_type=jnp.float32,
    )
    qkv_bias_grad = jnp.sum(query_key_value_gradient.astype(jnp.float32), axis=(0, 1))
    attention_backward = jnp.einsum(
        "nibo,hbo->nih",
        query_key_value_gradient,
        query_key_value_weight,
        preferred_element_type=jnp.float32,
    )
    normed_grad = lax.psum_scatter(
        attention_backward + perceptron_backward, "tp", scatter_dimension=1, tiled=True
    )
    value_in_grad, gain_part, shift_part = norm_pull(normed_grad)
    input_grad = (cotangent.astype(jnp.float32) + value_in_grad).astype(jnp.bfloat16)
    gain_local, shift_local = (
        lax.psum_scatter(gain_part, "tp", scatter_dimension=0, tiled=True),
        lax.psum_scatter(shift_part, "tp", scatter_dimension=0, tiled=True),
    )
    summed = lax.psum(
        (
            qkv_weight_grad,
            qkv_bias_grad,
            dense_weight_grad,
            gain_local,
            shift_local,
            in_weight_grad,
            in_bias_grad,
            out_weight_grad,
            out_bias_grad,
        ),
        "rows",
    )
    (
        qkv_weight_grad,
        qkv_bias_grad,
        dense_weight_grad,
        gain_grad,
        shift_grad,
        in_weight_grad,
        in_bias_grad,
        out_weight_grad,
        out_bias_grad,
    ) = summed
    return (
        layer_out,
        input_grad,
        gain_grad,
        shift_grad,
        qkv_weight_grad,
        qkv_bias_grad,
        dense_weight_grad,
        out_bias_grad,
        in_weight_grad,
        in_bias_grad,
        out_weight_grad,
        out_bias_grad,
        rms_values,
    )


def solution(mesh):
    in_specs = (
        P("rows", "tp", None),
        P("rows", None),
        P("rows", None),
        P(),
        P(),
        P(None, None, "tp"),
        P(None, "tp"),
        P("tp", None),
        P(),
        P(None, "tp"),
        P("tp"),
        P("tp", None),
        P(),
        P("rows", "tp", None),
    )
    out_specs = (
        P("rows", "tp", None),
        P("rows", "tp", None),
        P("tp"),
        P("tp"),
        P(None, None, "tp"),
        P(None, "tp"),
        P("tp", None),
        P("tp"),
        P(None, "tp"),
        P("tp"),
        P("tp", None),
        P("tp"),
        P(),
    )
    return jax.shard_map(body, mesh=mesh, in_specs=in_specs, out_specs=out_specs, check_vma=False)
```

profile of v0, /device:TPU:0, one launch (start us, length us, event | category | flops | bytes accessed | tf_op | source)
XLA Modules:
  0.0 2455.6 jit_solution(12116444957916753434)
XLA Ops:
  18.4 89.4 %all-gather.3.cloned.1.call-done = bf16[2,2048,2048]{2,1,0:T(8,128)(2,1)} async-done(((bf16[2,256,2048]{2,1,0:T(8,128)(2,1)}), bf16[2,2048,2048]{2,1,0:T(8,128)(2,1)}) %all-gather.3.cloned.1.call-update) | async-done | bytes 16777232 | tf_op jit(solution)/shard_map/all_gather | solution.py:57
  107.8 19.6 broadcast_add_fusion
  138.6 199.0 %while.27 = (s32[]{:T(128)}, bf16[4,2,512,4,64]{2,4,3,1,0:T(8,128)(2,1)}, f32[4,2,4,512,1]{3,2,1,4,0:T(4,128)S(1)}, s32[4]{0:T(128)S(1)}, s32[2,2048]{1,0:T(2,12...) while((s32[]{:T(128)}, ...), condition=%wide.region_5.6_spmd, body=%wide.region_2.5_spmd.sunk | while | flops 2253648384 | bytes 133333752 | solution.py:120
  142.5 17.8 fusion.113
  160.2 15.4 fusion.114
  175.7 15.0 fusion.115
  194.3 15.1 fusion.113
  209.5 15.1 fusion.114
  224.7 15.0 fusion.115
  243.3 15.1 fusion.113
  258.4 15.1 fusion.114
  273.6 15.0 fusion.115
  292.3 15.1 fusion.113
  307.4 15.1 fusion.114
  322.6 15.0 fusion.115
  337.6 11.9 convolution_convert_fusion
  349.5 475.6 %while.28 = (s32[]{:T(128)}, f32[2,2048,4,64]{1,3,2,0:T(8,128)}, f32[2,2048,4,64]{1,3,2,0:T(8,128)}, f32[4,2,512,4,64]{2,4,3,1,0:T(8,128)}, s32[4]{0:T(128)S(1)}...) while((s32[]{:T(128)}, f32[2,2048,4,64]{1,3,2,0:T(8,128)}, ...), condition=%wide.region_10.11_spmd.clone, body=%wide.region_8.10_spmd.clone.sunk | while | flops 5505282560 | bytes 305283904 | solution.py:215
  365.4 14.2 fusion.125
  381.6 26.6 %multiply_reduce_fusion.5 = (f32[2,4,512]{2,1,0:T(4,128)S(1)}, f32[2,4,512,2048]{3,2,1,0:T(8,128)}) fusion(f32[2,4,512,2048]{3,2,1,0:T(8,128)} %fusion.125, f32[2,4,512]{2,1,0:T(4,128)S(1)} %dynamic-slice_bitcast_fusion.2, pred[2,512,2048]{2,1,0:T(8,128)(4,1)} %compare_and_fusion.5, bf16[2,2048,4,64]{1,3,2,0:T(8,128)(2,1)} %get-tuple-element.443, ...), kind=kOutput, calls=%fused_computation.20.clone.1 | convolution fusion | flops 1115680768 | bytes 71860224 | tf_op jit(solution)/shard_map/while/body/eval_jaxpr/sqhe,skhe->shqk/dot_general | solution.py:193
  408.2 28.5 %multiply_convert_fusion.5 = bf16[2,4,512,2048]{3,2,1,0:T(8,128)(2,1)} fusion(f32[2,4,512,2048]{3,2,1,0:T(8,128)} %get-tuple-element.363, f32[2,4,512,2048]{3,2,1,0:T(8,128)} %fusion.125, f32[2,4,512]{2,1,0:T(4,128)S(1)} %get-tuple-element.364, f32[2,4,512]{2,1,0:T(4,128)S(1)} %dynamic-slice_bitcast_fusion.2, pred[2,512,2048]{2,1,0:T(8,128)(4,1)} %compare_and_fusion.5), kind=kLoop, calls=%fused_computation.19.clone.1 | loop fusion | flops 50331648 | bytes 86016000 | tf_op jit(solution)/shard_map/while/body/eval_jaxpr/convert_element_type | solution.py:197
  436.7 11.1 bitcast_add_fusion.5
  447.8 9.7 fusion.126
  457.6 17.3 bitcast_add_fusion.6
  479.5 14.2 fusion.125
  495.7 26.6 %multiply_reduce_fusion.5 = (f32[2,4,512]{2,1,0:T(4,128)S(1)}, f32[2,4,512,2048]{3,2,1,0:T(8,128)}) fusion(f32[2,4,512,2048]{3,2,1,0:T(8,128)} %fusion.125, f32[2,4,512]{2,1,0:T(4,128)S(1)} %dynamic-slice_bitcast_fusion.2, pred[2,512,2048]{2,1,0:T(8,128)(4,1)} %compare_and_fusion.5, bf16[2,2048,4,64]{1,3,2,0:T(8,128)(2,1)} %get-tuple-element.443, ...), kind=kOutput, calls=%fused_computation.20.clone.1 | convolution fusion | flops 1115680768 | bytes 71860224 | tf_op jit(solution)/shard_map/while/body/eval_jaxpr/sqhe,skhe->shqk/dot_general | solution.py:193
  522.3 28.5 %multiply_convert_fusion.5 = bf16[2,4,512,2048]{3,2,1,0:T(8,128)(2,1)} fusion(f32[2,4,512,2048]{3,2,1,0:T(8,128)} %get-tuple-element.363, f32[2,4,512,2048]{3,2,1,0:T(8,128)} %fusion.125, f32[2,4,512]{2,1,0:T(4,128)S(1)} %get-tuple-element.364, f32[2,4,512]{2,1,0:T(4,128)S(1)} %dynamic-slice_bitcast_fusion.2, pred[2,512,2048]{2,1,0:T(8,128)(4,1)} %compare_and_fusion.5), kind=kLoop, calls=%fused_computation.19.clone.1 | loop fusion | flops 50331648 | bytes 86016000 | tf_op jit(solution)/shard_map/while/body/eval_jaxpr/convert_element_type | solution.py:197
  550.8 12.3 bitcast_add_fusion.5
  563.1 9.7 fusion.126
  572.9 18.6 bitcast_add_fusion.6
  596.1 14.2 fusion.125
  612.3 26.6 %multiply_reduce_fusion.5 = (f32[2,4,512]{2,1,0:T(4,128)S(1)}, f32[2,4,512,2048]{3,2,1,0:T(8,128)}) fusion(f32[2,4,512,2048]{3,2,1,0:T(8,128)} %fusion.125, f32[2,4,512]{2,1,0:T(4,128)S(1)} %dynamic-slice_bitcast_fusion.2, pred[2,512,2048]{2,1,0:T(8,128)(4,1)} %compare_and_fusion.5, bf16[2,2048,4,64]{1,3,2,0:T(8,128)(2,1)} %get-tuple-element.443, ...), kind=kOutput, calls=%fused_computation.20.clone.1 | convolution fusion | flops 1115680768 | bytes 71860224 | tf_op jit(solution)/shard_map/while/body/eval_jaxpr/sqhe,skhe->shqk/dot_general | solution.py:193
  638.9 28.5 %multiply_convert_fusion.5 = bf16[2,4,512,2048]{3,2,1,0:T(8,128)(2,1)} fusion(f32[2,4,512,2048]{3,2,1,0:T(8,128)} %get-tuple-element.363, f32[2,4,512,2048]{3,2,1,0:T(8,128)} %fusion.125, f32[2,4,512]{2,1,0:T(4,128)S(1)} %get-tuple-element.364, f32[2,4,512]{2,1,0:T(4,128)S(1)} %dynamic-slice_bitcast_fusion.2, pred[2,512,2048]{2,1,0:T(8,128)(4,1)} %compare_and_fusion.5), kind=kLoop, calls=%fused_computation.19.clone.1 | loop fusion | flops 50331648 | bytes 86016000 | tf_op jit(solution)/shard_map/while/body/eval_jaxpr/convert_element_type | solution.py:197
  667.4 12.3 bitcast_add_fusion.5
  679.7 9.7 fusion.126
  689.5 18.6 bitcast_add_fusion.6
  712.7 14.2 fusion.125
  728.9 26.6 %multiply_reduce_fusion.5 = (f32[2,4,512]{2,1,0:T(4,128)S(1)}, f32[2,4,512,2048]{3,2,1,0:T(8,128)}) fusion(f32[2,4,512,2048]{3,2,1,0:T(8,128)} %fusion.125, f32[2,4,512]{2,1,0:T(4,128)S(1)} %dynamic-slice_bitcast_fusion.2, pred[2,512,2048]{2,1,0:T(8,128)(4,1)} %compare_and_fusion.5, bf16[2,2048,4,64]{1,3,2,0:T(8,128)(2,1)} %get-tuple-element.443, ...), kind=kOutput, calls=%fused_computation.20.clone.1 | convolution fusion | flops 1115680768 | bytes 71860224 | tf_op jit(solution)/shard_map/while/body/eval_jaxpr/sqhe,skhe->shqk/dot_general | solution.py:193
  755.5 28.5 %multiply_convert_fusion.5 = bf16[2,4,512,2048]{3,2,1,0:T(8,128)(2,1)} fusion(f32[2,4,512,2048]{3,2,1,0:T(8,128)} %get-tuple-element.363, f32[2,4,512,2048]{3,2,1,0:T(8,128)} %fusion.125, f32[2,4,512]{2,1,0:T(4,128)S(1)} %get-tuple-element.364, f32[2,4,512]{2,1,0:T(4,128)S(1)} %dynamic-slice_bitcast_fusion.2, pred[2,512,2048]{2,1,0:T(8,128)(4,1)} %compare_and_fusion.5), kind=kLoop, calls=%fused_computation.19.clone.1 | loop fusion | flops 50331648 | bytes 86016000 | tf_op jit(solution)/shard_map/while/body/eval_jaxpr/convert_element_type | solution.py:197
  784.0 12.3 bitcast_add_fusion.5
  796.4 9.7 fusion.126
  806.1 18.6 bitcast_add_fusion.6
  851.6 23.4 fusion.62
  875.0 36.5 %convert_reduce_fusion = (f32[1024]{0:T(1024)}, bf16[2,2048,1024]{2,1,0:T(8,128)(2,1)}) fusion(f32[2,2048,1024]{2,1,0:T(8,128)} %fusion.62, f32[1024]{0:T(1024)S(1)} %copy-done.30, bf16[2,2048,2048]{2,1,0:T(8,128)(2,1)} %all-gather.5.cloned.1.call-done, bf16[1024,2048]{1,0:T(8,128)(2,1)} %param.29), kind=kOutput, calls=%fused_computation.61 | convolution fusion | flops 17276338176 | bytes 46145536 | tf_op jit(solution)/shard_map/rmu,xu->rmx/dot_general | solution.py:159
  911.5 24.6 %fusion.60 = f32[2,2048,2048]{2,1,0:T(8,128)} fusion(bf16[2,2048,1024]{2,1,0:T(8,128)(2,1)} %get-tuple-element.238, bf16[2048,1024]{1,0:T(8,128)(2,1)S(1)} %copy-done.35), kind=kOutput, calls=%fused_computation.90 | convolution fusion | flops 17179869184 | bytes 46137344 | tf_op jit(solution)/shard_map/inj,rj->inr/dot_general | solution.py:170
  936.1 28.3 %bitcast_add_fusion.2 = f32[2,2048,2048]{2,1,0:T(8,128)} fusion(f32[2,2048,2048]{2,1,0:T(8,128)} %fusion.60, bf16[2048,3,256]{2,0,1:T(8,128)(2,1)S(1)} %copy-done, bf16[2,2048,1,256]{3,1,2,0:T(8,128)(2,1)} %copy.53, bf16[2,2048,1,256]{3,1,2,0:T(8,128)(2,1)} %copy.52, bf16[2,2048,1,256]{3,1,2,0:T(8,128)(2,1)} %copy.51), kind=kOutput, calls=%fused_computation.47 | convolution fusion | flops 12899581952 | bytes 76546048 | tf_op jit(solution)/shard_map/nibo,hbo->nih/dot_general | solution.py:231
  964.4 4.5 copy.48
  969.0 4.9 reshape.163
  973.8 25.0 %fusion.71 = f32[2,2048,2048]{2,1,0:T(8,128)} fusion(bf16[2,2048,256]{1,2,0:T(8,128)(2,1)} %reshape.163, bf16[256,2048]{1,0:T(8,128)(2,1)} %param.25), kind=kOutput, calls=%fused_computation.114 | convolution fusion | flops 4294967296 | bytes 36700160 | tf_op jit(solution)/shard_map/xpu,uw->xpw/dot_general | solution.py:127
  998.9 30.0 %fusion.58 = f32[2,2048,2048]{2,1,0:T(8,128)} fusion(bf16[1024,2048]{1,0:T(8,128)(2,1)} %param.29, f32[2,2048,1024]{2,1,0:T(8,128)} %fusion.62, f32[1024]{0:T(1024)S(1)} %copy-done.30), kind=kOutput, calls=%fused_computation.88 | convolution fusion | flops 17221812224 | bytes 54530048 | tf_op jit(solution)/shard_map/xpu,uw->xpw/dot_general | solution.py:130
  1029.4 12.9 convolution_bitcast_fusion.2
  1042.3 29.3 %convolution_bitcast_fusion = f32[1024,2048]{1,0:T(8,128)} fusion(bf16[2,2048,2048]{2,1,0:T(8,128)(2,1)} %all-gather.5.cloned.1.call-done, f32[2,2048,1024]{2,1,0:T(8,128)} %fusion.62, f32[1024]{0:T(1024)S(1)} %copy-done.30), kind=kOutput, calls=%fused_computation.77 | convolution fusion | flops 17221812224 | bytes 41947136 | tf_op jit(solution)/shard_map/yaw,yak->wk/dot_general | solution.py:162
  1071.6 21.9 convolution_bitcast_fusion.1
  1093.6 19.8 fusion.64
  1119.2 50.6 %reduce-scatter.8.cloned.1.call-done = f32[2,256,2048]{2,1,0:T(8,128)} async-done(((f32[2,2048,2048]{2,1,0:T(8,128)}), f32[2,256,2048]{2,1,0:T(8,128)}) %reduce-scatter.8.cloned.1.call-update) | async-done | bytes 4194320 | tf_op jit(solution)/shard_map/reduce_scatter | solution.py:237
  1169.8 5.2 fusion.76
  1175.1 203.9 %reduce-scatter.4.cloned.1.call-done = f32[2,256,2048]{2,1,0:T(8,128)} async-done(((f32[2,2048,2048]{2,1,0:T(8,128)}), f32[2,256,2048]{2,1,0:T(8,128)}) %reduce-scatter.4.cloned.1.call-update) | async-done | bytes 4194320 | tf_op jit(solution)/shard_map/reduce_scatter | solution.py:134
  1378.9 208.7 %reduce-scatter.6.cloned.1.call-done = f32[2,256,2048]{2,1,0:T(8,128)} async-done(((f32[2,2048,2048]{2,1,0:T(8,128)}), f32[2,256,2048]{2,1,0:T(8,128)}) %reduce-scatter.6.cloned.1.call-update) | async-done | bytes 4194320 | tf_op jit(solution)/shard_map/reduce_scatter | solution.py:135
  1587.7 9.0 multiply_reduce_fusion.3
  1601.5 45.2 %psum.79 = f32[4]{0:T(128)S(1)} all-reduce(f32[4]{0:T(128)S(1)} %pad_maximum_fusion.5), channel_id=1, replica_groups=mesh['rows'=4,'tp'=8] {'rows','tp'}, use_global_device_ids=true, to_apply=%region_34.35 | all-reduce | flops 4 | bytes 32 | tf_op jit(solution)/shard_map/psum | solution.py:149
  1646.7 24.7 %all-reduce.2 = (f32[2048]{0:T(1024)S(1)}, f32[2048]{0:T(1024)S(1)}) all-reduce(f32[2048]{0:T(1024)S(1)} %get-tuple-element.165, f32[2048]{0:T(1024)S(1)} %get-tuple-element.161), channel_id=5, replica_groups=mesh['rows'=4,'tp'=8] {'tp'}, use_global_device_ids=true, to_apply=%region_15.16.clone | all-reduce | flops 4096 | bytes 32768
  1671.5 20.6 all-reduce.3
  1692.6 5.3 add_convert_fusion
  1698.0 732.2 %all-reduce.7.cloned.1.call-done = (f32[2048,3,256]{2,0,1:T(8,128)}, f32[256,2048]{1,0:T(8,128)}, f32[2048,1024]{1,0:T(8,128)}, f32[1024,2048]{1,0:T(8,128)}) async-done(((f32[2048,3,256]{2,0,1:T(8,128)}, f32[256,2048]{1,0:T(8,128)}, f32[2048,1024]{1,0:T(8,128)}, f32[1024,2048]{1,0:T(8,128)}), (f32[2048,3,256]{2,0,1:T(8,128)}, f32[256,2048]{1,0:T(8,128)}, f32[2048,1024]{1,0:T(8,128)}, ...) | async-done | bytes 25165840 | tf_op jit(solution)/shard_map/psum | solution.py:246
  2430.7 6.6 copy.99
  (219 shorter events, 99.1 us)
Async XLA Ops:
  7.2 100.7 %copy-start = (bf16[2048,3,256]{2,0,1:T(8,128)(2,1)S(1)}, bf16[2048,3,256]{2,0,1:T(8,128)(2,1)}, u32[]{:S(2)}) copy-start(bf16[2048,3,256]{2,0,1:T(8,128)(2,1)} %param.23) | copy-start | bytes 9437188
  7.2 5.1 copy-start.26
  7.2 5.1 copy-start.27
  7.2 100.6 %all-gather.3.cloned.1.call-start = ((), (), s32[]{:S(2)}) async-start(), calls=%async_computation.3 | async-start | bytes 18874368 | tf_op jit(solution)/shard_map/all_gather | solution.py:57
  7.3 5.7 copy-start.5
  9.4 3.0 copy-start.19
  11.7 0.6 copy-start.23
  12.3 0.6 copy-start.21
  12.3 0.6 copy-start.17
  12.9 3.1 copy-start.32
  12.9 3.1 copy-start.25
  12.9 3.1 copy-start.33
  15.1 322.5 %all-gather.5.cloned.1.call-start = ((), (), s32[]{:S(2)}) async-start(), calls=%async_computation.6 | async-start | bytes 18874368 | tf_op jit(solution)/shard_map/all_gather | solution.py:153
  15.9 1153.9 %reduce-scatter.8.cloned.1.call-start = ((), (), s32[]{:S(2)}) async-start(), calls=%async_computation.7 | async-start | bytes 37748736 | tf_op jit(solution)/shard_map/reduce_scatter | solution.py:237
  18.4 117.2 %copy-start.12 = (f32[2,2048,16]{1,2,0:T(8,128)}, f32[2,2048,16]{1,2,0:T(8,128)S(1)}, u32[]{:S(2)}) copy-start(f32[2,2048,16]{1,2,0:T(8,128)S(1)} %get-tuple-element.236) | copy-start | bytes 786436
  131.4 4.2 copy-start.16
  136.3 2.2 copy-start.11
  140.1 2.4 copy-start.1
  160.2 15.4 copy-start.6
  191.9 2.4 copy-start.1
  209.5 15.2 copy-start.6
  240.9 2.4 copy-start.1
  258.4 15.2 copy-start.6
  289.9 2.4 copy-start.1
  307.4 15.2 copy-start.6
  362.0 3.3 copy-start.2
  436.7 11.1 copy-start.3
  476.1 3.3 copy-start.2
  550.8 12.3 copy-start.3
  592.8 3.3 copy-start.2
  667.4 12.3 copy-start.3
  709.4 3.3 copy-start.2
  784.0 12.3 copy-start.3
  825.1 3.5 copy-start.4
  828.1 1.6 copy-start.13
  828.1 1.6 copy-start.15
  851.6 23.4 copy-start.30
  875.0 36.5 %copy-start.35 = (bf16[2048,1024]{1,0:T(8,128)(2,1)S(1)}, bf16[2048,1024]{1,0:T(8,128)(2,1)}, u32[]{:S(2)}) copy-start(bf16[2048,1024]{1,0:T(8,128)(2,1)} %param.27) | copy-start | bytes 12582916
  964.4 414.6 %reduce-scatter.4.cloned.1.call-start = ((), (), s32[]{:S(2)}) async-start(), calls=%async_computation.4 | async-start | bytes 37748736 | tf_op jit(solution)/shard_map/reduce_scatter | solution.py:134
  998.8 588.8 %reduce-scatter.6.cloned.1.call-start = ((), (), s32[]{:S(2)}) async-start(), calls=%async_computation.5 | async-start | bytes 37748736 | tf_op jit(solution)/shard_map/reduce_scatter | solution.py:135
  1028.9 1401.2 %all-reduce.7.cloned.1.call-start = ((), (), s32[]{:S(2)}) async-start(), calls=%async_computation.8 | async-start | bytes 50331648 | tf_op jit(solution)/shard_map/psum | solution.py:246
  1029.4 42.2 %slice-start.2 = ((s8[8388608]{0:T(1024)(128)(4,1)}), s8[4194304]{0:T(1024)(128)(4,1)S(1)}, s32[]{:S(2)}) async-start(s8[8388608]{0:T(1024)(128)(4,1)} %bitcast.152), calls=%async_computation.11 | async-start | bytes 8388608
  1042.3 29.3 %slice-start.3 = ((s8[8388608]{0:T(1024)(128)(4,1)}), s8[4194304]{0:T(1024)(128)(4,1)S(1)}, s32[]{:S(2)}) async-start(s8[8388608]{0:T(1024)(128)(4,1)} %bitcast.152), calls=%async_computation.12 | async-start | bytes 8388608
  1071.6 22.0 copy-start.8
  1071.6 22.0 copy-start.9
  1071.6 22.0 copy-start.10
  1113.4 0.7 copy-start.28
  1113.4 0.7 copy-start.29
  1113.4 0.7 copy-start.36
  1113.4 56.4 %copy-start.18 = (f32[2048]{0:T(1024)S(1)}, f32[2048]{0:T(1024)}, u32[]{:S(2)}) copy-start(f32[2048]{0:T(1024)} %copy-done.17) | copy-start | bytes 24580
  1113.4 56.4 %copy-start.20 = (f32[2,256]{1,0:T(2,128)S(1)}, f32[2,256]{1,0:T(2,128)}, u32[]{:S(2)}) copy-start(f32[2,256]{1,0:T(2,128)} %copy-done.19) | copy-start | bytes 6148
  1119.2 55.9 %copy-start.24 = (f32[2,256]{1,0:T(2,128)S(1)}, f32[2,256]{1,0:T(2,128)}, u32[]{:S(2)}) copy-start(f32[2,256]{1,0:T(2,128)} %copy-done.23) | copy-start | bytes 6148
  1119.2 468.4 %copy-start.22 = (f32[2,256]{1,0:T(2,128)S(1)}, f32[2,256]{1,0:T(2,128)}, u32[]{:S(2)}) copy-start(f32[2,256]{1,0:T(2,128)} %copy-done.21) | copy-start | bytes 6148
  1175.1 496.4 %copy-start.31 = (f32[1024]{0:T(1024)S(1)}, f32[1024]{0:T(1024)}, u32[]{:S(2)}) copy-start(f32[1024]{0:T(1024)} %get-tuple-element.237) | copy-start | bytes 12292
  1692.1 738.0 %copy-start.34 = (f32[256]{0:T(256)}, f32[256]{0:T(256)S(1)}, u32[]{:S(2)}) copy-start(f32[256]{0:T(256)S(1)} %get-tuple-element.482) | copy-start | bytes 3076
  2430.7 6.6 copy-start.14
  2430.7 8.9 copy-start.7
  2437.3 6.6 slice-start
  2439.6 5.6 slice-start.1
Sparse Core Ops, SparseCore 0:
  15.2 92.5 all-gather.2
  109.7 89.8 all-gather.4
  964.5 205.2 reduce-scatter.7
  1173.6 205.2 reduce-scatter.3
  1382.4 205.2 reduce-scatter.5
  1591.8 838.2 all-reduce.6
where the time goes:
time: 2460 us
  waiting for transfers between devices  1290 us (52%)
  matrix products  730 us (30%)
  other arithmetic  248 us (10%)
  blocking collectives  90.4 us (4%)
  local copies, waits for them, and re-layouts  59.9 us (2%)
  loops' own time  25.4 us (1%)
    psum x1, waiting for transfers between devices, body(): lax.psum((qkv_weight_grad, qkv_bias_grad, dense_weight_grad, gain_local,...  732 us
    reduce_scatter x1, waiting for transfers between devices, body(): lax.psum_scatter(perceptron_branch, 'tp', scatter_dimension=1, tiled=True)  209 us
    reduce_scatter x1, waiting for transfers between devices, body(): lax.psum_scatter(attention_part, 'tp', scatter_dimension=1, tiled=True)  204 us
    convert_element_type x4, other arithmetic, backward_block(): score_grad = (soft_weights * (prob_grad - inner_sum)).astype(jnp.bfloat16)  114 us
    dot_general x4, matrix products, backward_block(): jnp.einsum('sqhe,skhe->shqk', grad_block, values_low, preferred_element_t...  106 us
    all_gather x1, waiting for transfers between devices, share_normed(): return lax.all_gather(normed_low, 'tp', axis=1, tiled=True)  89.4 us
    dot_general x4, matrix products, backward_block(): jnp.einsum('shqk,sqhe->skhe', soft_low, grad_block, preferred_element_typ...  73.2 us
    dot_general x4, matrix products, forward_block(): jnp.einsum('sqhe,skhe->shqk', query_block, keys_low, preferred_element_ty...  63.2 us
  transfers between devices with their start and end apart: 6, of which 5 were waited for; matrix products, arithmetic and copies ran while one was open for 17% of the time, Pallas kernels for 0%

commit v1 on v0

v1 whole, which is shorter than its diff:
```python
import functools

import jax
import jax.numpy as jnp
from jax import lax
from jax.experimental import pallas as pl
from jax.experimental.pallas import tpu as pltpu
from jax.sharding import PartitionSpec as P

HD = 64
ROT = 32
epsilon = 1e-05
big_negative = -1e30
rope_base = 10000.0
f32 = jnp.float32
bf16 = jnp.bfloat16
VMEM_LIMIT = 56 << 20


def dot(a, b, ca, cb):
    return lax.dot_general(a, b, (((ca,), (cb,)), ((), ())), preferred_element_type=f32)


def cost(flops, nbytes, trans=0):
    return pl.CostEstimate(flops=int(flops), bytes_accessed=int(nbytes), transcendentals=int(trans))


def params():
    return pltpu.CompilerParams(vmem_limit_bytes=VMEM_LIMIT)


def rope_swap(x):
    width = x.shape[-1]
    lane = lax.broadcasted_iota(jnp.int32, (1, width), 1) % HD
    up = pltpu.roll(x, width - ROT // 2, 1)
    down = pltpu.roll(x, ROT // 2, 1)
    return jnp.where(lane < ROT // 2, up, -down)


def qkv_kernel(x_ref, w_ref, b_ref, c_ref, s_ref, o_ref):
    x = x_ref[...]
    tile = c_ref.shape[-1]
    local = w_ref.shape[-1]
    cosine, sine = c_ref[...], s_ref[...]
    for part in range(3):
        full = dot(x, w_ref[part], 1, 0) + b_ref[part : part + 1, :]
        for at in range(0, local, tile):
            piece = full[:, at : at + tile]
            if part < 2:
                piece = piece * cosine - rope_swap(piece) * sine
            if part == 0:
                piece = piece * (HD**-0.5)
            o_ref[part, :, at : at + tile] = piece.astype(bf16)


def project_qkv(x, w3, bias, cosine, sine, tm=512):
    n, width = x.shape
    local = w3.shape[2]
    tile = cosine.shape[1]
    return pl.pallas_call(
        qkv_kernel,
        grid=(n // tm,),
        in_specs=[
            pl.BlockSpec((tm, width), lambda i: (i, 0)),
            pl.BlockSpec((3, width, local), lambda i: (0, 0, 0)),
            pl.BlockSpec((3, local), lambda i: (0, 0)),
            pl.BlockSpec((tm, tile), lambda i: (i, 0)),
            pl.BlockSpec((tm, tile), lambda i: (i, 0)),
        ],
        out_specs=pl.BlockSpec((3, tm, local), lambda i: (0, i, 0)),
        out_shape=jax.ShapeDtypeStruct((3, n, local), bf16),
        compiler_params=params(),
        cost_estimate=cost(6 * n * width * local, 2 * n * width + 6 * width * local + 6 * n * local),
        name="qkv_rope",
    )(x, w3, bias, cosine, sine)


def hidden_kernel(x_ref, w_ref, b_ref, act_ref, slope_ref):
    x = x_ref[...]
    width = w_ref.shape[1]
    step = min(256, width)
    for at in range(0, width, step):
        h = dot(x, w_ref[:, at : at + step], 1, 0) + b_ref[:, at : at + step]
        square = h * h
        inner = (0.7978845608028654 * h) * (1.0 + 0.044715 * square)
        t = jnp.tanh(inner)
        half = 0.5 + 0.5 * t
        act_ref[:, at : at + step] = (h * half).astype(bf16)
        slope = half + (0.3989422804014327 * h) * (1.0 - t * t) * (1.0 + 0.134145 * square)
        slope_ref[:, at : at + step] = slope.astype(bf16)


def mlp_hidden(x, w, bias, tm=512):
    n, width = x.shape
    units = w.shape[1]
    block = pl.BlockSpec((tm, units), lambda i: (i, 0))
    return pl.pallas_call(
        hidden_kernel,
        grid=(n // tm,),
        in_specs=[
            pl.BlockSpec((tm, width), lambda i: (i, 0)),
            pl.BlockSpec((width, units), lambda i: (0, 0)),
            pl.BlockSpec((1, units), lambda i: (0, 0)),
        ],
        out_specs=[block, block],
        out_shape=[jax.ShapeDtypeStruct((n, units), bf16)] * 2,
        compiler_params=params(),
        cost_estimate=cost(2 * n * width * units, 2 * n * width + 2 * width * units + 4 * n * units, n * units),
        name="mlp_hidden",
    )(x, w, bias)


def grad_in_kernel(g_ref, wo_ref, wd_ref, slope_ref, hg_ref, at_ref, sum_ref):
    g = g_ref[...]
    units = wo_ref.shape[0]
    step = min(256, units)
    ones = jnp.ones((8, g.shape[0]), bf16)

    @pl.when(pl.program_id(0) == 0)
    def _():
        sum_ref[...] = jnp.zeros_like(sum_ref)

    for at in range(0, units, step):
        slope = slope_ref[:, at : at + step].astype(f32)
        hg = (dot(g, wo_ref[at : at + step, :], 1, 1) * slope).astype(bf16)
        hg_ref[:, at : at + step] = hg
        sum_ref[:, at : at + step] += dot(ones, hg, 1, 0)
    at_ref[...] = dot(g, wd_ref[...], 1, 1).astype(bf16)


def grad_in(g, wo, wd, slope, tm=512):
    n, width = g.shape
    units, local = wo.shape[0], wd.shape[0]
    return pl.pallas_call(
        grad_in_kernel,
        grid=(n // tm,),
        in_specs=[
            pl.BlockSpec((tm, width), lambda i: (i, 0)),
            pl.BlockSpec((units, width), lambda i: (0, 0)),
            pl.BlockSpec((local, width), lambda i: (0, 0)),
            pl.BlockSpec((tm, units), lambda i: (i, 0)),
        ],
        out_specs=[
            pl.BlockSpec((tm, units), lambda i: (i, 0)),
            pl.BlockSpec((tm, local), lambda i: (i, 0)),
            pl.BlockSpec((8, units), lambda i: (0, 0)),
        ],
        out_shape=[
            jax.ShapeDtypeStruct((n, units), bf16),
            jax.ShapeDtypeStruct((n, local), bf16),
            jax.ShapeDtypeStruct((8, units), f32),
        ],
        compiler_params=params(),
        cost_estimate=cost(2 * n * width * (units + local), 2 * n * width + 2 * width * (units + local) + 4 * n * units),
        name="grad_in",
    )(g, wo, wd, slope)


def normed_grad_kernel(hg_ref, dq_ref, wi_ref, w3_ref, o_ref, sum_ref):
    @pl.when(pl.program_id(0) == 0)
    def _():
        sum_ref[...] = jnp.zeros_like(sum_ref)

    ones = jnp.ones((8, hg_ref.shape[0]), bf16)
    for part in range(3):
        sum_ref[part] += dot(ones, dq_ref[part], 1, 0)
    width = o_ref.shape[1]
    step = min(512, width)
    for at in range(0, width, step):
        total = dot(hg_ref[...], wi_ref[at : at + step, :], 1, 1)
        for part in range(3):
            total += dot(dq_ref[part], w3_ref[part, at : at + step, :], 1, 1)
        o_ref[:, at : at + step] = total.astype(bf16)


def normed_grad(hg, dqkv, wi, w3, tm=512):
    n, units = hg.shape
    width, local = w3.shape[1:]
    return pl.pallas_call(
        normed_grad_kernel,
        grid=(n // tm,),
        in_specs=[
            pl.BlockSpec((tm, units), lambda i: (i, 0)),
            pl.BlockSpec((3, tm, local), lambda i: (0, i, 0)),
            pl.BlockSpec((width, units), lambda i: (0, 0)),
            pl.BlockSpec((3, width, local), lambda i: (0, 0, 0)),
        ],
        out_specs=[
            pl.BlockSpec((tm, width), lambda i: (i, 0)),
            pl.BlockSpec((3, 8, local), lambda i: (0, 0, 0)),
        ],
        out_shape=[jax.ShapeDtypeStruct((n, width), bf16), jax.ShapeDtypeStruct((3, 8, local), f32)],
        compiler_params=params(),
        cost_estimate=cost(2 * n * width * (units + 3 * local), 2 * n * (width + units + 3 * local) + 2 * width * (units + 3 * local)),
        name="normed_grad",
    )(hg, dqkv, wi, w3)


def attention_kernel(start_ref, q_ref, k_ref, v_ref, do_ref, c_ref, s_ref, o_ref, g_ref, dk_acc, dv_acc, *, bq):
    span, width = q_ref.shape
    lane = lax.broadcasted_iota(jnp.int32, (1, width), 1) // HD
    zero = jnp.zeros((), bf16)

    def turn_back(x, at, n):
        return x * c_ref[at : at + n, :] + rope_swap(x) * s_ref[at : at + n, :]

    for block in range(span // bq):
        at = block * bq
        n = at + bq
        qb = q_ref[at:n, :]
        gb = do_ref[at:n, :]
        keys, vals = k_ref[0:n, :], v_ref[0:n, :]
        key = lax.broadcasted_iota(jnp.int32, (bq, n), 1)
        row = lax.broadcasted_iota(jnp.int32, (bq, n), 0) + at
        allowed = (key >= start_ref[at:n, :]) & (key <= row)
        out = jnp.zeros((bq, width), f32)
        dq = jnp.zeros((bq, width), f32)
        dk = jnp.zeros((n, width), f32)
        dv = jnp.zeros((n, width), f32)
        for head in range(width // HD):
            mine = lane == head
            qh, gh = jnp.where(mine, qb, zero), jnp.where(mine, gb, zero)
            kh, vh = jnp.where(mine, keys, zero), jnp.where(mine, vals, zero)
            scores = jnp.where(allowed, dot(qh, keys, 1, 1), big_negative)
            expd = jnp.exp(scores - jnp.max(scores, axis=1, keepdims=True))
            probs = expd * (1.0 / jnp.sum(expd, axis=1, keepdims=True))
            low = probs.astype(bf16)
            out = out + dot(low, vh, 1, 0)
            prob_grad = dot(gh, vals, 1, 1)
            inner = jnp.sum(probs * prob_grad, axis=1, keepdims=True)
            score_grad = (probs * (prob_grad - inner)).astype(bf16)
            dq = dq + dot(score_grad, kh, 1, 0)
            dk = dk + dot(score_grad, qh, 0, 0)
            dv = dv + dot(low, gh, 0, 0)
        o_ref[at:n, :] = out.astype(bf16)
        g_ref[0, at:n, :] = turn_back(dq * (HD**-0.5), at, bq).astype(bf16)
        if block:
            dk_acc[0:at, :] += dk[0:at]
            dv_acc[0:at, :] += dv[0:at]
        dk_acc[at:n, :] = dk[at:n]
        dv_acc[at:n, :] = dv[at:n]
    g_ref[1] = turn_back(dk_acc[...], 0, span).astype(bf16)
    g_ref[2] = dv_acc[...].astype(bf16)


def attention_both(start, qkv, grad, cosine, sine, span, bq=512):
    n, local = grad.shape
    width = cosine.shape[1]
    bq = min(bq, span)
    part = lambda which: pl.BlockSpec((None, span, width), lambda t, p: (which, t, p))
    table = pl.BlockSpec((span, width), lambda t, p: (t, 0))
    return pl.pallas_call(
        functools.partial(attention_kernel, bq=bq),
        grid=(n // span, local // width),
        in_specs=[
            pl.BlockSpec((span, 1), lambda t, p: (t, 0)),
            part(0),
            part(1),
            part(2),
            pl.BlockSpec((span, width), lambda t, p: (t, p)),
            table,
            table,
        ],
        out_specs=[
            pl.BlockSpec((span, width), lambda t, p: (t, p)),
            pl.BlockSpec((3, span, width), lambda t, p: (0, t, p)),
        ],
        out_shape=[jax.ShapeDtypeStruct((n, local), bf16), jax.ShapeDtypeStruct((3, n, local), bf16)],
        scratch_shapes=[pltpu.VMEM((span, width), f32)] * 2,
        compiler_params=params(),
        cost_estimate=cost(n * span * 0.75 * local * 2 * 6 * 4, 2 * n * local * 9, n * span * local // HD),
        name="attention_both",
    )(start, qkv, qkv, qkv, grad, cosine, sine)


def line_ok(size):
    return size >= 4 and size & (size - 1) == 0


def sum_rows(part, size):
    kind = part.dtype
    if not line_ok(size):
        return lax.psum(part, "rows").astype(kind)
    groups = range(0, size, 4)
    send = lambda a, perm: lax.ppermute(a, "rows", perm)
    add = lambda a, b: (a.astype(f32) + b.astype(f32)).astype(kind)
    part = add(part, send(part, [(g + a, g + b) for g in groups for a, b in ((0, 1), (3, 2))]))
    part = add(part, send(part, [(g + a, g + b) for g in groups for a, b in ((1, 2), (2, 1))]))
    hop = 4
    while hop < size:
        part = add(part, send(part, [(i, i ^ hop) for i in range(size)]))
        hop *= 2
    back = send(part, [(g + a, g + b) for g in groups for a, b in ((1, 0), (2, 3))])
    place = lax.axis_index("rows") % 4
    return jnp.where((place == 1) | (place == 2), part, back)


def sum_tp(part, size):
    if size & (size - 1):
        return lax.psum(part, "tp")
    hop = 1
    while hop < size:
        part = part + lax.ppermute(part, "tp", [(i, i ^ hop) for i in range(size)])
        hop *= 2
    return part


def body(
    tokens,
    segment_ids,
    positions,
    norm_gain,
    norm_shift,
    query_key_value_weight,
    b_qkv,
    dense_weight,
    b_dense,
    inward_weight,
    b_in,
    outward_weight,
    b_out,
    cotangent,
):
    rows, tp = lax.axis_size("rows"), lax.axis_size("tp")
    seqs, here, width = tokens.shape
    length = here * tp
    n = seqs * length
    local = query_key_value_weight.shape[2]
    tile = min(128, local)
    span = length // 2

    values = tokens.astype(f32)
    gain, shift = norm_gain.astype(f32), norm_shift.astype(f32)
    center = values - jnp.mean(values, axis=-1, keepdims=True)
    inverse = lax.rsqrt(jnp.mean(center * center, axis=-1, keepdims=True) + epsilon)
    unit = center * inverse
    normed_low = (unit * gain + shift).astype(bf16)
    gather = lambda a: lax.all_gather(a, "tp", axis=1, tiled=True).reshape(n, width)
    normed = gather(normed_low)
    grad = gather(cotangent)
    dense_full = lax.all_gather(dense_weight, "tp", axis=0, tiled=True)

    half_rot = ROT // 2
    frequency = rope_base ** (-2.0 * jnp.arange(half_rot, dtype=f32) / ROT)
    place = positions.reshape(n, 1)
    angles = place.astype(f32) * frequency
    heads = tile // HD
    rest = HD - ROT
    cosine, sine = jnp.cos(angles), jnp.sin(angles)
    ones, zeros = jnp.ones((n, rest), f32), jnp.zeros((n, rest), f32)
    cosine = jnp.concatenate([cosine, cosine, ones] * heads, axis=1)
    sine = jnp.concatenate([sine, sine, zeros] * heads, axis=1)
    start = jnp.arange(n, dtype=jnp.int32)[:, None] % span - place

    w3 = jnp.transpose(query_key_value_weight, (1, 0, 2))
    qkv = project_qkv(normed, w3, b_qkv.astype(f32), cosine, sine)
    act, slope = mlp_hidden(normed, inward_weight, b_in.astype(f32)[None])

    contract = lambda a, b: dot(a, b, 0, 0).astype(bf16)
    out_wg = sum_rows(contract(act, grad), rows)
    hidden_grad, attended_grad, in_bias = grad_in(grad, outward_weight, dense_weight, slope)
    in_wg = sum_rows(contract(normed, hidden_grad), rows)
    mlp_part = dot(act, outward_weight, 1, 0).astype(bf16).reshape(seqs, length, width)
    mlp_tok = lax.psum_scatter(mlp_part, "tp", scatter_dimension=1, tiled=True)

    attended, dqkv = attention_both(start, qkv, attended_grad, cosine, sine, span)
    mine = lax.all_to_all(attended.reshape(seqs, length, local), "tp", split_axis=1, concat_axis=2, tiled=True)
    part, qkv_bias = normed_grad(hidden_grad, dqkv, inward_weight, w3)
    back_tok = lax.psum_scatter(part.reshape(seqs, length, width), "tp", scatter_dimension=1, tiled=True)
    qkv_wg = jnp.stack([contract(normed, dqkv[i]) for i in range(3)])
    qkv_wg = sum_rows(qkv_wg, rows)
    dense_wg = sum_rows(contract(attended, grad), rows)

    attention = dot(mine.reshape(seqs * here, width), dense_full, 1, 0).reshape(seqs, here, width) + b_dense.astype(f32)
    mlp = mlp_tok.astype(f32) + b_out.astype(f32)
    layer_sum = values + attention + mlp
    layer_out = layer_sum.astype(bf16)
    squares = jnp.stack([jnp.sum(a * a) for a in (values, attention, mlp, layer_sum)])

    bias_cols = lax.dynamic_slice_in_dim(grad, lax.axis_index("tp") * (width // tp), width // tp, 1)
    out_bias = jnp.sum(bias_cols.astype(f32), axis=0)
    units = in_bias.shape[1]
    small = jnp.concatenate([in_bias[0], qkv_bias[:, 0].reshape(-1), out_bias])
    small = sum_rows(small.reshape(-1, 128), rows).reshape(-1)
    in_bias_grad = small[:units]
    qkv_bias_grad = small[units : units + 3 * local].reshape(3, local)
    out_bias_grad = small[units + 3 * local :]

    normed_back = back_tok.astype(f32)
    unit_grad = normed_back * gain
    mean_grad = jnp.mean(unit_grad, axis=-1, keepdims=True)
    mean_both = jnp.mean(unit_grad * unit, axis=-1, keepdims=True)
    value_grad = (unit_grad - mean_grad - unit * mean_both) * inverse
    input_grad = (cotangent.astype(f32) + value_grad).astype(bf16)
    gain_part = jnp.sum(normed_back * unit, axis=(0, 1))
    shift_part = jnp.sum(normed_back, axis=(0, 1))
    pad = jnp.zeros((124,), f32)
    packed = jnp.concatenate([gain_part, shift_part, squares, pad]).reshape(-1, 128)
    packed = sum_rows(sum_tp(packed, tp), rows).reshape(-1)
    slice_at = lambda a: lax.dynamic_slice_in_dim(a, lax.axis_index("tp") * (width // tp), width // tp, 0)
    gain_grad, shift_grad = slice_at(packed[:width]), slice_at(packed[width : 2 * width])
    rms_values = jnp.sqrt(packed[2 * width : 2 * width + 4] / (seqs * rows * length * width))

    return (
        layer_out,
        input_grad,
        gain_grad,
        shift_grad,
        jnp.transpose(qkv_wg.astype(f32), (1, 0, 2)),
        qkv_bias_grad,
        dense_wg.astype(f32),
        out_bias_grad,
        in_wg.astype(f32),
        in_bias_grad,
        out_wg.astype(f32),
        out_bias_grad,
        rms_values,
    )


def solution(mesh):
    in_specs = (
        P("rows", "tp", None),
        P("rows", None),
        P("rows", None),
        P(),
        P(),
        P(None, None, "tp"),
        P(None, "tp"),
        P("tp", None),
        P(),
        P(None, "tp"),
        P("tp"),
        P("tp", None),
        P(),
        P("rows", "tp", None),
    )
    out_specs = (
        P("rows", "tp", None),
        P("rows", "tp", None),
        P("tp"),
        P("tp"),
        P(None, None, "tp"),
        P(None, "tp"),
        P("tp", None),
        P("tp"),
        P(None, "tp"),
        P("tp"),
        P("tp", None),
        P("tp"),
        P(),
    )
    return jax.shard_map(body, mesh=mesh, in_specs=in_specs, out_specs=out_specs, check_vma=False)
```

time: 2460 us -> 1080 us (0.44)
  waiting for transfers between devices: 1290 us -> 557 us
  matrix products: 730 us -> 116 us
  Pallas kernels: 0 us -> 199 us
  other arithmetic: 248 us -> 93.3 us
  blocking collectives: 90.4 us -> 0 us
  starting transfers between devices: 0.65 us -> 46.4 us
  loops' own time: 25.4 us -> 0 us
    psum x1 -> x0, waiting for transfers between devices: 732 us -> none  [body(): lax.psum((qkv_weight_grad, qkv_bias_grad, dense_weight_grad, gain_local,...]
    dot_general x40 -> x8, matrix products: 730 us -> 116 us  [dot(): lax.dot_general(a, b, (((ca,), (cb,)), ((), ())), preferred_element_type=...]
    ppermute x0 -> x21, waiting for transfers between devices: none -> 464 us  [the longest x18 464 us: sum_rows(): send = lambda a, perm: lax.ppermute(a, 'rows', perm)]
    reduce_scatter x3 -> x2, waiting for transfers between devices: 463 us -> 0.03 us  [the longest x1 0.02 us: body(): mlp_tok = lax.psum_scatter(mlp_part, 'tp', scatter_dimension=1, tiled=True)]
    pallas_call x0 -> x5, Pallas kernels: none -> 199 us  [the longest x1 59.4 us: attention_both(): pl.pallas_call(functools.partial(attention_kernel, bq=bq), grid=(n // spa...]
    reduce_sum x10 -> x3, other arithmetic: 85.5 us -> 6.45 us  [the longest x1 2.27 us: body(): jnp.mean(center * center, axis=-1, keepdims=True) + epsilon]
    psum x2 -> x0, blocking collectives: 65.8 us -> none  [the longest x1 45.2 us: body(): total_squares = lax.psum(local_squares, ('rows', 'tp'))]
    convert_element_type x13 -> x18, other arithmetic: 122 us -> 66.1 us  [the longest x8 43.7 us: sum_rows(): add = lambda a, b: (a.astype(f32) + b.astype(f32)).astype(kind)]
  transfers between devices with their start and end apart: 6 -> 27, of which waited for: 5 -> 7; matrix products, arithmetic and copies ran while one was open for 17% -> 23% of each run, Pallas kernels for 0% -> 19%
where the time goes in v1:
time: 1080 us; the launch traced here: 1070 us
  waiting for transfers between devices  557 us (52%)
  Pallas kernels  199 us (18%)
  matrix products  116 us (11%)
  other arithmetic  93.3 us (9%)
  local copies, waits for them, and re-layouts  47.5 us (4%)
  starting transfers between devices  46.4 us (4%)
  between operations  14.7 us (1%)
    ppermute x18, waiting for transfers between devices, sum_rows(): send = lambda a, perm: lax.ppermute(a, 'rows', perm)  464 us
    dot_general x8, matrix products, dot(): lax.dot_general(a, b, (((ca,), (cb,)), ((), ())), preferred_element_type=...  116 us
    all_gather x2, waiting for transfers between devices, body(): lax.all_gather(a, 'tp', axis=1, tiled=True).reshape(n, width)  90.6 us
    pallas_call x1, Pallas kernels, attention_both(): pl.pallas_call(functools.partial(attention_kernel, bq=bq), grid=(n // spa...  59.4 us
    pallas_call x1, Pallas kernels, grad_in(): pl.pallas_call(grad_in_kernel, grid=(n // tm,), in_specs=[pl.BlockSpec((t...  48.9 us
    convert_element_type x8, other arithmetic, sum_rows(): add = lambda a, b: (a.astype(f32) + b.astype(f32)).astype(kind)  43.7 us
    ppermute x18, starting transfers between devices, sum_rows(): send = lambda a, perm: lax.ppermute(a, 'rows', perm)  39.6 us
    pallas_call x1, Pallas kernels, normed_grad(): pl.pallas_call(normed_grad_kernel, grid=(n // tm,), in_specs=[pl.BlockSpe...  38.7 us
  transfers between devices with their start and end apart: 27, of which 7 were waited for; matrix products, arithmetic and copies ran while one was open for 23% of the time, Pallas kernels for 19%

profile of v1, /device:TPU:0, one launch (start us, length us, event | category | flops | bytes accessed | tf_op | source)
XLA Modules:
  0.0 1072.9 jit_solution(3564036220856126002)
XLA Ops:
  8.8 1.9 convert_reduce_fusion
  10.7 2.3 fusion.15
  13.6 2.2 fusion.10
  17.9 90.6 %all-gather.4.cloned.1.call-done = bf16[2,2048,2048]{2,1,0:T(8,128)(2,1)} async-done(((bf16[2,256,2048]{2,1,0:T(8,128)(2,1)}), bf16[2,2048,2048]{2,1,0:T(8,128)(2,1)}) %all-gather.4.cloned.1.call-update) | async-done | bytes 16777232 | tf_op jit(solution)/shard_map/all_gather | solution.py:338
  108.5 31.6 %mlp_hidden.1 = (bf16[4096,1024]{1,0:T(8,128)(2,1)}, bf16[4096,1024]{1,0:T(8,128)(2,1)}) custom-call(bf16[4096,2048]{1,0:T(8,128)(2,1)} %bitcast.100, bf16[2048,1024]{1,0:T(8,128)(2,1)} %wi_ref.1, f32[1,1024]{1,0:T(1,128)} %bitcast.99), custom_call_target="tpu_custom_call" | custom-call | flops 17179869184 | bytes 37748736 | tf_op jit(solution)/shard_map/mlp_hidden/pallas_call | solution.py:97
  140.1 23.6 %convolution_convert_fusion = bf16[4096,2048]{1,0:T(8,128)(2,1)} fusion(bf16[4096,1024]{1,0:T(8,128)(2,1)} %get-tuple-element.25, bf16[1024,2048]{1,0:T(8,128)(2,1)S(1)} %copy-done.20), kind=kOutput, calls=%fused_computation | convolution fusion | flops 17188257792 | bytes 29360128 | tf_op jit(solution)/shard_map/dot_general | solution.py:21
  164.5 2.0 copy.37
  167.1 9.2 multiply_sine_fusion
  176.3 1.5 broadcast_in_dim.10
  177.7 10.8 %concatenate.12.c_ref = f32[4096,128]{1,0:T(8,128)} concatenate(f32[4096,16]{1,0:T(8,128)} %get-tuple-element.46, f32[4096,16]{1,0:T(8,128)} %get-tuple-element.46, f32[4096,32]{1,0:T(8,128)} %broadcast_in_dim.10, f32[4096,16]{1,0:T(8,128)} %get-tuple-element.46, f32[4096,16]{1,0:T(8,128)} %get-tuple-element.46, f32[4096,32]{1,0:T(8,128)} %broadcast_in_dim.10), dimensions={1} | concatenate | bytes 4194304 | tf_op jit(solution)/shard_map/concatenate | solution.py:351
  188.5 1.5 broadcast_in_dim.11
  190.0 7.6 concatenate.13.s_ref
  197.6 3.1 fusion.23.start_ref
  200.7 20.1 %qkv_rope.1.q_ref.k_ref.v_ref = bf16[3,4096,256]{2,1,0:T(8,128)(2,1)} custom-call(bf16[4096,2048]{1,0:T(8,128)(2,1)} %bitcast.101, bf16[3,2048,256]{2,1,0:T(8,128)(2,1)} %bitcast.108, f32[3,256]{1,0:T(4,128)} %convert_element_type.158.b_ref, f32[4096,128]{1,0:T(8,128)} %concatenate.12.c_ref, f32[4096,128]{1,0:T(8,128)} %concatenate.13.s_ref), custom_call_target="tpu_custom_call" | custom-call | flops 12884901888 | bytes 26214400 | tf_op jit(solution)/shard_map/qkv_rope/pallas_call | solution.py:60
  220.8 48.9 %grad_in.1 = (bf16[4096,1024]{1,0:T(8,128)(2,1)}, bf16[4096,256]{1,0:T(8,128)(2,1)}, f32[8,1024]{1,0:T(8,128)}) custom-call(bf16[4096,2048]{1,0:T(8,128)(2,1)} %bitcast.79, bf16[1024,2048]{1,0:T(8,128)(2,1)} %wo_ref.1, bf16[256,2048]{1,0:T(8,128)(2,1)} %wd_ref.1, bf16[4096,1024]{1,0:T(8,128)(2,1)} %get-tuple-element.22.slope_ref), custom_call_target="tpu_custom_call" | custom-call | flops 21474836480 | bytes 38797312 | tf_op jit(solution)/shard_map/grad_in/pallas_call | solution.py:134
  269.6 59.4 %attention_both.1 = (bf16[4096,256]{1,0:T(8,128)(2,1)}, bf16[3,4096,256]{2,1,0:T(8,128)(2,1)}) custom-call(s32[4096,1]{1,0:T(8,128)} %fusion.23.start_ref, bf16[3,4096,256]{2,1,0:T(8,128)(2,1)} %qkv_rope.1.q_ref.k_ref.v_ref, bf16[3,4096,256]{2,1,0:T(8,128)(2,1)} %qkv_rope.1.q_ref.k_ref.v_ref, bf16[3,4096,256]{2,1,0:T(8,128)(2,1)} %qkv_rope.1.q_ref.k_ref.v_ref, ...), custom_call_target="tpu_custom_call" | custom-call | flops 38654705664 | bytes 18874368 | tf_op jit(solution)/shard_map/attention_both/pallas_call | solution.py:252
  329.0 38.7 %normed_grad.1 = (bf16[4096,2048]{1,0:T(8,128)(2,1)}, f32[3,8,256]{2,1,0:T(8,128)}) custom-call(bf16[4096,1024]{1,0:T(8,128)(2,1)} %get-tuple-element.26.hg_ref, bf16[3,4096,256]{2,1,0:T(8,128)(2,1)} %get-tuple-element.27.dq_ref, bf16[2048,1024]{1,0:T(8,128)(2,1)} %wi_ref.1, bf16[3,2048,256]{2,1,0:T(8,128)(2,1)} %bitcast.109), custom_call_target="tpu_custom_call" | custom-call | flops 30064771072 | bytes 38797312 | tf_op jit(solution)/shard_map/normed_grad/pallas_call | solution.py:179
  367.8 11.7 %fusion.22 = bf16[1,2048,256]{2,1,0:T(8,128)(2,1)S(1)} fusion(bf16[4096,2048]{1,0:T(8,128)(2,1)} %bitcast.102, bf16[3,4096,256]{2,1,0:T(8,128)(2,1)} %get-tuple-element.27.dq_ref), kind=kOutput, calls=%fused_computation.54 | convolution fusion | flops 4295491584 | bytes 19922944 | tf_op jit(solution)/shard_map/dot_general | solution.py:21
  379.5 9.6 fusion.21
  390.0 5.2 fusion.20
  396.3 2.1 pad_maximum_fusion
  398.4 4.0 collective-permute-start.6
  402.5 25.9 %convolution_convert_fusion.2 = bf16[2048,1024]{1,0:T(8,128)(2,1)} fusion(bf16[4096,2048]{1,0:T(8,128)(2,1)} %bitcast.104, bf16[4096,1024]{1,0:T(8,128)(2,1)} %get-tuple-element.26.hg_ref), kind=kOutput, calls=%fused_computation.43 | convolution fusion | flops 17181966336 | bytes 29360128 | tf_op jit(solution)/shard_map/dot_general | solution.py:21
  428.4 3.8 collective-permute-start.15
  432.2 20.7 %convolution_convert_fusion.1 = bf16[1024,2048]{1,0:T(8,128)(2,1)} fusion(bf16[4096,1024]{1,0:T(8,128)(2,1)S(1)} %bitcast.113, bf16[4096,2048]{1,0:T(8,128)(2,1)S(1)} %bitcast.83), kind=kOutput, calls=%fused_computation.42 | convolution fusion | flops 17181966336 | bytes 29360128 | tf_op jit(solution)/shard_map/dot_general | solution.py:21
  452.9 3.4 collective-permute-start.18
  456.3 5.8 copy.34
  462.0 4.3 all-to-all-start
  467.9 2.2 convert_reduce_fusion.2
  471.5 3.5 add_convert_fusion.5
  475.0 2.8 collective-permute-start.7
  477.8 83.0 %collective-permute-done.15 = bf16[2048,1024]{1,0:T(8,128)(2,1)} collective-permute-done((bf16[2048,1024]{1,0:T(8,128)(2,1)}, bf16[2048,1024]{1,0:T(8,128)(2,1)}, u32[]{:S(2)}, u32[]{:S(2)}) %collective-permute-start.15) | collective-permute-done | bytes 4194336 | tf_op jit(solution)/shard_map/ppermute | solution.py:285
  560.9 7.6 add_convert_fusion.3
  568.5 2.9 collective-permute-start.16
  571.4 79.1 %collective-permute-done.18 = bf16[1024,2048]{1,0:T(8,128)(2,1)} collective-permute-done((bf16[1024,2048]{1,0:T(8,128)(2,1)}, bf16[1024,2048]{1,0:T(8,128)(2,1)}, u32[]{:S(2)}, u32[]{:S(2)}) %collective-permute-start.18) | collective-permute-done | bytes 4194336 | tf_op jit(solution)/shard_map/ppermute | solution.py:285
  650.5 7.8 add_convert_fusion.1
  658.2 2.9 collective-permute-start.19
  661.1 5.5 convolution_convert_fusion.3
  666.6 6.0 collective-permute-start.12
  673.3 1.3 collective-permute-start.11
  674.7 83.6 %collective-permute-done.11 = f32[16,128]{1,0:T(8,128)S(1)} collective-permute-done((f32[16,128]{1,0:T(8,128)S(1)}, f32[16,128]{1,0:T(8,128)S(1)}, u32[]{:S(2)}, u32[]{:S(2)}) %collective-permute-start.11) | collective-permute-done | bytes 8224 | tf_op jit(solution)/shard_map/ppermute | solution.py:285
  759.5 2.9 add_convert_fusion.7
  762.4 1.6 collective-permute-start.13
  764.1 4.1 copy.40
  768.1 4.2 dot_general.26
  772.3 4.6 add_convert_fusion.4
  776.9 1.5 collective-permute-start.8
  778.4 7.6 add_convert_fusion.2
  787.3 1.9 add_convert_fusion.6
  789.2 1.4 collective-permute-start.14
  790.7 7.8 add_convert_fusion
  799.9 13.6 %multiply_reduce_fusion = (f32[]{:T(128)}, f32[]{:T(128)}, f32[]{:T(128)}, f32[2,256]{1,0:T(2,128)S(1)}, f32[2,256]{1,0:T(2,128)S(1)}, /*index=5*/f32[2048]{0:T(...) fusion(f32[2048]{0:T(1024)S(1)} %convert_element_type.164, ...), kind=kOutput, calls=%fused_computation.38 | convolution fusion | flops 4321176576 | bytes 18923536 | tf_op jit(solution)/shard_map/dot_general | solution.py:21
  813.5 2.7 concatenate.14
  816.2 146.3 %collective-permute-done.14 = bf16[256,2048]{1,0:T(8,128)(2,1)} collective-permute-done((bf16[256,2048]{1,0:T(8,128)(2,1)S(1)}, bf16[256,2048]{1,0:T(8,128)(2,1)}, u32[]{:S(2)}, u32[]{:S(2)}) %collective-permute-start.14) | collective-permute-done | bytes 1048608 | tf_op jit(solution)/shard_map/ppermute | solution.py:285
  962.5 2.7 select_convert_fusion.2
  965.2 1.6 collective-permute-start.1
  966.8 5.0 convert_bitcast_fusion
  972.3 6.1 select_convert_fusion.1
  978.4 1.6 collective-permute-start.3
  980.0 69.4 %collective-permute-done.20 = bf16[1024,2048]{1,0:T(8,128)(2,1)} collective-permute-done((bf16[1024,2048]{1,0:T(8,128)(2,1)}, bf16[1024,2048]{1,0:T(8,128)(2,1)}, u32[]{:S(2)}, u32[]{:S(2)}) %collective-permute-start.20) | collective-permute-done | bytes 4194336 | tf_op jit(solution)/shard_map/ppermute | solution.py:285
  1049.4 6.1 select_convert_fusion
  1056.2 1.3 collective-permute-start.5
  1057.6 3.2 fusion.14
  1060.8 3.0 collective-permute-done.5
  (152 shorter events, 18.5 us)
Async XLA Ops:
  7.2 6.4 copy-start
  7.2 101.3 %all-gather.4.cloned.1.call-start = ((), (), s32[]{:S(2)}) async-start(), calls=%async_computation.3 | async-start | bytes 18874368 | tf_op jit(solution)/shard_map/all_gather | solution.py:338
  8.8 4.3 copy-start.8
  10.7 2.3 copy-start.11
  13.0 0.6 copy-start.13
  13.6 3.7 copy-start.18
  15.8 204.9 %all-gather.6.cloned.1.call-start = ((), (), s32[]{:S(2)}) async-start(), calls=%async_computation.4 | async-start | bytes 18874368 | tf_op jit(solution)/shard_map/all_gather | solution.py:338
  16.6 783.2 %all-gather.8.cloned.1.call-start = ((), (), s32[]{:S(2)}) async-start(), calls=%async_computation.5 | async-start | bytes 9437184 | tf_op jit(solution)/shard_map/all_gather | solution.py:341
  17.3 782.5 %reduce-scatter.3.cloned.1.call-start = ((), (), s32[]{:S(2)}) async-start(), calls=%async_computation.6 | async-start | bytes 18874368 | tf_op jit(solution)/shard_map/reduce_scatter | solution.py:364
  108.5 31.6 %copy-start.20 = (bf16[1024,2048]{1,0:T(8,128)(2,1)S(1)}, bf16[1024,2048]{1,0:T(8,128)(2,1)}, u32[]{:S(2)}) copy-start(bf16[1024,2048]{1,0:T(8,128)(2,1)} %wo_ref.1) | copy-start | bytes 12582916
  163.7 0.7 copy-start.10
  163.7 2.7 copy-start.19
  163.8 636.1 %reduce-scatter.5.cloned.1.call-start = ((), (), s32[]{:S(2)}) async-start(), calls=%async_computation.7 | async-start | bytes 18874368 | tf_op jit(solution)/shard_map/reduce_scatter | solution.py:369
  367.8 11.7 %slice-start.12 = ((s8[6291456]{0:T(1024)(128)(4,1)}), s8[2097152]{0:T(1024)(128)(4,1)S(1)}, s32[]{:S(2)}) async-start(s8[6291456]{0:T(1024)(128)(4,1)} %bitcast.110), calls=%async_computation.20 | async-start | bytes 4194304
  367.8 11.7 %slice-start.13 = ((s8[6291456]{0:T(1024)(128)(4,1)}), s8[4194304]{0:T(1024)(128)(4,1)S(1)}, s32[]{:S(2)}) async-start(s8[6291456]{0:T(1024)(128)(4,1)} %bitcast.110), calls=%async_computation.21 | async-start | bytes 8388608
  367.8 21.4 %slice-start.8 = ((s8[16777216]{0:T(1024)(128)(4,1)}), s8[4194304]{0:T(1024)(128)(4,1)S(1)}, s32[]{:S(2)}) async-start(s8[16777216]{0:T(1024)(128)(4,1)} %bitcast.105), calls=%async_computation.16 | async-start | bytes 8388608
  367.8 21.4 %slice-start.9 = ((s8[16777216]{0:T(1024)(128)(4,1)}), s8[4194304]{0:T(1024)(128)(4,1)S(1)}, s32[]{:S(2)}) async-start(s8[16777216]{0:T(1024)(128)(4,1)} %bitcast.105), calls=%async_computation.17 | async-start | bytes 8388608
  379.5 15.7 %copy-start.3 = (bf16[1,2048,256]{2,1,0:T(8,128)(2,1)}, bf16[1,2048,256]{2,1,0:T(8,128)(2,1)S(1)}, u32[]{:S(2)}) copy-start(bf16[1,2048,256]{2,1,0:T(8,128)(2,1)S(1)} %fusion.22) | copy-start | bytes 3145732
  379.5 9.7 slice-start.10
  379.5 10.4 slice-start.11
  390.0 5.2 copy-start.4
  395.2 1.1 copy-start.5
  396.3 35.9 %slice-start = ((s8[16777216]{0:T(1024)(128)(4,1)}), s8[4194304]{0:T(1024)(128)(4,1)S(1)}, s32[]{:S(2)}) async-start(s8[16777216]{0:T(1024)(128)(4,1)} %bitcast.81), calls=%async_computation.8 | async-start | bytes 8388608
  396.3 35.9 %slice-start.14 = ((s8[8388608]{0:T(1024)(128)(4,1)}), s8[4194304]{0:T(1024)(128)(4,1)S(1)}, s32[]{:S(2)}) async-start(s8[8388608]{0:T(1024)(128)(4,1)} %bitcast.112), calls=%async_computation.22 | async-start | bytes 8388608
  398.4 33.8 %slice-start.1 = ((s8[16777216]{0:T(1024)(128)(4,1)}), s8[4194304]{0:T(1024)(128)(4,1)S(1)}, s32[]{:S(2)}) async-start(s8[16777216]{0:T(1024)(128)(4,1)} %bitcast.81), calls=%async_computation.9 | async-start | bytes 8388608
  398.4 33.8 %slice-start.2 = ((s8[16777216]{0:T(1024)(128)(4,1)}), s8[4194304]{0:T(1024)(128)(4,1)S(1)}, s32[]{:S(2)}) async-start(s8[16777216]{0:T(1024)(128)(4,1)} %bitcast.81), calls=%async_computation.10 | async-start | bytes 8388608
  398.4 33.8 %slice-start.3 = ((s8[16777216]{0:T(1024)(128)(4,1)}), s8[4194304]{0:T(1024)(128)(4,1)S(1)}, s32[]{:S(2)}) async-start(s8[16777216]{0:T(1024)(128)(4,1)} %bitcast.81), calls=%async_computation.11 | async-start | bytes 8388608
  398.4 33.8 %slice-start.15 = ((s8[8388608]{0:T(1024)(128)(4,1)}), s8[4194304]{0:T(1024)(128)(4,1)S(1)}, s32[]{:S(2)}) async-start(s8[8388608]{0:T(1024)(128)(4,1)} %bitcast.112), calls=%async_computation.23 | async-start | bytes 8388608
  398.4 73.0 %collective-permute-start.6 = (bf16[3,2048,256]{2,1,0:T(8,128)(2,1)}, bf16[3,2048,256]{2,1,0:T(8,128)(2,1)S(1)}, u32[]{:S(2)}, u32[]{:S(2)}) collective-permute-start(bf16[3,2048,256]{2,1,0:T(8,128)(2,1)} %pad_maximum_fusion), channel_id=1, source_target_pairs={{0,8},{24,16},{1,9},{25,17},{2,10},{26,18},{3,11},{27,19},{4,12},{... | collective-permute-start | bytes 9437192 | tf_op jit(solution)/shard_map/ppermute | solution.py:285
  428.4 132.5 %collective-permute-start.15 = (bf16[2048,1024]{1,0:T(8,128)(2,1)}, bf16[2048,1024]{1,0:T(8,128)(2,1)}, u32[]{:S(2)}, u32[]{:S(2)}) collective-permute-start(bf16[2048,1024]{1,0:T(8,128)(2,1)} %convolution_convert_fusion.2), channel_id=1, source_target_pairs={{0,8},{24,16},{1,9},{25,17},{2,10},{26,18},{3,11},{27,19},{4,12},{... | collective-permute-start | bytes 12582920 | tf_op jit(solution)/shard_map/ppermute | solution.py:285
  452.9 197.6 %collective-permute-start.18 = (bf16[1024,2048]{1,0:T(8,128)(2,1)}, bf16[1024,2048]{1,0:T(8,128)(2,1)}, u32[]{:S(2)}, u32[]{:S(2)}) collective-permute-start(bf16[1024,2048]{1,0:T(8,128)(2,1)} %convolution_convert_fusion.1), channel_id=1, source_target_pairs={{0,8},{24,16},{1,9},{25,17},{2,10},{26,18},{3,11},{27,19},{4,12},{... | collective-permute-start | bytes 12582920 | tf_op jit(solution)/shard_map/ppermute | solution.py:285
  462.0 302.0 %all-to-all-start = ((bf16[2,2048,256]{2,0,1:T(2,128)(2,1)}), bf16[2,2048,256]{2,0,1:T(2,128)(2,1)}, u32[]{:S(2)}, u32[]{:S(2)}) async-start(bf16[2,2048,256]{2,0,1:T(2,128)(2,1)} %copy.34), calls=%async_computation | async-start | bytes 4194304 | tf_op jit(solution)/shard_map/all_to_all | solution.py:367
  470.2 202.5 %collective-permute-start.9 = (f32[16,128]{1,0:T(8,128)S(1)}, f32[16,128]{1,0:T(8,128)S(1)}, u32[]{:S(2)}, u32[]{:S(2)}) collective-permute-start(f32[16,128]{1,0:T(8,128)S(1)} %maximum_bitcast_fusion), channel_id=1, source_target_pairs={{0,8},{24,16},{1,9},{25,17},{2,10},{26,18},{3,11},{27,19},{4,12},{... | collective-permute-start | bytes 24584 | tf_op jit(solution)/shard_map/ppermute | solution.py:285
  471.5 189.6 %slice-start.4 = ((s8[16777216]{0:T(1024)(128)(4,1)}), s8[4194304]{0:T(1024)(128)(4,1)S(1)}, s32[]{:S(2)}) async-start(s8[16777216]{0:T(1024)(128)(4,1)} %bitcast.84), calls=%async_computation.12 | async-start | bytes 8388608
  471.5 189.6 %slice-start.5 = ((s8[16777216]{0:T(1024)(128)(4,1)}), s8[4194304]{0:T(1024)(128)(4,1)S(1)}, s32[]{:S(2)}) async-start(s8[16777216]{0:T(1024)(128)(4,1)} %bitcast.84), calls=%async_computation.13 | async-start | bytes 8388608
  475.0 186.1 %slice-start.6 = ((s8[16777216]{0:T(1024)(128)(4,1)}), s8[4194304]{0:T(1024)(128)(4,1)S(1)}, s32[]{:S(2)}) async-start(s8[16777216]{0:T(1024)(128)(4,1)} %bitcast.84), calls=%async_computation.14 | async-start | bytes 8388608
  475.0 297.3 %collective-permute-start.7 = (bf16[3,2048,256]{2,1,0:T(8,128)(2,1)}, bf16[3,2048,256]{2,1,0:T(8,128)(2,1)}, u32[]{:S(2)}, u32[]{:S(2)}) collective-permute-start(bf16[3,2048,256]{2,1,0:T(8,128)(2,1)} %add_convert_fusion.5), channel_id=1, source_target_pairs={{8,16},{16,8},{9,17},{17,9},{10,18},{18,10},{11,19},{19,11},{12,20... | collective-permute-start | bytes 9437192 | tf_op jit(solution)/shard_map/ppermute | solution.py:285
  568.4 92.7 %slice-start.7 = ((s8[16777216]{0:T(1024)(128)(4,1)}), s8[4194304]{0:T(1024)(128)(4,1)S(1)}, s32[]{:S(2)}) async-start(s8[16777216]{0:T(1024)(128)(4,1)} %bitcast.84), calls=%async_computation.15 | async-start | bytes 8388608
  568.5 92.7 %copy-start.2 = (bf16[4096,256]{1,0:T(8,128)(2,1)S(1)}, bf16[4096,256]{1,0:T(8,128)(2,1)}, u32[]{:S(2)}) copy-start(bf16[4096,256]{1,0:T(8,128)(2,1)} %get-tuple-element.24) | copy-start | bytes 6291460
  568.5 209.9 %collective-permute-start.16 = (bf16[2048,1024]{1,0:T(8,128)(2,1)}, bf16[2048,1024]{1,0:T(8,128)(2,1)}, u32[]{:S(2)}, u32[]{:S(2)}) collective-permute-start(bf16[2048,1024]{1,0:T(8,128)(2,1)} %add_convert_fusion.3), channel_id=1, source_target_pairs={{8,16},{16,8},{9,17},{17,9},{10,18},{18,10},{11,19},{19,11},{12,20... | collective-permute-start | bytes 12582920 | tf_op jit(solution)/shard_map/ppermute | solution.py:285
  658.2 16.4 %copy-start.15 = (bf16[2048]{0:T(1024)(128)(2,1)S(1)}, bf16[2048]{0:T(1024)(128)(2,1)}, u32[]{:S(2)}) copy-start(bf16[2048]{0:T(1024)(128)(2,1)} %param.25) | copy-start | bytes 12292
  658.2 16.4 %copy-start.16 = (bf16[2048]{0:T(1024)(128)(2,1)S(1)}, bf16[2048]{0:T(1024)(128)(2,1)}, u32[]{:S(2)}) copy-start(bf16[2048]{0:T(1024)(128)(2,1)} %param.21) | copy-start | bytes 12292
  658.2 132.4 %collective-permute-start.19 = (bf16[1024,2048]{1,0:T(8,128)(2,1)}, bf16[1024,2048]{1,0:T(8,128)(2,1)}, u32[]{:S(2)}, u32[]{:S(2)}) collective-permute-start(bf16[1024,2048]{1,0:T(8,128)(2,1)} %add_convert_fusion.1), channel_id=1, source_target_pairs={{8,16},{16,8},{9,17},{17,9},{10,18},{18,10},{11,19},{19,11},{12,20... | collective-permute-start | bytes 12582920 | tf_op jit(solution)/shard_map/ppermute | solution.py:285
  666.6 92.9 %collective-permute-start.12 = (bf16[256,2048]{1,0:T(8,128)(2,1)}, bf16[256,2048]{1,0:T(8,128)(2,1)}, u32[]{:S(2)}, u32[]{:S(2)}) collective-permute-start(bf16[256,2048]{1,0:T(8,128)(2,1)} %convolution_convert_fusion.3), channel_id=1, source_target_pairs={{0,8},{24,16},{1,9},{25,17},{2,10},{26,18},{3,11},{27,19},{4,12},{... | collective-permute-start | bytes 3145736 | tf_op jit(solution)/shard_map/ppermute | solution.py:285
  672.6 0.7 collective-permute-start.10
  673.3 84.9 %collective-permute-start.11 = (f32[16,128]{1,0:T(8,128)S(1)}, f32[16,128]{1,0:T(8,128)S(1)}, u32[]{:S(2)}, u32[]{:S(2)}) collective-permute-start(f32[16,128]{1,0:T(8,128)S(1)} %fusion.49), channel_id=1, source_target_pairs={{8,0},{16,24},{9,1},{17,25},{10,2},{18,26},{11,3},{19,27},{12,4},{... | collective-permute-start | bytes 24584 | tf_op jit(solution)/shard_map/ppermute | solution.py:285
  758.9 306.7 %copy-start.17 = (f32[256]{0:T(256)}, f32[256]{0:T(256)S(1)}, u32[]{:S(2)}) copy-start(f32[256]{0:T(256)S(1)} %slice_bitcast_fusion.3) | copy-start | bytes 3076
  762.4 24.8 %collective-permute-start.13 = (bf16[256,2048]{1,0:T(8,128)(2,1)}, bf16[256,2048]{1,0:T(8,128)(2,1)}, u32[]{:S(2)}, u32[]{:S(2)}) collective-permute-start(bf16[256,2048]{1,0:T(8,128)(2,1)} %add_convert_fusion.7), channel_id=1, source_target_pairs={{8,16},{16,8},{9,17},{17,9},{10,18},{18,10},{11,19},{19,11},{12,20... | collective-permute-start | bytes 3145736 | tf_op jit(solution)/shard_map/ppermute | solution.py:285
  776.9 189.9 %collective-permute-start.8 = (bf16[3,2048,256]{2,1,0:T(8,128)(2,1)}, bf16[3,2048,256]{2,1,0:T(8,128)(2,1)}, u32[]{:S(2)}, u32[]{:S(2)}) collective-permute-start(bf16[3,2048,256]{2,1,0:T(8,128)(2,1)} %add_convert_fusion.4), channel_id=1, source_target_pairs={{8,0},{16,24},{9,1},{17,25},{10,2},{18,26},{11,3},{19,27},{12,4},{... | collective-permute-start | bytes 9437192 | tf_op jit(solution)/shard_map/ppermute | solution.py:285
  786.0 186.3 %collective-permute-start.17 = (bf16[2048,1024]{1,0:T(8,128)(2,1)}, bf16[2048,1024]{1,0:T(8,128)(2,1)}, u32[]{:S(2)}, u32[]{:S(2)}) collective-permute-start(bf16[2048,1024]{1,0:T(8,128)(2,1)} %add_convert_fusion.2), channel_id=1, source_target_pairs={{8,0},{16,24},{9,1},{17,25},{10,2},{18,26},{11,3},{19,27},{12,4},{... | collective-permute-start | bytes 12582920 | tf_op jit(solution)/shard_map/ppermute | solution.py:285
  789.2 10.6 copy-start.1
  789.2 10.6 copy-start.9
  789.2 10.6 copy-start.12
  789.2 10.6 copy-start.14
  789.2 173.3 %collective-permute-start.14 = (bf16[256,2048]{1,0:T(8,128)(2,1)S(1)}, bf16[256,2048]{1,0:T(8,128)(2,1)}, u32[]{:S(2)}, u32[]{:S(2)}) collective-permute-start(bf16[256,2048]{1,0:T(8,128)(2,1)S(1)} %add_convert_fusion.6), channel_id=1, source_target_pairs={{8,0},{16,24},{9,1},{17,25},{10,2},{18,26},{11,3},{19,27},{12,4},{... | collective-permute-start | bytes 3145736 | tf_op jit(solution)/shard_map/ppermute | solution.py:285
  798.5 250.9 %collective-permute-start.20 = (bf16[1024,2048]{1,0:T(8,128)(2,1)}, bf16[1024,2048]{1,0:T(8,128)(2,1)}, u32[]{:S(2)}, u32[]{:S(2)}) collective-permute-start(bf16[1024,2048]{1,0:T(8,128)(2,1)} %add_convert_fusion), channel_id=1, source_target_pairs={{8,0},{16,24},{9,1},{17,25},{10,2},{18,26},{11,3},{19,27},{12,4},{... | collective-permute-start | bytes 12582920 | tf_op jit(solution)/shard_map/ppermute | solution.py:285
  816.1 149.0 %collective-permute-start = (f32[33,128]{1,0:T(8,128)S(1)}, f32[33,128]{1,0:T(8,128)S(1)}, u32[]{:S(2)}, u32[]{:S(2)}) collective-permute-start(f32[33,128]{1,0:T(8,128)S(1)} %bitcast.91), channel_id=1, source_target_pairs={{0,1},{1,0},{2,3},{3,2},{4,5},{5,4},{6,7},{7,6},{8,9},{9,8},{10,11... | collective-permute-start | bytes 50696 | tf_op jit(solution)/shard_map/ppermute | solution.py:303
  965.2 6.6 collective-permute-start.1
  971.8 6.6 collective-permute-start.2
  978.4 79.1 %copy-start.6 = (bf16[2,256,2048]{2,1,0:T(8,128)(2,1)S(1)}, bf16[2,256,2048]{2,1,0:T(8,128)(2,1)}, u32[]{:S(2)}) copy-start(bf16[2,256,2048]{2,1,0:T(8,128)(2,1)} %param.26) | copy-start | bytes 6291460
  978.4 79.1 %copy-start.7 = (bf16[2,256,2048]{2,1,0:T(8,128)(2,1)S(1)}, bf16[2,256,2048]{2,1,0:T(8,128)(2,1)}, u32[]{:S(2)}) copy-start(bf16[2,256,2048]{2,1,0:T(8,128)(2,1)} %reduce-scatter.5.cloned.1.call-done) | copy-start | bytes 6291460
  978.4 77.1 %collective-permute-start.3 = (f32[33,128]{1,0:T(8,128)S(1)}, f32[33,128]{1,0:T(8,128)S(1)}, u32[]{:S(2)}, u32[]{:S(2)}) collective-permute-start(f32[33,128]{1,0:T(8,128)S(1)} %add.136), channel_id=1, source_target_pairs={{0,8},{24,16},{1,9},{25,17},{2,10},{26,18},{3,11},{27,19},{4,12},{... | collective-permute-start | bytes 50696 | tf_op jit(solution)/shard_map/ppermute | solution.py:285
  1055.5 0.7 collective-permute-start.4
  1056.2 7.5 collective-permute-start.5
Sparse Core Ops, SparseCore 0:
  15.9 92.5 all-gather.3
  110.4 89.8 all-gather.5
  202.2 54.3 all-gather.7
  260.1 115.9 reduce-scatter.2
  379.5 136.4 reduce-scatter.4

commit v2 on v1

v2 whole, which is shorter than its diff:
```python
import functools

import jax
import jax.numpy as jnp
from jax import lax
from jax.experimental import pallas as pl
from jax.experimental.pallas import tpu as pltpu
from jax.sharding import PartitionSpec as P

HD = 64
ROT = 32
epsilon = 1e-05
big_negative = -1e30
rope_base = 10000.0
f32 = jnp.float32
bf16 = jnp.bfloat16
VMEM_LIMIT = 56 << 20
FINISH_WEIGHT = int(1.45e11)


def dot(a, b, ca, cb):
    return lax.dot_general(a, b, (((ca,), (cb,)), ((), ())), preferred_element_type=f32)


SMALL = pl.CostEstimate(flops=1, bytes_accessed=1, transcendentals=0)


def params():
    return pltpu.CompilerParams(vmem_limit_bytes=VMEM_LIMIT)


class Order:
    def __init__(self):
        self.last = ()

    def __call__(self, op, *operands):
        operands, _ = lax.optimization_barrier((operands, self.last))
        result = op(*operands)
        self.last = jax.tree.leaves(result)
        return result


def rope_swap(x):
    width = x.shape[-1]
    lane = lax.broadcasted_iota(jnp.int32, (1, width), 1) % HD
    up = pltpu.roll(x, width - ROT // 2, 1)
    down = pltpu.roll(x, ROT // 2, 1)
    return jnp.where(lane < ROT // 2, up, -down)


def qkv_kernel(x_ref, w_ref, b_ref, c_ref, s_ref, o_ref):
    x = x_ref[...]
    tile = c_ref.shape[-1]
    local = w_ref.shape[-1]
    cosine, sine = c_ref[...], s_ref[...]
    for part in range(3):
        full = dot(x, w_ref[part], 1, 0) + b_ref[part : part + 1, :]
        for at in range(0, local, tile):
            piece = full[:, at : at + tile]
            if part < 2:
                piece = piece * cosine - rope_swap(piece) * sine
            if part == 0:
                piece = piece * (HD**-0.5)
            o_ref[part, :, at : at + tile] = piece.astype(bf16)


def project_qkv(x, w3, bias, cosine, sine, tm=512):
    n, width = x.shape
    local = w3.shape[2]
    tile = cosine.shape[1]
    return pl.pallas_call(
        qkv_kernel,
        grid=(n // tm,),
        in_specs=[
            pl.BlockSpec((tm, width), lambda i: (i, 0)),
            pl.BlockSpec((3, width, local), lambda i: (0, 0, 0)),
            pl.BlockSpec((3, local), lambda i: (0, 0)),
            pl.BlockSpec((tm, tile), lambda i: (i, 0)),
            pl.BlockSpec((tm, tile), lambda i: (i, 0)),
        ],
        out_specs=pl.BlockSpec((3, tm, local), lambda i: (0, i, 0)),
        out_shape=jax.ShapeDtypeStruct((3, n, local), bf16),
        compiler_params=params(),
        cost_estimate=SMALL,
        name="qkv_rope",
    )(x, w3, bias, cosine, sine)


def hidden_kernel(x_ref, w_ref, b_ref, act_ref, slope_ref):
    x = x_ref[...]
    width = w_ref.shape[1]
    step = min(256, width)
    for at in range(0, width, step):
        h = dot(x, w_ref[:, at : at + step], 1, 0) + b_ref[:, at : at + step]
        square = h * h
        inner = (0.7978845608028654 * h) * (1.0 + 0.044715 * square)
        t = jnp.tanh(inner)
        half = 0.5 + 0.5 * t
        act_ref[:, at : at + step] = (h * half).astype(bf16)
        slope = half + (0.3989422804014327 * h) * (1.0 - t * t) * (1.0 + 0.134145 * square)
        slope_ref[:, at : at + step] = slope.astype(bf16)


def mlp_hidden(x, w, bias, tm=512):
    n, width = x.shape
    units = w.shape[1]
    block = pl.BlockSpec((tm, units), lambda i: (i, 0))
    return pl.pallas_call(
        hidden_kernel,
        grid=(n // tm,),
        in_specs=[
            pl.BlockSpec((tm, width), lambda i: (i, 0)),
            pl.BlockSpec((width, units), lambda i: (0, 0)),
            pl.BlockSpec((1, units), lambda i: (0, 0)),
        ],
        out_specs=[block, block],
        out_shape=[jax.ShapeDtypeStruct((n, units), bf16)] * 2,
        compiler_params=params(),
        cost_estimate=SMALL,
        name="mlp_hidden",
    )(x, w, bias)


def grad_in_kernel(g_ref, wo_ref, wd_ref, slope_ref, hg_ref, at_ref, sum_ref):
    g = g_ref[...]
    units = wo_ref.shape[0]
    step = min(256, units)

    @pl.when(pl.program_id(0) == 0)
    def _():
        sum_ref[...] = jnp.zeros_like(sum_ref)

    for at in range(0, units, step):
        slope = slope_ref[:, at : at + step].astype(f32)
        hg = (dot(g, wo_ref[at : at + step, :], 1, 1) * slope).astype(bf16)
        hg_ref[:, at : at + step] = hg
        sum_ref[0:1, at : at + step] += jnp.sum(hg.astype(f32), axis=0, keepdims=True)
    at_ref[...] = dot(g, wd_ref[...], 1, 1).astype(bf16)


def grad_in(g, wo, wd, slope, tm=512):
    n, width = g.shape
    units, local = wo.shape[0], wd.shape[0]
    return pl.pallas_call(
        grad_in_kernel,
        grid=(n // tm,),
        in_specs=[
            pl.BlockSpec((tm, width), lambda i: (i, 0)),
            pl.BlockSpec((units, width), lambda i: (0, 0)),
            pl.BlockSpec((local, width), lambda i: (0, 0)),
            pl.BlockSpec((tm, units), lambda i: (i, 0)),
        ],
        out_specs=[
            pl.BlockSpec((tm, units), lambda i: (i, 0)),
            pl.BlockSpec((tm, local), lambda i: (i, 0)),
            pl.BlockSpec((8, units), lambda i: (0, 0)),
        ],
        out_shape=[
            jax.ShapeDtypeStruct((n, units), bf16),
            jax.ShapeDtypeStruct((n, local), bf16),
            jax.ShapeDtypeStruct((8, units), f32),
        ],
        compiler_params=params(),
        cost_estimate=SMALL,
        name="grad_in",
    )(g, wo, wd, slope)


def tokens_kernel(x_ref, w_ref, o_ref):
    width = w_ref.shape[1]
    step = min(512, width)
    for at in range(0, width, step):
        o_ref[:, at : at + step] = dot(x_ref[...], w_ref[:, at : at + step], 1, 0).astype(o_ref.dtype)


def tokens_by_weight(x, w, tm=512):
    n, depth = x.shape
    width = w.shape[1]
    return pl.pallas_call(
        tokens_kernel,
        grid=(n // tm,),
        in_specs=[pl.BlockSpec((tm, depth), lambda i: (i, 0)), pl.BlockSpec((depth, width), lambda i: (0, 0))],
        out_specs=pl.BlockSpec((tm, width), lambda i: (i, 0)),
        out_shape=jax.ShapeDtypeStruct((n, width), bf16),
        compiler_params=params(),
        cost_estimate=SMALL,
        name="tokens_by_weight",
    )(x, w)


def weight_grad_kernel(a_ref, b_ref, *o_refs):
    full = dot(a_ref[...], b_ref[...], 0, 0).astype(bf16)
    high = full.shape[0] // len(o_refs)
    for i, o_ref in enumerate(o_refs):
        o_ref[...] = full[i * high : (i + 1) * high]


def weight_grad(a, b, pieces, tile=512):
    n, rows = a.shape
    cols = b.shape[1]
    tile = min(tile, cols)
    high = rows // pieces
    return pl.pallas_call(
        weight_grad_kernel,
        grid=(cols // tile,),
        in_specs=[
            pl.BlockSpec((n, rows), lambda j: (0, 0), pipeline_mode=pl.Buffered(1)),
            pl.BlockSpec((n, tile), lambda j: (0, j)),
        ],
        out_specs=[pl.BlockSpec((high, tile), lambda j: (0, j))] * pieces,
        out_shape=[jax.ShapeDtypeStruct((high, cols), bf16)] * pieces,
        compiler_params=params(),
        cost_estimate=SMALL,
        name="weight_grad",
    )(a, b)


def weight_grad_rows_kernel(a_ref, b_ref, *o_refs, counts):
    full = dot(a_ref[...], b_ref[...], 0, 0).astype(bf16)
    step = pl.program_id(0)
    first = 0
    for o_ref, count in zip(o_refs, counts):

        @pl.when((step >= first) & (step < first + count))
        def _(o_ref=o_ref):
            o_ref[...] = full

        first += count


def weight_grad_rows(a, b, shares, tile=512):
    n, rows = a.shape
    cols = b.shape[1]
    counts = [rows * share // sum(shares) // tile for share in shares]
    firsts = [sum(counts[:i]) for i in range(len(counts))]
    out = lambda i: pl.BlockSpec((tile, cols), lambda j: (jnp.clip(j - firsts[i], 0, counts[i] - 1), 0))
    return pl.pallas_call(
        functools.partial(weight_grad_rows_kernel, counts=counts),
        grid=(rows // tile,),
        in_specs=[
            pl.BlockSpec((n, tile), lambda j: (0, j)),
            pl.BlockSpec((n, cols), lambda j: (0, 0), pipeline_mode=pl.Buffered(1)),
        ],
        out_specs=[out(i) for i in range(len(counts))],
        out_shape=[jax.ShapeDtypeStruct((count * tile, cols), bf16) for count in counts],
        compiler_params=params(),
        cost_estimate=SMALL,
        name="weight_grad_rows",
    )(a, b)


def weight_grad_parts_kernel(a_ref, b_ref, *o_refs):
    for part, o_ref in enumerate(o_refs):
        o_ref[...] = dot(a_ref[...], b_ref[part], 0, 0).astype(bf16)


def weight_grad_parts(a, b, tile=512):
    n, rows = a.shape
    parts, _, cols = b.shape
    return pl.pallas_call(
        weight_grad_parts_kernel,
        grid=(rows // tile,),
        in_specs=[
            pl.BlockSpec((n, tile), lambda j: (0, j)),
            pl.BlockSpec((parts, n, cols), lambda j: (0, 0, 0), pipeline_mode=pl.Buffered(1)),
        ],
        out_specs=[pl.BlockSpec((tile, cols), lambda j: (j, 0))] * parts,
        out_shape=[jax.ShapeDtypeStruct((rows, cols), bf16)] * parts,
        compiler_params=params(),
        cost_estimate=SMALL,
        name="weight_grad_parts",
    )(a, b)


def normed_grad_kernel(hg_ref, dq_ref, wi_ref, w3_ref, x_ref, shift_ref, o_ref, sum_ref, norm_ref):
    @pl.when(pl.program_id(0) == 0)
    def _():
        sum_ref[...] = jnp.zeros_like(sum_ref)
        norm_ref[...] = jnp.zeros_like(norm_ref)

    for part in range(3):
        sum_ref[part, 0:1] += jnp.sum(dq_ref[part].astype(f32), axis=0, keepdims=True)
    width = o_ref.shape[1]
    step = min(512, width)
    for at in range(0, width, step):
        cut = slice(at, at + step)
        total = dot(hg_ref[...], wi_ref[cut, :], 1, 1)
        for part in range(3):
            total += dot(dq_ref[part], w3_ref[part, cut, :], 1, 1)
        o_ref[:, cut] = total.astype(bf16)
        scaled = x_ref[:, cut].astype(f32) - shift_ref[:, cut]
        norm_ref[0:1, cut] += jnp.sum(total * scaled, axis=0, keepdims=True)
        norm_ref[1:2, cut] += jnp.sum(total, axis=0, keepdims=True)


def normed_grad(hg, dqkv, wi, w3, x, shift, tm=512):
    n, units = hg.shape
    width, local = w3.shape[1:]
    return pl.pallas_call(
        normed_grad_kernel,
        grid=(n // tm,),
        in_specs=[
            pl.BlockSpec((tm, units), lambda i: (i, 0)),
            pl.BlockSpec((3, tm, local), lambda i: (0, i, 0)),
            pl.BlockSpec((width, units), lambda i: (0, 0)),
            pl.BlockSpec((3, width, local), lambda i: (0, 0, 0)),
            pl.BlockSpec((tm, width), lambda i: (i, 0)),
            pl.BlockSpec((1, width), lambda i: (0, 0)),
        ],
        out_specs=[
            pl.BlockSpec((tm, width), lambda i: (i, 0)),
            pl.BlockSpec((3, 8, local), lambda i: (0, 0, 0)),
            pl.BlockSpec((8, width), lambda i: (0, 0)),
        ],
        out_shape=[
            jax.ShapeDtypeStruct((n, width), bf16),
            jax.ShapeDtypeStruct((3, 8, local), f32),
            jax.ShapeDtypeStruct((8, width), f32),
        ],
        compiler_params=params(),
        cost_estimate=SMALL,
        name="normed_grad",
    )(hg, dqkv, wi, w3, x, shift)


def attention_kernel(start_ref, q_ref, k_ref, v_ref, do_ref, c_ref, s_ref, o_ref, by_owner_ref, g_ref, dk_acc, dv_acc, *, bq):
    span, width = q_ref.shape
    lane = lax.broadcasted_iota(jnp.int32, (1, width), 1) // HD
    zero = jnp.zeros((), bf16)

    def turn_back(x, at, n):
        return x * c_ref[at : at + n, :] + rope_swap(x) * s_ref[at : at + n, :]

    for block in range(span // bq):
        at = block * bq
        n = at + bq
        qb = q_ref[at:n, :]
        gb = do_ref[at:n, :]
        keys, vals = k_ref[0:n, :], v_ref[0:n, :]
        key = lax.broadcasted_iota(jnp.int32, (bq, n), 1)
        row = lax.broadcasted_iota(jnp.int32, (bq, n), 0) + at
        allowed = (key >= start_ref[at:n, :]) & (key <= row)
        out = jnp.zeros((bq, width), f32)
        dq = jnp.zeros((bq, width), f32)
        dk = jnp.zeros((n, width), f32)
        dv = jnp.zeros((n, width), f32)
        for head in range(width // HD):
            mine = lane == head
            qh, gh = jnp.where(mine, qb, zero), jnp.where(mine, gb, zero)
            kh, vh = jnp.where(mine, keys, zero), jnp.where(mine, vals, zero)
            scores = jnp.where(allowed, dot(qh, keys, 1, 1), big_negative)
            expd = jnp.exp(scores - jnp.max(scores, axis=1, keepdims=True))
            probs = expd * (1.0 / jnp.sum(expd, axis=1, keepdims=True))
            low = probs.astype(bf16)
            out = out + dot(low, vh, 1, 0)
            prob_grad = dot(gh, vals, 1, 1)
            inner = jnp.sum(probs * prob_grad, axis=1, keepdims=True)
            score_grad = (probs * (prob_grad - inner)).astype(bf16)
            dq = dq + dot(score_grad, kh, 1, 0)
            dk = dk + dot(score_grad, qh, 0, 0)
            dv = dv + dot(low, gh, 0, 0)
        out = out.astype(bf16)
        o_ref[at:n, :] = out
        here = by_owner_ref.shape[1]
        for own in range(bq // here):
            by_owner_ref[at // here + own] = out[own * here : (own + 1) * here]
        g_ref[0, at:n, :] = turn_back(dq * (HD**-0.5), at, bq).astype(bf16)
        if block:
            dk_acc[0:at, :] += dk[0:at]
            dv_acc[0:at, :] += dv[0:at]
        dk_acc[at:n, :] = dk[at:n]
        dv_acc[at:n, :] = dv[at:n]
    g_ref[1] = turn_back(dk_acc[...], 0, span).astype(bf16)
    g_ref[2] = dv_acc[...].astype(bf16)


def attention_both(start, qkv, grad, cosine, sine, span, owners, bq=512):
    n, local = grad.shape
    here = 2 * span // owners
    width = cosine.shape[1]
    bq = min(bq, span)
    part = lambda which: pl.BlockSpec((None, span, width), lambda t, p: (which, t, p))
    table = pl.BlockSpec((span, width), lambda t, p: (t, 0))
    return pl.pallas_call(
        functools.partial(attention_kernel, bq=bq),
        grid=(n // span, local // width),
        in_specs=[
            pl.BlockSpec((span, 1), lambda t, p: (t, 0)),
            part(0),
            part(1),
            part(2),
            pl.BlockSpec((span, width), lambda t, p: (t, p)),
            table,
            table,
        ],
        out_specs=[
            pl.BlockSpec((span, width), lambda t, p: (t, p)),
            pl.BlockSpec((owners // 2, None, here, width), lambda t, p: (t % 2, t // 2, 0, p)),
            pl.BlockSpec((3, span, width), lambda t, p: (0, t, p)),
        ],
        out_shape=[
            jax.ShapeDtypeStruct((n, local), bf16),
            jax.ShapeDtypeStruct((owners, n // (2 * span), here, local), bf16),
            jax.ShapeDtypeStruct((3, n, local), bf16),
        ],
        scratch_shapes=[pltpu.VMEM((span, width), f32)] * 2,
        compiler_params=params(),
        cost_estimate=SMALL,
        name="attention_both",
    )(start, qkv, qkv, qkv, grad, cosine, sine)


def own_kernel(x_ref, w_ref, b_ref, o_ref):
    owners, seqs, here, local = x_ref.shape
    total = jnp.zeros(o_ref.shape, f32) + b_ref[...]
    for owner in range(owners):
        x = x_ref[owner].reshape(seqs * here, local)
        total += dot(x, w_ref[owner * local : (owner + 1) * local, :], 1, 0)
    o_ref[...] = total


def project_own(x, w, bias, tile=512):
    owners, seqs, here, local = x.shape
    width = w.shape[1]
    return pl.pallas_call(
        own_kernel,
        grid=(width // tile,),
        in_specs=[
            pl.BlockSpec(x.shape, lambda j: (0, 0, 0, 0)),
            pl.BlockSpec((owners * local, tile), lambda j: (0, j)),
            pl.BlockSpec((1, tile), lambda j: (0, j)),
        ],
        out_specs=pl.BlockSpec((seqs * here, tile), lambda j: (0, j)),
        out_shape=jax.ShapeDtypeStruct((seqs * here, width), f32),
        compiler_params=params(),
        cost_estimate=SMALL,
        name="project_own",
    )(x, w, bias)


def line_ok(size):
    return size >= 4 and size & (size - 1) == 0


class RowSum:
    def __init__(self, part, size):
        self.part, self.size, self.axis = part, size, "rows"
        groups = range(0, size, 4)
        pairs = lambda *ends: [(g + a, g + b) for g in groups for a, b in ends]
        self.hops = [pairs((0, 1), (3, 2)), pairs((1, 2), (2, 1))]
        hop = 4
        while hop < size:
            self.hops.append([(i, i ^ hop) for i in range(size)])
            hop *= 2
        self.hops.append(pairs((1, 0), (2, 3)))
        self.send()

    def send(self):
        if line_ok(self.size):
            self.came = lax.ppermute(self.part, self.axis, self.hops.pop(0))

    def fold(self, order):
        if line_ok(self.size) and self.hops:
            add = lambda a, b: (a.astype(f32) + b.astype(f32)).astype(a.dtype)
            self.part = order(add, self.part, self.came)
            self.send()

    def complete(self, order):
        while self.hops:
            self.fold(order)

    def result(self, order=None):
        if not line_ok(self.size):
            return lax.psum(self.part.astype(f32), "rows")
        self.complete(order or Order())
        place = lax.axis_index("rows") % 4
        return jnp.where((place == 1) | (place == 2), self.part, self.came).astype(f32)


def finish_kernel(inner_ref, *refs, counts):
    o_ref = refs[-1]
    step = pl.program_id(0)
    first = 0
    for i, count in enumerate(counts):
        kept, came = refs[2 * i], refs[2 * i + 1]
        mine = (step >= first) & (step < first + count)

        @pl.when(mine & (inner_ref[0] == 1))
        def _(kept=kept):
            o_ref[...] = kept[...].astype(f32)

        @pl.when(mine & (inner_ref[0] == 0))
        def _(came=came):
            o_ref[...] = came[...].astype(f32)

        first += count


def finish_rows(sums, order, tile=256, weight=1):
    if not line_ok(sums[0].size):
        return jnp.concatenate([a.result() for a in sums])
    for a in sums:
        a.complete(order)
    cols = sums[0].part.shape[1]
    tile = min([tile] + [a.part.shape[0] for a in sums])
    counts = [a.part.shape[0] // tile for a in sums]
    firsts = [sum(counts[:i]) for i in range(len(counts))]
    pair = lambda i: [pl.BlockSpec((tile, cols), lambda j: (jnp.clip(j - firsts[i], 0, counts[i] - 1), 0))] * 2
    place = lax.axis_index("rows") % 4
    inner = ((place == 1) | (place == 2)).astype(jnp.int32).reshape(1)
    call = pl.pallas_call(
        functools.partial(finish_kernel, counts=counts),
        grid=(sum(counts),),
        in_specs=[pl.BlockSpec(memory_space=pltpu.SMEM)] + [b for i in range(len(sums)) for b in pair(i)],
        out_specs=pl.BlockSpec((tile, cols), lambda j: (j, 0)),
        out_shape=jax.ShapeDtypeStruct((sum(counts) * tile, cols), f32),
        compiler_params=params(),
        cost_estimate=pl.CostEstimate(flops=int(weight), bytes_accessed=1, transcendentals=0),
        name="finish_rows",
    )
    return order(lambda *a: call(inner, *a), *[b for a in sums for b in (a.part, a.came)])


class Gather:
    core, x, y = 1, 2, 4

    def __init__(self, piece, size):
        self.piece, self.size = piece, size
        self.exchange = size == 8
        if self.exchange:
            self.from_x, self.from_y = self.send(piece, self.x), self.send(piece, self.y)
            self.from_core = self.send(piece, self.core)

    def send(self, a, step):
        return lax.ppermute(a, "tp", [(i, i ^ step) for i in range(self.size)])

    def forward(self, order):
        if self.exchange:
            half = self.piece.shape[1] // 2
            cut = lambda a, b: (a, b, a[:, :half], b[:, half:])
            self.from_x, self.from_y, low, high = order(cut, self.from_x, self.from_y)
            self.low, self.high = self.send(low, self.y), self.send(high, self.x)
            self.pair_x, self.pair_y = self.send(self.from_x, self.core), self.send(self.from_y, self.core)

    def near(self, order):
        if self.exchange:
            steps = (0, self.core, self.x, self.y, self.x | self.core, self.y | self.core)
            pieces = (self.piece, self.from_core, self.from_x, self.from_y, self.pair_x, self.pair_y)
            self.full = order(lambda *a: place_pieces(None, a, steps, (0,) * 6, self.size), *pieces)

    def near_pairs(self):
        if self.exchange:
            self.pair_low, self.pair_high = self.send(self.low, self.core), self.send(self.high, self.core)

    def far(self, order):
        seqs, here, width = self.piece.shape
        if not self.exchange:
            full = lax.all_gather(self.piece, "tp", axis=1, tiled=True)
            return full.reshape(seqs * self.size * here, width)
        far, half = self.x | self.y, here // 2
        steps, ats = (far, far, far | self.core, far | self.core), (0, half, 0, half)
        place = lambda full, *a: place_pieces(full, a, steps, ats, self.size)
        full = order(place, self.full, self.low, self.high, self.pair_low, self.pair_high)
        return full.reshape(seqs * self.size * here, width)


def place_kernel(me_ref, *refs, counts, held):
    pieces, o_ref = refs[held:-1], refs[-1]
    step = pl.program_id(0)
    first = 0
    for piece, count in zip(pieces, counts):

        @pl.when((step >= first) & (step < first + count))
        def _(piece=piece):
            o_ref[...] = piece[...]

        first += count


def place_pieces(full, pieces, steps, ats, size):
    seqs, _, width = pieces[0].shape
    here = max(a.shape[1] for a in pieces) if full is None else full.shape[2]
    held = 0 if full is None else 1
    unit = min(a.shape[1] for a in pieces)
    counts = [a.shape[1] // unit for a in pieces]
    firsts = [sum(counts[:i]) for i in range(len(counts))]

    def piece_spec(i):
        return pl.BlockSpec((seqs, unit, width), lambda j, me: (0, jnp.clip(j - firsts[i], 0, counts[i] - 1), 0))

    def target(j, me):
        device, at = me[0] ^ steps[0], j + ats[0] // unit
        for i in range(1, len(pieces)):
            device = jnp.where(j >= firsts[i], me[0] ^ steps[i], device)
            at = jnp.where(j >= firsts[i], j - firsts[i] + ats[i] // unit, at)
        return 0, device, at, 0

    hbm = pl.BlockSpec(memory_space=pl.ANY)
    me = lax.axis_index("tp").astype(jnp.int32).reshape(1)
    return pl.pallas_call(
        functools.partial(place_kernel, counts=counts, held=held),
        grid_spec=pltpu.PrefetchScalarGridSpec(
            num_scalar_prefetch=1,
            grid=(sum(counts),),
            in_specs=[hbm] * held + [piece_spec(i) for i in range(len(pieces))],
            out_specs=pl.BlockSpec((seqs, None, unit, width), target),
        ),
        out_shape=jax.ShapeDtypeStruct((seqs, size, here, width), bf16),
        input_output_aliases={1: 0} if held else {},
        compiler_params=params(),
        cost_estimate=SMALL,
        name="place_pieces",
    )(me, *([full] if held else []), *pieces)


class TpSum:
    def __init__(self, part, size):
        self.part, self.size, self.hop = part, size, 1
        self.send()

    def send(self):
        if self.size & (self.size - 1) == 0 and self.hop < self.size:
            self.came = lax.ppermute(self.part, "tp", [(i, i ^ self.hop) for i in range(self.size)])

    def fold(self, order):
        if self.size & (self.size - 1):
            self.part, self.size = lax.psum(self.part, "tp"), 1
        elif self.hop < self.size:
            self.part = order(lambda a, b: a + b, self.part, self.came)
            self.hop *= 2
            self.send()

    def result(self, order):
        while self.hop < self.size:
            self.fold(order)
        return self.part


def body(
    tokens,
    segment_ids,
    positions,
    norm_gain,
    norm_shift,
    query_key_value_weight,
    b_qkv,
    dense_weight,
    b_dense,
    inward_weight,
    b_in,
    outward_weight,
    b_out,
    cotangent,
):
    rows, tp = lax.axis_size("rows"), lax.axis_size("tp")
    seqs, here, width = tokens.shape
    length = here * tp
    n = seqs * length
    local = query_key_value_weight.shape[2]
    tile = min(128, local)
    span = length // 2

    order = Order()
    values = tokens.astype(f32)
    gain, shift = norm_gain.astype(f32), norm_shift.astype(f32)
    center = values - jnp.mean(values, axis=-1, keepdims=True)
    inverse = lax.rsqrt(jnp.mean(center * center, axis=-1, keepdims=True) + epsilon)
    unit = center * inverse
    normed_low = (unit * gain + shift).astype(bf16)
    gather_normed = Gather(normed_low, tp)

    def tables(positions, weight):
        half_rot = ROT // 2
        frequency = rope_base ** (-2.0 * jnp.arange(half_rot, dtype=f32) / ROT)
        place = positions.reshape(n, 1)
        angles = place.astype(f32) * frequency
        heads = tile // HD
        rest = HD - ROT
        cosine, sine = jnp.cos(angles), jnp.sin(angles)
        ones, zeros = jnp.ones((n, rest), f32), jnp.zeros((n, rest), f32)
        cosine = jnp.concatenate([cosine, cosine, ones] * heads, axis=1)
        sine = jnp.concatenate([sine, sine, zeros] * heads, axis=1)
        start = jnp.arange(n, dtype=jnp.int32)[:, None] % span - place
        return cosine, sine, start, jnp.transpose(weight, (1, 0, 2))

    order.last = [normed_low]
    cosine, sine, start, w3 = order(tables, positions, query_key_value_weight)
    gather_normed.forward(order)
    gather_normed.near(order)
    gather_grad = Gather(order(lambda a: a, cotangent), tp)
    gather_normed.near_pairs()
    normed = gather_normed.far(order)

    act, slope = order(mlp_hidden, normed, inward_weight, b_in.astype(f32)[None])
    gather_grad.forward(order)
    qkv = order(project_qkv, normed, w3, b_qkv.astype(f32), cosine, sine)
    gather_grad.near(order)
    gather_grad.near_pairs()
    mlp_part = order(tokens_by_weight, act, outward_weight)
    grad = gather_grad.far(order)
    mlp_part, dense_ready, _ = lax.optimization_barrier((mlp_part, dense_weight, grad))
    mlp_tok = lax.psum_scatter(mlp_part.reshape(seqs, length, width), "tp", scatter_dimension=1, tiled=True)
    dense_full = lax.all_gather(dense_ready, "tp", axis=0, tiled=True)

    row_sum = lambda parts: [RowSum(part, rows) for part in parts]
    o0, o1 = row_sum(order(lambda a, b: weight_grad(a, b, 2), act, grad))
    hidden_grad, attended_grad, in_bias = order(grad_in, grad, outward_weight, dense_weight, slope)
    i0, i1, i2 = row_sum(order(lambda a, b: weight_grad_rows(a, b, (2, 1, 1)), normed, hidden_grad))
    o0.fold(order)
    both = lambda *a: attention_both(*a, span, tp)
    attended, by_owner, dqkv = order(both, start, qkv, attended_grad, cosine, sine)
    mine = lax.all_to_all(by_owner, "tp", split_axis=0, concat_axis=0, tiled=True)
    o1.fold(order)
    o0.fold(order)
    back = lambda *a: normed_grad(*a, shift[None])
    part, qkv_bias, norm_sums = order(back, hidden_grad, dqkv, inward_weight, w3, normed)
    back_tok = lax.psum_scatter(part.reshape(seqs, length, width), "tp", scatter_dimension=1, tiled=True)
    i0.fold(order)
    o1.fold(order)
    qs, ks, vs = row_sum(order(weight_grad_parts, normed, dqkv))
    i1.fold(order)
    i0.fold(order)
    (ds,) = row_sum(order(lambda a, b: weight_grad(a, b, 1), attended, grad))

    units = in_bias.shape[1]
    cols = width // tp

    def column_sums(grad):
        mine = lax.dynamic_slice_in_dim(grad, lax.axis_index("tp") * cols, cols, 1)
        return jnp.sum(mine.astype(f32), axis=0)

    out_bias = order(column_sums, grad)
    i2.fold(order)
    out_grad = finish_rows([o0, o1], order, weight=FINISH_WEIGHT)
    qs.fold(order)
    i1.fold(order)

    def branch_sums(attention, mlp_tok, tokens):
        values = tokens.astype(f32)
        mlp = mlp_tok.astype(f32) + b_out.astype(f32)
        total = values + attention.reshape(values.shape) + mlp
        squares = jnp.stack([jnp.sum(a * a) for a in (values, attention, mlp, total)])
        return total.astype(bf16), squares

    own = order(project_own, mine, dense_full, b_dense.astype(f32)[None])
    layer_out, squares = order(branch_sums, own, mlp_tok, tokens)
    pad = jnp.zeros((124,), f32)
    packed = jnp.concatenate([norm_sums[0] / gain, norm_sums[1], squares, pad]).reshape(-1, 128)
    packed = TpSum(packed, tp)
    i2.fold(order)
    ks.fold(order)
    packed.fold(order)
    qs.fold(order)
    packed.fold(order)
    vs.fold(order)
    small = jnp.concatenate([in_bias[0], qkv_bias[:, 0].reshape(-1), out_bias]).reshape(-1, 128)
    small = RowSum(jnp.concatenate([packed.result(order), small]), rows)
    ks.fold(order)
    ds.fold(order)
    in_grad = finish_rows([i0, i1, i2], order)
    small.fold(order)
    vs.fold(order)
    ds.fold(order)

    def norm_back(back_tok, tokens, cotangent):
        values = tokens.astype(f32)
        center = values - jnp.mean(values, axis=-1, keepdims=True)
        inverse = lax.rsqrt(jnp.mean(center * center, axis=-1, keepdims=True) + epsilon)
        unit = center * inverse
        unit_grad = back_tok.astype(f32) * gain
        mean_grad = jnp.mean(unit_grad, axis=-1, keepdims=True)
        mean_both = jnp.mean(unit_grad * unit, axis=-1, keepdims=True)
        value_grad = (unit_grad - mean_grad - unit * mean_both) * inverse
        return (cotangent.astype(f32) + value_grad).astype(bf16)

    input_grad = order(norm_back, back_tok, tokens, cotangent)
    small.fold(order)
    qkv_grad = jnp.stack([a.result() for a in (qs, ks, vs)], axis=1)
    dense_grad = finish_rows([ds], order)
    small = small.result().reshape(-1)
    slice_at = lambda a: lax.dynamic_slice_in_dim(a, lax.axis_index("tp") * cols, cols, 0)
    gain_grad, shift_grad = slice_at(small[:width]), slice_at(small[width : 2 * width])
    rms_values = jnp.sqrt(small[2 * width : 2 * width + 4] / (seqs * rows * length * width))
    small = small[2 * width + 128 :]
    in_bias_grad = small[:units]
    qkv_bias_grad = small[units : units + 3 * local].reshape(3, local)
    out_bias_grad = small[units + 3 * local :]

    return (
        layer_out,
        input_grad,
        gain_grad,
        shift_grad,
        qkv_grad,
        qkv_bias_grad,
        dense_grad,
        out_bias_grad,
        in_grad,
        in_bias_grad,
        out_grad,
        out_bias_grad,
        rms_values,
    )


def solution(mesh):
    in_specs = (
        P("rows", "tp", None),
        P("rows", None),
        P("rows", None),
        P(),
        P(),
        P(None, None, "tp"),
        P(None, "tp"),
        P("tp", None),
        P(),
        P(None, "tp"),
        P("tp"),
        P("tp", None),
        P(),
        P("rows", "tp", None),
    )
    out_specs = (
        P("rows", "tp", None),
        P("rows", "tp", None),
        P("tp"),
        P("tp"),
        P(None, None, "tp"),
        P(None, "tp"),
        P("tp", None),
        P("tp"),
        P(None, "tp"),
        P("tp"),
        P("tp", None),
        P("tp"),
        P(),
    )
    return jax.shard_map(body, mesh=mesh, in_specs=in_specs, out_specs=out_specs, check_vma=False)
```

time: 1080 us -> 776 us (0.72)
  waiting for transfers between devices: 557 us -> 199 us
  Pallas kernels: 199 us -> 340 us
  matrix products: 116 us -> 0 us
  starting transfers between devices: 46.4 us -> 79.1 us
    ppermute x21 -> x51, waiting for transfers between devices: 464 us -> 198 us  [the longest x30 144 us: send(): self.came = lax.ppermute(self.part, self.axis, self.hops.pop(0))]
    pallas_call x0 -> x13, Pallas kernels: none -> 160 us  [the longest x2 34 us: weight_grad(): pl.pallas_call(weight_grad_kernel, grid=(cols // tile,), in_specs=[pl.Blo...]
    dot_general x8 -> x0, matrix products: 116 us -> none  [dot(): lax.dot_general(a, b, (((ca,), (cb,)), ((), ())), preferred_element_type=...]
    all_gather x3 -> x1, waiting for transfers between devices: 90.6 us -> 0.01 us  [body(): dense_full = lax.all_gather(dense_ready, 'tp', axis=0, tiled=True)]
    ppermute x21 -> x51, starting transfers between devices: 41.7 us -> 74.7 us  [the longest x30 61.8 us: send(): self.came = lax.ppermute(self.part, self.axis, self.hops.pop(0))]
    pallas_call x1, Pallas kernels: 48.9 us -> 29.4 us  [grad_in(): pl.pallas_call(grad_in_kernel, grid=(n // tm,), in_specs=[pl.BlockSpec((t...]
    reduce_sum x1 -> x6, other arithmetic: 2.23 us -> 13.4 us  [the longest x2 8.39 us: branch_sums(): jnp.sum(a * a)]
    convert_element_type x15 -> x21, other arithmetic: 62.5 us -> 51.7 us  [the longest x18 47.4 us: fold(): add = lambda a, b: (a.astype(f32) + b.astype(f32)).astype(a.dtype)]
  transfers between devices with their start and end apart: 27 -> 55, of which waited for: 7 -> 20; matrix products, arithmetic and copies ran while one was open for 23% -> 16% of each run, Pallas kernels for 19% -> 44%
where the time goes in v2:
time: 776 us; the launch traced here: 771 us
  Pallas kernels  340 us (44%)
  waiting for transfers between devices  199 us (26%)
  other arithmetic  94.6 us (12%)
  starting transfers between devices  79.1 us (10%)
  local copies, waits for them, and re-layouts  43.6 us (6%)
  between operations  14.8 us (2%)
    ppermute x30, waiting for transfers between devices, send(): self.came = lax.ppermute(self.part, self.axis, self.hops.pop(0))  144 us
    ppermute x30, starting transfers between devices, send(): self.came = lax.ppermute(self.part, self.axis, self.hops.pop(0))  61.8 us
    pallas_call x1, Pallas kernels, attention_both(): pl.pallas_call(functools.partial(attention_kernel, bq=bq), grid=(n // spa...  59.3 us
    ppermute x18, waiting for transfers between devices, send(): return lax.ppermute(a, 'tp', [(i, i ^ step) for i in range(self.size)])  52.5 us
    convert_element_type x18, other arithmetic, fold(): add = lambda a, b: (a.astype(f32) + b.astype(f32)).astype(a.dtype)  47.4 us
    pallas_call x1, Pallas kernels, normed_grad(): pl.pallas_call(normed_grad_kernel, grid=(n // tm,), in_specs=[pl.BlockSpe...  40 us
    pallas_call x2, Pallas kernels, weight_grad(): pl.pallas_call(weight_grad_kernel, grid=(cols // tile,), in_specs=[pl.Blo...  34 us
    pallas_call x1, Pallas kernels, mlp_hidden(): pl.pallas_call(hidden_kernel, grid=(n // tm,), in_specs=[pl.BlockSpec((tm...  31.4 us
  transfers between devices with their start and end apart: 55, of which 20 were waited for; matrix products, arithmetic and copies ran while one was open for 16% of the time, Pallas kernels for 44%

profile of v2, /device:TPU:0, one launch (start us, length us, event | category | flops | bytes accessed | tf_op | source)
XLA Modules:
  0.0 770.9 jit_solution(4919554082941923964)
XLA Ops:
  13.0 2.9 collective-permute-start.1
  19.4 9.4 %multiply_sine_fusion = (f32[4096,16]{1,0:T(8,128)S(1)}, f32[4096,16]{1,0:T(8,128)}) fusion(f32[4096]{0:T(1024)S(1)} %bitcast.63, f32[16]{0:T(128)S(1)} %multiply_power_fusion), kind=kLoop, calls=%fused_computation.39 | loop fusion | flops 65536 | bytes 540736 | tf_op jit(solution)/shard_map/sin | solution.py:679
  30.3 10.8 %concatenate.16.c_ref = f32[4096,128]{1,0:T(8,128)} concatenate(f32[4096,16]{1,0:T(8,128)} %get-tuple-element.324, f32[4096,16]{1,0:T(8,128)} %get-tuple-element.324, f32[4096,32]{1,0:T(8,128)} %broadcast_in_dim.36, f32[4096,16]{1,0:T(8,128)} %get-tuple-element.324, f32[4096,16]{1,0:T(8,128)} %get-tuple-element.324, f32[4096,32]{1,0:T(8,128)} %broadcast_in_dim.36), dimensions={1} | concatenate | bytes 4194304 | tf_op jit(solution)/shard_map/concatenate | solution.py:681
  42.5 7.7 concatenate.17.s_ref
  50.1 3.1 fusion.19.start_ref
  53.3 8.6 %collective-permute-done.1.refs_2_ = bf16[2,256,2048]{2,1,0:T(8,128)(2,1)} collective-permute-done((bf16[2,256,2048]{2,1,0:T(8,128)(2,1)}, bf16[2,256,2048]{2,1,0:T(8,128)(2,1)}, u32[]{:S(2)}, u32[]{:S(2)}) %collective-permute-start.1) | collective-permute-done | bytes 2097184 | tf_op jit(solution)/shard_map/ppermute | solution.py:535
  63.8 2.3 slice.60
  67.6 2.3 slice.61
  72.0 10.0 %place_pieces.4.refs_0_ = bf16[2,8,256,2048]{3,2,1,0:T(8,128)(2,1)} custom-call(s32[1]{0:T(128)} %bitcast.me_ref, bf16[2,256,2048]{2,1,0:T(8,128)(2,1)} %fusion.15.refs_0_, bf16[2,256,2048]{2,1,0:T(8,128)(2,1)} %collective-permute-done.refs_1_, bf16[2,256,2048]{2,1,0:T(8,128)(2,1)} %collective-permute-done.1.refs_2_, ...), custom_call_target="tpu_custom_call" | custom-call | flops 1 | bytes 1 | tf_op jit(solution)/shard_map/place_pieces/pallas_call | solution.py:600
  83.9 8.4 %collective-permute-done.5.refs_1_ = bf16[2,128,2048]{2,1,0:T(8,128)(2,1)S(1)} collective-permute-done((bf16[2,128,2048]{2,1,0:T(8,128)(2,1)}, bf16[2,128,2048]{2,1,0:T(8,128)(2,1)S(1)}, u32[]{:S(2)}, u32[]{:S(2)}) %collective-permute-start.5) | collective-permute-done | bytes 1048608 | tf_op jit(solution)/shard_map/ppermute | solution.py:535
  92.4 4.0 collective-permute-done.6.refs_2_
  99.3 4.6 place_pieces.5
  104.0 31.4 %mlp_hidden.1 = (bf16[4096,1024]{1,0:T(8,128)(2,1)}, bf16[4096,1024]{1,0:T(8,128)(2,1)}) custom-call(bf16[4096,2048]{1,0:T(8,128)(2,1)} %bitcast.45, bf16[2048,1024]{1,0:T(8,128)(2,1)} %wi_ref, f32[1,1024]{1,0:T(1,128)} %bitcast.70), custom_call_target="tpu_custom_call" | custom-call | flops 1 | bytes 1 | tf_op jit(solution)/shard_map/mlp_hidden/pallas_call | solution.py:108
  136.3 3.5 collective-permute-done.9.refs_2_
  141.7 23.9 %collective-permute-done.14.refs_1_ = bf16[2,128,2048]{2,1,0:T(8,128)(2,1)S(1)} collective-permute-done((bf16[2,128,2048]{2,1,0:T(8,128)(2,1)S(1)}, bf16[2,128,2048]{2,1,0:T(8,128)(2,1)S(1)}, u32[]{:S(2)}, u32[]{:S(2)}) %collective-permute-start.14) | collective-permute-done | bytes 1048608 | tf_op jit(solution)/shard_map/ppermute | solution.py:535
  166.8 19.9 %qkv_rope.1.q_ref.k_ref.v_ref = bf16[3,4096,256]{2,1,0:T(8,128)(2,1)} custom-call(bf16[4096,2048]{1,0:T(8,128)(2,1)} %bitcast.46, bf16[3,2048,256]{2,1,0:T(8,128)(2,1)} %bitcast.57, f32[3,256]{1,0:T(4,128)} %convert_element_type.229.b_ref, f32[4096,128]{1,0:T(8,128)} %concatenate.16.c_ref, f32[4096,128]{1,0:T(8,128)} %concatenate.17.s_ref), custom_call_target="tpu_custom_call" | custom-call | flops 1 | bytes 1 | tf_op jit(solution)/shard_map/qkv_rope/pallas_call | solution.py:71
  186.7 9.8 %place_pieces.6.refs_0_ = bf16[2,8,256,2048]{3,2,1,0:T(8,128)(2,1)} custom-call(s32[1]{0:T(128)} %bitcast.me_ref, bf16[2,256,2048]{2,1,0:T(8,128)(2,1)} %refs_0_, bf16[2,256,2048]{2,1,0:T(8,128)(2,1)} %collective-permute-done.11.refs_1_, bf16[2,256,2048]{2,1,0:T(8,128)(2,1)} %copy-done.7, bf16[2,256,2048]{2,1,0:T(8,128)(2,1)} %copy-done.6, ...), custom_call_target="tpu_custom_call" | custom-call | flops 1 | bytes 1 | tf_op jit(solution)/shard_map/place_pieces/pallas_call | solution.py:600
  196.6 22.8 %tokens_by_weight.1 = bf16[4096,2048]{1,0:T(8,128)(2,1)} custom-call(bf16[4096,1024]{1,0:T(8,128)(2,1)} %get-tuple-element.204.x_ref.a_ref, bf16[1024,2048]{1,0:T(8,128)(2,1)} %wo_ref), custom_call_target="tpu_custom_call" | custom-call | flops 1 | bytes 1 | tf_op jit(solution)/shard_map/tokens_by_weight/pallas_call | solution.py:179
  219.4 4.7 place_pieces.7
  224.9 23.7 %weight_grad.2 = (bf16[512,2048]{1,0:T(8,128)(2,1)}, bf16[512,2048]{1,0:T(8,128)(2,1)}) custom-call(bf16[4096,1024]{1,0:T(8,128)(2,1)} %get-tuple-element.204.x_ref.a_ref, bf16[4096,2048]{1,0:T(8,128)(2,1)} %bitcast.50), custom_call_target="tpu_custom_call" | custom-call | flops 1 | bytes 1 | tf_op jit(solution)/shard_map/weight_grad/pallas_call | solution.py:203
  248.6 3.6 collective-permute-start.18
  252.2 2.7 collective-permute-start.20
  254.9 29.4 %grad_in.1 = (bf16[4096,1024]{1,0:T(8,128)(2,1)}, bf16[4096,256]{1,0:T(8,128)(2,1)}, f32[8,1024]{1,0:T(8,128)}) custom-call(bf16[4096,2048]{1,0:T(8,128)(2,1)} %bitcast.51, bf16[1024,2048]{1,0:T(8,128)(2,1)} %wo_ref, bf16[256,2048]{1,0:T(8,128)(2,1)} %wd_ref, bf16[4096,1024]{1,0:T(8,128)(2,1)} %get-tuple-element.211.slope_ref), custom_call_target="tpu_custom_call" | custom-call | flops 1 | bytes 1 | tf_op jit(solution)/shard_map/grad_in/pallas_call | solution.py:144
  284.2 25.8 %weight_grad_rows.1 = (bf16[1024,1024]{1,0:T(8,128)(2,1)}, bf16[512,1024]{1,0:T(8,128)(2,1)}, bf16[512,1024]{1,0:T(8,128)(2,1)}) custom-call(bf16[4096,2048]{1,0:T(8,128)(2,1)} %bitcast.47, bf16[4096,1024]{1,0:T(8,128)(2,1)} %get-tuple-element.235.b_ref.hg_ref), custom_call_target="tpu_custom_call" | custom-call | flops 1 | bytes 1 | tf_op jit(solution)/shard_map/weight_grad_rows/pallas_call | solution.py:237
  311.4 2.6 add_convert_fusion.5
  316.2 3.5 collective-permute-start.22
  319.7 59.3 %attention_both.1 = (bf16[4096,256]{1,0:T(8,128)(2,1)}, bf16[8,2,256,256]{3,2,1,0:T(8,128)(2,1)}, bf16[3,4096,256]{2,1,0:T(8,128)(2,1)}) custom-call(s32[4096,1]{1,0:T(8,128)} %fusion.19.start_ref, bf16[3,4096,256]{2,1,0:T(8,128)(2,1)} %qkv_rope.1.q_ref.k_ref.v_ref, bf16[3,4096,256]{2,1,0:T(8,128)(2,1)} %qkv_rope.1.q_ref.k_ref.v_ref, ...), custom_call_target="tpu_custom_call" | custom-call | flops 1 | bytes 1 | tf_op jit(solution)/shard_map/attention_both/pallas_call | solution.py:384
  379.0 3.9 add_convert_fusion.4
  384.9 3.8 add_convert_fusion.3.refs_0_
  388.7 40.0 %normed_grad.1 = (bf16[4096,2048]{1,0:T(8,128)(2,1)}, f32[3,8,256]{2,1,0:T(8,128)}, f32[8,2048]{1,0:T(8,128)}) custom-call(bf16[4096,1024]{1,0:T(8,128)(2,1)} %get-tuple-element.235.b_ref.hg_ref, bf16[3,4096,256]{2,1,0:T(8,128)(2,1)} %get-tuple-element.248.dq_ref.b_ref, bf16[2048,1024]{1,0:T(8,128)(2,1)} %wi_ref, bf16[3,2048,256]{2,1,0:T(8,128)(2,1)} %bitcast.58, ...), custom_call_target="tpu_custom_call" | custom-call | flops 1 | bytes 1 | tf_op jit(solution)/shard_map/normed_grad/pallas_call | solution.py:299
  428.7 2.3 collective-permute-start.19
  431.0 3.3 add_convert_fusion.2
  436.5 5.2 add_convert_fusion.1.refs_2_
  445.5 8.3 %collective-permute-start.28 = (bf16[512,1024]{1,0:T(8,128)(2,1)S(1)}, bf16[512,1024]{1,0:T(8,128)(2,1)}, u32[]{:S(2)}, u32[]{:S(2)}) collective-permute-start(bf16[512,1024]{1,0:T(8,128)(2,1)S(1)} %copy-done.20), channel_id=1, source_target_pairs={{0,8},{24,16},{1,9},{25,17},{2,10},{26,18},{3,11},{27,19},{4,12},{... | collective-permute-start | bytes 3145736 | tf_op jit(solution)/shard_map/ppermute | solution.py:460
  455.2 4.3 all-to-all-start
  459.5 18.7 %weight_grad_parts.1 = (bf16[2048,256]{1,0:T(8,128)(2,1)}, bf16[2048,256]{1,0:T(8,128)(2,1)}, bf16[2048,256]{1,0:T(8,128)(2,1)}) custom-call(bf16[4096,2048]{1,0:T(8,128)(2,1)} %bitcast.49, bf16[3,4096,256]{2,1,0:T(8,128)(2,1)} %get-tuple-element.248.dq_ref.b_ref), custom_call_target="tpu_custom_call" | custom-call | flops 1 | bytes 1 | tf_op jit(solution)/shard_map/weight_grad_parts/pallas_call | solution.py:260
  478.3 2.3 collective-permute-start.25
  484.0 2.9 add_convert_fusion.17
  488.7 4.1 add_convert_fusion.refs_0_
  492.7 10.3 %weight_grad.3 = bf16[256,2048]{1,0:T(8,128)(2,1)} custom-call(bf16[4096,256]{1,0:T(8,128)(2,1)} %get-tuple-element.256.a_ref, bf16[4096,2048]{1,0:T(8,128)(2,1)} %bitcast.52), custom_call_target="tpu_custom_call" | custom-call | flops 1 | bytes 1 | tf_op jit(solution)/shard_map/weight_grad/pallas_call | solution.py:203
  503.1 2.7 convert_reduce_fusion.2
  508.0 2.7 add_convert_fusion.16
  510.7 2.3 collective-permute-start.38
  513.0 23.0 %collective-permute-done.26.refs_1_ = bf16[512,2048]{1,0:T(8,128)(2,1)} collective-permute-done((bf16[512,2048]{1,0:T(8,128)(2,1)}, bf16[512,2048]{1,0:T(8,128)(2,1)}, u32[]{:S(2)}, u32[]{:S(2)}) %collective-permute-start.26) | collective-permute-done | bytes 2097184 | tf_op jit(solution)/shard_map/ppermute | solution.py:460
  537.7 7.7 finish_rows.3
  545.4 5.0 collective-permute-start.30
  550.4 2.5 add_convert_fusion.15
  554.6 2.9 add_convert_fusion.14.refs_2_
  557.5 9.4 %project_own.1 = f32[512,2048]{1,0:T(8,128)} custom-call(bf16[8,2,256,256]{3,2,1,0:T(8,128)(2,1)} %all-to-all-done.x_ref, bf16[2048,2048]{1,0:T(8,128)(2,1)} %all-gather.2.cloned.1.call-done.w_ref, f32[1,2048]{1,0:T(1,128)} %bitcast.66), custom_call_target="tpu_custom_call" | custom-call | flops 1 | bytes 1 | tf_op jit(solution)/shard_map/project_own/pallas_call | solution.py:425
  566.9 6.7 multiply_reduce_fusion
  576.6 2.7 concatenate.18
  584.5 2.8 add_convert_fusion.11
  598.0 48.7 %collective-permute-done.43.refs_3_ = bf16[512,1024]{1,0:T(8,128)(2,1)S(1)} collective-permute-done((bf16[512,1024]{1,0:T(8,128)(2,1)S(1)}, bf16[512,1024]{1,0:T(8,128)(2,1)S(1)}, u32[]{:S(2)}, u32[]{:S(2)}) %collective-permute-start.43) | collective-permute-done | bytes 1048608 | tf_op jit(solution)/shard_map/ppermute | solution.py:460
  651.2 18.1 %collective-permute-done.44.refs_5_ = bf16[512,1024]{1,0:T(8,128)(2,1)S(1)} collective-permute-done((bf16[512,1024]{1,0:T(8,128)(2,1)S(1)}, bf16[512,1024]{1,0:T(8,128)(2,1)S(1)}, u32[]{:S(2)}, u32[]{:S(2)}) %collective-permute-start.44) | collective-permute-done | bytes 1048608 | tf_op jit(solution)/shard_map/ppermute | solution.py:460
  671.9 9.7 %finish_rows.4 = f32[2048,1024]{1,0:T(8,128)} custom-call(s32[1]{0:T(128)} %bitcast.7.inner_ref, bf16[1024,1024]{1,0:T(8,128)(2,1)} %add_convert_fusion.refs_0_, bf16[1024,1024]{1,0:T(8,128)(2,1)} %collective-permute-done.42.refs_1_, bf16[512,1024]{1,0:T(8,128)(2,1)} %add_convert_fusion.14.refs_2_, bf16[512,1024]{1,0:T(8,128)(2,1)} %copy-done.22, ...), custom_call_target="tpu_custom_call" | custom-call | flops 1 | bytes 1 | tf_op jit(solution)/shard_map/finish_rows/pallas_call | solution.py:521
  682.2 9.6 %collective-permute-done.47 = bf16[2048,256]{1,0:T(8,128)(2,1)} collective-permute-done((bf16[2048,256]{1,0:T(8,128)(2,1)}, bf16[2048,256]{1,0:T(8,128)(2,1)}, u32[]{:S(2)}, u32[]{:S(2)}) %collective-permute-start.47) | collective-permute-done | bytes 1048608 | tf_op jit(solution)/shard_map/ppermute | solution.py:460
  691.8 2.4 select_bitcast_fusion.2
  699.0 15.3 %collective-permute-done.48 = bf16[2048,256]{1,0:T(8,128)(2,1)} collective-permute-done((bf16[2048,256]{1,0:T(8,128)(2,1)}, bf16[2048,256]{1,0:T(8,128)(2,1)}, u32[]{:S(2)}, u32[]{:S(2)}) %collective-permute-start.48) | collective-permute-done | bytes 1048608 | tf_op jit(solution)/shard_map/ppermute | solution.py:460
  714.3 2.3 select_bitcast_fusion.1
  716.6 20.1 %collective-permute-done.49 = bf16[2048,256]{1,0:T(8,128)(2,1)S(1)} collective-permute-done((bf16[2048,256]{1,0:T(8,128)(2,1)S(1)}, bf16[2048,256]{1,0:T(8,128)(2,1)S(1)}, u32[]{:S(2)}, u32[]{:S(2)}) %collective-permute-start.49) | collective-permute-done | bytes 1048608 | tf_op jit(solution)/shard_map/ppermute | solution.py:460
  740.9 3.2 fusion.10
  745.5 3.2 maximum_convert_fusion
  748.7 8.9 %collective-permute-done.50.refs_1_ = bf16[256,2048]{1,0:T(8,128)(2,1)} collective-permute-done((bf16[256,2048]{1,0:T(8,128)(2,1)S(1)}, bf16[256,2048]{1,0:T(8,128)(2,1)}, u32[]{:S(2)}, u32[]{:S(2)}) %collective-permute-start.50) | collective-permute-done | bytes 1048608 | tf_op jit(solution)/shard_map/ppermute | solution.py:460
  757.6 3.0 finish_rows.5
  (237 shorter events, 91.2 us)
Async XLA Ops:
  7.2 550.3 %all-gather.2.cloned.1.call-start = ((), (), s32[]{:S(2)}) async-start(), calls=%async_computation.3 | async-start | bytes 9437184 | tf_op jit(solution)/shard_map/all_gather | solution.py:703
  13.0 48.9 %collective-permute-start.1 = (bf16[2,256,2048]{2,1,0:T(8,128)(2,1)}, bf16[2,256,2048]{2,1,0:T(8,128)(2,1)}, u32[]{:S(2)}, u32[]{:S(2)}) collective-permute-start(bf16[2,256,2048]{2,1,0:T(8,128)(2,1)} %fusion.15.refs_0_), channel_id=1, source_target_pairs={{0,2},{1,3},{2,0},{3,1},{4,6},{5,7},{6,4},{7,5},{8,10},{9,11},{10,... | collective-permute-start | bytes 6291464 | tf_op jit(solution)/shard_map/ppermute | solution.py:535
  15.9 47.4 %collective-permute-start.2 = (bf16[2,256,2048]{2,1,0:T(8,128)(2,1)}, bf16[2,256,2048]{2,1,0:T(8,128)(2,1)}, u32[]{:S(2)}, u32[]{:S(2)}) collective-permute-start(bf16[2,256,2048]{2,1,0:T(8,128)(2,1)} %fusion.15.refs_0_), channel_id=1, source_target_pairs={{0,4},{1,5},{2,6},{3,7},{4,0},{5,1},{6,2},{7,3},{8,12},{9,13},{10,... | collective-permute-start | bytes 6291464 | tf_op jit(solution)/shard_map/ppermute | solution.py:535
  17.4 53.1 %collective-permute-start = (bf16[2,256,2048]{2,1,0:T(8,128)(2,1)}, bf16[2,256,2048]{2,1,0:T(8,128)(2,1)}, u32[]{:S(2)}, u32[]{:S(2)}) collective-permute-start(bf16[2,256,2048]{2,1,0:T(8,128)(2,1)} %fusion.15.refs_0_), channel_id=1, source_target_pairs={{0,1},{1,0},{2,3},{3,2},{4,5},{5,4},{6,7},{7,6},{8,9},{9,8},{10,11... | collective-permute-start | bytes 6291464 | tf_op jit(solution)/shard_map/ppermute | solution.py:535
  63.3 7.3 collective-permute-start.3
  63.3 7.5 collective-permute-start.4
  66.1 26.2 %collective-permute-start.5 = (bf16[2,128,2048]{2,1,0:T(8,128)(2,1)}, bf16[2,128,2048]{2,1,0:T(8,128)(2,1)S(1)}, u32[]{:S(2)}, u32[]{:S(2)}) collective-permute-start(bf16[2,128,2048]{2,1,0:T(8,128)(2,1)} %slice.60), channel_id=1, source_target_pairs={{0,4},{1,5},{2,6},{3,7},{4,0},{5,1},{6,2},{7,3},{8,12},{9,13},{10,... | collective-permute-start | bytes 3145736 | tf_op jit(solution)/shard_map/ppermute | solution.py:535
  69.9 26.4 %collective-permute-start.6 = (bf16[2,128,2048]{2,1,0:T(8,128)(2,1)}, bf16[2,128,2048]{2,1,0:T(8,128)(2,1)}, u32[]{:S(2)}, u32[]{:S(2)}) collective-permute-start(bf16[2,128,2048]{2,1,0:T(8,128)(2,1)} %slice.61), channel_id=1, source_target_pairs={{0,2},{1,3},{2,0},{3,1},{4,6},{5,7},{6,4},{7,5},{8,10},{9,11},{10,... | collective-permute-start | bytes 3145736 | tf_op jit(solution)/shard_map/ppermute | solution.py:535
  71.9 24.4 %copy-start.42 = (bf16[1024]{0:T(1024)(128)(2,1)S(1)}, bf16[1024]{0:T(1024)(128)(2,1)}, u32[]{:S(2)}) copy-start(bf16[1024]{0:T(1024)(128)(2,1)} %param.23) | copy-start | bytes 6148
  81.9 54.4 %collective-permute-start.10 = (bf16[2,256,2048]{2,1,0:T(8,128)(2,1)S(1)}, bf16[2,256,2048]{2,1,0:T(8,128)(2,1)S(1)}, u32[]{:S(2)}, u32[]{:S(2)}) collective-permute-start(bf16[2,256,2048]{2,1,0:T(8,128)(2,1)S(1)} %copy-done.4), channel_id=1, source_target_pairs={{0,4},{1,5},{2,6},{3,7},{4,0},{5,1},{6,2},{7,3},{8,12},{9,13},{10,... | collective-permute-start | bytes 6291464 | tf_op jit(solution)/shard_map/ppermute | solution.py:535
  83.4 56.5 %collective-permute-start.9 = (bf16[2,256,2048]{2,1,0:T(8,128)(2,1)S(1)}, bf16[2,256,2048]{2,1,0:T(8,128)(2,1)S(1)}, u32[]{:S(2)}, u32[]{:S(2)}) collective-permute-start(bf16[2,256,2048]{2,1,0:T(8,128)(2,1)S(1)} %copy-done.4), channel_id=1, source_target_pairs={{0,2},{1,3},{2,0},{3,1},{4,6},{5,7},{6,4},{7,5},{8,10},{9,11},{10,... | collective-permute-start | bytes 6291464 | tf_op jit(solution)/shard_map/ppermute | solution.py:535
  92.4 5.1 collective-permute-start.7
  96.3 3.0 collective-permute-start.8
  96.9 89.8 %collective-permute-start.11 = (bf16[2,256,2048]{2,1,0:T(8,128)(2,1)S(1)}, bf16[2,256,2048]{2,1,0:T(8,128)(2,1)}, u32[]{:S(2)}, u32[]{:S(2)}) collective-permute-start(bf16[2,256,2048]{2,1,0:T(8,128)(2,1)S(1)} %copy-done.4), channel_id=1, source_target_pairs={{0,1},{1,0},{2,3},{3,2},{4,5},{5,4},{6,7},{7,6},{8,9},{9,8},{10,11... | collective-permute-start | bytes 6291464 | tf_op jit(solution)/shard_map/ppermute | solution.py:535
  139.9 26.3 %copy-start.43 = (bf16[3,256]{1,0:T(4,128)(2,1)S(1)}, bf16[3,256]{1,0:T(4,128)(2,1)}, u32[]{:S(2)}) copy-start(bf16[3,256]{1,0:T(4,128)(2,1)} %param.19) | copy-start | bytes 4612
  139.9 46.8 %collective-permute-start.12 = (bf16[2,256,2048]{2,1,0:T(8,128)(2,1)S(1)}, bf16[2,256,2048]{2,1,0:T(8,128)(2,1)}, u32[]{:S(2)}, u32[]{:S(2)}) collective-permute-start(bf16[2,256,2048]{2,1,0:T(8,128)(2,1)S(1)} %collective-permute-done.9.refs_2_), channel_id=1, source_target_pairs={{0,1},{1,0},{2,3},{3,2},{4,5},{5,4},{6,7},{7,6},{8,9},{9,8},{10,11... | collective-permute-start | bytes 6291464 | tf_op jit(solution)/shard_map/ppermute | solution.py:535
  139.9 46.8 %collective-permute-start.13 = (bf16[2,256,2048]{2,1,0:T(8,128)(2,1)S(1)}, bf16[2,256,2048]{2,1,0:T(8,128)(2,1)}, u32[]{:S(2)}, u32[]{:S(2)}) collective-permute-start(bf16[2,256,2048]{2,1,0:T(8,128)(2,1)S(1)} %collective-permute-done.10.refs_3_), channel_id=1, source_target_pairs={{0,1},{1,0},{2,3},{3,2},{4,5},{5,4},{6,7},{7,6},{8,9},{9,8},{10,11... | collective-permute-start | bytes 6291464 | tf_op jit(solution)/shard_map/ppermute | solution.py:535
  140.5 25.2 %collective-permute-start.14 = (bf16[2,128,2048]{2,1,0:T(8,128)(2,1)S(1)}, bf16[2,128,2048]{2,1,0:T(8,128)(2,1)S(1)}, u32[]{:S(2)}, u32[]{:S(2)}) collective-permute-start(bf16[2,128,2048]{2,1,0:T(8,128)(2,1)S(1)} %slice.62), channel_id=1, source_target_pairs={{0,4},{1,5},{2,6},{3,7},{4,0},{5,1},{6,2},{7,3},{8,12},{9,13},{10,... | collective-permute-start | bytes 3145736 | tf_op jit(solution)/shard_map/ppermute | solution.py:535
  141.2 24.9 %collective-permute-start.15 = (bf16[2,128,2048]{2,1,0:T(8,128)(2,1)S(1)}, bf16[2,128,2048]{2,1,0:T(8,128)(2,1)}, u32[]{:S(2)}, u32[]{:S(2)}) collective-permute-start(bf16[2,128,2048]{2,1,0:T(8,128)(2,1)S(1)} %slice.63), channel_id=1, source_target_pairs={{0,2},{1,3},{2,0},{3,1},{4,6},{5,7},{6,4},{7,5},{8,10},{9,11},{10,... | collective-permute-start | bytes 3145736 | tf_op jit(solution)/shard_map/ppermute | solution.py:535
  165.7 21.0 %copy-start.25 = (bf16[2,128,2048]{2,1,0:T(8,128)(2,1)}, bf16[2,128,2048]{2,1,0:T(8,128)(2,1)S(1)}, u32[]{:S(2)}) copy-start(bf16[2,128,2048]{2,1,0:T(8,128)(2,1)S(1)} %collective-permute-done.14.refs_1_) | copy-start | bytes 3145732
  165.7 53.7 %collective-permute-start.16 = (bf16[2,128,2048]{2,1,0:T(8,128)(2,1)S(1)}, bf16[2,128,2048]{2,1,0:T(8,128)(2,1)}, u32[]{:S(2)}, u32[]{:S(2)}) collective-permute-start(bf16[2,128,2048]{2,1,0:T(8,128)(2,1)S(1)} %collective-permute-done.14.refs_1_), channel_id=1, source_target_pairs={{0,1},{1,0},{2,3},{3,2},{4,5},{5,4},{6,7},{7,6},{8,9},{9,8},{10,11... | collective-permute-start | bytes 3145736 | tf_op jit(solution)/shard_map/ppermute | solution.py:535
  166.1 53.3 %collective-permute-start.17 = (bf16[2,128,2048]{2,1,0:T(8,128)(2,1)}, bf16[2,128,2048]{2,1,0:T(8,128)(2,1)}, u32[]{:S(2)}, u32[]{:S(2)}) collective-permute-start(bf16[2,128,2048]{2,1,0:T(8,128)(2,1)} %collective-permute-done.15.refs_2_), channel_id=1, source_target_pairs={{0,1},{1,0},{2,3},{3,2},{4,5},{5,4},{6,7},{7,6},{8,9},{9,8},{10,11... | collective-permute-start | bytes 3145736 | tf_op jit(solution)/shard_map/ppermute | solution.py:535
  224.1 342.8 %reduce-scatter.3.cloned.1.call-start = ((), (), s32[]{:S(2)}) async-start(), calls=%async_computation.4 | async-start | bytes 18874368 | tf_op jit(solution)/shard_map/reduce_scatter | solution.py:702
  224.8 512.9 %reduce-scatter.5.cloned.1.call-start = ((), (), s32[]{:S(2)}) async-start(), calls=%async_computation.5 | async-start | bytes 18874368 | tf_op jit(solution)/shard_map/reduce_scatter | solution.py:717
  248.6 61.4 %collective-permute-start.18 = (bf16[512,2048]{1,0:T(8,128)(2,1)}, bf16[512,2048]{1,0:T(8,128)(2,1)S(1)}, u32[]{:S(2)}, u32[]{:S(2)}) collective-permute-start(bf16[512,2048]{1,0:T(8,128)(2,1)} %get-tuple-element.220), channel_id=1, source_target_pairs={{0,8},{24,16},{1,9},{25,17},{2,10},{26,18},{3,11},{27,19},{4,12},{... | collective-permute-start | bytes 6291464 | tf_op jit(solution)/shard_map/ppermute | solution.py:460
  252.2 126.8 %collective-permute-start.20 = (bf16[512,2048]{1,0:T(8,128)(2,1)}, bf16[512,2048]{1,0:T(8,128)(2,1)}, u32[]{:S(2)}, u32[]{:S(2)}) collective-permute-start(bf16[512,2048]{1,0:T(8,128)(2,1)} %get-tuple-element.231), channel_id=1, source_target_pairs={{0,8},{24,16},{1,9},{25,17},{2,10},{26,18},{3,11},{27,19},{4,12},{... | collective-permute-start | bytes 6291464 | tf_op jit(solution)/shard_map/ppermute | solution.py:460
  284.2 27.1 %copy-start.17 = (bf16[512,2048]{1,0:T(8,128)(2,1)S(1)}, bf16[512,2048]{1,0:T(8,128)(2,1)}, u32[]{:S(2)}) copy-start(bf16[512,2048]{1,0:T(8,128)(2,1)} %get-tuple-element.220) | copy-start | bytes 6291460
  314.0 65.0 %copy-start.16 = (bf16[512,2048]{1,0:T(8,128)(2,1)S(1)}, bf16[512,2048]{1,0:T(8,128)(2,1)}, u32[]{:S(2)}) copy-start(bf16[512,2048]{1,0:T(8,128)(2,1)} %get-tuple-element.231) | copy-start | bytes 6291460
  314.0 70.9 %collective-permute-start.23 = (bf16[512,2048]{1,0:T(8,128)(2,1)S(1)}, bf16[512,2048]{1,0:T(8,128)(2,1)}, u32[]{:S(2)}, u32[]{:S(2)}) collective-permute-start(bf16[512,2048]{1,0:T(8,128)(2,1)S(1)} %add_convert_fusion.5), channel_id=1, source_target_pairs={{8,16},{16,8},{9,17},{17,9},{10,18},{18,10},{11,19},{19,11},{12,20... | collective-permute-start | bytes 6291464 | tf_op jit(solution)/shard_map/ppermute | solution.py:460
  316.2 114.8 %collective-permute-start.22 = (bf16[1024,1024]{1,0:T(8,128)(2,1)S(1)}, bf16[1024,1024]{1,0:T(8,128)(2,1)}, u32[]{:S(2)}, u32[]{:S(2)}) collective-permute-start(bf16[1024,1024]{1,0:T(8,128)(2,1)S(1)} %copy-done.15), channel_id=1, source_target_pairs={{0,8},{24,16},{1,9},{25,17},{2,10},{26,18},{3,11},{27,19},{4,12},{... | collective-permute-start | bytes 6291464 | tf_op jit(solution)/shard_map/ppermute | solution.py:460
  382.9 53.6 %collective-permute-start.21 = (bf16[512,2048]{1,0:T(8,128)(2,1)}, bf16[512,2048]{1,0:T(8,128)(2,1)}, u32[]{:S(2)}, u32[]{:S(2)}) collective-permute-start(bf16[512,2048]{1,0:T(8,128)(2,1)} %add_convert_fusion.4), channel_id=1, source_target_pairs={{8,16},{16,8},{9,17},{17,9},{10,18},{18,10},{11,19},{19,11},{12,20... | collective-permute-start | bytes 6291464 | tf_op jit(solution)/shard_map/ppermute | solution.py:460
  428.7 49.5 %collective-permute-start.19 = (bf16[512,1024]{1,0:T(8,128)(2,1)}, bf16[512,1024]{1,0:T(8,128)(2,1)}, u32[]{:S(2)}, u32[]{:S(2)}) collective-permute-start(bf16[512,1024]{1,0:T(8,128)(2,1)} %get-tuple-element.252), channel_id=1, source_target_pairs={{0,8},{24,16},{1,9},{25,17},{2,10},{26,18},{3,11},{27,19},{4,12},{... | collective-permute-start | bytes 3145736 | tf_op jit(solution)/shard_map/ppermute | solution.py:460
  434.3 52.6 %collective-permute-start.29 = (bf16[1024,1024]{1,0:T(8,128)(2,1)S(1)}, bf16[1024,1024]{1,0:T(8,128)(2,1)}, u32[]{:S(2)}, u32[]{:S(2)}) collective-permute-start(bf16[1024,1024]{1,0:T(8,128)(2,1)S(1)} %add_convert_fusion.2), channel_id=1, source_target_pairs={{8,16},{16,8},{9,17},{17,9},{10,18},{18,10},{11,19},{19,11},{12,20... | collective-permute-start | bytes 6291464 | tf_op jit(solution)/shard_map/ppermute | solution.py:460
  441.7 69.0 %collective-permute-start.27 = (bf16[512,2048]{1,0:T(8,128)(2,1)}, bf16[512,2048]{1,0:T(8,128)(2,1)}, u32[]{:S(2)}, u32[]{:S(2)}) collective-permute-start(bf16[512,2048]{1,0:T(8,128)(2,1)} %add_convert_fusion.1.refs_2_), channel_id=1, source_target_pairs={{8,0},{16,24},{9,1},{17,25},{10,2},{18,26},{11,3},{19,27},{12,4},{... | collective-permute-start | bytes 6291464 | tf_op jit(solution)/shard_map/ppermute | solution.py:460
  443.0 93.1 %collective-permute-start.26 = (bf16[512,2048]{1,0:T(8,128)(2,1)}, bf16[512,2048]{1,0:T(8,128)(2,1)}, u32[]{:S(2)}, u32[]{:S(2)}) collective-permute-start(bf16[512,2048]{1,0:T(8,128)(2,1)} %add_convert_fusion.3.refs_0_), channel_id=1, source_target_pairs={{8,0},{16,24},{9,1},{17,25},{10,2},{18,26},{11,3},{19,27},{12,4},{... | collective-permute-start | bytes 6291464 | tf_op jit(solution)/shard_map/ppermute | solution.py:460
  445.5 60.2 %collective-permute-start.28 = (bf16[512,1024]{1,0:T(8,128)(2,1)S(1)}, bf16[512,1024]{1,0:T(8,128)(2,1)}, u32[]{:S(2)}, u32[]{:S(2)}) collective-permute-start(bf16[512,1024]{1,0:T(8,128)(2,1)S(1)} %copy-done.20), channel_id=1, source_target_pairs={{0,8},{24,16},{1,9},{25,17},{2,10},{26,18},{3,11},{27,19},{4,12},{... | collective-permute-start | bytes 3145736 | tf_op jit(solution)/shard_map/ppermute | solution.py:460
  455.2 102.3 %all-to-all-start = ((bf16[8,2,256,256]{3,2,1,0:T(8,128)(2,1)}), bf16[8,2,256,256]{3,2,1,0:T(8,128)(2,1)}, u32[]{:S(2)}, u32[]{:S(2)}) async-start(bf16[8,2,256,256]{3,2,1,0:T(8,128)(2,1)} %get-tuple-element.227), calls=%async_computation | async-start | bytes 4194304 | tf_op jit(solution)/shard_map/all_to_all | solution.py:712
  459.5 23.9 %copy-start.34 = (bf16[2048]{0:T(1024)(128)(2,1)S(1)}, bf16[2048]{0:T(1024)(128)(2,1)}, u32[]{:S(2)}) copy-start(bf16[2048]{0:T(1024)(128)(2,1)} %param.16) | copy-start | bytes 12292
  478.3 67.1 %collective-permute-start.25 = (bf16[2048,256]{1,0:T(8,128)(2,1)}, bf16[2048,256]{1,0:T(8,128)(2,1)}, u32[]{:S(2)}, u32[]{:S(2)}) collective-permute-start(bf16[2048,256]{1,0:T(8,128)(2,1)} %get-tuple-element.265), channel_id=1, source_target_pairs={{0,8},{24,16},{1,9},{25,17},{2,10},{26,18},{3,11},{27,19},{4,12},{... | collective-permute-start | bytes 3145736 | tf_op jit(solution)/shard_map/ppermute | solution.py:460
  487.0 66.0 %collective-permute-start.24 = (bf16[512,1024]{1,0:T(8,128)(2,1)}, bf16[512,1024]{1,0:T(8,128)(2,1)}, u32[]{:S(2)}, u32[]{:S(2)}) collective-permute-start(bf16[512,1024]{1,0:T(8,128)(2,1)} %add_convert_fusion.17), channel_id=1, source_target_pairs={{8,16},{16,8},{9,17},{17,9},{10,18},{18,10},{11,19},{19,11},{12,20... | collective-permute-start | bytes 3145736 | tf_op jit(solution)/shard_map/ppermute | solution.py:460
  505.8 75.5 %collective-permute-start.31 = (bf16[2048,256]{1,0:T(8,128)(2,1)}, bf16[2048,256]{1,0:T(8,128)(2,1)}, u32[]{:S(2)}, u32[]{:S(2)}) collective-permute-start(bf16[2048,256]{1,0:T(8,128)(2,1)} %get-tuple-element.278), channel_id=1, source_target_pairs={{0,8},{24,16},{1,9},{25,17},{2,10},{26,18},{3,11},{27,19},{4,12},{... | collective-permute-start | bytes 3145736 | tf_op jit(solution)/shard_map/ppermute | solution.py:460
  510.7 78.8 %collective-permute-start.38 = (bf16[2048,256]{1,0:T(8,128)(2,1)}, bf16[2048,256]{1,0:T(8,128)(2,1)}, u32[]{:S(2)}, u32[]{:S(2)}) collective-permute-start(bf16[2048,256]{1,0:T(8,128)(2,1)} %get-tuple-element.286), channel_id=1, source_target_pairs={{0,8},{24,16},{1,9},{25,17},{2,10},{26,18},{3,11},{27,19},{4,12},{... | collective-permute-start | bytes 3145736 | tf_op jit(solution)/shard_map/ppermute | solution.py:460
  536.0 37.6 %collective-permute-start.32 = (bf16[512,1024]{1,0:T(8,128)(2,1)}, bf16[512,1024]{1,0:T(8,128)(2,1)}, u32[]{:S(2)}, u32[]{:S(2)}) collective-permute-start(bf16[512,1024]{1,0:T(8,128)(2,1)} %add_convert_fusion.16), channel_id=1, source_target_pairs={{8,16},{16,8},{9,17},{17,9},{10,18},{18,10},{11,19},{19,11},{12,20... | collective-permute-start | bytes 3145736 | tf_op jit(solution)/shard_map/ppermute | solution.py:460
  537.7 12.7 %copy-start.21 = (bf16[2048,256]{1,0:T(8,128)(2,1)S(1)}, bf16[2048,256]{1,0:T(8,128)(2,1)}, u32[]{:S(2)}) copy-start(bf16[2048,256]{1,0:T(8,128)(2,1)} %get-tuple-element.265) | copy-start | bytes 3145732
  545.4 51.9 %collective-permute-start.30 = (bf16[256,2048]{1,0:T(8,128)(2,1)S(1)}, bf16[256,2048]{1,0:T(8,128)(2,1)}, u32[]{:S(2)}, u32[]{:S(2)}) collective-permute-start(bf16[256,2048]{1,0:T(8,128)(2,1)S(1)} %copy-done.8), channel_id=1, source_target_pairs={{0,8},{24,16},{1,9},{25,17},{2,10},{26,18},{3,11},{27,19},{4,12},{... | collective-permute-start | bytes 3145736 | tf_op jit(solution)/shard_map/ppermute | solution.py:460
  552.9 31.4 %collective-permute-start.36 = (bf16[2048,256]{1,0:T(8,128)(2,1)}, bf16[2048,256]{1,0:T(8,128)(2,1)}, u32[]{:S(2)}, u32[]{:S(2)}) collective-permute-start(bf16[2048,256]{1,0:T(8,128)(2,1)} %add_convert_fusion.15), channel_id=1, source_target_pairs={{8,16},{16,8},{9,17},{17,9},{10,18},{18,10},{11,19},{19,11},{12,20... | collective-permute-start | bytes 3145736 | tf_op jit(solution)/shard_map/ppermute | solution.py:460
  573.6 76.2 %collective-permute-start.42 = (bf16[1024,1024]{1,0:T(8,128)(2,1)}, bf16[1024,1024]{1,0:T(8,128)(2,1)}, u32[]{:S(2)}, u32[]{:S(2)}) collective-permute-start(bf16[1024,1024]{1,0:T(8,128)(2,1)} %add_convert_fusion.refs_0_), channel_id=1, source_target_pairs={{8,0},{16,24},{9,1},{17,25},{10,2},{18,26},{11,3},{19,27},{12,4},{... | collective-permute-start | bytes 6291464 | tf_op jit(solution)/shard_map/ppermute | solution.py:460
  581.3 2.2 collective-permute-start.34
  583.5 11.2 %collective-permute-start.33 = (bf16[2048,256]{1,0:T(8,128)(2,1)S(1)}, bf16[2048,256]{1,0:T(8,128)(2,1)S(1)}, u32[]{:S(2)}, u32[]{:S(2)}) collective-permute-start(bf16[2048,256]{1,0:T(8,128)(2,1)S(1)} %add_convert_fusion.12), channel_id=1, source_target_pairs={{8,16},{16,8},{9,17},{17,9},{10,18},{18,10},{11,19},{19,11},{12,20... | collective-permute-start | bytes 3145736 | tf_op jit(solution)/shard_map/ppermute | solution.py:460
  584.4 3.8 collective-permute-start.35
  588.2 58.5 %collective-permute-start.43 = (bf16[512,1024]{1,0:T(8,128)(2,1)S(1)}, bf16[512,1024]{1,0:T(8,128)(2,1)S(1)}, u32[]{:S(2)}, u32[]{:S(2)}) collective-permute-start(bf16[512,1024]{1,0:T(8,128)(2,1)S(1)} %copy-done.9), channel_id=1, source_target_pairs={{8,0},{16,24},{9,1},{17,25},{10,2},{18,26},{11,3},{19,27},{12,4},{... | collective-permute-start | bytes 3145736 | tf_op jit(solution)/shard_map/ppermute | solution.py:460
  589.5 3.8 collective-permute-start.37
  593.4 75.9 %collective-permute-start.44 = (bf16[512,1024]{1,0:T(8,128)(2,1)S(1)}, bf16[512,1024]{1,0:T(8,128)(2,1)S(1)}, u32[]{:S(2)}, u32[]{:S(2)}) collective-permute-start(bf16[512,1024]{1,0:T(8,128)(2,1)S(1)} %add_convert_fusion.13.refs_4_), channel_id=1, source_target_pairs={{8,0},{16,24},{9,1},{17,25},{10,2},{18,26},{11,3},{19,27},{12,4},{... | collective-permute-start | bytes 3145736 | tf_op jit(solution)/shard_map/ppermute | solution.py:460
  594.7 97.1 %collective-permute-start.47 = (bf16[2048,256]{1,0:T(8,128)(2,1)}, bf16[2048,256]{1,0:T(8,128)(2,1)}, u32[]{:S(2)}, u32[]{:S(2)}) collective-permute-start(bf16[2048,256]{1,0:T(8,128)(2,1)} %add_convert_fusion.11), channel_id=1, source_target_pairs={{8,0},{16,24},{9,1},{17,25},{10,2},{18,26},{11,3},{19,27},{12,4},{... | collective-permute-start | bytes 3145736 | tf_op jit(solution)/shard_map/ppermute | solution.py:460
  597.3 96.9 %collective-permute-start.40 = (bf16[2048,256]{1,0:T(8,128)(2,1)S(1)}, bf16[2048,256]{1,0:T(8,128)(2,1)S(1)}, u32[]{:S(2)}, u32[]{:S(2)}) collective-permute-start(bf16[2048,256]{1,0:T(8,128)(2,1)S(1)} %add_convert_fusion.10), channel_id=1, source_target_pairs={{8,16},{16,8},{9,17},{17,9},{10,18},{18,10},{11,19},{19,11},{12,20... | collective-permute-start | bytes 3145736 | tf_op jit(solution)/shard_map/ppermute | solution.py:460
  646.8 22.5 %copy-start.22 = (bf16[512,1024]{1,0:T(8,128)(2,1)}, bf16[512,1024]{1,0:T(8,128)(2,1)S(1)}, u32[]{:S(2)}) copy-start(bf16[512,1024]{1,0:T(8,128)(2,1)S(1)} %collective-permute-done.43.refs_3_) | copy-start | bytes 3145732
  646.8 34.8 %collective-permute-start.41 = (f32[49,128]{1,0:T(8,128)S(1)}, f32[49,128]{1,0:T(8,128)S(1)}, u32[]{:S(2)}, u32[]{:S(2)}) collective-permute-start(f32[49,128]{1,0:T(8,128)S(1)} %pad_maximum_fusion), channel_id=1, source_target_pairs={{0,8},{24,16},{1,9},{25,17},{2,10},{26,18},{3,11},{27,19},{4,12},{... | collective-permute-start | bytes 75272 | tf_op jit(solution)/shard_map/ppermute | solution.py:460
  649.9 64.4 %collective-permute-start.48 = (bf16[2048,256]{1,0:T(8,128)(2,1)}, bf16[2048,256]{1,0:T(8,128)(2,1)}, u32[]{:S(2)}, u32[]{:S(2)}) collective-permute-start(bf16[2048,256]{1,0:T(8,128)(2,1)} %add_convert_fusion.9), channel_id=1, source_target_pairs={{8,0},{16,24},{9,1},{17,25},{10,2},{18,26},{11,3},{19,27},{12,4},{... | collective-permute-start | bytes 3145736 | tf_op jit(solution)/shard_map/ppermute | solution.py:460
  670.2 25.6 %collective-permute-start.39 = (bf16[256,2048]{1,0:T(8,128)(2,1)S(1)}, bf16[256,2048]{1,0:T(8,128)(2,1)}, u32[]{:S(2)}, u32[]{:S(2)}) collective-permute-start(bf16[256,2048]{1,0:T(8,128)(2,1)S(1)} %add_convert_fusion.8), channel_id=1, source_target_pairs={{8,16},{16,8},{9,17},{17,9},{10,18},{18,10},{11,19},{19,11},{12,20... | collective-permute-start | bytes 3145736 | tf_op jit(solution)/shard_map/ppermute | solution.py:460
  681.6 62.6 %collective-permute-start.45 = (f32[49,128]{1,0:T(8,128)S(1)}, f32[49,128]{1,0:T(8,128)S(1)}, u32[]{:S(2)}, u32[]{:S(2)}) collective-permute-start(f32[49,128]{1,0:T(8,128)S(1)} %add.172), channel_id=1, source_target_pairs={{8,16},{16,8},{9,17},{17,9},{10,18},{18,10},{11,19},{19,11},{12,20... | collective-permute-start | bytes 75272 | tf_op jit(solution)/shard_map/ppermute | solution.py:460
  694.5 42.2 %collective-permute-start.49 = (bf16[2048,256]{1,0:T(8,128)(2,1)S(1)}, bf16[2048,256]{1,0:T(8,128)(2,1)S(1)}, u32[]{:S(2)}, u32[]{:S(2)}) collective-permute-start(bf16[2048,256]{1,0:T(8,128)(2,1)S(1)} %add_convert_fusion.7), channel_id=1, source_target_pairs={{8,0},{16,24},{9,1},{17,25},{10,2},{18,26},{11,3},{19,27},{12,4},{... | collective-permute-start | bytes 3145736 | tf_op jit(solution)/shard_map/ppermute | solution.py:460
  697.4 40.3 %copy-start.11 = (bf16[256,2048]{1,0:T(8,128)(2,1)}, bf16[256,2048]{1,0:T(8,128)(2,1)S(1)}, u32[]{:S(2)}) copy-start(bf16[256,2048]{1,0:T(8,128)(2,1)S(1)} %add_convert_fusion.6.refs_0_) | copy-start | bytes 3145732
  697.4 60.1 %collective-permute-start.50 = (bf16[256,2048]{1,0:T(8,128)(2,1)S(1)}, bf16[256,2048]{1,0:T(8,128)(2,1)}, u32[]{:S(2)}, u32[]{:S(2)}) collective-permute-start(bf16[256,2048]{1,0:T(8,128)(2,1)S(1)} %add_convert_fusion.6.refs_0_), channel_id=1, source_target_pairs={{8,0},{16,24},{9,1},{17,25},{10,2},{18,26},{11,3},{19,27},{12,4},{... | collective-permute-start | bytes 3145736 | tf_op jit(solution)/shard_map/ppermute | solution.py:460
  744.1 16.4 %collective-permute-start.46 = (f32[49,128]{1,0:T(8,128)S(1)}, f32[49,128]{1,0:T(8,128)S(1)}, u32[]{:S(2)}, u32[]{:S(2)}) collective-permute-start(f32[49,128]{1,0:T(8,128)S(1)} %add.177), channel_id=1, source_target_pairs={{8,0},{16,24},{9,1},{17,25},{10,2},{18,26},{11,3},{19,27},{12,4},{... | collective-permute-start | bytes 75272 | tf_op jit(solution)/shard_map/ppermute | solution.py:460
  (35 other events, 184.5 us)
Sparse Core Ops, SparseCore 0:
  224.2 54.8 all-gather.1
  282.7 115.9 reduce-scatter.2
  428.8 132.8 reduce-scatter.4

commit v3 on v2

v3 whole, which is shorter than its diff:
```python
import functools

import jax
import jax.numpy as jnp
from jax import lax
from jax.experimental import pallas as pl
from jax.experimental.pallas import tpu as pltpu
from jax.sharding import PartitionSpec as P

HD = 64
ROT = 32
epsilon = 1e-05
big_negative = -1e30
rope_base = 10000.0
f32 = jnp.float32
bf16 = jnp.bfloat16
VMEM_LIMIT = 56 << 20
ORDER_WEIGHT = int(1.85e11)
EARLY_WEIGHT = 1


def dot(a, b, ca, cb):
    return lax.dot_general(a, b, (((ca,), (cb,)), ((), ())), preferred_element_type=f32)


SMALL = pl.CostEstimate(flops=1, bytes_accessed=1, transcendentals=0)


def params():
    return pltpu.CompilerParams(vmem_limit_bytes=VMEM_LIMIT)


class Order:
    def __init__(self):
        self.last = ()

    def __call__(self, op, *operands):
        operands, _ = lax.optimization_barrier((operands, self.last))
        result = op(*operands)
        self.last = jax.tree.leaves(result)
        return result


def rope_swap(x):
    width = x.shape[-1]
    lane = lax.broadcasted_iota(jnp.int32, (1, width), 1) % HD
    up = pltpu.roll(x, width - ROT // 2, 1)
    down = pltpu.roll(x, ROT // 2, 1)
    return jnp.where(lane < ROT // 2, up, -down)


def norm_kernel(x_ref, gain_ref, shift_ref, first_ref, second_ref, *, per):
    x = x_ref[...].astype(f32)
    center = x - jnp.mean(x, axis=-1, keepdims=True)
    inverse = lax.rsqrt(jnp.mean(center * center, axis=-1, keepdims=True) + epsilon)
    out = (center * inverse * gain_ref[...] + shift_ref[...]).astype(bf16)

    @pl.when(pl.program_id(0) < per)
    def _():
        first_ref[...] = out

    @pl.when(pl.program_id(0) >= per)
    def _():
        second_ref[...] = out


def norm_halves(x, gain, shift, tm=128):
    n, width = x.shape
    per = n // 2 // tm
    vector = pl.BlockSpec((1, width), lambda i: (0, 0))
    return pl.pallas_call(
        functools.partial(norm_kernel, per=per),
        grid=(2 * per,),
        in_specs=[pl.BlockSpec((tm, width), lambda i: (i, 0)), vector, vector],
        out_specs=[
            pl.BlockSpec((tm, width), lambda i: (jnp.minimum(i, per - 1), 0)),
            pl.BlockSpec((tm, width), lambda i: (jnp.maximum(i - per, 0), 0)),
        ],
        out_shape=[jax.ShapeDtypeStruct((n // 2, width), bf16)] * 2,
        compiler_params=params(),
        cost_estimate=SMALL,
        name="norm_halves",
    )(x, gain[None], shift[None])


def table_kernel(place_ref, frequency_ref, c_ref, s_ref):
    angle = place_ref[...].astype(f32) * frequency_ref[...]
    lane = lax.broadcasted_iota(jnp.int32, angle.shape, 1) % HD
    turned = lane < ROT
    c_ref[...] = jnp.where(turned, jnp.cos(angle), 1.0)
    s_ref[...] = jnp.where(turned, jnp.sin(angle), 0.0)


def rope_tables(place, tile, tm=1024):
    n = place.shape[0]
    lane = jnp.arange(tile, dtype=jnp.int32) % (ROT // 2)
    frequency = (rope_base ** (-2.0 * lane.astype(f32) / ROT))[None]
    table = pl.BlockSpec((tm, tile), lambda i: (i, 0))
    return pl.pallas_call(
        table_kernel,
        grid=(n // tm,),
        in_specs=[pl.BlockSpec((tm, 1), lambda i: (i, 0)), pl.BlockSpec((1, tile), lambda i: (0, 0))],
        out_specs=[table, table],
        out_shape=[jax.ShapeDtypeStruct((n, tile), f32)] * 2,
        compiler_params=params(),
        cost_estimate=SMALL,
        name="rope_tables",
    )(place, frequency)


def qkv_kernel(x_ref, w_ref, b_ref, c_ref, s_ref, o_ref):
    x = x_ref[...]
    tile = c_ref.shape[-1]
    local = w_ref.shape[-1]
    cosine, sine = c_ref[...], s_ref[...]
    for part in range(3):
        full = dot(x, w_ref[part], 1, 0) + b_ref[part : part + 1, :]
        for at in range(0, local, tile):
            piece = full[:, at : at + tile]
            if part < 2:
                piece = piece * cosine - rope_swap(piece) * sine
            if part == 0:
                piece = piece * (HD**-0.5)
            o_ref[part, :, at : at + tile] = piece.astype(bf16)


def project_qkv(x, w3, bias, cosine, sine, tm=512):
    n, width = x.shape
    local = w3.shape[2]
    tile = cosine.shape[1]
    return pl.pallas_call(
        qkv_kernel,
        grid=(n // tm,),
        in_specs=[
            pl.BlockSpec((tm, width), lambda i: (i, 0)),
            pl.BlockSpec((3, width, local), lambda i: (0, 0, 0)),
            pl.BlockSpec((3, local), lambda i: (0, 0)),
            pl.BlockSpec((tm, tile), lambda i: (i, 0)),
            pl.BlockSpec((tm, tile), lambda i: (i, 0)),
        ],
        out_specs=pl.BlockSpec((3, tm, local), lambda i: (0, i, 0)),
        out_shape=jax.ShapeDtypeStruct((3, n, local), bf16),
        compiler_params=params(),
        cost_estimate=SMALL,
        name="qkv_rope",
    )(x, w3, bias, cosine, sine)


def chosen_kernel(me_ref, *refs, held):
    x_ref, w_ref, b_ref, act_ref, slope_ref = refs[held:]
    seqs, here, width = x_ref.shape
    x = x_ref[...].reshape(seqs * here, width)
    units = w_ref.shape[1]
    step = min(256, units)
    for at in range(0, units, step):
        cut = slice(at, at + step)
        h = dot(x, w_ref[:, cut], 1, 0) + b_ref[:, cut]
        square = h * h
        t = jnp.tanh(h * (0.7978845608028654 + 0.035677408136300125 * square))
        half = 0.5 + 0.5 * t
        act = h * half
        slope = half + (act - act * half) * (1.5957691216057308 + 0.21406444881780074 * square)
        act_ref[:, :, cut] = act.astype(bf16).reshape(seqs, here, step)
        slope_ref[:, :, cut] = slope.astype(bf16).reshape(seqs, here, step)


def mlp_hidden_of(x, w, bias, steps, before=()):
    seqs, owners, here, width = x.shape
    units = w.shape[1]
    held = len(before)

    def device(j, me):
        chosen = me[0] ^ steps[0]
        for i in range(1, len(steps)):
            chosen = jnp.where(j == i, me[0] ^ steps[i], chosen)
        return 0, chosen, 0, 0

    out = pl.BlockSpec((seqs, None, here, units), device)
    me = lax.axis_index("tp").astype(jnp.int32).reshape(1)
    return pl.pallas_call(
        functools.partial(chosen_kernel, held=held),
        grid_spec=pltpu.PrefetchScalarGridSpec(
            num_scalar_prefetch=1,
            grid=(len(steps),),
            in_specs=[pl.BlockSpec(memory_space=pl.ANY)] * held
            + [
                pl.BlockSpec((seqs, None, here, width), device),
                pl.BlockSpec((width, units), lambda j, me: (0, 0)),
                pl.BlockSpec((1, units), lambda j, me: (0, 0)),
            ],
            out_specs=[out, out],
        ),
        out_shape=[jax.ShapeDtypeStruct((seqs, owners, here, units), bf16)] * 2,
        input_output_aliases={1 + i: i for i in range(held)},
        compiler_params=params(),
        cost_estimate=SMALL,
        name="mlp_hidden_of",
    )(me, *before, x, w, bias)


def grad_in_kernel(g_ref, wo_ref, wd_ref, slope_ref, hg_ref, at_ref, sum_ref):
    g = g_ref[...]
    units = wo_ref.shape[0]
    step = min(256, units)

    @pl.when(pl.program_id(0) == 0)
    def _():
        sum_ref[...] = jnp.zeros_like(sum_ref)

    for at in range(0, units, step):
        slope = slope_ref[:, at : at + step].astype(f32)
        hg = (dot(g, wo_ref[at : at + step, :], 1, 1) * slope).astype(bf16)
        hg_ref[:, at : at + step] = hg
        sum_ref[0:1, at : at + step] += jnp.sum(hg.astype(f32), axis=0, keepdims=True)
    at_ref[...] = dot(g, wd_ref[...], 1, 1).astype(bf16)


def grad_in(g, wo, wd, slope, tm=512):
    n, width = g.shape
    units, local = wo.shape[0], wd.shape[0]
    return pl.pallas_call(
        grad_in_kernel,
        grid=(n // tm,),
        in_specs=[
            pl.BlockSpec((tm, width), lambda i: (i, 0)),
            pl.BlockSpec((units, width), lambda i: (0, 0)),
            pl.BlockSpec((local, width), lambda i: (0, 0)),
            pl.BlockSpec((tm, units), lambda i: (i, 0)),
        ],
        out_specs=[
            pl.BlockSpec((tm, units), lambda i: (i, 0)),
            pl.BlockSpec((tm, local), lambda i: (i, 0)),
            pl.BlockSpec((8, units), lambda i: (0, 0)),
        ],
        out_shape=[
            jax.ShapeDtypeStruct((n, units), bf16),
            jax.ShapeDtypeStruct((n, local), bf16),
            jax.ShapeDtypeStruct((8, units), f32),
        ],
        compiler_params=params(),
        cost_estimate=SMALL,
        name="grad_in",
    )(g, wo, wd, slope)


def tokens_kernel(x_ref, w_ref, o_ref):
    width = w_ref.shape[1]
    step = min(512, width)
    for at in range(0, width, step):
        o_ref[:, at : at + step] = dot(x_ref[...], w_ref[:, at : at + step], 1, 0).astype(o_ref.dtype)


def tokens_by_weight(x, w, share, shares, tm=512):
    n, depth = x.shape
    n //= shares
    width = w.shape[1]
    first = share * (n // tm)
    return pl.pallas_call(
        tokens_kernel,
        grid=(n // tm,),
        in_specs=[pl.BlockSpec((tm, depth), lambda i: (first + i, 0)), pl.BlockSpec((depth, width), lambda i: (0, 0))],
        out_specs=pl.BlockSpec((tm, width), lambda i: (i, 0)),
        out_shape=jax.ShapeDtypeStruct((n, width), bf16),
        compiler_params=params(),
        cost_estimate=SMALL,
        name="tokens_by_weight",
    )(x, w)


def weight_grad_kernel(a_ref, b_ref, o_ref):
    o_ref[...] = dot(a_ref[...], b_ref[...], 0, 0).astype(bf16)


def weight_grad(a, b, share=0, shares=1, tile=512, weight=1):
    n, rows = a.shape
    rows //= shares
    cols = b.shape[1]
    tile = min(tile, cols)
    return pl.pallas_call(
        weight_grad_kernel,
        grid=(cols // tile,),
        in_specs=[
            pl.BlockSpec((n, rows), lambda j: (0, share), pipeline_mode=pl.Buffered(1)),
            pl.BlockSpec((n, tile), lambda j: (0, j)),
        ],
        out_specs=pl.BlockSpec((rows, tile), lambda j: (0, j)),
        out_shape=jax.ShapeDtypeStruct((rows, cols), bf16),
        compiler_params=params(),
        cost_estimate=pl.CostEstimate(flops=int(weight), bytes_accessed=1, transcendentals=0),
        name="weight_grad",
    )(a, b)


def weight_grad_rows_kernel(a_ref, b_ref, *o_refs, counts):
    full = dot(a_ref[...], b_ref[...], 0, 0).astype(bf16)
    step = pl.program_id(0)
    first = 0
    for o_ref, count in zip(o_refs, counts):

        @pl.when((step >= first) & (step < first + count))
        def _(o_ref=o_ref):
            o_ref[...] = full

        first += count


def weight_grad_rows(a, b, shares, tile=512):
    n, rows = a.shape
    cols = b.shape[1]
    counts = [rows * share // sum(shares) // tile for share in shares]
    firsts = [sum(counts[:i]) for i in range(len(counts))]
    out = lambda i: pl.BlockSpec((tile, cols), lambda j: (jnp.clip(j - firsts[i], 0, counts[i] - 1), 0))
    return pl.pallas_call(
        functools.partial(weight_grad_rows_kernel, counts=counts),
        grid=(rows // tile,),
        in_specs=[
            pl.BlockSpec((n, tile), lambda j: (0, j)),
            pl.BlockSpec((n, cols), lambda j: (0, 0), pipeline_mode=pl.Buffered(1)),
        ],
        out_specs=[out(i) for i in range(len(counts))],
        out_shape=[jax.ShapeDtypeStruct((count * tile, cols), bf16) for count in counts],
        compiler_params=params(),
        cost_estimate=SMALL,
        name="weight_grad_rows",
    )(a, b)


def weight_grad_parts_kernel(a_ref, b_ref, first_ref, last_ref):
    for part in range(2):
        first_ref[part] = dot(a_ref[...], b_ref[part], 0, 0).astype(bf16)
    last_ref[...] = dot(a_ref[...], b_ref[2], 0, 0).astype(bf16)


def weight_grad_parts(a, b, tile=512, weight=1):
    n, rows = a.shape
    parts, _, cols = b.shape
    return pl.pallas_call(
        weight_grad_parts_kernel,
        grid=(rows // tile,),
        in_specs=[
            pl.BlockSpec((n, tile), lambda j: (0, j)),
            pl.BlockSpec((parts, n, cols), lambda j: (0, 0, 0), pipeline_mode=pl.Buffered(1)),
        ],
        out_specs=[pl.BlockSpec((2, tile, cols), lambda j: (0, j, 0)), pl.BlockSpec((tile, cols), lambda j: (j, 0))],
        out_shape=[jax.ShapeDtypeStruct((2, rows, cols), bf16), jax.ShapeDtypeStruct((rows, cols), bf16)],
        compiler_params=params(),
        cost_estimate=pl.CostEstimate(flops=int(weight), bytes_accessed=1, transcendentals=0),
        name="weight_grad_parts",
    )(a, b)


def normed_grad_kernel(*refs, held):
    hg_ref, dq_ref, wi_ref, w3_ref, x_ref, shift_ref, o_ref, sum_ref, norm_ref = refs[held:]

    @pl.when(pl.program_id(0) == 0)
    def _():
        sum_ref[...] = jnp.zeros_like(sum_ref)
        norm_ref[...] = jnp.zeros_like(norm_ref)

    for part in range(3):
        sum_ref[part, 0:1] += jnp.sum(dq_ref[part].astype(f32), axis=0, keepdims=True)
    width = o_ref.shape[1]
    step = min(512, width)
    for at in range(0, width, step):
        cut = slice(at, at + step)
        total = dot(hg_ref[...], wi_ref[cut, :], 1, 1)
        for part in range(3):
            total += dot(dq_ref[part], w3_ref[part, cut, :], 1, 1)
        o_ref[:, cut] = total.astype(bf16)
        scaled = x_ref[:, cut].astype(f32) - shift_ref[:, cut]
        norm_ref[0:1, cut] += jnp.sum(total * scaled, axis=0, keepdims=True)
        norm_ref[1:2, cut] += jnp.sum(total, axis=0, keepdims=True)


def normed_grad(hg, dqkv, wi, w3, x, shift, share, shares, before=(), tm=512):
    n, units = hg.shape
    held = len(before)
    steps = n // shares // tm
    first = share * steps
    width, local = w3.shape[1:]
    return pl.pallas_call(
        functools.partial(normed_grad_kernel, held=held),
        grid=(steps,),
        in_specs=[pl.BlockSpec(memory_space=pl.ANY)] * held
        + [
            pl.BlockSpec((tm, units), lambda i: (first + i, 0)),
            pl.BlockSpec((3, tm, local), lambda i: (0, first + i, 0)),
            pl.BlockSpec((width, units), lambda i: (0, 0)),
            pl.BlockSpec((3, width, local), lambda i: (0, 0, 0)),
            pl.BlockSpec((tm, width), lambda i: (first + i, 0)),
            pl.BlockSpec((1, width), lambda i: (0, 0)),
        ],
        out_specs=[
            pl.BlockSpec((tm, width), lambda i: (first + i, 0)),
            pl.BlockSpec((3, 8, local), lambda i: (0, 0, 0)),
            pl.BlockSpec((8, width), lambda i: (0, 0)),
        ],
        out_shape=[
            jax.ShapeDtypeStruct((n, width), bf16),
            jax.ShapeDtypeStruct((3, 8, local), f32),
            jax.ShapeDtypeStruct((8, width), f32),
        ],
        input_output_aliases={i: i for i in range(held)},
        compiler_params=params(),
        cost_estimate=SMALL,
        name="normed_grad",
    )(*before, hg, dqkv, wi, w3, x, shift)


def attention_kernel(*refs, bq, held):
    start_ref, q_ref, k_ref, v_ref, do_ref, c_ref, s_ref, o_ref, by_owner_ref, g_ref, dk_acc, dv_acc = refs[held:]
    span, width = q_ref.shape
    lane = lax.broadcasted_iota(jnp.int32, (1, width), 1) // HD
    zero = jnp.zeros((), bf16)

    def turn_back(x, at, n):
        return x * c_ref[at : at + n, :] + rope_swap(x) * s_ref[at : at + n, :]

    for block in range(span // bq):
        at = block * bq
        n = at + bq
        qb = q_ref[at:n, :]
        gb = do_ref[at:n, :]
        keys, vals = k_ref[0:n, :], v_ref[0:n, :]
        key = lax.broadcasted_iota(jnp.int32, (bq, n), 1)
        row = lax.broadcasted_iota(jnp.int32, (bq, n), 0) + at
        allowed = (key >= start_ref[at:n, :]) & (key <= row)
        out = jnp.zeros((bq, width), f32)
        dq = jnp.zeros((bq, width), f32)
        dk = jnp.zeros((n, width), f32)
        dv = jnp.zeros((n, width), f32)
        for head in range(width // HD):
            mine = lane == head
            qh, gh = jnp.where(mine, qb, zero), jnp.where(mine, gb, zero)
            kh, vh = jnp.where(mine, keys, zero), jnp.where(mine, vals, zero)
            scores = jnp.where(allowed, dot(qh, keys, 1, 1), big_negative)
            expd = jnp.exp(scores - jnp.max(scores, axis=1, keepdims=True))
            probs = expd * (1.0 / jnp.sum(expd, axis=1, keepdims=True))
            low = probs.astype(bf16)
            out = out + dot(low, vh, 1, 0)
            prob_grad = dot(gh, vals, 1, 1)
            inner = jnp.sum(probs * prob_grad, axis=1, keepdims=True)
            score_grad = (probs * (prob_grad - inner)).astype(bf16)
            dq = dq + dot(score_grad, kh, 1, 0)
            dk = dk + dot(score_grad, qh, 0, 0)
            dv = dv + dot(low, gh, 0, 0)
        out = out.astype(bf16)
        o_ref[at:n, :] = out
        here = by_owner_ref.shape[1]
        for own in range(bq // here):
            by_owner_ref[at // here + own] = out[own * here : (own + 1) * here]
        g_ref[0, at:n, :] = turn_back(dq * (HD**-0.5), at, bq).astype(bf16)
        if block:
            dk_acc[0:at, :] += dk[0:at]
            dv_acc[0:at, :] += dv[0:at]
        dk_acc[at:n, :] = dk[at:n]
        dv_acc[at:n, :] = dv[at:n]
    g_ref[1] = turn_back(dk_acc[...], 0, span).astype(bf16)
    g_ref[2] = dv_acc[...].astype(bf16)


def attention_both(start, qkv, grad, cosine, sine, span, owners, row, before=(), bq=512):
    n, local = grad.shape
    here = 2 * span // owners
    width = cosine.shape[1]
    bq = min(bq, span)
    held = len(before)
    first = 2 * row
    part = lambda which: pl.BlockSpec((None, span, width), lambda t, p: (which, first + t, p))
    table = pl.BlockSpec((span, width), lambda t, p: (first + t, 0))
    return pl.pallas_call(
        functools.partial(attention_kernel, bq=bq, held=held),
        grid=(2, local // width),
        in_specs=[pl.BlockSpec(memory_space=pl.ANY)] * held
        + [
            pl.BlockSpec((span, 1), lambda t, p: (first + t, 0)),
            part(0),
            part(1),
            part(2),
            pl.BlockSpec((span, width), lambda t, p: (first + t, p)),
            table,
            table,
        ],
        out_specs=[
            pl.BlockSpec((span, width), lambda t, p: (first + t, p)),
            pl.BlockSpec((owners // 2, None, here, width), lambda t, p: (t, row, 0, p)),
            pl.BlockSpec((3, span, width), lambda t, p: (0, first + t, p)),
        ],
        out_shape=[
            jax.ShapeDtypeStruct((n, local), bf16),
            jax.ShapeDtypeStruct((owners, n // (2 * span), here, local), bf16),
            jax.ShapeDtypeStruct((3, n, local), bf16),
        ],
        scratch_shapes=[pltpu.VMEM((span, width), f32)] * 2,
        input_output_aliases={i: i for i in range(held)},
        compiler_params=params(),
        cost_estimate=SMALL,
        name="attention_both",
    )(*before, start, qkv, qkv, qkv, grad, cosine, sine)


def own_kernel(x_ref, w_ref, bd_ref, bo_ref, token_ref, *refs):
    *mlp_refs, o_ref, sum_ref = refs
    owners, seqs, here, local = x_ref.shape
    attention = jnp.zeros((seqs * here, w_ref.shape[1]), f32) + bd_ref[...]
    for owner in range(owners):
        x = x_ref[owner].reshape(seqs * here, local)
        attention += dot(x, w_ref[owner * local : (owner + 1) * local, :], 1, 0)
    tokens = token_ref[...].astype(f32)
    mlp = jnp.concatenate([a[...] for a in mlp_refs], axis=0).astype(f32) + bo_ref[...]
    total = tokens + attention + mlp
    o_ref[...] = total.astype(bf16)

    @pl.when(pl.program_id(0) == 0)
    def _():
        sum_ref[...] = jnp.zeros_like(sum_ref)

    for i, a in enumerate((tokens, attention, mlp, total)):
        sum_ref[i : i + 1, :] += jnp.sum(a * a, axis=0, keepdims=True)


def project_own(x, w, bd, bo, tokens, mlp_parts, tile=512):
    owners, seqs, here, local = x.shape
    width = w.shape[1]
    rows = seqs * here
    column = lambda high: pl.BlockSpec((high, tile), lambda j: (0, j))
    return pl.pallas_call(
        own_kernel,
        grid=(width // tile,),
        in_specs=[
            pl.BlockSpec(x.shape, lambda j: (0, 0, 0, 0)),
            column(owners * local),
            column(1),
            column(1),
            column(rows),
        ]
        + [column(a.shape[0]) for a in mlp_parts],
        out_specs=[column(rows), pl.BlockSpec((8, tile), lambda j: (0, 0))],
        out_shape=[jax.ShapeDtypeStruct((rows, width), bf16), jax.ShapeDtypeStruct((8, tile), f32)],
        compiler_params=params(),
        cost_estimate=SMALL,
        name="project_own",
    )(x, w, bd, bo, tokens, *mlp_parts)


def line_ok(size):
    return size >= 4 and size & (size - 1) == 0


class RowSum:
    def __init__(self, part, size):
        self.part, self.size, self.axis = part, size, "rows"
        groups = range(0, size, 4)
        pairs = lambda *ends: [(g + a, g + b) for g in groups for a, b in ends]
        self.hops = [pairs((0, 1), (3, 2)), pairs((1, 2), (2, 1))]
        hop = 4
        while hop < size:
            self.hops.append([(i, i ^ hop) for i in range(size)])
            hop *= 2
        self.hops.append(pairs((1, 0), (2, 3)))
        self.send()

    def send(self):
        if line_ok(self.size):
            self.came = lax.ppermute(self.part, self.axis, self.hops.pop(0))

    def fold(self, order):
        if line_ok(self.size) and self.hops:
            add = lambda a, b: (a.astype(f32) + b.astype(f32)).astype(a.dtype)
            self.part = order(add, self.part, self.came)
            self.send()

    def complete(self, order):
        while self.hops:
            self.fold(order)

    def result(self, order=None):
        if not line_ok(self.size):
            return lax.psum(self.part.astype(f32), "rows")
        self.complete(order or Order())
        place = lax.axis_index("rows") % 4
        return jnp.where((place == 1) | (place == 2), self.part, self.came).astype(f32)


def finish_kernel(inner_ref, kept_ref, came_ref, *refs):
    o_ref = refs[-1]

    @pl.when(inner_ref[0] == 1)
    def _():
        o_ref[...] = kept_ref[...].astype(f32)

    @pl.when(inner_ref[0] == 0)
    def _():
        o_ref[...] = came_ref[...].astype(f32)


def finish(total, order, high, first=0, before=None, tile=512):
    flat = lambda a: a.reshape(-1, a.shape[-1])
    rows, cols = flat(total.part).shape
    if not line_ok(total.size):
        before = jnp.zeros((high, cols), f32) if before is None else before
        return lax.dynamic_update_slice(before, flat(total.result()), (first, 0))
    total.complete(order)
    tile = min(tile, rows)
    held = [] if before is None else [before]
    block = pl.BlockSpec((tile, cols), lambda j: (j, 0))
    place = lax.axis_index("rows") % 4
    inner = ((place == 1) | (place == 2)).astype(jnp.int32).reshape(1)
    call = pl.pallas_call(
        finish_kernel,
        grid=(rows // tile,),
        in_specs=[pl.BlockSpec(memory_space=pltpu.SMEM), block, block] + [pl.BlockSpec(memory_space=pl.ANY)] * len(held),
        out_specs=pl.BlockSpec((tile, cols), lambda j: (first // tile + j, 0)),
        out_shape=jax.ShapeDtypeStruct((high, cols), f32),
        input_output_aliases={3: 0} if held else {},
        compiler_params=params(),
        cost_estimate=SMALL,
        name="finish",
    )
    return order(lambda *a: call(inner, *a), flat(total.part), flat(total.came), *held)


class Gather:
    core, x, y = 1, 2, 4

    def __init__(self, first, second, size):
        self.first, self.second, self.size = first, second, size
        self.x0, self.y1 = self.send(first, self.x), self.send(second, self.y)

    def send(self, a, step):
        return lax.ppermute(a, "tp", [(i, i ^ step) for i in range(self.size)])

    def others(self, order=None):
        first, second = self.first, self.second
        if order:
            first, second = order(lambda a, b: (a, b), first, second)
        self.x1, self.y0 = self.send(second, self.x), self.send(first, self.y)
        self.c0 = self.send(first, self.core)

    def forward(self, order):
        came = (self.x0, self.y1, self.c0, self.second)
        self.x0, self.y1, self.c0, self.second = order(lambda *a: a, *came)
        self.c1 = self.send(self.second, self.core)
        self.d0, self.d1 = self.send(self.x0, self.y), self.send(self.y1, self.x)

    def pairs(self, order):
        came = (self.x0, self.y1, self.x1, self.y0, self.c1)
        self.x0, self.y1, self.x1, self.y0, self.c1 = order(lambda *a: a, *came)
        self.px0, self.py1 = self.send(self.x0, self.core), self.send(self.y1, self.core)
        self.px1, self.py0 = self.send(self.x1, self.core), self.send(self.y0, self.core)

    def near(self, order):
        steps = [step for step in (0, self.core, self.x, self.y, self.x | self.core, self.y | self.core) for _ in range(2)]
        pieces = (self.first, self.second, self.c0, self.c1, self.x0, self.x1, self.y0, self.y1)
        pieces += (self.px0, self.px1, self.py0, self.py1)
        self.full = order(lambda *a: place_pieces(None, a, steps, (0, 1) * 6, self.size), *pieces)

    def far_pairs(self, order):
        self.d0, self.d1 = order(lambda a, b: (a, b), self.d0, self.d1)
        self.pd0, self.pd1 = self.send(self.d0, self.core), self.send(self.d1, self.core)

    def far(self, order):
        far = self.x | self.y
        steps = (far, far, far | self.core, far | self.core)
        place = lambda full, *a: place_pieces(full, a, steps, (0, 1, 0, 1), self.size)
        self.full = order(place, self.full, self.d0, self.d1, self.pd0, self.pd1)
        return self.full


def place_kernel(me_ref, *refs, held):
    pieces, o_ref = refs[held:-1], refs[-1]
    for i, piece in enumerate(pieces):

        @pl.when(pl.program_id(0) == i)
        def _(piece=piece):
            o_ref[...] = piece[...].reshape(o_ref.shape)


def place_pieces(full, pieces, steps, halves, size):
    held = 0 if full is None else 1
    here, width = pieces[0].shape

    def target(j, me):
        device, half = me[0] ^ steps[0], halves[0]
        for i in range(1, len(pieces)):
            device = jnp.where(j == i, me[0] ^ steps[i], device)
            half = jnp.where(j == i, halves[i], half)
        return half, device, 0, 0

    hbm = pl.BlockSpec(memory_space=pl.ANY)
    me = lax.axis_index("tp").astype(jnp.int32).reshape(1)
    return pl.pallas_call(
        functools.partial(place_kernel, held=held),
        grid_spec=pltpu.PrefetchScalarGridSpec(
            num_scalar_prefetch=1,
            grid=(len(pieces),),
            in_specs=[hbm] * held + [pl.BlockSpec((here, width), lambda j, me: (0, 0))] * len(pieces),
            out_specs=pl.BlockSpec((1, None, here, width), target),
        ),
        out_shape=jax.ShapeDtypeStruct((2, size, here, width), bf16),
        input_output_aliases={1: 0} if held else {},
        compiler_params=params(),
        cost_estimate=SMALL,
        name="place_pieces",
    )(me, *([full] if held else []), *pieces)


class TpSum:
    def __init__(self, part, size):
        self.part, self.size, self.hop = part, size, 1
        self.send()

    def send(self):
        if self.size & (self.size - 1) == 0 and self.hop < self.size:
            self.came = lax.ppermute(self.part, "tp", [(i, i ^ self.hop) for i in range(self.size)])

    def fold(self, order):
        if self.size & (self.size - 1):
            self.part, self.size = lax.psum(self.part, "tp"), 1
        elif self.hop < self.size:
            self.part = order(lambda a, b: a + b, self.part, self.came)
            self.hop *= 2
            self.send()

    def result(self, order):
        while self.hop < self.size:
            self.fold(order)
        return self.part


def body(
    tokens,
    segment_ids,
    positions,
    norm_gain,
    norm_shift,
    query_key_value_weight,
    b_qkv,
    dense_weight,
    b_dense,
    inward_weight,
    b_in,
    outward_weight,
    b_out,
    cotangent,
):
    rows, tp = lax.axis_size("rows"), lax.axis_size("tp")
    seqs, here, width = tokens.shape
    length = here * tp
    n = seqs * length
    local = query_key_value_weight.shape[2]
    tile = min(128, local)
    span = length // 2

    exchange = tp == 8 and seqs == 2

    order = Order()
    gain, shift = norm_gain.astype(f32), norm_shift.astype(f32)
    norm = lambda a: norm_halves(a.reshape(seqs * here, width), gain, shift)
    halves = order(norm, tokens)

    if exchange:
        gather_normed = Gather(*halves, tp)
        gather_normed.others()

    def tables(positions, weight):
        place = positions.reshape(n, 1)
        cosine, sine = rope_tables(place, tile)
        start = jnp.arange(n, dtype=jnp.int32)[:, None] % span - place
        return cosine, sine, start, jnp.transpose(weight, (1, 0, 2))

    cosine, sine, start, w3 = order(tables, positions, query_key_value_weight)
    in_bias_row = b_in.astype(f32)[None]
    token_rows = lambda a: a.reshape(n, a.shape[-1])
    later = lambda a: lax.all_gather(order(lambda b: b, a), "tp", axis=1, tiled=True).reshape(n, width)
    if exchange:
        gather_normed.forward(order)
        gather_normed.pairs(order)
        grad = later(cotangent)
        gather_normed.near(order)
        hidden_of = lambda *a: mlp_hidden_of(*a, tuple(range(6)))
        hidden = order(hidden_of, gather_normed.full, inward_weight, in_bias_row)
        gather_normed.far_pairs(order)
        normed_full = gather_normed.far(order)
        hidden_of = lambda x, w, b, *before: mlp_hidden_of(x, w, b, (6, 7), before)
        act, slope = order(hidden_of, normed_full, inward_weight, in_bias_row, *hidden)
    else:
        normed_full = jnp.concatenate(halves).reshape(seqs, here, width)
        normed_full = lax.all_gather(normed_full, "tp", axis=1).reshape(seqs, tp, here, width)
        grad = later(cotangent)
        hidden_of = lambda *a: mlp_hidden_of(*a, tuple(range(tp)))
        act, slope = order(hidden_of, normed_full, inward_weight, in_bias_row)
    normed, act, slope = token_rows(normed_full), token_rows(act), token_rows(slope)
    qkv = order(project_qkv, normed, w3, b_qkv.astype(f32), cosine, sine)
    mlp_part = order(lambda *a: tokens_by_weight(*a, 0, 1), act, outward_weight).reshape(seqs, length, width)
    mlp_part, dense_ready, _ = lax.optimization_barrier((mlp_part, dense_weight, grad))
    mlp_tok = lax.psum_scatter(mlp_part, "tp", scatter_dimension=1, tiled=True).reshape(seqs * here, width)
    dense_full = lax.all_gather(dense_ready, "tp", axis=0, tiled=True)

    o0 = RowSum(order(lambda *a: weight_grad(*a, 0, 2), act, grad), rows)
    o1 = RowSum(order(lambda *a: weight_grad(*a, 1, 2), act, grad), rows)
    row_sum = lambda parts: [RowSum(part, rows) for part in parts]
    hidden_grad, attended_grad, in_bias = order(grad_in, grad, outward_weight, dense_weight, slope)
    o0.fold(order)
    i0, i1 = row_sum(order(lambda a, b: weight_grad_rows(a, b, (1, 1)), normed, hidden_grad))
    both = lambda row: lambda s, q, g, c, t, *before: attention_both(s, q, g, c, t, span, tp, row, before)
    attended, by_owner, dqkv = order(both(0), start, qkv, attended_grad, cosine, sine)
    o1.fold(order)
    o0.fold(order)
    for row in range(1, seqs):
        kept = (attended, by_owner, dqkv)
        attended, by_owner, dqkv = order(both(row), start, qkv, attended_grad, cosine, sine, *kept)
    mine = lax.all_to_all(by_owner, "tp", split_axis=0, concat_axis=0, tiled=True)
    i0.fold(order)
    o1.fold(order)
    qs, vs = row_sum(order(lambda a, b: weight_grad_parts(a, b, weight=EARLY_WEIGHT), normed, dqkv))
    units = in_bias.shape[1]
    out_grad = finish(o0, order, units)
    back = lambda share: lambda *a: normed_grad(*a[:5], shift[None], share, 2, a[5:])
    part, bias_a, norm_a = order(back(0), hidden_grad, dqkv, inward_weight, w3, normed)
    i1.fold(order)
    i0.fold(order)
    out_grad = finish(o1, order, units, units // 2, out_grad)
    part, bias_b, norm_b = order(back(1), hidden_grad, dqkv, inward_weight, w3, normed, part)
    back_tok = lax.psum_scatter(part.reshape(seqs, length, width), "tp", scatter_dimension=1, tiled=True)
    qs.fold(order)
    i1.fold(order)
    vs.fold(order)
    in_grad = finish(i0, order, width)
    (ds,) = row_sum([order(lambda a, b: weight_grad(a, b, weight=ORDER_WEIGHT), attended, grad)])

    cols = width // tp

    def column_sums(grad):
        mine = lax.dynamic_slice_in_dim(grad, lax.axis_index("tp") * cols, cols, 1)
        return jnp.sum(mine.astype(f32), axis=0)

    out_bias = order(column_sums, grad)
    rows_of = lambda a: a.reshape(seqs * here, width)
    own = lambda x, w, t, *m: project_own(x, w, b_dense.astype(f32)[None], b_out.astype(f32)[None], rows_of(t), m)
    layer_out, squares = order(own, mine, dense_full, tokens, mlp_tok)
    layer_out = layer_out.reshape(tokens.shape)

    def pack(norm_a, norm_b, squares):
        norm_sums = norm_a + norm_b
        squares = jnp.sum(squares[:4], axis=1)
        pad = jnp.zeros((124,), f32)
        return jnp.concatenate([norm_sums[0] / gain, norm_sums[1], squares, pad]).reshape(-1, 128)

    packed = TpSum(order(pack, norm_a, norm_b, squares), tp)
    qs.fold(order)
    packed.fold(order)
    vs.fold(order)
    in_grad = finish(i1, order, width, width // 2, in_grad)
    packed.fold(order)
    ds.fold(order)
    qkv_bias = bias_a + bias_b
    small = jnp.concatenate([in_bias[0], qkv_bias[:, 0].reshape(-1), out_bias]).reshape(-1, 128)
    small = RowSum(jnp.concatenate([packed.result(order), small]), rows)
    qkv_grad = finish(qs, order, 3 * width)
    ds.fold(order)
    small.fold(order)
    qkv_grad = finish(vs, order, 3 * width, 2 * width, qkv_grad)
    small.fold(order)

    def norm_back(back_tok, tokens, cotangent):
        values = tokens.astype(f32)
        center = values - jnp.mean(values, axis=-1, keepdims=True)
        inverse = lax.rsqrt(jnp.mean(center * center, axis=-1, keepdims=True) + epsilon)
        unit = center * inverse
        unit_grad = back_tok.astype(f32) * gain
        mean_grad = jnp.mean(unit_grad, axis=-1, keepdims=True)
        mean_both = jnp.mean(unit_grad * unit, axis=-1, keepdims=True)
        value_grad = (unit_grad - mean_grad - unit * mean_both) * inverse
        return (cotangent.astype(f32) + value_grad).astype(bf16)

    input_grad = order(norm_back, back_tok, tokens, cotangent)
    qkv_grad = jnp.transpose(qkv_grad.reshape(3, width, local), (1, 0, 2))
    dense_grad = finish(ds, order, local)
    small = small.result().reshape(-1)
    slice_at = lambda a: lax.dynamic_slice_in_dim(a, lax.axis_index("tp") * cols, cols, 0)
    gain_grad, shift_grad = slice_at(small[:width]), slice_at(small[width : 2 * width])
    rms_values = jnp.sqrt(small[2 * width : 2 * width + 4] / (seqs * rows * length * width))
    small = small[2 * width + 128 :]
    in_bias_grad = small[:units]
    qkv_bias_grad = small[units : units + 3 * local].reshape(3, local)
    out_bias_grad = small[units + 3 * local :]

    return (
        layer_out,
        input_grad,
        gain_grad,
        shift_grad,
        qkv_grad,
        qkv_bias_grad,
        dense_grad,
        out_bias_grad,
        in_grad,
        in_bias_grad,
        out_grad,
        out_bias_grad,
        rms_values,
    )


def solution(mesh):
    in_specs = (
        P("rows", "tp", None),
        P("rows", None),
        P("rows", None),
        P(),
        P(),
        P(None, None, "tp"),
        P(None, "tp"),
        P("tp", None),
        P(),
        P(None, "tp"),
        P("tp"),
        P("tp", None),
        P(),
        P("rows", "tp", None),
    )
    out_specs = (
        P("rows", "tp", None),
        P("rows", "tp", None),
        P("tp"),
        P("tp"),
        P(None, None, "tp"),
        P(None, "tp"),
        P("tp", None),
        P("tp"),
        P(None, "tp"),
        P("tp"),
        P("tp", None),
        P("tp"),
        P(),
    )
    return jax.shard_map(body, mesh=mesh, in_specs=in_specs, out_specs=out_specs, check_vma=False)
```

time: 776 us -> 661 us (0.85)
  waiting for transfers between devices: 199 us -> 111 us
  local copies, waits for them, and re-layouts: 43.6 us -> 8.66 us
  other arithmetic: 94.6 us -> 60.2 us
  Pallas kernels: 340 us -> 372 us
  starting transfers between devices: 79.1 us -> 89 us
    ppermute x30 -> x24, waiting for transfers between devices: 144 us -> 69.3 us  [send(): self.came = lax.ppermute(self.part, self.axis, self.hops.pop(0))]
    pallas_call x10 -> x17, Pallas kernels: 180 us -> 205 us  [the longest x2 61.5 us: attention_both(): pl.pallas_call(functools.partial(attention_kernel, bq=bq, held=held), gri...]
    concatenate x3 -> x1, local copies, waits for them, and re-layouts: 21.1 us -> 0.08 us  [pack(): jnp.concatenate([norm_sums[0] / gain, norm_sums[1], squares, pad])]
    ppermute x18 -> x14, waiting for transfers between devices: 52.5 us -> 38.5 us  [send(): return lax.ppermute(a, 'tp', [(i, i ^ step) for i in range(self.size)])]
    reduce_sum x4 -> x1, other arithmetic: 11 us -> 0.83 us  [pack(): squares = jnp.sum(squares[:4], axis=1)]
    sin x1 -> x0, other arithmetic: 9.37 us -> none  [tables(): cosine, sine = (jnp.cos(angles), jnp.sin(angles))]
    another operation x4 -> x0, other arithmetic: 8.99 us -> none  [body(): qkv_grad = jnp.stack([a.result() for a in (qs, ks, vs)], axis=1)]
    ppermute x30 -> x24, starting transfers between devices: 61.8 us -> 67.9 us  [send(): self.came = lax.ppermute(self.part, self.axis, self.hops.pop(0))]
  transfers between devices with their start and end apart: 55 -> 46, of which waited for: 20 -> 18; matrix products, arithmetic and copies ran while one was open for 16% -> 10% of each run, Pallas kernels for 44% -> 56%
where the time goes in v3:
time: 661 us; the launch traced here: 656 us
  Pallas kernels  372 us (56%)
  waiting for transfers between devices  111 us (17%)
  starting transfers between devices  89 us (13%)
  other arithmetic  60.2 us (9%)
  between operations  14.9 us (2%)
  local copies, waits for them, and re-layouts  8.66 us (1%)
    ppermute x24, waiting for transfers between devices, send(): self.came = lax.ppermute(self.part, self.axis, self.hops.pop(0))  69.3 us
    ppermute x24, starting transfers between devices, send(): self.came = lax.ppermute(self.part, self.axis, self.hops.pop(0))  67.9 us
    pallas_call x2, Pallas kernels, attention_both(): pl.pallas_call(functools.partial(attention_kernel, bq=bq, held=held), gri...  61.5 us
    pallas_call x2, Pallas kernels, normed_grad(): pl.pallas_call(functools.partial(normed_grad_kernel, held=held), grid=(st...  45.3 us
    convert_element_type x14, other arithmetic, fold(): add = lambda a, b: (a.astype(f32) + b.astype(f32)).astype(a.dtype)  43.2 us
    ppermute x14, waiting for transfers between devices, send(): return lax.ppermute(a, 'tp', [(i, i ^ step) for i in range(self.size)])  38.5 us
    pallas_call x3, Pallas kernels, weight_grad(): pl.pallas_call(weight_grad_kernel, grid=(cols // tile,), in_specs=[pl.Blo...  38.3 us
    pallas_call x2, Pallas kernels, mlp_hidden_of(): pl.pallas_call(functools.partial(chosen_kernel, held=held), grid_spec=plt...  34.7 us
  transfers between devices with their start and end apart: 46, of which 18 were waited for; matrix products, arithmetic and copies ran while one was open for 10% of the time, Pallas kernels for 56%

profile of v3, /device:TPU:0, one launch (start us, length us, event | category | flops | bytes accessed | tf_op | source)
XLA Modules:
  0.0 655.6 jit_solution(3491420100852447136)
XLA Ops:
  9.8 4.7 norm_halves.1
  14.6 2.9 collective-permute-start.3
  20.1 2.0 copy.39
  22.1 9.9 %rope_tables.1 = (f32[4096,128]{1,0:T(8,128)}, f32[4096,128]{1,0:T(8,128)}) custom-call(s32[4096,1]{1,0:T(8,128)} %bitcast.65, f32[1,128]{1,0:T(1,128)} %fusion.18.frequency_ref), custom_call_target="tpu_custom_call" | custom-call | flops 1 | bytes 1 | tf_op jit(solution)/shard_map/rope_tables/pallas_call | solution.py:99
  33.6 10.2 %collective-permute-done.1.refs_7_ = bf16[256,2048]{1,0:T(8,128)(2,1)S(1)} collective-permute-done((bf16[256,2048]{1,0:T(8,128)(2,1)}, bf16[256,2048]{1,0:T(8,128)(2,1)S(1)}, u32[]{:S(2)}, u32[]{:S(2)}) %collective-permute-start.1) | collective-permute-done | bytes 1048608 | tf_op jit(solution)/shard_map/ppermute | solution.py:631
  43.8 19.6 %collective-permute-done.refs_4_ = bf16[256,2048]{1,0:T(8,128)(2,1)} collective-permute-done((bf16[256,2048]{1,0:T(8,128)(2,1)}, bf16[256,2048]{1,0:T(8,128)(2,1)}, u32[]{:S(2)}, u32[]{:S(2)}) %collective-permute-start) | collective-permute-done | bytes 1048608 | tf_op jit(solution)/shard_map/ppermute | solution.py:631
  73.9 13.5 %place_pieces.2.refs_0_ = bf16[2,8,256,2048]{3,2,1,0:T(8,128)(2,1)} custom-call(s32[1]{0:T(128)} %bitcast.3.me_ref, bf16[256,2048]{1,0:T(8,128)(2,1)} %get-tuple-element.210.refs_0_, bf16[256,2048]{1,0:T(8,128)(2,1)} %get-tuple-element.211.refs_1_, bf16[256,2048]{1,0:T(8,128)(2,1)} %collective-permute-done.2.refs_2_, ...), custom_call_target="tpu_custom_call" | custom-call | flops 1 | bytes 1 | tf_op jit(solution)/shard_map/place_pieces/pallas_call | solution.py:692
  87.4 23.6 %mlp_hidden_of.2 = (bf16[2,8,256,1024]{3,2,1,0:T(8,128)(2,1)}, bf16[2,8,256,1024]{3,2,1,0:T(8,128)(2,1)}) custom-call(s32[1]{0:T(128)} %bitcast.3.me_ref, bf16[2,8,256,2048]{3,2,1,0:T(8,128)(2,1)} %place_pieces.2.refs_0_, bf16[2048,1024]{1,0:T(8,128)(2,1)} %refs_3_.1, f32[1,1024]{1,0:T(1,128)} %bitcast.76), custom_call_target="tpu_custom_call" | custom-call | flops 1 | bytes 1 | tf_op jit(solution)/shard_map/mlp_hidden_of/pallas_call | solution.py:180
  112.7 3.0 collective-permute-done.12.refs_3_
  117.7 4.7 place_pieces.3.refs_2_
  122.3 11.1 %mlp_hidden_of.3 = (bf16[2,8,256,1024]{3,2,1,0:T(8,128)(2,1)}, bf16[2,8,256,1024]{3,2,1,0:T(8,128)(2,1)}) custom-call(s32[1]{0:T(128)} %bitcast.3.me_ref, bf16[2,8,256,1024]{3,2,1,0:T(8,128)(2,1)} %get-tuple-element.234.refs_0_, bf16[2,8,256,1024]{3,2,1,0:T(8,128)(2,1)} %get-tuple-element.235.refs_1_, ...), custom_call_target="tpu_custom_call", output_to_operand_aliasing={{0}: (1, {}), {1}: (2, {})} | custom-call | flops 1 | bytes 1 | tf_op jit(solution)/shard_map/mlp_hidden_of/pallas_call | solution.py:180
  133.4 20.0 %qkv_rope.1.refs_1_.refs_2_.refs_3_.refs_4_.refs_5_.refs_6_ = bf16[3,4096,256]{2,1,0:T(8,128)(2,1)} custom-call(bf16[4096,2048]{1,0:T(8,128)(2,1)} %bitcast.43, bf16[3,2048,256]{2,1,0:T(8,128)(2,1)} %bitcast.61, f32[3,256]{1,0:T(4,128)} %convert_element_type.170.b_ref, f32[4096,128]{1,0:T(8,128)} %get-tuple-element.283.c_ref.refs_5_.refs_8_, ...), custom_call_target="tpu_custom_call" | custom-call | flops 1 | bytes 1 | tf_op jit(solution)/shard_map/qkv_rope/pallas_call | solution.py:131
  153.4 22.6 %tokens_by_weight.1 = bf16[4096,2048]{1,0:T(8,128)(2,1)} custom-call(bf16[4096,1024]{1,0:T(8,128)(2,1)} %bitcast.53, bf16[1024,2048]{1,0:T(8,128)(2,1)} %wo_ref), custom_call_target="tpu_custom_call" | custom-call | flops 1 | bytes 1 | tf_op jit(solution)/shard_map/tokens_by_weight/pallas_call | solution.py:258
  176.8 14.2 %weight_grad.3 = bf16[512,2048]{1,0:T(8,128)(2,1)} custom-call(bf16[4096,1024]{1,0:T(8,128)(2,1)} %bitcast.54, bf16[4096,2048]{1,0:T(8,128)(2,1)} %bitcast.48), custom_call_target="tpu_custom_call" | custom-call | flops 1 | bytes 1 | tf_op jit(solution)/shard_map/weight_grad/pallas_call | solution.py:279
  191.0 3.5 collective-permute-start.14
  194.5 13.8 %weight_grad.4 = bf16[512,2048]{1,0:T(8,128)(2,1)} custom-call(bf16[4096,1024]{1,0:T(8,128)(2,1)} %bitcast.55, bf16[4096,2048]{1,0:T(8,128)(2,1)} %bitcast.49), custom_call_target="tpu_custom_call" | custom-call | flops 1 | bytes 1 | tf_op jit(solution)/shard_map/weight_grad/pallas_call | solution.py:279
  208.3 2.6 collective-permute-start.16
  210.9 29.6 %grad_in.1 = (bf16[4096,1024]{1,0:T(8,128)(2,1)}, bf16[4096,256]{1,0:T(8,128)(2,1)}, f32[8,1024]{1,0:T(8,128)}) custom-call(bf16[4096,2048]{1,0:T(8,128)(2,1)} %bitcast.50, bf16[1024,2048]{1,0:T(8,128)(2,1)} %wo_ref, bf16[256,2048]{1,0:T(8,128)(2,1)} %wd_ref, bf16[4096,1024]{1,0:T(8,128)(2,1)} %bitcast.60), custom_call_target="tpu_custom_call" | custom-call | flops 1 | bytes 1 | tf_op jit(solution)/shard_map/grad_in/pallas_call | solution.py:221
  241.4 2.2 collective-permute-start.15
  243.6 26.3 %weight_grad_rows.1 = (bf16[1024,1024]{1,0:T(8,128)(2,1)}, bf16[1024,1024]{1,0:T(8,128)(2,1)}) custom-call(bf16[4096,2048]{1,0:T(8,128)(2,1)} %bitcast.44, bf16[4096,1024]{1,0:T(8,128)(2,1)} %get-tuple-element.316.b_ref.refs_0_.refs_1_), custom_call_target="tpu_custom_call" | custom-call | flops 1 | bytes 1 | tf_op jit(solution)/shard_map/weight_grad_rows/pallas_call | solution.py:313
  269.9 8.1 %collective-permute-start.17 = (bf16[1024,1024]{1,0:T(8,128)(2,1)}, bf16[1024,1024]{1,0:T(8,128)(2,1)}, u32[]{:S(2)}, u32[]{:S(2)}) collective-permute-start(bf16[1024,1024]{1,0:T(8,128)(2,1)} %get-tuple-element.290), channel_id=1, source_target_pairs={{0,8},{24,16},{1,9},{25,17},{2,10},{26,18},{3,11},{27,19},{4,12},{... | collective-permute-start | bytes 6291464 | tf_op jit(solution)/shard_map/ppermute | solution.py:565
  278.0 30.8 %attention_both.2 = (bf16[4096,256]{1,0:T(8,128)(2,1)}, bf16[8,2,256,256]{3,2,1,0:T(8,128)(2,1)}, bf16[3,4096,256]{2,1,0:T(8,128)(2,1)}) custom-call(s32[4096,1]{1,0:T(8,128)} %fusion.11.refs_0_.refs_3_, bf16[3,4096,256]{2,1,0:T(8,128)(2,1)} %qkv_rope.1.refs_1_.refs_2_.refs_3_.refs_4_.refs_5_.refs_6_, ...), custom_call_target="tpu_custom_call" | custom-call | flops 1 | bytes 1 | tf_op jit(solution)/shard_map/attention_both/pallas_call | solution.py:471
  308.8 2.5 add_convert_fusion.8
  311.3 2.0 collective-permute-start.21
  313.4 2.7 collective-permute-start.19
  316.0 2.4 add_convert_fusion.7.kept_ref
  320.2 30.7 %attention_both.3 = (bf16[4096,256]{1,0:T(8,128)(2,1)}, bf16[8,2,256,256]{3,2,1,0:T(8,128)(2,1)}, bf16[3,4096,256]{2,1,0:T(8,128)(2,1)}) custom-call(bf16[4096,256]{1,0:T(8,128)(2,1)} %get-tuple-element.277.refs_0_, bf16[8,2,256,256]{3,2,1,0:T(8,128)(2,1)} %get-tuple-element.278.refs_1_, ...), custom_call_target="tpu_custom_call", output_to_operand_aliasing={{0}: (0, {}), {1}: (1, {}), {2}: (2, {})} | custom-call | flops 1 | bytes 1 | tf_op jit(solution)/shard_map/attention_both/pallas_call | solution.py:471
  351.0 3.9 add_convert_fusion.6
  356.8 3.8 add_convert_fusion.5.kept_ref
  362.1 18.9 %weight_grad_parts.1 = (bf16[2,2048,256]{2,1,0:T(8,128)(2,1)}, bf16[2048,256]{1,0:T(8,128)(2,1)}) custom-call(bf16[4096,2048]{1,0:T(8,128)(2,1)} %bitcast.45, bf16[3,4096,256]{2,1,0:T(8,128)(2,1)} %get-tuple-element.317.b_ref.refs_1_.refs_2_), custom_call_target="tpu_custom_call" | custom-call | flops 1 | bytes 1 | tf_op jit(solution)/shard_map/weight_grad_parts/pallas_call | solution.py:337
  381.0 9.5 %collective-permute-start.25 = (bf16[2,2048,256]{2,1,0:T(8,128)(2,1)}, bf16[2,2048,256]{2,1,0:T(8,128)(2,1)}, u32[]{:S(2)}, u32[]{:S(2)}) collective-permute-start(bf16[2,2048,256]{2,1,0:T(8,128)(2,1)} %get-tuple-element.324), channel_id=1, source_target_pairs={{0,8},{24,16},{1,9},{25,17},{2,10},{26,18},{3,11},{27,19},{4,12},{... | collective-permute-start | bytes 6291464 | tf_op jit(solution)/shard_map/ppermute | solution.py:565
  390.5 4.5 finish.7.refs_0_
  395.0 22.6 %normed_grad.2 = (bf16[4096,2048]{1,0:T(8,128)(2,1)}, f32[3,8,256]{2,1,0:T(8,128)}, f32[8,2048]{1,0:T(8,128)}) custom-call(bf16[4096,1024]{1,0:T(8,128)(2,1)} %get-tuple-element.316.b_ref.refs_0_.refs_1_, bf16[3,4096,256]{2,1,0:T(8,128)(2,1)} %get-tuple-element.317.b_ref.refs_1_.refs_2_, bf16[2048,1024]{1,0:T(8,128)(2,1)} %refs_3_.1, ...), custom_call_target="tpu_custom_call" | custom-call | flops 1 | bytes 1 | tf_op jit(solution)/shard_map/normed_grad/pallas_call | solution.py:381
  417.6 4.5 add_convert_fusion.4
  422.1 2.0 collective-permute-start.24
  424.2 3.2 add_convert_fusion.3.kept_ref
  427.4 5.5 finish.8
  432.9 22.6 %normed_grad.3 = (bf16[4096,2048]{1,0:T(8,128)(2,1)}, f32[3,8,256]{2,1,0:T(8,128)}, f32[8,2048]{1,0:T(8,128)}) custom-call(bf16[4096,2048]{1,0:T(8,128)(2,1)} %get-tuple-element.315.refs_0_, bf16[4096,1024]{1,0:T(8,128)(2,1)} %get-tuple-element.316.b_ref.refs_0_.refs_1_, ...), custom_call_target="tpu_custom_call", output_to_operand_aliasing={{0}: (0, {})} | custom-call | flops 1 | bytes 1 | tf_op jit(solution)/shard_map/normed_grad/pallas_call | solution.py:381
  457.0 6.9 %collective-permute-start.23 = (bf16[2048,256]{1,0:T(8,128)(2,1)S(1)}, bf16[2048,256]{1,0:T(8,128)(2,1)}, u32[]{:S(2)}, u32[]{:S(2)}) collective-permute-start(bf16[2048,256]{1,0:T(8,128)(2,1)S(1)} %copy-done.12), channel_id=1, source_target_pairs={{0,8},{24,16},{1,9},{25,17},{2,10},{26,18},{3,11},{27,19},{4,12},{... | collective-permute-start | bytes 3145736 | tf_op jit(solution)/shard_map/ppermute | solution.py:565
  465.1 5.6 all-to-all-start
  470.7 4.8 add_convert_fusion.2
  477.4 5.3 add_convert_fusion.1.kept_ref
  484.0 2.5 add_convert_fusion.13
  488.2 18.1 %collective-permute-done.22.came_ref = bf16[1024,1024]{1,0:T(8,128)(2,1)} collective-permute-done((bf16[1024,1024]{1,0:T(8,128)(2,1)S(1)}, bf16[1024,1024]{1,0:T(8,128)(2,1)}, u32[]{:S(2)}, u32[]{:S(2)}) %collective-permute-start.22) | collective-permute-done | bytes 2097184 | tf_op jit(solution)/shard_map/ppermute | solution.py:565
  506.3 3.9 finish.9.refs_0_
  510.2 10.3 %weight_grad.5 = bf16[256,2048]{1,0:T(8,128)(2,1)} custom-call(bf16[4096,256]{1,0:T(8,128)(2,1)} %get-tuple-element.332.a_ref, bf16[4096,2048]{1,0:T(8,128)(2,1)} %bitcast.51), custom_call_target="tpu_custom_call" | custom-call | flops 185000001536 | bytes 1 | tf_op jit(solution)/shard_map/weight_grad/pallas_call | solution.py:279
  520.5 2.4 collective-permute-start.33
  522.9 2.3 convert_reduce_fusion.1
  525.3 10.7 %project_own.1 = (bf16[512,2048]{1,0:T(8,128)(2,1)}, f32[8,512]{1,0:T(8,128)}) custom-call(bf16[8,2,256,256]{3,2,1,0:T(8,128)(2,1)} %all-to-all-done.x_ref, bf16[2048,2048]{1,0:T(8,128)(2,1)} %all-gather.5.cloned.1.call-done.w_ref, f32[1,2048]{1,0:T(1,128)} %bitcast.78, f32[1,2048]{1,0:T(1,128)} %bitcast.79, bf16[512,2048]{1,0:T(8,128)(2,1)} %bitcast.57, ...), custom_call_target="tpu_custom_call" | custom-call | flops 1 | bytes 1 | tf_op jit(solution)/shard_map/project_own/pallas_call | solution.py:527
  537.1 2.9 add_convert_fusion
  541.3 3.4 collective-permute-start.29
  544.6 2.8 add_convert_fusion.12.kept_ref
  547.4 2.1 collective-permute-done.30.came_ref
  549.6 3.7 finish.10
  561.3 2.6 collective-permute-done.32
  563.9 6.7 %collective-permute-start.34 = (f32[49,128]{1,0:T(8,128)S(1)}, f32[49,128]{1,0:T(8,128)S(1)}, u32[]{:S(2)}, u32[]{:S(2)}) collective-permute-start(f32[49,128]{1,0:T(8,128)S(1)} %pad_maximum_fusion), channel_id=1, source_target_pairs={{0,8},{24,16},{1,9},{25,17},{2,10},{26,18},{3,11},{27,19},{4,12},{... | collective-permute-start | bytes 75272 | tf_op jit(solution)/shard_map/ppermute | solution.py:565
  570.6 23.9 %collective-permute-done.36 = bf16[2,2048,256]{2,1,0:T(8,128)(2,1)} collective-permute-done((bf16[2,2048,256]{2,1,0:T(8,128)(2,1)S(1)}, bf16[2,2048,256]{2,1,0:T(8,128)(2,1)}, u32[]{:S(2)}, u32[]{:S(2)}) %collective-permute-start.36) | collective-permute-done | bytes 2097184 | tf_op jit(solution)/shard_map/ppermute | solution.py:565
  594.5 6.5 finish.11.refs_0_
  603.9 10.9 %collective-permute-done.38.came_ref = bf16[2048,256]{1,0:T(8,128)(2,1)} collective-permute-done((bf16[2048,256]{1,0:T(8,128)(2,1)}, bf16[2048,256]{1,0:T(8,128)(2,1)}, u32[]{:S(2)}, u32[]{:S(2)}) %collective-permute-start.38) | collective-permute-done | bytes 1048608 | tf_op jit(solution)/shard_map/ppermute | solution.py:565
  614.7 3.8 finish.12
  621.4 3.2 collective-permute-done.39
  630.9 3.2 fusion.8
  634.0 11.0 %collective-permute-done.40.came_ref = bf16[256,2048]{1,0:T(8,128)(2,1)} collective-permute-done((bf16[256,2048]{1,0:T(8,128)(2,1)S(1)}, bf16[256,2048]{1,0:T(8,128)(2,1)}, u32[]{:S(2)}, u32[]{:S(2)}) %collective-permute-start.40) | collective-permute-done | bytes 1048608 | tf_op jit(solution)/shard_map/ppermute | solution.py:565
  645.0 3.0 finish.13
  (176 shorter events, 57.9 us)
Async XLA Ops:
  7.2 12.9 %copy-start.24 = (s32[2,2048]{1,0:T(2,128)S(1)}, s32[2,2048]{1,0:T(2,128)}, u32[]{:S(2)}) copy-start(s32[2,2048]{1,0:T(2,128)} %param.15) | copy-start | bytes 49156
  7.2 168.8 %all-gather.3.cloned.1.call-start = ((), (), s32[]{:S(2)}) async-start(), calls=%async_computation.3 | async-start | bytes 18874368 | tf_op jit(solution)/shard_map/all_gather | solution.py:775
  14.6 48.9 %collective-permute-start.3 = (bf16[256,2048]{1,0:T(8,128)(2,1)}, bf16[256,2048]{1,0:T(8,128)(2,1)S(1)}, u32[]{:S(2)}, u32[]{:S(2)}) collective-permute-start(bf16[256,2048]{1,0:T(8,128)(2,1)} %get-tuple-element.211.refs_1_), channel_id=1, source_target_pairs={{0,2},{1,3},{2,0},{3,1},{4,6},{5,7},{6,4},{7,5},{8,10},{9,11},{10,... | collective-permute-start | bytes 3145736 | tf_op jit(solution)/shard_map/ppermute | solution.py:631
  17.5 26.3 %collective-permute-start.1 = (bf16[256,2048]{1,0:T(8,128)(2,1)}, bf16[256,2048]{1,0:T(8,128)(2,1)S(1)}, u32[]{:S(2)}, u32[]{:S(2)}) collective-permute-start(bf16[256,2048]{1,0:T(8,128)(2,1)} %get-tuple-element.211.refs_1_), channel_id=1, source_target_pairs={{0,4},{1,5},{2,6},{3,7},{4,0},{5,1},{6,2},{7,3},{8,12},{9,13},{10,... | collective-permute-start | bytes 3145736 | tf_op jit(solution)/shard_map/ppermute | solution.py:631
  19.0 45.9 %collective-permute-start.4 = (bf16[256,2048]{1,0:T(8,128)(2,1)}, bf16[256,2048]{1,0:T(8,128)(2,1)}, u32[]{:S(2)}, u32[]{:S(2)}) collective-permute-start(bf16[256,2048]{1,0:T(8,128)(2,1)} %get-tuple-element.210.refs_0_), channel_id=1, source_target_pairs={{0,4},{1,5},{2,6},{3,7},{4,0},{5,1},{6,2},{7,3},{8,12},{9,13},{10,... | collective-permute-start | bytes 3145736 | tf_op jit(solution)/shard_map/ppermute | solution.py:631
  19.5 24.3 %collective-permute-start.2 = (bf16[256,2048]{1,0:T(8,128)(2,1)}, bf16[256,2048]{1,0:T(8,128)(2,1)}, u32[]{:S(2)}, u32[]{:S(2)}) collective-permute-start(bf16[256,2048]{1,0:T(8,128)(2,1)} %get-tuple-element.210.refs_0_), channel_id=1, source_target_pairs={{0,1},{1,0},{2,3},{3,2},{4,5},{5,4},{6,7},{7,6},{8,9},{9,8},{10,11... | collective-permute-start | bytes 3145736 | tf_op jit(solution)/shard_map/ppermute | solution.py:631
  19.5 43.9 %collective-permute-start = (bf16[256,2048]{1,0:T(8,128)(2,1)}, bf16[256,2048]{1,0:T(8,128)(2,1)}, u32[]{:S(2)}, u32[]{:S(2)}) collective-permute-start(bf16[256,2048]{1,0:T(8,128)(2,1)} %get-tuple-element.210.refs_0_), channel_id=1, source_target_pairs={{0,2},{1,3},{2,0},{3,1},{4,6},{5,7},{6,4},{7,5},{8,10},{9,11},{10,... | collective-permute-start | bytes 3145736 | tf_op jit(solution)/shard_map/ppermute | solution.py:631
  32.0 31.4 %copy-start.14 = (bf16[256,2048]{1,0:T(8,128)(2,1)S(1)}, bf16[256,2048]{1,0:T(8,128)(2,1)}, u32[]{:S(2)}) copy-start(bf16[256,2048]{1,0:T(8,128)(2,1)} %get-tuple-element.211.refs_1_) | copy-start | bytes 3145732
  33.6 37.9 %copy-start.28 = (bf16[1024]{0:T(1024)(128)(2,1)S(1)}, bf16[1024]{0:T(1024)(128)(2,1)}, u32[]{:S(2)}) copy-start(bf16[1024]{0:T(1024)(128)(2,1)} %param.23) | copy-start | bytes 6148
  43.8 30.1 %copy-start.13 = (bf16[256,2048]{1,0:T(8,128)(2,1)}, bf16[256,2048]{1,0:T(8,128)(2,1)S(1)}, u32[]{:S(2)}) copy-start(bf16[256,2048]{1,0:T(8,128)(2,1)S(1)} %collective-permute-done.1.refs_7_) | copy-start | bytes 3145732
  63.4 2.8 collective-permute-start.5
  66.3 459.0 %all-gather.5.cloned.1.call-start = ((), (), s32[]{:S(2)}) async-start(), calls=%async_computation.4 | async-start | bytes 9437184 | tf_op jit(solution)/shard_map/all_gather | solution.py:798
  66.5 3.2 collective-permute-start.6
  66.7 5.5 collective-permute-start.7
  67.1 5.6 collective-permute-start.8
  67.2 6.6 %collective-permute-start.9 = (bf16[256,2048]{1,0:T(8,128)(2,1)S(1)}, bf16[256,2048]{1,0:T(8,128)(2,1)}, u32[]{:S(2)}, u32[]{:S(2)}) collective-permute-start(bf16[256,2048]{1,0:T(8,128)(2,1)S(1)} %collective-permute-done.1.refs_7_), channel_id=1, source_target_pairs={{0,1},{1,0},{2,3},{3,2},{4,5},{5,4},{6,7},{7,6},{8,9},{9,8},{10,11... | collective-permute-start | bytes 3145736 | tf_op jit(solution)/shard_map/ppermute | solution.py:631
  67.6 43.5 %collective-permute-start.10 = (bf16[256,2048]{1,0:T(8,128)(2,1)}, bf16[256,2048]{1,0:T(8,128)(2,1)S(1)}, u32[]{:S(2)}, u32[]{:S(2)}) collective-permute-start(bf16[256,2048]{1,0:T(8,128)(2,1)} %collective-permute-done.refs_4_), channel_id=1, source_target_pairs={{0,4},{1,5},{2,6},{3,7},{4,0},{5,1},{6,2},{7,3},{8,12},{9,13},{10,... | collective-permute-start | bytes 3145736 | tf_op jit(solution)/shard_map/ppermute | solution.py:631
  69.7 41.8 %collective-permute-start.11 = (bf16[256,2048]{1,0:T(8,128)(2,1)S(1)}, bf16[256,2048]{1,0:T(8,128)(2,1)}, u32[]{:S(2)}, u32[]{:S(2)}) collective-permute-start(bf16[256,2048]{1,0:T(8,128)(2,1)S(1)} %collective-permute-done.1.refs_7_), channel_id=1, source_target_pairs={{0,2},{1,3},{2,0},{3,1},{4,6},{5,7},{6,4},{7,5},{8,10},{9,11},{10,... | collective-permute-start | bytes 3145736 | tf_op jit(solution)/shard_map/ppermute | solution.py:631
  87.4 24.7 %copy-start.29 = (bf16[3,256]{1,0:T(4,128)(2,1)S(1)}, bf16[3,256]{1,0:T(4,128)(2,1)}, u32[]{:S(2)}) copy-start(bf16[3,256]{1,0:T(4,128)(2,1)} %param.19) | copy-start | bytes 4612
  111.6 4.1 collective-permute-start.12
  111.6 4.4 collective-permute-start.13
  176.1 349.2 %reduce-scatter.3.cloned.1.call-start = ((), (), s32[]{:S(2)}) async-start(), calls=%async_computation.5 | async-start | bytes 18874368 | tf_op jit(solution)/shard_map/reduce_scatter | solution.py:797
  176.8 450.9 %reduce-scatter.5.cloned.1.call-start = ((), (), s32[]{:S(2)}) async-start(), calls=%async_computation.6 | async-start | bytes 18874368 | tf_op jit(solution)/shard_map/reduce_scatter | solution.py:825
  191.0 49.5 %collective-permute-start.14 = (bf16[512,2048]{1,0:T(8,128)(2,1)}, bf16[512,2048]{1,0:T(8,128)(2,1)S(1)}, u32[]{:S(2)}, u32[]{:S(2)}) collective-permute-start(bf16[512,2048]{1,0:T(8,128)(2,1)} %weight_grad.3), channel_id=1, source_target_pairs={{0,8},{24,16},{1,9},{25,17},{2,10},{26,18},{3,11},{27,19},{4,12},{... | collective-permute-start | bytes 6291464 | tf_op jit(solution)/shard_map/ppermute | solution.py:565
  208.3 100.5 %collective-permute-start.16 = (bf16[512,2048]{1,0:T(8,128)(2,1)}, bf16[512,2048]{1,0:T(8,128)(2,1)}, u32[]{:S(2)}, u32[]{:S(2)}) collective-permute-start(bf16[512,2048]{1,0:T(8,128)(2,1)} %weight_grad.4), channel_id=1, source_target_pairs={{0,8},{24,16},{1,9},{25,17},{2,10},{26,18},{3,11},{27,19},{4,12},{... | collective-permute-start | bytes 6291464 | tf_op jit(solution)/shard_map/ppermute | solution.py:565
  210.9 29.6 %copy-start.8 = (bf16[512,2048]{1,0:T(8,128)(2,1)S(1)}, bf16[512,2048]{1,0:T(8,128)(2,1)}, u32[]{:S(2)}) copy-start(bf16[512,2048]{1,0:T(8,128)(2,1)} %weight_grad.3) | copy-start | bytes 6291460
  241.4 74.6 %collective-permute-start.15 = (bf16[512,2048]{1,0:T(8,128)(2,1)S(1)}, bf16[512,2048]{1,0:T(8,128)(2,1)}, u32[]{:S(2)}, u32[]{:S(2)}) collective-permute-start(bf16[512,2048]{1,0:T(8,128)(2,1)S(1)} %add_convert_fusion.9), channel_id=1, source_target_pairs={{8,16},{16,8},{9,17},{17,9},{10,18},{18,10},{11,19},{19,11},{12,20... | collective-permute-start | bytes 6291464 | tf_op jit(solution)/shard_map/ppermute | solution.py:565
  269.9 81.1 %collective-permute-start.17 = (bf16[1024,1024]{1,0:T(8,128)(2,1)}, bf16[1024,1024]{1,0:T(8,128)(2,1)}, u32[]{:S(2)}, u32[]{:S(2)}) collective-permute-start(bf16[1024,1024]{1,0:T(8,128)(2,1)} %get-tuple-element.290), channel_id=1, source_target_pairs={{0,8},{24,16},{1,9},{25,17},{2,10},{26,18},{3,11},{27,19},{4,12},{... | collective-permute-start | bytes 6291464 | tf_op jit(solution)/shard_map/ppermute | solution.py:565
  278.0 30.8 %copy-start.7 = (bf16[512,2048]{1,0:T(8,128)(2,1)S(1)}, bf16[512,2048]{1,0:T(8,128)(2,1)}, u32[]{:S(2)}) copy-start(bf16[512,2048]{1,0:T(8,128)(2,1)} %weight_grad.4) | copy-start | bytes 6291460
  311.3 45.5 %collective-permute-start.21 = (bf16[512,2048]{1,0:T(8,128)(2,1)S(1)}, bf16[512,2048]{1,0:T(8,128)(2,1)}, u32[]{:S(2)}, u32[]{:S(2)}) collective-permute-start(bf16[512,2048]{1,0:T(8,128)(2,1)S(1)} %add_convert_fusion.8), channel_id=1, source_target_pairs={{8,16},{16,8},{9,17},{17,9},{10,18},{18,10},{11,19},{19,11},{12,20... | collective-permute-start | bytes 6291464 | tf_op jit(solution)/shard_map/ppermute | solution.py:565
  313.4 104.3 %collective-permute-start.19 = (bf16[1024,1024]{1,0:T(8,128)(2,1)}, bf16[1024,1024]{1,0:T(8,128)(2,1)}, u32[]{:S(2)}, u32[]{:S(2)}) collective-permute-start(bf16[1024,1024]{1,0:T(8,128)(2,1)} %get-tuple-element.308), channel_id=1, source_target_pairs={{0,8},{24,16},{1,9},{25,17},{2,10},{26,18},{3,11},{27,19},{4,12},{... | collective-permute-start | bytes 6291464 | tf_op jit(solution)/shard_map/ppermute | solution.py:565
  318.5 32.5 %copy-start.2 = (bf16[512,2048]{1,0:T(8,128)(2,1)}, bf16[512,2048]{1,0:T(8,128)(2,1)S(1)}, u32[]{:S(2)}) copy-start(bf16[512,2048]{1,0:T(8,128)(2,1)S(1)} %add_convert_fusion.7.kept_ref) | copy-start | bytes 6291460
  318.5 32.5 %copy-start.11 = (bf16[1024,1024]{1,0:T(8,128)(2,1)S(1)}, bf16[1024,1024]{1,0:T(8,128)(2,1)}, u32[]{:S(2)}) copy-start(bf16[1024,1024]{1,0:T(8,128)(2,1)} %get-tuple-element.290) | copy-start | bytes 6291460
  318.5 72.0 %collective-permute-start.20 = (bf16[512,2048]{1,0:T(8,128)(2,1)S(1)}, bf16[512,2048]{1,0:T(8,128)(2,1)}, u32[]{:S(2)}, u32[]{:S(2)}) collective-permute-start(bf16[512,2048]{1,0:T(8,128)(2,1)S(1)} %add_convert_fusion.7.kept_ref), channel_id=1, source_target_pairs={{8,0},{16,24},{9,1},{17,25},{10,2},{18,26},{11,3},{19,27},{12,4},{... | collective-permute-start | bytes 6291464 | tf_op jit(solution)/shard_map/ppermute | solution.py:565
  354.9 69.3 %collective-permute-start.18 = (bf16[1024,1024]{1,0:T(8,128)(2,1)}, bf16[1024,1024]{1,0:T(8,128)(2,1)}, u32[]{:S(2)}, u32[]{:S(2)}) collective-permute-start(bf16[1024,1024]{1,0:T(8,128)(2,1)} %add_convert_fusion.6), channel_id=1, source_target_pairs={{8,16},{16,8},{9,17},{17,9},{10,18},{18,10},{11,19},{19,11},{12,20... | collective-permute-start | bytes 6291464 | tf_op jit(solution)/shard_map/ppermute | solution.py:565
  360.6 66.7 %collective-permute-start.26 = (bf16[512,2048]{1,0:T(8,128)(2,1)}, bf16[512,2048]{1,0:T(8,128)(2,1)}, u32[]{:S(2)}, u32[]{:S(2)}) collective-permute-start(bf16[512,2048]{1,0:T(8,128)(2,1)} %add_convert_fusion.5.kept_ref), channel_id=1, source_target_pairs={{8,0},{16,24},{9,1},{17,25},{10,2},{18,26},{11,3},{19,27},{12,4},{... | collective-permute-start | bytes 6291464 | tf_op jit(solution)/shard_map/ppermute | solution.py:565
  381.0 89.6 %collective-permute-start.25 = (bf16[2,2048,256]{2,1,0:T(8,128)(2,1)}, bf16[2,2048,256]{2,1,0:T(8,128)(2,1)}, u32[]{:S(2)}, u32[]{:S(2)}) collective-permute-start(bf16[2,2048,256]{2,1,0:T(8,128)(2,1)} %get-tuple-element.324), channel_id=1, source_target_pairs={{0,8},{24,16},{1,9},{25,17},{2,10},{26,18},{3,11},{27,19},{4,12},{... | collective-permute-start | bytes 6291464 | tf_op jit(solution)/shard_map/ppermute | solution.py:565
  422.1 55.3 %collective-permute-start.24 = (bf16[1024,1024]{1,0:T(8,128)(2,1)}, bf16[1024,1024]{1,0:T(8,128)(2,1)}, u32[]{:S(2)}, u32[]{:S(2)}) collective-permute-start(bf16[1024,1024]{1,0:T(8,128)(2,1)} %add_convert_fusion.4), channel_id=1, source_target_pairs={{8,16},{16,8},{9,17},{17,9},{10,18},{18,10},{11,19},{19,11},{12,20... | collective-permute-start | bytes 6291464 | tf_op jit(solution)/shard_map/ppermute | solution.py:565
  427.4 28.2 %copy-start.3 = (bf16[1024,1024]{1,0:T(8,128)(2,1)}, bf16[1024,1024]{1,0:T(8,128)(2,1)S(1)}, u32[]{:S(2)}) copy-start(bf16[1024,1024]{1,0:T(8,128)(2,1)S(1)} %add_convert_fusion.3.kept_ref) | copy-start | bytes 6291460
  455.6 50.7 %collective-permute-start.22 = (bf16[1024,1024]{1,0:T(8,128)(2,1)S(1)}, bf16[1024,1024]{1,0:T(8,128)(2,1)}, u32[]{:S(2)}, u32[]{:S(2)}) collective-permute-start(bf16[1024,1024]{1,0:T(8,128)(2,1)S(1)} %add_convert_fusion.3.kept_ref), channel_id=1, source_target_pairs={{8,0},{16,24},{9,1},{17,25},{10,2},{18,26},{11,3},{19,27},{12,4},{... | collective-permute-start | bytes 6291464 | tf_op jit(solution)/shard_map/ppermute | solution.py:565
  457.0 27.0 %collective-permute-start.23 = (bf16[2048,256]{1,0:T(8,128)(2,1)S(1)}, bf16[2048,256]{1,0:T(8,128)(2,1)}, u32[]{:S(2)}, u32[]{:S(2)}) collective-permute-start(bf16[2048,256]{1,0:T(8,128)(2,1)S(1)} %copy-done.12), channel_id=1, source_target_pairs={{0,8},{24,16},{1,9},{25,17},{2,10},{26,18},{3,11},{27,19},{4,12},{... | collective-permute-start | bytes 3145736 | tf_op jit(solution)/shard_map/ppermute | solution.py:565
  465.1 60.2 %all-to-all-start = ((bf16[8,2,256,256]{3,2,1,0:T(8,128)(2,1)}), bf16[8,2,256,256]{3,2,1,0:T(8,128)(2,1)}, u32[]{:S(2)}, u32[]{:S(2)}) async-start(bf16[8,2,256,256]{3,2,1,0:T(8,128)(2,1)} %get-tuple-element.285), calls=%async_computation | async-start | bytes 4194304 | tf_op jit(solution)/shard_map/all_to_all | solution.py:813
  475.4 61.6 %collective-permute-start.28 = (bf16[2,2048,256]{2,1,0:T(8,128)(2,1)}, bf16[2,2048,256]{2,1,0:T(8,128)(2,1)}, u32[]{:S(2)}, u32[]{:S(2)}) collective-permute-start(bf16[2,2048,256]{2,1,0:T(8,128)(2,1)} %add_convert_fusion.2), channel_id=1, source_target_pairs={{8,16},{16,8},{9,17},{17,9},{10,18},{18,10},{11,19},{19,11},{12,20... | collective-permute-start | bytes 6291464 | tf_op jit(solution)/shard_map/ppermute | solution.py:565
  482.7 66.9 %collective-permute-start.30 = (bf16[1024,1024]{1,0:T(8,128)(2,1)}, bf16[1024,1024]{1,0:T(8,128)(2,1)}, u32[]{:S(2)}, u32[]{:S(2)}) collective-permute-start(bf16[1024,1024]{1,0:T(8,128)(2,1)} %add_convert_fusion.1.kept_ref), channel_id=1, source_target_pairs={{8,0},{16,24},{9,1},{17,25},{10,2},{18,26},{11,3},{19,27},{12,4},{... | collective-permute-start | bytes 6291464 | tf_op jit(solution)/shard_map/ppermute | solution.py:565
  486.5 58.1 %collective-permute-start.31 = (bf16[2048,256]{1,0:T(8,128)(2,1)}, bf16[2048,256]{1,0:T(8,128)(2,1)}, u32[]{:S(2)}, u32[]{:S(2)}) collective-permute-start(bf16[2048,256]{1,0:T(8,128)(2,1)} %add_convert_fusion.13), channel_id=1, source_target_pairs={{8,16},{16,8},{9,17},{17,9},{10,18},{18,10},{11,19},{19,11},{12,20... | collective-permute-start | bytes 3145736 | tf_op jit(solution)/shard_map/ppermute | solution.py:565
  520.5 32.8 %collective-permute-start.33 = (bf16[256,2048]{1,0:T(8,128)(2,1)}, bf16[256,2048]{1,0:T(8,128)(2,1)}, u32[]{:S(2)}, u32[]{:S(2)}) collective-permute-start(bf16[256,2048]{1,0:T(8,128)(2,1)} %weight_grad.5), channel_id=1, source_target_pairs={{0,8},{24,16},{1,9},{25,17},{2,10},{26,18},{3,11},{27,19},{4,12},{... | collective-permute-start | bytes 3145736 | tf_op jit(solution)/shard_map/ppermute | solution.py:565
  525.3 10.7 %copy-start.21 = (f32[8,2048]{1,0:T(8,128)S(1)}, f32[8,2048]{1,0:T(8,128)}, u32[]{:S(2)}) copy-start(f32[8,2048]{1,0:T(8,128)} %get-tuple-element.341) | copy-start | bytes 196612
  525.3 10.7 %copy-start.22 = (f32[8,2048]{1,0:T(8,128)S(1)}, f32[8,2048]{1,0:T(8,128)}, u32[]{:S(2)}) copy-start(f32[8,2048]{1,0:T(8,128)} %get-tuple-element.342) | copy-start | bytes 196612
  525.3 11.6 %copy-start.23 = (bf16[2048]{0:T(1024)(128)(2,1)S(1)}, bf16[2048]{0:T(1024)(128)(2,1)}, u32[]{:S(2)}) copy-start(bf16[2048]{0:T(1024)(128)(2,1)} %param.16) | copy-start | bytes 12292
  537.0 4.2 collective-permute-start.27
  539.9 13.4 %copy-start.4 = (bf16[2,2048,256]{2,1,0:T(8,128)(2,1)}, bf16[2,2048,256]{2,1,0:T(8,128)(2,1)S(1)}, u32[]{:S(2)}) copy-start(bf16[2,2048,256]{2,1,0:T(8,128)(2,1)S(1)} %add_convert_fusion) | copy-start | bytes 6291460
  539.9 54.6 %collective-permute-start.36 = (bf16[2,2048,256]{2,1,0:T(8,128)(2,1)S(1)}, bf16[2,2048,256]{2,1,0:T(8,128)(2,1)}, u32[]{:S(2)}, u32[]{:S(2)}) collective-permute-start(bf16[2,2048,256]{2,1,0:T(8,128)(2,1)S(1)} %add_convert_fusion), channel_id=1, source_target_pairs={{8,0},{16,24},{9,1},{17,25},{10,2},{18,26},{11,3},{19,27},{12,4},{... | collective-permute-start | bytes 6291464 | tf_op jit(solution)/shard_map/ppermute | solution.py:565
  541.3 12.0 %collective-permute-start.29 = (f32[33,128]{1,0:T(8,128)S(1)}, f32[33,128]{1,0:T(8,128)S(1)}, u32[]{:S(2)}, u32[]{:S(2)}) collective-permute-start(f32[33,128]{1,0:T(8,128)S(1)} %add.140), channel_id=1, source_target_pairs={{0,2},{1,3},{2,0},{3,1},{4,6},{5,7},{6,4},{7,5},{8,10},{9,11},{10,... | collective-permute-start | bytes 50696 | tf_op jit(solution)/shard_map/ppermute | solution.py:715
  555.1 46.0 %copy-start.10 = (bf16[256,2048]{1,0:T(8,128)(2,1)}, bf16[256,2048]{1,0:T(8,128)(2,1)S(1)}, u32[]{:S(2)}) copy-start(bf16[256,2048]{1,0:T(8,128)(2,1)S(1)} %add_convert_fusion.11) | copy-start | bytes 3145732
  555.1 46.0 %collective-permute-start.35 = (bf16[256,2048]{1,0:T(8,128)(2,1)S(1)}, bf16[256,2048]{1,0:T(8,128)(2,1)}, u32[]{:S(2)}, u32[]{:S(2)}) collective-permute-start(bf16[256,2048]{1,0:T(8,128)(2,1)S(1)} %add_convert_fusion.11), channel_id=1, source_target_pairs={{8,16},{16,8},{9,17},{17,9},{10,18},{18,10},{11,19},{19,11},{12,20... | collective-permute-start | bytes 3145736 | tf_op jit(solution)/shard_map/ppermute | solution.py:565
  556.8 57.9 %collective-permute-start.38 = (bf16[2048,256]{1,0:T(8,128)(2,1)}, bf16[2048,256]{1,0:T(8,128)(2,1)}, u32[]{:S(2)}, u32[]{:S(2)}) collective-permute-start(bf16[2048,256]{1,0:T(8,128)(2,1)} %add_convert_fusion.12.kept_ref), channel_id=1, source_target_pairs={{8,0},{16,24},{9,1},{17,25},{10,2},{18,26},{11,3},{19,27},{12,4},{... | collective-permute-start | bytes 3145736 | tf_op jit(solution)/shard_map/ppermute | solution.py:565
  559.6 4.3 collective-permute-start.32
  563.9 39.1 %collective-permute-start.34 = (f32[49,128]{1,0:T(8,128)S(1)}, f32[49,128]{1,0:T(8,128)S(1)}, u32[]{:S(2)}, u32[]{:S(2)}) collective-permute-start(f32[49,128]{1,0:T(8,128)S(1)} %pad_maximum_fusion), channel_id=1, source_target_pairs={{0,8},{24,16},{1,9},{25,17},{2,10},{26,18},{3,11},{27,19},{4,12},{... | collective-permute-start | bytes 75272 | tf_op jit(solution)/shard_map/ppermute | solution.py:565
  603.0 16.8 %copy-start.9 = (bf16[256,2048]{1,0:T(8,128)(2,1)}, bf16[256,2048]{1,0:T(8,128)(2,1)S(1)}, u32[]{:S(2)}) copy-start(bf16[256,2048]{1,0:T(8,128)(2,1)S(1)} %add_convert_fusion.10.kept_ref) | copy-start | bytes 3145732
  603.0 24.6 %copy-start = (bf16[2,256,2048]{2,1,0:T(8,128)(2,1)S(1)}, bf16[2,256,2048]{2,1,0:T(8,128)(2,1)}, u32[]{:S(2)}) copy-start(bf16[2,256,2048]{2,1,0:T(8,128)(2,1)} %param.14) | copy-start | bytes 6291460
  603.1 15.4 %collective-permute-start.37 = (f32[49,128]{1,0:T(8,128)S(1)}, f32[49,128]{1,0:T(8,128)S(1)}, u32[]{:S(2)}, u32[]{:S(2)}) collective-permute-start(f32[49,128]{1,0:T(8,128)S(1)} %add.147), channel_id=1, source_target_pairs={{8,16},{16,8},{9,17},{17,9},{10,18},{18,10},{11,19},{19,11},{12,20... | collective-permute-start | bytes 75272 | tf_op jit(solution)/shard_map/ppermute | solution.py:565
  618.5 6.1 collective-permute-start.39
  619.8 25.2 %collective-permute-start.40 = (bf16[256,2048]{1,0:T(8,128)(2,1)S(1)}, bf16[256,2048]{1,0:T(8,128)(2,1)}, u32[]{:S(2)}, u32[]{:S(2)}) collective-permute-start(bf16[256,2048]{1,0:T(8,128)(2,1)S(1)} %add_convert_fusion.10.kept_ref), channel_id=1, source_target_pairs={{8,0},{16,24},{9,1},{17,25},{10,2},{18,26},{11,3},{19,27},{12,4},{... | collective-permute-start | bytes 3145736 | tf_op jit(solution)/shard_map/ppermute | solution.py:565
  624.6 23.4 %copy-start.27 = (f32[256]{0:T(256)}, f32[256]{0:T(256)S(1)}, u32[]{:S(2)}) copy-start(f32[256]{0:T(256)S(1)} %slice_bitcast_fusion.3) | copy-start | bytes 3076
  (12 other events, 56.2 us)
Sparse Core Ops, SparseCore 0:
  66.4 107.6 all-gather.2
  176.2 58.1 all-gather.4
  238.0 115.9 reduce-scatter.2
  455.7 118.0 reduce-scatter.4

commit v4 on v3

--- a/solution.py
+++ b/solution.py
@@ -15,8 +15,8 @@
 f32 = jnp.float32
 bf16 = jnp.bfloat16
 VMEM_LIMIT = 56 << 20
-ORDER_WEIGHT = int(1.85e11)
-EARLY_WEIGHT = 1
+ORDER_WEIGHT = int(2e11)
+EARLY_WEIGHT = int(2.1e11)
 
 
 def dot(a, b, ca, cb):
@@ -164,7 +164,7 @@
         slope_ref[:, :, cut] = slope.astype(bf16).reshape(seqs, here, step)
 
 
-def mlp_hidden_of(x, w, bias, steps, before=()):
+def mlp_hidden_of(x, w, bias, steps, before=(), weight=1):
     seqs, owners, here, width = x.shape
     units = w.shape[1]
     held = len(before)
@@ -193,7 +193,7 @@
         out_shape=[jax.ShapeDtypeStruct((seqs, owners, here, units), bf16)] * 2,
         input_output_aliases={1 + i: i for i in range(held)},
         compiler_params=params(),
-        cost_estimate=SMALL,
+        cost_estimate=pl.CostEstimate(flops=int(weight), bytes_accessed=1, transcendentals=0),
         name="mlp_hidden_of",
     )(me, *before, x, w, bias)
 
@@ -410,46 +410,51 @@
 def attention_kernel(*refs, bq, held):
     start_ref, q_ref, k_ref, v_ref, do_ref, c_ref, s_ref, o_ref, by_owner_ref, g_ref, dk_acc, dv_acc = refs[held:]
     span, width = q_ref.shape
+    here = by_owner_ref.shape[1]
     lane = lax.broadcasted_iota(jnp.int32, (1, width), 1) // HD
     zero = jnp.zeros((), bf16)
+    heads = range(width // HD)
+    cuts = [slice(head * HD, (head + 1) * HD) for head in heads]
+    blocks = span // bq
+    keys_across, vals_across = k_ref[...].T, v_ref[...].T
 
     def turn_back(x, at, n):
         return x * c_ref[at : at + n, :] + rope_swap(x) * s_ref[at : at + n, :]
 
-    for block in range(span // bq):
-        at = block * bq
-        n = at + bq
-        qb = q_ref[at:n, :]
-        gb = do_ref[at:n, :]
+    def products(block):
+        at, n = block * bq, (block + 1) * bq
         keys, vals = k_ref[0:n, :], v_ref[0:n, :]
-        key = lax.broadcasted_iota(jnp.int32, (bq, n), 1)
-        row = lax.broadcasted_iota(jnp.int32, (bq, n), 0) + at
-        allowed = (key >= start_ref[at:n, :]) & (key <= row)
-        out = jnp.zeros((bq, width), f32)
-        dq = jnp.zeros((bq, width), f32)
-        dk = jnp.zeros((n, width), f32)
-        dv = jnp.zeros((n, width), f32)
-        for head in range(width // HD):
-            mine = lane == head
-            qh, gh = jnp.where(mine, qb, zero), jnp.where(mine, gb, zero)
-            kh, vh = jnp.where(mine, keys, zero), jnp.where(mine, vals, zero)
-            scores = jnp.where(allowed, dot(qh, keys, 1, 1), big_negative)
-            expd = jnp.exp(scores - jnp.max(scores, axis=1, keepdims=True))
-            probs = expd * (1.0 / jnp.sum(expd, axis=1, keepdims=True))
-            low = probs.astype(bf16)
-            out = out + dot(low, vh, 1, 0)
-            prob_grad = dot(gh, vals, 1, 1)
-            inner = jnp.sum(probs * prob_grad, axis=1, keepdims=True)
-            score_grad = (probs * (prob_grad - inner)).astype(bf16)
-            dq = dq + dot(score_grad, kh, 1, 0)
-            dk = dk + dot(score_grad, qh, 0, 0)
-            dv = dv + dot(low, gh, 0, 0)
-        out = out.astype(bf16)
+        queries = [jnp.where(lane == head, q_ref[at:n, :], zero) for head in heads]
+        grads = [jnp.where(lane == head, do_ref[at:n, :], zero) for head in heads]
+        return queries, grads, [dot(keys, q, 1, 1) for q in queries], [dot(vals, g, 1, 1) for g in grads]
+
+    ahead = products(0)
+    for block in range(blocks):
+        at, n = block * bq, (block + 1) * bq
+        queries, grads, scores, prob_grads = ahead
+        key = lax.broadcasted_iota(jnp.int32, (n, bq), 0)
+        place = lax.broadcasted_iota(jnp.int32, (1, bq), 1) + at
+        allowed = (key >= start_ref[:, at:n]) & (key <= place)
+        if block + 1 < blocks:
+            ahead = products(block + 1)
+        probs = []
+        for head in heads:
+            score = jnp.where(allowed, scores[head], big_negative)
+            expd = jnp.exp(score - jnp.max(score, axis=0, keepdims=True))
+            probs.append(expd * (1.0 / jnp.sum(expd, axis=0, keepdims=True)))
+        low = [p.astype(bf16) for p in probs]
+        out = [dot(vals_across[cut, 0:n], p, 1, 0) for cut, p in zip(cuts, low)]
+        dv = sum(dot(p, g, 1, 0) for p, g in zip(low, grads))
+        score_grads = []
+        for p, g in zip(probs, prob_grads):
+            both = p * g
+            score_grads.append((both - p * jnp.sum(both, axis=0, keepdims=True)).astype(bf16))
+        dq = [dot(keys_across[cut, 0:n], g, 1, 0) for cut, g in zip(cuts, score_grads)]
+        dk = sum(dot(g, q, 1, 0) for g, q in zip(score_grads, queries))
+        out = jnp.concatenate(out, axis=0).T.astype(bf16)
         o_ref[at:n, :] = out
-        here = by_owner_ref.shape[1]
-        for own in range(bq // here):
-            by_owner_ref[at // here + own] = out[own * here : (own + 1) * here]
-        g_ref[0, at:n, :] = turn_back(dq * (HD**-0.5), at, bq).astype(bf16)
+        by_owner_ref[at // here, at % here : at % here + bq] = out
+        g_ref[0, at:n, :] = turn_back(jnp.concatenate(dq, axis=0).T * (HD**-0.5), at, bq).astype(bf16)
         if block:
             dk_acc[0:at, :] += dk[0:at]
             dv_acc[0:at, :] += dv[0:at]
@@ -459,11 +464,11 @@
     g_ref[2] = dv_acc[...].astype(bf16)
 
 
-def attention_both(start, qkv, grad, cosine, sine, span, owners, row, before=(), bq=512):
+def attention_both(start, qkv, grad, cosine, sine, span, owners, row, before=(), bq=128):
     n, local = grad.shape
     here = 2 * span // owners
     width = cosine.shape[1]
-    bq = min(bq, span)
+    bq = min(bq, here)
     held = len(before)
     first = 2 * row
     part = lambda which: pl.BlockSpec((None, span, width), lambda t, p: (which, first + t, p))
@@ -473,7 +478,7 @@
         grid=(2, local // width),
         in_specs=[pl.BlockSpec(memory_space=pl.ANY)] * held
         + [
-            pl.BlockSpec((span, 1), lambda t, p: (first + t, 0)),
+            pl.BlockSpec((1, span), lambda t, p: (0, first + t)),
             part(0),
             part(1),
             part(2),
@@ -519,7 +524,7 @@
         sum_ref[i : i + 1, :] += jnp.sum(a * a, axis=0, keepdims=True)
 
 
-def project_own(x, w, bd, bo, tokens, mlp_parts, tile=512):
+def project_own(x, w, bd, bo, tokens, mlp_parts, tile=512, weight=1):
     owners, seqs, here, local = x.shape
     width = w.shape[1]
     rows = seqs * here
@@ -538,7 +543,7 @@
         out_specs=[column(rows), pl.BlockSpec((8, tile), lambda j: (0, 0))],
         out_shape=[jax.ShapeDtypeStruct((rows, width), bf16), jax.ShapeDtypeStruct((8, tile), f32)],
         compiler_params=params(),
-        cost_estimate=SMALL,
+        cost_estimate=pl.CostEstimate(flops=int(weight), bytes_accessed=1, transcendentals=0),
         name="project_own",
     )(x, w, bd, bo, tokens, *mlp_parts)
 
@@ -569,6 +574,10 @@
             add = lambda a, b: (a.astype(f32) + b.astype(f32)).astype(a.dtype)
             self.part = order(add, self.part, self.came)
             self.send()
+
+    def settle(self, order):
+        if line_ok(self.size):
+            self.came = order(lambda a: a, self.came)
 
     def complete(self, order):
         while self.hops:
@@ -766,7 +775,7 @@
     def tables(positions, weight):
         place = positions.reshape(n, 1)
         cosine, sine = rope_tables(place, tile)
-        start = jnp.arange(n, dtype=jnp.int32)[:, None] % span - place
+        start = jnp.arange(n, dtype=jnp.int32)[None] % span - positions.reshape(1, n)
         return cosine, sine, start, jnp.transpose(weight, (1, 0, 2))
 
     cosine, sine, start, w3 = order(tables, positions, query_key_value_weight)
@@ -792,42 +801,41 @@
         act, slope = order(hidden_of, normed_full, inward_weight, in_bias_row)
     normed, act, slope = token_rows(normed_full), token_rows(act), token_rows(slope)
     qkv = order(project_qkv, normed, w3, b_qkv.astype(f32), cosine, sine)
-    mlp_part = order(lambda *a: tokens_by_weight(*a, 0, 1), act, outward_weight).reshape(seqs, length, width)
-    mlp_part, dense_ready, _ = lax.optimization_barrier((mlp_part, dense_weight, grad))
-    mlp_tok = lax.psum_scatter(mlp_part, "tp", scatter_dimension=1, tiled=True).reshape(seqs * here, width)
+    dense_ready, _ = lax.optimization_barrier((dense_weight, act))
     dense_full = lax.all_gather(dense_ready, "tp", axis=0, tiled=True)
-
     o0 = RowSum(order(lambda *a: weight_grad(*a, 0, 2), act, grad), rows)
     o1 = RowSum(order(lambda *a: weight_grad(*a, 1, 2), act, grad), rows)
     row_sum = lambda parts: [RowSum(part, rows) for part in parts]
     hidden_grad, attended_grad, in_bias = order(grad_in, grad, outward_weight, dense_weight, slope)
     o0.fold(order)
+    mlp_part = order(lambda *a: tokens_by_weight(*a, 0, 1), act, outward_weight).reshape(seqs, length, width)
+    mlp_tok = lax.psum_scatter(mlp_part, "tp", scatter_dimension=1, tiled=True).reshape(seqs * here, width)
     i0, i1 = row_sum(order(lambda a, b: weight_grad_rows(a, b, (1, 1)), normed, hidden_grad))
+    o1.fold(order)
+    o0.fold(order)
     both = lambda row: lambda s, q, g, c, t, *before: attention_both(s, q, g, c, t, span, tp, row, before)
     attended, by_owner, dqkv = order(both(0), start, qkv, attended_grad, cosine, sine)
-    o1.fold(order)
-    o0.fold(order)
     for row in range(1, seqs):
         kept = (attended, by_owner, dqkv)
         attended, by_owner, dqkv = order(both(row), start, qkv, attended_grad, cosine, sine, *kept)
     mine = lax.all_to_all(by_owner, "tp", split_axis=0, concat_axis=0, tiled=True)
+    o1.fold(order)
     i0.fold(order)
-    o1.fold(order)
+    o0.settle(order)
     qs, vs = row_sum(order(lambda a, b: weight_grad_parts(a, b, weight=EARLY_WEIGHT), normed, dqkv))
     units = in_bias.shape[1]
-    out_grad = finish(o0, order, units)
     back = lambda share: lambda *a: normed_grad(*a[:5], shift[None], share, 2, a[5:])
+    i1.fold(order)
     part, bias_a, norm_a = order(back(0), hidden_grad, dqkv, inward_weight, w3, normed)
-    i1.fold(order)
     i0.fold(order)
-    out_grad = finish(o1, order, units, units // 2, out_grad)
+    o1.settle(order)
     part, bias_b, norm_b = order(back(1), hidden_grad, dqkv, inward_weight, w3, normed, part)
     back_tok = lax.psum_scatter(part.reshape(seqs, length, width), "tp", scatter_dimension=1, tiled=True)
+    i1.fold(order)
     qs.fold(order)
-    i1.fold(order)
+    (ds,) = row_sum([order(weight_grad, attended, grad)])
     vs.fold(order)
-    in_grad = finish(i0, order, width)
-    (ds,) = row_sum([order(lambda a, b: weight_grad(a, b, weight=ORDER_WEIGHT), attended, grad)])
+    i0.settle(order)
 
     cols = width // tp
 
@@ -837,7 +845,8 @@
 
     out_bias = order(column_sums, grad)
     rows_of = lambda a: a.reshape(seqs * here, width)
-    own = lambda x, w, t, *m: project_own(x, w, b_dense.astype(f32)[None], b_out.astype(f32)[None], rows_of(t), m)
+    bias_rows = (b_dense.astype(f32)[None], b_out.astype(f32)[None])
+    own = lambda x, w, t, *m: project_own(x, w, *bias_rows, rows_of(t), m, weight=ORDER_WEIGHT)
     layer_out, squares = order(own, mine, dense_full, tokens, mlp_tok)
     layer_out = layer_out.reshape(tokens.shape)
 
@@ -848,20 +857,24 @@
         return jnp.concatenate([norm_sums[0] / gain, norm_sums[1], squares, pad]).reshape(-1, 128)
 
     packed = TpSum(order(pack, norm_a, norm_b, squares), tp)
+    ds.fold(order)
     qs.fold(order)
+    vs.fold(order)
     packed.fold(order)
-    vs.fold(order)
-    in_grad = finish(i1, order, width, width // 2, in_grad)
+    out_grad = finish(o0, order, units)
     packed.fold(order)
-    ds.fold(order)
+    out_grad = finish(o1, order, units, units // 2, out_grad)
+    packed.fold(order)
     qkv_bias = bias_a + bias_b
     small = jnp.concatenate([in_bias[0], qkv_bias[:, 0].reshape(-1), out_bias]).reshape(-1, 128)
     small = RowSum(jnp.concatenate([packed.result(order), small]), rows)
+    in_grad = finish(i0, order, width)
+    ds.fold(order)
+    in_grad = finish(i1, order, width, width // 2, in_grad)
+    small.fold(order)
+    small.fold(order)
     qkv_grad = finish(qs, order, 3 * width)
-    ds.fold(order)
-    small.fold(order)
     qkv_grad = finish(vs, order, 3 * width, 2 * width, qkv_grad)
-    small.fold(order)
 
     def norm_back(back_tok, tokens, cotangent):
         values = tokens.astype(f32)

time: 661 us -> 651 us (0.985)
  waiting for transfers between devices: 111 us -> 91.9 us
  Pallas kernels: 372 us -> 354 us
  starting transfers between devices: 89 us -> 107 us
    ppermute x24, waiting for transfers between devices: 69.3 us -> 32.6 us  [send(): self.came = lax.ppermute(self.part, self.axis, self.hops.pop(0))]
    ppermute x24, starting transfers between devices: 67.9 us -> 90.7 us  [send(): self.came = lax.ppermute(self.part, self.axis, self.hops.pop(0))]
    pallas_call x2, Pallas kernels: 61.5 us -> 44.8 us  [attention_both(): pl.pallas_call(functools.partial(attention_kernel, bq=bq, held=held), gri...]
    all_gather x1, waiting for transfers between devices: 0.01 us -> 15.3 us  [body(): lax.all_gather(order(lambda b: b, a), 'tp', axis=1, tiled=True)]
  transfers between devices with their start and end apart: 46 -> 46, of which waited for: 18 -> 14; matrix products, arithmetic and copies ran while one was open for 10% -> 10% of each run, Pallas kernels for 56% -> 54%
where the time goes in v4:
time: 651 us; the launch traced here: 641 us
  Pallas kernels  354 us (54%)
  starting transfers between devices  107 us (16%)
  waiting for transfers between devices  91.9 us (14%)
  other arithmetic  62.9 us (10%)
  between operations  14.6 us (2%)
  local copies, waits for them, and re-layouts  10.2 us (2%)
    ppermute x24, starting transfers between devices, send(): self.came = lax.ppermute(self.part, self.axis, self.hops.pop(0))  90.7 us
    convert_element_type x14, other arithmetic, fold(): add = lambda a, b: (a.astype(f32) + b.astype(f32)).astype(a.dtype)  46.2 us
    pallas_call x2, Pallas kernels, normed_grad(): pl.pallas_call(functools.partial(normed_grad_kernel, held=held), grid=(st...  45.4 us
    pallas_call x2, Pallas kernels, attention_both(): pl.pallas_call(functools.partial(attention_kernel, bq=bq, held=held), gri...  44.8 us
    ppermute x14, waiting for transfers between devices, send(): return lax.ppermute(a, 'tp', [(i, i ^ step) for i in range(self.size)])  44 us
    pallas_call x3, Pallas kernels, weight_grad(): pl.pallas_call(weight_grad_kernel, grid=(cols // tile,), in_specs=[pl.Blo...  38.4 us
    pallas_call x2, Pallas kernels, mlp_hidden_of(): pl.pallas_call(functools.partial(chosen_kernel, held=held), grid_spec=plt...  36 us
    ppermute x24, waiting for transfers between devices, send(): self.came = lax.ppermute(self.part, self.axis, self.hops.pop(0))  32.6 us
  transfers between devices with their start and end apart: 46, of which 14 were waited for; matrix products, arithmetic and copies ran while one was open for 10% of the time, Pallas kernels for 54%

profile of v4, /device:TPU:0, one launch (start us, length us, event | category | flops | bytes accessed | tf_op | source)
XLA Modules:
  0.0 640.7 jit_solution(4481765357614785903)
XLA Ops:
  9.8 4.7 norm_halves.1
  14.5 3.0 collective-permute-start.1
  22.2 9.8 %rope_tables.1 = (f32[4096,128]{1,0:T(8,128)}, f32[4096,128]{1,0:T(8,128)}) custom-call(s32[4096,1]{1,0:T(8,128)} %bitcast.68, f32[1,128]{1,0:T(1,128)} %fusion.15.frequency_ref), custom_call_target="tpu_custom_call" | custom-call | flops 1 | bytes 1 | tf_op jit(solution)/shard_map/rope_tables/pallas_call | solution.py:99
  32.6 9.1 %collective-permute-done.1.refs_7_ = bf16[256,2048]{1,0:T(8,128)(2,1)S(1)} collective-permute-done((bf16[256,2048]{1,0:T(8,128)(2,1)}, bf16[256,2048]{1,0:T(8,128)(2,1)S(1)}, u32[]{:S(2)}, u32[]{:S(2)}) %collective-permute-start.1) | collective-permute-done | bytes 1048608 | tf_op jit(solution)/shard_map/ppermute | solution.py:640
  43.7 22.2 %collective-permute-done.3.refs_5_ = bf16[256,2048]{1,0:T(8,128)(2,1)} collective-permute-done((bf16[256,2048]{1,0:T(8,128)(2,1)}, bf16[256,2048]{1,0:T(8,128)(2,1)}, u32[]{:S(2)}, u32[]{:S(2)}) %collective-permute-start.3) | collective-permute-done | bytes 1048608 | tf_op jit(solution)/shard_map/ppermute | solution.py:640
  67.3 2.1 collective-permute-done.6.refs_8_
  73.5 13.1 %place_pieces.2.refs_0_ = bf16[2,8,256,2048]{3,2,1,0:T(8,128)(2,1)} custom-call(s32[1]{0:T(128)} %bitcast.3.me_ref, bf16[256,2048]{1,0:T(8,128)(2,1)} %get-tuple-element.212.refs_0_, bf16[256,2048]{1,0:T(8,128)(2,1)} %get-tuple-element.213.refs_1_, bf16[256,2048]{1,0:T(8,128)(2,1)} %collective-permute-done.2.refs_2_, ...), custom_call_target="tpu_custom_call" | custom-call | flops 1 | bytes 1 | tf_op jit(solution)/shard_map/place_pieces/pallas_call | solution.py:701
  86.6 23.6 %mlp_hidden_of.2 = (bf16[2,8,256,1024]{3,2,1,0:T(8,128)(2,1)}, bf16[2,8,256,1024]{3,2,1,0:T(8,128)(2,1)}) custom-call(s32[1]{0:T(128)} %bitcast.3.me_ref, bf16[2,8,256,2048]{3,2,1,0:T(8,128)(2,1)} %place_pieces.2.refs_0_, bf16[2048,1024]{1,0:T(8,128)(2,1)} %refs_3_.1, f32[1,1024]{1,0:T(1,128)} %bitcast.78), custom_call_target="tpu_custom_call" | custom-call | flops 1 | bytes 1 | tf_op jit(solution)/shard_map/mlp_hidden_of/pallas_call | solution.py:180
  110.3 3.7 collective-permute-done.11.refs_2_
  114.5 3.6 collective-permute-done.12.refs_3_
  120.1 4.7 place_pieces.3.refs_2_
  124.8 12.4 %mlp_hidden_of.3 = (bf16[2,8,256,1024]{3,2,1,0:T(8,128)(2,1)}, bf16[2,8,256,1024]{3,2,1,0:T(8,128)(2,1)}) custom-call(s32[1]{0:T(128)} %bitcast.3.me_ref, bf16[2,8,256,1024]{3,2,1,0:T(8,128)(2,1)} %get-tuple-element.236.refs_0_, bf16[2,8,256,1024]{3,2,1,0:T(8,128)(2,1)} %get-tuple-element.237.refs_1_, ...), custom_call_target="tpu_custom_call", output_to_operand_aliasing={{0}: (1, {}), {1}: (2, {})} | custom-call | flops 1 | bytes 1 | tf_op jit(solution)/shard_map/mlp_hidden_of/pallas_call | solution.py:180
  138.3 19.9 %qkv_rope.1.refs_1_.refs_2_.refs_3_.refs_4_.refs_5_.refs_6_ = bf16[3,4096,256]{2,1,0:T(8,128)(2,1)} custom-call(bf16[4096,2048]{1,0:T(8,128)(2,1)} %bitcast.45, bf16[3,2048,256]{2,1,0:T(8,128)(2,1)} %bitcast.63, f32[3,256]{1,0:T(4,128)} %convert_element_type.170.b_ref, f32[4096,128]{1,0:T(8,128)} %get-tuple-element.285.c_ref.refs_5_.refs_8_, ...), custom_call_target="tpu_custom_call" | custom-call | flops 1 | bytes 1 | tf_op jit(solution)/shard_map/qkv_rope/pallas_call | solution.py:131
  158.3 15.3 %all-gather.3.cloned.1.call-done = bf16[2,2048,2048]{2,1,0:T(8,128)(2,1)} async-done(((bf16[2,256,2048]{2,1,0:T(8,128)(2,1)}), bf16[2,2048,2048]{2,1,0:T(8,128)(2,1)}) %all-gather.3.cloned.1.call-update) | async-done | bytes 16777232 | tf_op jit(solution)/shard_map/all_gather | solution.py:784
  173.6 14.2 %weight_grad.3 = bf16[512,2048]{1,0:T(8,128)(2,1)} custom-call(bf16[4096,1024]{1,0:T(8,128)(2,1)} %bitcast.55, bf16[4096,2048]{1,0:T(8,128)(2,1)} %bitcast.50), custom_call_target="tpu_custom_call" | custom-call | flops 1 | bytes 1 | tf_op jit(solution)/shard_map/weight_grad/pallas_call | solution.py:279
  187.8 3.5 collective-permute-start.14
  191.3 13.8 %weight_grad.4 = bf16[512,2048]{1,0:T(8,128)(2,1)} custom-call(bf16[4096,1024]{1,0:T(8,128)(2,1)} %bitcast.56, bf16[4096,2048]{1,0:T(8,128)(2,1)} %bitcast.51), custom_call_target="tpu_custom_call" | custom-call | flops 1 | bytes 1 | tf_op jit(solution)/shard_map/weight_grad/pallas_call | solution.py:279
  205.2 2.6 collective-permute-start.16
  207.8 29.6 %grad_in.1 = (bf16[4096,1024]{1,0:T(8,128)(2,1)}, bf16[4096,256]{1,0:T(8,128)(2,1)}, f32[8,1024]{1,0:T(8,128)}) custom-call(bf16[4096,2048]{1,0:T(8,128)(2,1)} %bitcast.52, bf16[1024,2048]{1,0:T(8,128)(2,1)} %w_ref, bf16[256,2048]{1,0:T(8,128)(2,1)} %wd_ref, bf16[4096,1024]{1,0:T(8,128)(2,1)} %bitcast.62), custom_call_target="tpu_custom_call" | custom-call | flops 1 | bytes 1 | tf_op jit(solution)/shard_map/grad_in/pallas_call | solution.py:221
  238.3 2.0 collective-permute-start.15
  240.3 22.6 %tokens_by_weight.1 = bf16[4096,2048]{1,0:T(8,128)(2,1)} custom-call(bf16[4096,1024]{1,0:T(8,128)(2,1)} %bitcast.57, bf16[1024,2048]{1,0:T(8,128)(2,1)} %w_ref), custom_call_target="tpu_custom_call" | custom-call | flops 1 | bytes 1 | tf_op jit(solution)/shard_map/tokens_by_weight/pallas_call | solution.py:258
  262.9 24.6 %weight_grad_rows.1 = (bf16[1024,1024]{1,0:T(8,128)(2,1)}, bf16[1024,1024]{1,0:T(8,128)(2,1)}) custom-call(bf16[4096,2048]{1,0:T(8,128)(2,1)} %bitcast.46, bf16[4096,1024]{1,0:T(8,128)(2,1)} %get-tuple-element.314.b_ref.refs_0_.refs_1_), custom_call_target="tpu_custom_call" | custom-call | flops 1 | bytes 1 | tf_op jit(solution)/shard_map/weight_grad_rows/pallas_call | solution.py:313
  287.6 3.1 add_convert_fusion.8
  290.7 2.0 collective-permute-start.18
  292.7 7.5 %collective-permute-start.17 = (bf16[1024,1024]{1,0:T(8,128)(2,1)}, bf16[1024,1024]{1,0:T(8,128)(2,1)}, u32[]{:S(2)}, u32[]{:S(2)}) collective-permute-start(bf16[1024,1024]{1,0:T(8,128)(2,1)} %get-tuple-element.293), channel_id=1, source_target_pairs={{0,8},{24,16},{1,9},{25,17},{2,10},{26,18},{3,11},{27,19},{4,12},{... | collective-permute-start | bytes 6291464 | tf_op jit(solution)/shard_map/ppermute | solution.py:570
  300.2 2.7 add_convert_fusion.7.kept_ref
  304.2 6.2 collective-permute-start.20
  310.4 22.4 %attention_both.2 = (bf16[4096,256]{1,0:T(8,128)(2,1)}, bf16[8,2,256,256]{3,2,1,0:T(8,128)(2,1)}, bf16[3,4096,256]{2,1,0:T(8,128)(2,1)}) custom-call(s32[1,4096]{1,0:T(1,128)} %fusion.11.refs_0_.refs_3_, bf16[3,4096,256]{2,1,0:T(8,128)(2,1)} %qkv_rope.1.refs_1_.refs_2_.refs_3_.refs_4_.refs_5_.refs_6_, ...), custom_call_target="tpu_custom_call" | custom-call | flops 1 | bytes 1 | tf_op jit(solution)/shard_map/attention_both/pallas_call | solution.py:476
  332.8 22.4 %attention_both.3 = (bf16[4096,256]{1,0:T(8,128)(2,1)}, bf16[8,2,256,256]{3,2,1,0:T(8,128)(2,1)}, bf16[3,4096,256]{2,1,0:T(8,128)(2,1)}) custom-call(bf16[4096,256]{1,0:T(8,128)(2,1)} %get-tuple-element.279.refs_0_, bf16[8,2,256,256]{3,2,1,0:T(8,128)(2,1)} %get-tuple-element.280.refs_1_, ...), custom_call_target="tpu_custom_call", output_to_operand_aliasing={{0}: (0, {}), {1}: (1, {}), {2}: (2, {})} | custom-call | flops 1 | bytes 1 | tf_op jit(solution)/shard_map/attention_both/pallas_call | solution.py:476
  355.2 4.1 add_convert_fusion.6.kept_ref
  360.6 4.8 add_convert_fusion.5
  365.4 2.4 collective-permute-start.19
  367.8 19.7 %weight_grad_parts.1 = (bf16[2,2048,256]{2,1,0:T(8,128)(2,1)}, bf16[2048,256]{1,0:T(8,128)(2,1)}) custom-call(bf16[4096,2048]{1,0:T(8,128)(2,1)} %bitcast.47, bf16[3,4096,256]{2,1,0:T(8,128)(2,1)} %get-tuple-element.315.b_ref.refs_1_.refs_2_), custom_call_target="tpu_custom_call" | custom-call | flops 210000003072 | bytes 1 | tf_op jit(solution)/shard_map/weight_grad_parts/pallas_call | solution.py:337
  387.5 4.5 add_convert_fusion.4
  394.0 8.8 %collective-permute-start.24 = (bf16[2,2048,256]{2,1,0:T(8,128)(2,1)}, bf16[2,2048,256]{2,1,0:T(8,128)(2,1)}, u32[]{:S(2)}, u32[]{:S(2)}) collective-permute-start(bf16[2,2048,256]{2,1,0:T(8,128)(2,1)} %get-tuple-element.324), channel_id=1, source_target_pairs={{0,8},{24,16},{1,9},{25,17},{2,10},{26,18},{3,11},{27,19},{4,12},{... | collective-permute-start | bytes 6291464 | tf_op jit(solution)/shard_map/ppermute | solution.py:570
  402.7 22.7 %normed_grad.2 = (bf16[4096,2048]{1,0:T(8,128)(2,1)}, f32[3,8,256]{2,1,0:T(8,128)}, f32[8,2048]{1,0:T(8,128)}) custom-call(bf16[4096,1024]{1,0:T(8,128)(2,1)} %get-tuple-element.314.b_ref.refs_0_.refs_1_, bf16[3,4096,256]{2,1,0:T(8,128)(2,1)} %get-tuple-element.315.b_ref.refs_1_.refs_2_, bf16[2048,1024]{1,0:T(8,128)(2,1)} %refs_3_.1, ...), custom_call_target="tpu_custom_call" | custom-call | flops 1 | bytes 1 | tf_op jit(solution)/shard_map/normed_grad/pallas_call | solution.py:381
  425.5 3.2 add_convert_fusion.3.kept_ref
  430.4 22.7 %normed_grad.3 = (bf16[4096,2048]{1,0:T(8,128)(2,1)}, f32[3,8,256]{2,1,0:T(8,128)}, f32[8,2048]{1,0:T(8,128)}) custom-call(bf16[4096,2048]{1,0:T(8,128)(2,1)} %get-tuple-element.313.refs_0_, bf16[4096,1024]{1,0:T(8,128)(2,1)} %get-tuple-element.314.b_ref.refs_0_.refs_1_, ...), custom_call_target="tpu_custom_call", output_to_operand_aliasing={{0}: (0, {})} | custom-call | flops 1 | bytes 1 | tf_op jit(solution)/shard_map/normed_grad/pallas_call | solution.py:381
  453.1 4.5 all-to-all-start
  457.6 7.1 %collective-permute-start.23 = (bf16[2048,256]{1,0:T(8,128)(2,1)S(1)}, bf16[2048,256]{1,0:T(8,128)(2,1)}, u32[]{:S(2)}, u32[]{:S(2)}) collective-permute-start(bf16[2048,256]{1,0:T(8,128)(2,1)S(1)} %copy-done.10), channel_id=1, source_target_pairs={{0,8},{24,16},{1,9},{25,17},{2,10},{26,18},{3,11},{27,19},{4,12},{... | collective-permute-start | bytes 3145736 | tf_op jit(solution)/shard_map/ppermute | solution.py:570
  467.3 5.3 add_convert_fusion.2.kept_ref
  472.6 4.8 add_convert_fusion.1
  477.4 2.0 collective-permute-start.28
  480.7 10.4 %weight_grad.5 = bf16[256,2048]{1,0:T(8,128)(2,1)} custom-call(bf16[4096,256]{1,0:T(8,128)(2,1)} %get-tuple-element.326.a_ref, bf16[4096,2048]{1,0:T(8,128)(2,1)} %bitcast.53), custom_call_target="tpu_custom_call" | custom-call | flops 1 | bytes 1 | tf_op jit(solution)/shard_map/weight_grad/pallas_call | solution.py:279
  491.0 6.9 %collective-permute-start.29 = (bf16[256,2048]{1,0:T(8,128)(2,1)}, bf16[256,2048]{1,0:T(8,128)(2,1)}, u32[]{:S(2)}, u32[]{:S(2)}) collective-permute-start(bf16[256,2048]{1,0:T(8,128)(2,1)} %weight_grad.5), channel_id=1, source_target_pairs={{0,8},{24,16},{1,9},{25,17},{2,10},{26,18},{3,11},{27,19},{4,12},{... | collective-permute-start | bytes 3145736 | tf_op jit(solution)/shard_map/ppermute | solution.py:570
  497.9 2.5 add_convert_fusion.13
  502.0 3.0 convert_reduce_fusion.1
  505.0 10.5 %project_own.1 = (bf16[512,2048]{1,0:T(8,128)(2,1)}, f32[8,512]{1,0:T(8,128)}) custom-call(bf16[8,2,256,256]{3,2,1,0:T(8,128)(2,1)} %all-to-all-done.x_ref, bf16[2048,2048]{1,0:T(8,128)(2,1)} %all-gather.5.cloned.1.call-done.w_ref, f32[1,2048]{1,0:T(1,128)} %bitcast.84, f32[1,2048]{1,0:T(1,128)} %bitcast.85, bf16[512,2048]{1,0:T(8,128)(2,1)} %bitcast.61, ...), custom_call_target="tpu_custom_call" | custom-call | flops 199999995904 | bytes 1 | tf_op jit(solution)/shard_map/project_own/pallas_call | solution.py:532
  516.4 3.0 collective-permute-done.29
  519.5 2.7 add_convert_fusion.12
  523.8 3.0 add_convert_fusion
  532.5 4.6 finish.7.refs_0_
  538.5 4.6 finish.8
  543.1 23.2 %collective-permute-start.35 = (f32[49,128]{1,0:T(8,128)S(1)}, f32[49,128]{1,0:T(8,128)S(1)}, u32[]{:S(2)}, u32[]{:S(2)}) collective-permute-start(f32[49,128]{1,0:T(8,128)S(1)} %pad_maximum_fusion), channel_id=1, source_target_pairs={{0,8},{24,16},{1,9},{25,17},{2,10},{26,18},{3,11},{27,19},{4,12},{... | collective-permute-start | bytes 75272 | tf_op jit(solution)/shard_map/ppermute | solution.py:570
  566.3 3.7 finish.9.refs_0_
  570.0 3.0 add_convert_fusion.10.kept_ref
  573.0 3.7 finish.10
  581.3 5.3 collective-permute-done.39
  589.7 6.5 %finish.11.refs_0_ = f32[6144,256]{1,0:T(8,128)} custom-call(s32[1]{0:T(128)} %bitcast.17.inner_ref, bf16[4096,256]{1,0:T(8,128)(2,1)} %bitcast.67, bf16[4096,256]{1,0:T(8,128)(2,1)} %bitcast.22.came_ref), custom_call_target="tpu_custom_call" | custom-call | flops 1 | bytes 1 | tf_op jit(solution)/shard_map/finish/pallas_call | solution.py:629
  596.3 13.8 %collective-permute-done.30.came_ref = bf16[2048,256]{1,0:T(8,128)(2,1)} collective-permute-done((bf16[2048,256]{1,0:T(8,128)(2,1)S(1)}, bf16[2048,256]{1,0:T(8,128)(2,1)}, u32[]{:S(2)}, u32[]{:S(2)}) %collective-permute-start.30) | collective-permute-done | bytes 1048608 | tf_op jit(solution)/shard_map/ppermute | solution.py:570
  610.0 3.8 finish.12
  617.0 3.2 fusion.8
  620.2 10.3 %collective-permute-done.40.came_ref = bf16[256,2048]{1,0:T(8,128)(2,1)} collective-permute-done((bf16[256,2048]{1,0:T(8,128)(2,1)}, bf16[256,2048]{1,0:T(8,128)(2,1)}, u32[]{:S(2)}, u32[]{:S(2)}) %collective-permute-start.40) | collective-permute-done | bytes 1048608 | tf_op jit(solution)/shard_map/ppermute | solution.py:570
  630.4 3.0 finish.13
  (176 shorter events, 52.7 us)
Async XLA Ops:
  7.2 12.4 %copy-start.23 = (s32[2,2048]{1,0:T(2,128)S(1)}, s32[2,2048]{1,0:T(2,128)}, u32[]{:S(2)}) copy-start(s32[2,2048]{1,0:T(2,128)} %param.15) | copy-start | bytes 49156
  7.2 166.4 %all-gather.3.cloned.1.call-start = ((), (), s32[]{:S(2)}) async-start(), calls=%async_computation.3 | async-start | bytes 18874368 | tf_op jit(solution)/shard_map/all_gather | solution.py:784
  14.5 27.2 %collective-permute-start.1 = (bf16[256,2048]{1,0:T(8,128)(2,1)}, bf16[256,2048]{1,0:T(8,128)(2,1)S(1)}, u32[]{:S(2)}, u32[]{:S(2)}) collective-permute-start(bf16[256,2048]{1,0:T(8,128)(2,1)} %get-tuple-element.213.refs_1_), channel_id=1, source_target_pairs={{0,4},{1,5},{2,6},{3,7},{4,0},{5,1},{6,2},{7,3},{8,12},{9,13},{10,... | collective-permute-start | bytes 3145736 | tf_op jit(solution)/shard_map/ppermute | solution.py:640
  17.5 24.2 %collective-permute-start.2 = (bf16[256,2048]{1,0:T(8,128)(2,1)}, bf16[256,2048]{1,0:T(8,128)(2,1)}, u32[]{:S(2)}, u32[]{:S(2)}) collective-permute-start(bf16[256,2048]{1,0:T(8,128)(2,1)} %get-tuple-element.212.refs_0_), channel_id=1, source_target_pairs={{0,1},{1,0},{2,3},{3,2},{4,5},{5,4},{6,7},{7,6},{8,9},{9,8},{10,11... | collective-permute-start | bytes 3145736 | tf_op jit(solution)/shard_map/ppermute | solution.py:640
  17.5 26.2 %collective-permute-start = (bf16[256,2048]{1,0:T(8,128)(2,1)}, bf16[256,2048]{1,0:T(8,128)(2,1)S(1)}, u32[]{:S(2)}, u32[]{:S(2)}) collective-permute-start(bf16[256,2048]{1,0:T(8,128)(2,1)} %get-tuple-element.212.refs_0_), channel_id=1, source_target_pairs={{0,2},{1,3},{2,0},{3,1},{4,6},{5,7},{6,4},{7,5},{8,10},{9,11},{10,... | collective-permute-start | bytes 3145736 | tf_op jit(solution)/shard_map/ppermute | solution.py:640
  19.0 46.9 %collective-permute-start.3 = (bf16[256,2048]{1,0:T(8,128)(2,1)}, bf16[256,2048]{1,0:T(8,128)(2,1)}, u32[]{:S(2)}, u32[]{:S(2)}) collective-permute-start(bf16[256,2048]{1,0:T(8,128)(2,1)} %get-tuple-element.213.refs_1_), channel_id=1, source_target_pairs={{0,2},{1,3},{2,0},{3,1},{4,6},{5,7},{6,4},{7,5},{8,10},{9,11},{10,... | collective-permute-start | bytes 3145736 | tf_op jit(solution)/shard_map/ppermute | solution.py:640
  19.5 46.3 %collective-permute-start.4 = (bf16[256,2048]{1,0:T(8,128)(2,1)}, bf16[256,2048]{1,0:T(8,128)(2,1)}, u32[]{:S(2)}, u32[]{:S(2)}) collective-permute-start(bf16[256,2048]{1,0:T(8,128)(2,1)} %get-tuple-element.212.refs_0_), channel_id=1, source_target_pairs={{0,4},{1,5},{2,6},{3,7},{4,0},{5,1},{6,2},{7,3},{8,12},{9,13},{10,... | collective-permute-start | bytes 3145736 | tf_op jit(solution)/shard_map/ppermute | solution.py:640
  19.6 24.0 %copy-start.12 = (bf16[256,2048]{1,0:T(8,128)(2,1)S(1)}, bf16[256,2048]{1,0:T(8,128)(2,1)}, u32[]{:S(2)}) copy-start(bf16[256,2048]{1,0:T(8,128)(2,1)} %get-tuple-element.213.refs_1_) | copy-start | bytes 3145732
  22.2 49.7 %copy-start.28 = (bf16[1024]{0:T(1024)(128)(2,1)S(1)}, bf16[1024]{0:T(1024)(128)(2,1)}, u32[]{:S(2)}) copy-start(bf16[1024]{0:T(1024)(128)(2,1)} %param.23) | copy-start | bytes 6148
  41.7 31.8 %copy-start.11 = (bf16[256,2048]{1,0:T(8,128)(2,1)}, bf16[256,2048]{1,0:T(8,128)(2,1)S(1)}, u32[]{:S(2)}) copy-start(bf16[256,2048]{1,0:T(8,128)(2,1)S(1)} %collective-permute-done.1.refs_7_) | copy-start | bytes 3145732
  43.7 29.8 %copy-start.13 = (bf16[256,2048]{1,0:T(8,128)(2,1)}, bf16[256,2048]{1,0:T(8,128)(2,1)S(1)}, u32[]{:S(2)}) copy-start(bf16[256,2048]{1,0:T(8,128)(2,1)S(1)} %collective-permute-done.refs_4_) | copy-start | bytes 3145732
  43.7 22.2 %collective-permute-start.5 = (bf16[256,2048]{1,0:T(8,128)(2,1)S(1)}, bf16[256,2048]{1,0:T(8,128)(2,1)}, u32[]{:S(2)}, u32[]{:S(2)}) collective-permute-start(bf16[256,2048]{1,0:T(8,128)(2,1)S(1)} %copy-done.12), channel_id=1, source_target_pairs={{0,1},{1,0},{2,3},{3,2},{4,5},{5,4},{6,7},{7,6},{8,9},{9,8},{10,11... | collective-permute-start | bytes 3145736 | tf_op jit(solution)/shard_map/ppermute | solution.py:640
  65.9 439.0 %all-gather.5.cloned.1.call-start = ((), (), s32[]{:S(2)}) async-start(), calls=%async_computation.4 | async-start | bytes 9437184 | tf_op jit(solution)/shard_map/all_gather | solution.py:805
  66.0 3.4 collective-permute-start.6
  66.0 6.4 %collective-permute-start.7 = (bf16[256,2048]{1,0:T(8,128)(2,1)}, bf16[256,2048]{1,0:T(8,128)(2,1)}, u32[]{:S(2)}, u32[]{:S(2)}) collective-permute-start(bf16[256,2048]{1,0:T(8,128)(2,1)} %collective-permute-done.3.refs_5_), channel_id=1, source_target_pairs={{0,1},{1,0},{2,3},{3,2},{4,5},{5,4},{6,7},{7,6},{8,9},{9,8},{10,11... | collective-permute-start | bytes 3145736 | tf_op jit(solution)/shard_map/ppermute | solution.py:640
  66.5 7.0 %collective-permute-start.8 = (bf16[256,2048]{1,0:T(8,128)(2,1)}, bf16[256,2048]{1,0:T(8,128)(2,1)}, u32[]{:S(2)}, u32[]{:S(2)}) collective-permute-start(bf16[256,2048]{1,0:T(8,128)(2,1)} %collective-permute-done.4.refs_6_), channel_id=1, source_target_pairs={{0,1},{1,0},{2,3},{3,2},{4,5},{5,4},{6,7},{7,6},{8,9},{9,8},{10,11... | collective-permute-start | bytes 3145736 | tf_op jit(solution)/shard_map/ppermute | solution.py:640
  66.6 6.9 %collective-permute-start.9 = (bf16[256,2048]{1,0:T(8,128)(2,1)S(1)}, bf16[256,2048]{1,0:T(8,128)(2,1)}, u32[]{:S(2)}, u32[]{:S(2)}) collective-permute-start(bf16[256,2048]{1,0:T(8,128)(2,1)S(1)} %collective-permute-done.1.refs_7_), channel_id=1, source_target_pairs={{0,1},{1,0},{2,3},{3,2},{4,5},{5,4},{6,7},{7,6},{8,9},{9,8},{10,11... | collective-permute-start | bytes 3145736 | tf_op jit(solution)/shard_map/ppermute | solution.py:640
  67.0 43.2 %collective-permute-start.10 = (bf16[256,2048]{1,0:T(8,128)(2,1)S(1)}, bf16[256,2048]{1,0:T(8,128)(2,1)S(1)}, u32[]{:S(2)}, u32[]{:S(2)}) collective-permute-start(bf16[256,2048]{1,0:T(8,128)(2,1)S(1)} %collective-permute-done.refs_4_), channel_id=1, source_target_pairs={{0,4},{1,5},{2,6},{3,7},{4,0},{5,1},{6,2},{7,3},{8,12},{9,13},{10,... | collective-permute-start | bytes 3145736 | tf_op jit(solution)/shard_map/ppermute | solution.py:640
  70.4 43.6 %collective-permute-start.11 = (bf16[256,2048]{1,0:T(8,128)(2,1)S(1)}, bf16[256,2048]{1,0:T(8,128)(2,1)}, u32[]{:S(2)}, u32[]{:S(2)}) collective-permute-start(bf16[256,2048]{1,0:T(8,128)(2,1)S(1)} %collective-permute-done.1.refs_7_), channel_id=1, source_target_pairs={{0,2},{1,3},{2,0},{3,1},{4,6},{5,7},{6,4},{7,5},{8,10},{9,11},{10,... | collective-permute-start | bytes 3145736 | tf_op jit(solution)/shard_map/ppermute | solution.py:640
  114.0 4.1 collective-permute-start.12
  114.0 4.4 collective-permute-start.13
  124.8 12.9 %copy-start.29 = (bf16[3,256]{1,0:T(4,128)(2,1)S(1)}, bf16[3,256]{1,0:T(4,128)(2,1)}, u32[]{:S(2)}) copy-start(bf16[3,256]{1,0:T(4,128)(2,1)} %param.19) | copy-start | bytes 4612
  137.2 367.7 %reduce-scatter.3.cloned.1.call-start = ((), (), s32[]{:S(2)}) async-start(), calls=%async_computation.5 | async-start | bytes 18874368 | tf_op jit(solution)/shard_map/reduce_scatter | solution.py:812
  187.8 49.7 %collective-permute-start.14 = (bf16[512,2048]{1,0:T(8,128)(2,1)}, bf16[512,2048]{1,0:T(8,128)(2,1)S(1)}, u32[]{:S(2)}, u32[]{:S(2)}) collective-permute-start(bf16[512,2048]{1,0:T(8,128)(2,1)} %weight_grad.3), channel_id=1, source_target_pairs={{0,8},{24,16},{1,9},{25,17},{2,10},{26,18},{3,11},{27,19},{4,12},{... | collective-permute-start | bytes 6291464 | tf_op jit(solution)/shard_map/ppermute | solution.py:570
  205.2 82.3 %collective-permute-start.16 = (bf16[512,2048]{1,0:T(8,128)(2,1)}, bf16[512,2048]{1,0:T(8,128)(2,1)}, u32[]{:S(2)}, u32[]{:S(2)}) collective-permute-start(bf16[512,2048]{1,0:T(8,128)(2,1)} %weight_grad.4), channel_id=1, source_target_pairs={{0,8},{24,16},{1,9},{25,17},{2,10},{26,18},{3,11},{27,19},{4,12},{... | collective-permute-start | bytes 6291464 | tf_op jit(solution)/shard_map/ppermute | solution.py:570
  207.8 29.7 %copy-start.6 = (bf16[512,2048]{1,0:T(8,128)(2,1)S(1)}, bf16[512,2048]{1,0:T(8,128)(2,1)}, u32[]{:S(2)}) copy-start(bf16[512,2048]{1,0:T(8,128)(2,1)} %weight_grad.3) | copy-start | bytes 6291460
  238.3 61.9 %collective-permute-start.15 = (bf16[512,2048]{1,0:T(8,128)(2,1)S(1)}, bf16[512,2048]{1,0:T(8,128)(2,1)}, u32[]{:S(2)}, u32[]{:S(2)}) collective-permute-start(bf16[512,2048]{1,0:T(8,128)(2,1)S(1)} %add_convert_fusion.9), channel_id=1, source_target_pairs={{8,16},{16,8},{9,17},{17,9},{10,18},{18,10},{11,19},{19,11},{12,20... | collective-permute-start | bytes 6291464 | tf_op jit(solution)/shard_map/ppermute | solution.py:570
  287.5 326.3 %reduce-scatter.5.cloned.1.call-start = ((), (), s32[]{:S(2)}) async-start(), calls=%async_computation.6 | async-start | bytes 18874368 | tf_op jit(solution)/shard_map/reduce_scatter | solution.py:833
  290.7 64.5 %collective-permute-start.18 = (bf16[512,2048]{1,0:T(8,128)(2,1)S(1)}, bf16[512,2048]{1,0:T(8,128)(2,1)}, u32[]{:S(2)}, u32[]{:S(2)}) collective-permute-start(bf16[512,2048]{1,0:T(8,128)(2,1)S(1)} %add_convert_fusion.8), channel_id=1, source_target_pairs={{8,16},{16,8},{9,17},{17,9},{10,18},{18,10},{11,19},{19,11},{12,20... | collective-permute-start | bytes 6291464 | tf_op jit(solution)/shard_map/ppermute | solution.py:570
  292.7 67.9 %collective-permute-start.17 = (bf16[1024,1024]{1,0:T(8,128)(2,1)}, bf16[1024,1024]{1,0:T(8,128)(2,1)}, u32[]{:S(2)}, u32[]{:S(2)}) collective-permute-start(bf16[1024,1024]{1,0:T(8,128)(2,1)} %get-tuple-element.293), channel_id=1, source_target_pairs={{0,8},{24,16},{1,9},{25,17},{2,10},{26,18},{3,11},{27,19},{4,12},{... | collective-permute-start | bytes 6291464 | tf_op jit(solution)/shard_map/ppermute | solution.py:570
  302.9 29.9 %copy-start.1 = (bf16[512,2048]{1,0:T(8,128)(2,1)}, bf16[512,2048]{1,0:T(8,128)(2,1)S(1)}, u32[]{:S(2)}) copy-start(bf16[512,2048]{1,0:T(8,128)(2,1)S(1)} %add_convert_fusion.7.kept_ref) | copy-start | bytes 6291460
  302.9 64.8 %collective-permute-start.21 = (bf16[512,2048]{1,0:T(8,128)(2,1)S(1)}, bf16[512,2048]{1,0:T(8,128)(2,1)S(1)}, u32[]{:S(2)}, u32[]{:S(2)}) collective-permute-start(bf16[512,2048]{1,0:T(8,128)(2,1)S(1)} %add_convert_fusion.7.kept_ref), channel_id=1, source_target_pairs={{8,0},{16,24},{9,1},{17,25},{10,2},{18,26},{11,3},{19,27},{12,4},{... | collective-permute-start | bytes 6291464 | tf_op jit(solution)/shard_map/ppermute | solution.py:570
  304.2 83.3 %collective-permute-start.20 = (bf16[1024,1024]{1,0:T(8,128)(2,1)}, bf16[1024,1024]{1,0:T(8,128)(2,1)}, u32[]{:S(2)}, u32[]{:S(2)}) collective-permute-start(bf16[1024,1024]{1,0:T(8,128)(2,1)} %get-tuple-element.300), channel_id=1, source_target_pairs={{0,8},{24,16},{1,9},{25,17},{2,10},{26,18},{3,11},{27,19},{4,12},{... | collective-permute-start | bytes 6291464 | tf_op jit(solution)/shard_map/ppermute | solution.py:570
  359.3 71.1 %collective-permute-start.26 = (bf16[512,2048]{1,0:T(8,128)(2,1)}, bf16[512,2048]{1,0:T(8,128)(2,1)}, u32[]{:S(2)}, u32[]{:S(2)}) collective-permute-start(bf16[512,2048]{1,0:T(8,128)(2,1)} %add_convert_fusion.6.kept_ref), channel_id=1, source_target_pairs={{8,0},{16,24},{9,1},{17,25},{10,2},{18,26},{11,3},{19,27},{12,4},{... | collective-permute-start | bytes 6291464 | tf_op jit(solution)/shard_map/ppermute | solution.py:570
  365.4 60.1 %collective-permute-start.19 = (bf16[1024,1024]{1,0:T(8,128)(2,1)}, bf16[1024,1024]{1,0:T(8,128)(2,1)}, u32[]{:S(2)}, u32[]{:S(2)}) collective-permute-start(bf16[1024,1024]{1,0:T(8,128)(2,1)} %add_convert_fusion.5), channel_id=1, source_target_pairs={{8,16},{16,8},{9,17},{17,9},{10,18},{18,10},{11,19},{19,11},{12,20... | collective-permute-start | bytes 6291464 | tf_op jit(solution)/shard_map/ppermute | solution.py:570
  367.7 19.8 %copy-start.9 = (bf16[512,2048]{1,0:T(8,128)(2,1)}, bf16[512,2048]{1,0:T(8,128)(2,1)S(1)}, u32[]{:S(2)}) copy-start(bf16[512,2048]{1,0:T(8,128)(2,1)S(1)} %collective-permute-done.21.came_ref) | copy-start | bytes 6291460
  392.0 75.3 %collective-permute-start.25 = (bf16[1024,1024]{1,0:T(8,128)(2,1)}, bf16[1024,1024]{1,0:T(8,128)(2,1)}, u32[]{:S(2)}, u32[]{:S(2)}) collective-permute-start(bf16[1024,1024]{1,0:T(8,128)(2,1)} %add_convert_fusion.4), channel_id=1, source_target_pairs={{8,16},{16,8},{9,17},{17,9},{10,18},{18,10},{11,19},{19,11},{12,20... | collective-permute-start | bytes 6291464 | tf_op jit(solution)/shard_map/ppermute | solution.py:570
  394.0 78.6 %collective-permute-start.24 = (bf16[2,2048,256]{2,1,0:T(8,128)(2,1)}, bf16[2,2048,256]{2,1,0:T(8,128)(2,1)}, u32[]{:S(2)}, u32[]{:S(2)}) collective-permute-start(bf16[2,2048,256]{2,1,0:T(8,128)(2,1)} %get-tuple-element.324), channel_id=1, source_target_pairs={{0,8},{24,16},{1,9},{25,17},{2,10},{26,18},{3,11},{27,19},{4,12},{... | collective-permute-start | bytes 6291464 | tf_op jit(solution)/shard_map/ppermute | solution.py:570
  428.6 24.4 %copy-start.2 = (bf16[1024,1024]{1,0:T(8,128)(2,1)}, bf16[1024,1024]{1,0:T(8,128)(2,1)S(1)}, u32[]{:S(2)}) copy-start(bf16[1024,1024]{1,0:T(8,128)(2,1)S(1)} %add_convert_fusion.3.kept_ref) | copy-start | bytes 6291460
  428.7 73.3 %collective-permute-start.22 = (bf16[1024,1024]{1,0:T(8,128)(2,1)S(1)}, bf16[1024,1024]{1,0:T(8,128)(2,1)}, u32[]{:S(2)}, u32[]{:S(2)}) collective-permute-start(bf16[1024,1024]{1,0:T(8,128)(2,1)S(1)} %add_convert_fusion.3.kept_ref), channel_id=1, source_target_pairs={{8,0},{16,24},{9,1},{17,25},{10,2},{18,26},{11,3},{19,27},{12,4},{... | collective-permute-start | bytes 6291464 | tf_op jit(solution)/shard_map/ppermute | solution.py:570
  453.1 11.6 %copy-start.25 = (bf16[2048]{0:T(1024)(128)(2,1)S(1)}, bf16[2048]{0:T(1024)(128)(2,1)}, u32[]{:S(2)}) copy-start(bf16[2048]{0:T(1024)(128)(2,1)} %param.21) | copy-start | bytes 12292
  453.1 12.2 %copy-start.26 = (bf16[2048]{0:T(1024)(128)(2,1)S(1)}, bf16[2048]{0:T(1024)(128)(2,1)}, u32[]{:S(2)}) copy-start(bf16[2048]{0:T(1024)(128)(2,1)} %param.25) | copy-start | bytes 12292
  453.1 51.8 %all-to-all-start = ((bf16[8,2,256,256]{3,2,1,0:T(8,128)(2,1)}), bf16[8,2,256,256]{3,2,1,0:T(8,128)(2,1)}, u32[]{:S(2)}, u32[]{:S(2)}) async-start(bf16[8,2,256,256]{3,2,1,0:T(8,128)(2,1)} %get-tuple-element.287), calls=%async_computation | async-start | bytes 4194304 | tf_op jit(solution)/shard_map/all_to_all | solution.py:821
  457.6 40.3 %collective-permute-start.23 = (bf16[2048,256]{1,0:T(8,128)(2,1)S(1)}, bf16[2048,256]{1,0:T(8,128)(2,1)}, u32[]{:S(2)}, u32[]{:S(2)}) collective-permute-start(bf16[2048,256]{1,0:T(8,128)(2,1)S(1)} %copy-done.10), channel_id=1, source_target_pairs={{0,8},{24,16},{1,9},{25,17},{2,10},{26,18},{3,11},{27,19},{4,12},{... | collective-permute-start | bytes 3145736 | tf_op jit(solution)/shard_map/ppermute | solution.py:570
  477.4 46.4 %collective-permute-start.28 = (bf16[2,2048,256]{2,1,0:T(8,128)(2,1)}, bf16[2,2048,256]{2,1,0:T(8,128)(2,1)}, u32[]{:S(2)}, u32[]{:S(2)}) collective-permute-start(bf16[2,2048,256]{2,1,0:T(8,128)(2,1)} %add_convert_fusion.1), channel_id=1, source_target_pairs={{8,16},{16,8},{9,17},{17,9},{10,18},{18,10},{11,19},{19,11},{12,20... | collective-permute-start | bytes 6291464 | tf_op jit(solution)/shard_map/ppermute | solution.py:570
  479.4 93.7 %collective-permute-start.36 = (bf16[1024,1024]{1,0:T(8,128)(2,1)}, bf16[1024,1024]{1,0:T(8,128)(2,1)}, u32[]{:S(2)}, u32[]{:S(2)}) collective-permute-start(bf16[1024,1024]{1,0:T(8,128)(2,1)} %add_convert_fusion.2.kept_ref), channel_id=1, source_target_pairs={{8,0},{16,24},{9,1},{17,25},{10,2},{18,26},{11,3},{19,27},{12,4},{... | collective-permute-start | bytes 6291464 | tf_op jit(solution)/shard_map/ppermute | solution.py:570
  491.0 28.4 %collective-permute-start.29 = (bf16[256,2048]{1,0:T(8,128)(2,1)}, bf16[256,2048]{1,0:T(8,128)(2,1)}, u32[]{:S(2)}, u32[]{:S(2)}) collective-permute-start(bf16[256,2048]{1,0:T(8,128)(2,1)} %weight_grad.5), channel_id=1, source_target_pairs={{0,8},{24,16},{1,9},{25,17},{2,10},{26,18},{3,11},{27,19},{4,12},{... | collective-permute-start | bytes 3145736 | tf_op jit(solution)/shard_map/ppermute | solution.py:570
  500.4 27.8 %collective-permute-start.27 = (bf16[2048,256]{1,0:T(8,128)(2,1)}, bf16[2048,256]{1,0:T(8,128)(2,1)}, u32[]{:S(2)}, u32[]{:S(2)}) collective-permute-start(bf16[2048,256]{1,0:T(8,128)(2,1)} %add_convert_fusion.13), channel_id=1, source_target_pairs={{8,16},{16,8},{9,17},{17,9},{10,18},{18,10},{11,19},{19,11},{12,20... | collective-permute-start | bytes 3145736 | tf_op jit(solution)/shard_map/ppermute | solution.py:570
  504.9 10.5 %copy-start.20 = (f32[8,2048]{1,0:T(8,128)S(1)}, f32[8,2048]{1,0:T(8,128)}, u32[]{:S(2)}) copy-start(f32[8,2048]{1,0:T(8,128)} %get-tuple-element.339) | copy-start | bytes 196612
  504.9 11.4 %copy-start.21 = (bf16[2048]{0:T(1024)(128)(2,1)S(1)}, bf16[2048]{0:T(1024)(128)(2,1)}, u32[]{:S(2)}) copy-start(bf16[2048]{0:T(1024)(128)(2,1)} %param.16) | copy-start | bytes 12292
  505.0 14.5 %copy-start.8 = (bf16[256,2048]{1,0:T(8,128)(2,1)S(1)}, bf16[256,2048]{1,0:T(8,128)(2,1)}, u32[]{:S(2)}) copy-start(bf16[256,2048]{1,0:T(8,128)(2,1)} %weight_grad.5) | copy-start | bytes 3145732
  516.4 13.5 %collective-permute-start.32 = (f32[33,128]{1,0:T(8,128)S(1)}, f32[33,128]{1,0:T(8,128)S(1)}, u32[]{:S(2)}, u32[]{:S(2)}) collective-permute-start(f32[33,128]{1,0:T(8,128)S(1)} %bitcast.76), channel_id=1, source_target_pairs={{0,1},{1,0},{2,3},{3,2},{4,5},{5,4},{6,7},{7,6},{8,9},{9,8},{10,11... | collective-permute-start | bytes 50696 | tf_op jit(solution)/shard_map/ppermute | solution.py:724
  522.1 47.9 %collective-permute-start.37 = (bf16[256,2048]{1,0:T(8,128)(2,1)}, bf16[256,2048]{1,0:T(8,128)(2,1)}, u32[]{:S(2)}, u32[]{:S(2)}) collective-permute-start(bf16[256,2048]{1,0:T(8,128)(2,1)} %add_convert_fusion.12), channel_id=1, source_target_pairs={{8,16},{16,8},{9,17},{17,9},{10,18},{18,10},{11,19},{19,11},{12,20... | collective-permute-start | bytes 3145736 | tf_op jit(solution)/shard_map/ppermute | solution.py:570
  526.8 62.9 %collective-permute-start.31 = (bf16[2,2048,256]{2,1,0:T(8,128)(2,1)S(1)}, bf16[2,2048,256]{2,1,0:T(8,128)(2,1)}, u32[]{:S(2)}, u32[]{:S(2)}) collective-permute-start(bf16[2,2048,256]{2,1,0:T(8,128)(2,1)S(1)} %add_convert_fusion), channel_id=1, source_target_pairs={{8,0},{16,24},{9,1},{17,25},{10,2},{18,26},{11,3},{19,27},{12,4},{... | collective-permute-start | bytes 6291464 | tf_op jit(solution)/shard_map/ppermute | solution.py:570
  530.0 48.8 %copy-start.7 = (bf16[2048,256]{1,0:T(8,128)(2,1)}, bf16[2048,256]{1,0:T(8,128)(2,1)S(1)}, u32[]{:S(2)}) copy-start(bf16[2048,256]{1,0:T(8,128)(2,1)S(1)} %add_convert_fusion.11.kept_ref) | copy-start | bytes 3145732
  530.0 7.1 %collective-permute-start.33 = (f32[33,128]{1,0:T(8,128)S(1)}, f32[33,128]{1,0:T(8,128)S(1)}, u32[]{:S(2)}, u32[]{:S(2)}) collective-permute-start(f32[33,128]{1,0:T(8,128)S(1)} %add.142), channel_id=1, source_target_pairs={{0,2},{1,3},{2,0},{3,1},{4,6},{5,7},{6,4},{7,5},{8,10},{9,11},{10,... | collective-permute-start | bytes 50696 | tf_op jit(solution)/shard_map/ppermute | solution.py:724
  537.1 6.0 collective-permute-start.34
  543.1 33.6 %collective-permute-start.35 = (f32[49,128]{1,0:T(8,128)S(1)}, f32[49,128]{1,0:T(8,128)S(1)}, u32[]{:S(2)}, u32[]{:S(2)}) collective-permute-start(f32[49,128]{1,0:T(8,128)S(1)} %pad_maximum_fusion), channel_id=1, source_target_pairs={{0,8},{24,16},{1,9},{25,17},{2,10},{26,18},{3,11},{27,19},{4,12},{... | collective-permute-start | bytes 75272 | tf_op jit(solution)/shard_map/ppermute | solution.py:570
  576.7 0.7 collective-permute-start.38
  577.4 9.2 %collective-permute-start.39 = (f32[49,128]{1,0:T(8,128)S(1)}, f32[49,128]{1,0:T(8,128)S(1)}, u32[]{:S(2)}, u32[]{:S(2)}) collective-permute-start(f32[49,128]{1,0:T(8,128)S(1)} %add.148), channel_id=1, source_target_pairs={{8,0},{16,24},{9,1},{17,25},{10,2},{18,26},{11,3},{19,27},{12,4},{... | collective-permute-start | bytes 75272 | tf_op jit(solution)/shard_map/ppermute | solution.py:570
  578.7 31.3 %collective-permute-start.30 = (bf16[2048,256]{1,0:T(8,128)(2,1)S(1)}, bf16[2048,256]{1,0:T(8,128)(2,1)}, u32[]{:S(2)}, u32[]{:S(2)}) collective-permute-start(bf16[2048,256]{1,0:T(8,128)(2,1)S(1)} %add_convert_fusion.11.kept_ref), channel_id=1, source_target_pairs={{8,0},{16,24},{9,1},{17,25},{10,2},{18,26},{11,3},{19,27},{12,4},{... | collective-permute-start | bytes 3145736 | tf_op jit(solution)/shard_map/ppermute | solution.py:570
  580.0 50.4 %collective-permute-start.40 = (bf16[256,2048]{1,0:T(8,128)(2,1)}, bf16[256,2048]{1,0:T(8,128)(2,1)}, u32[]{:S(2)}, u32[]{:S(2)}) collective-permute-start(bf16[256,2048]{1,0:T(8,128)(2,1)} %add_convert_fusion.10.kept_ref), channel_id=1, source_target_pairs={{8,0},{16,24},{9,1},{17,25},{10,2},{18,26},{11,3},{19,27},{12,4},{... | collective-permute-start | bytes 3145736 | tf_op jit(solution)/shard_map/ppermute | solution.py:570
  586.7 46.7 %copy-start.27 = (f32[256]{0:T(256)}, f32[256]{0:T(256)S(1)}, u32[]{:S(2)}) copy-start(f32[256]{0:T(256)S(1)} %slice_bitcast_fusion.3) | copy-start | bytes 3076
  596.3 17.5 %copy-start = (bf16[2,256,2048]{2,1,0:T(8,128)(2,1)S(1)}, bf16[2,256,2048]{2,1,0:T(8,128)(2,1)}, u32[]{:S(2)}) copy-start(bf16[2,256,2048]{2,1,0:T(8,128)(2,1)} %param.14) | copy-start | bytes 6291460
  (12 other events, 52.7 us)
Sparse Core Ops, SparseCore 0:
  66.0 107.4 all-gather.2
  175.4 54.3 all-gather.4
  287.6 116.4 reduce-scatter.2
  453.2 117.5 reduce-scatter.4

commit v5 on v4

--- a/solution.py
+++ b/solution.py
@@ -15,8 +15,8 @@
 f32 = jnp.float32
 bf16 = jnp.bfloat16
 VMEM_LIMIT = 56 << 20
-ORDER_WEIGHT = int(2e11)
-EARLY_WEIGHT = int(2.1e11)
+ORDER_WEIGHT = int(2.1e11)
+EARLY_WEIGHT = int(2.2e11)
 
 
 def dot(a, b, ca, cb):
@@ -808,26 +808,26 @@
     row_sum = lambda parts: [RowSum(part, rows) for part in parts]
     hidden_grad, attended_grad, in_bias = order(grad_in, grad, outward_weight, dense_weight, slope)
     o0.fold(order)
+    i0, i1 = row_sum(order(lambda a, b: weight_grad_rows(a, b, (1, 1)), normed, hidden_grad))
     mlp_part = order(lambda *a: tokens_by_weight(*a, 0, 1), act, outward_weight).reshape(seqs, length, width)
     mlp_tok = lax.psum_scatter(mlp_part, "tp", scatter_dimension=1, tiled=True).reshape(seqs * here, width)
-    i0, i1 = row_sum(order(lambda a, b: weight_grad_rows(a, b, (1, 1)), normed, hidden_grad))
     o1.fold(order)
     o0.fold(order)
     both = lambda row: lambda s, q, g, c, t, *before: attention_both(s, q, g, c, t, span, tp, row, before)
     attended, by_owner, dqkv = order(both(0), start, qkv, attended_grad, cosine, sine)
+    i0.fold(order)
     for row in range(1, seqs):
         kept = (attended, by_owner, dqkv)
         attended, by_owner, dqkv = order(both(row), start, qkv, attended_grad, cosine, sine, *kept)
     mine = lax.all_to_all(by_owner, "tp", split_axis=0, concat_axis=0, tiled=True)
     o1.fold(order)
-    i0.fold(order)
     o0.settle(order)
     qs, vs = row_sum(order(lambda a, b: weight_grad_parts(a, b, weight=EARLY_WEIGHT), normed, dqkv))
     units = in_bias.shape[1]
     back = lambda share: lambda *a: normed_grad(*a[:5], shift[None], share, 2, a[5:])
     i1.fold(order)
+    i0.fold(order)
     part, bias_a, norm_a = order(back(0), hidden_grad, dqkv, inward_weight, w3, normed)
-    i0.fold(order)
     o1.settle(order)
     part, bias_b, norm_b = order(back(1), hidden_grad, dqkv, inward_weight, w3, normed, part)
     back_tok = lax.psum_scatter(part.reshape(seqs, length, width), "tp", scatter_dimension=1, tiled=True)
@@ -858,23 +858,21 @@
 
     packed = TpSum(order(pack, norm_a, norm_b, squares), tp)
     ds.fold(order)
+    packed.fold(order)
     qs.fold(order)
-    vs.fold(order)
-    packed.fold(order)
-    out_grad = finish(o0, order, units)
-    packed.fold(order)
-    out_grad = finish(o1, order, units, units // 2, out_grad)
     packed.fold(order)
     qkv_bias = bias_a + bias_b
     small = jnp.concatenate([in_bias[0], qkv_bias[:, 0].reshape(-1), out_bias]).reshape(-1, 128)
     small = RowSum(jnp.concatenate([packed.result(order), small]), rows)
+    vs.fold(order)
+    small.fold(order)
+    out_grad = finish(o0, order, units)
+    out_grad = finish(o1, order, units, units // 2, out_grad)
     in_grad = finish(i0, order, width)
     ds.fold(order)
+    small.fold(order)
     in_grad = finish(i1, order, width, width // 2, in_grad)
-    small.fold(order)
-    small.fold(order)
     qkv_grad = finish(qs, order, 3 * width)
-    qkv_grad = finish(vs, order, 3 * width, 2 * width, qkv_grad)
 
     def norm_back(back_tok, tokens, cotangent):
         values = tokens.astype(f32)
@@ -888,6 +886,7 @@
         return (cotangent.astype(f32) + value_grad).astype(bf16)
 
     input_grad = order(norm_back, back_tok, tokens, cotangent)
+    qkv_grad = finish(vs, order, 3 * width, 2 * width, qkv_grad)
     qkv_grad = jnp.transpose(qkv_grad.reshape(3, width, local), (1, 0, 2))
     dense_grad = finish(ds, order, local)
     small = small.result().reshape(-1)

time: 651 us -> 647 us (level)
  starting transfers between devices: 107 us -> 98.4 us
    ppermute x24, starting transfers between devices: 90.7 us -> 82.1 us  [send(): self.came = lax.ppermute(self.part, self.axis, self.hops.pop(0))]
  transfers between devices with their start and end apart: 46 -> 46, of which waited for: 14 -> 15; matrix products, arithmetic and copies ran while one was open for 10% -> 10% of each run, Pallas kernels for 54% -> 55%
where the time goes in v5:
time: 647 us; the launch traced here: 637 us
  Pallas kernels  357 us (55%)
  starting transfers between devices  98.4 us (15%)
  waiting for transfers between devices  95.8 us (15%)
  other arithmetic  59.3 us (9%)
  between operations  14.9 us (2%)
  local copies, waits for them, and re-layouts  12.2 us (2%)
    ppermute x24, starting transfers between devices, send(): self.came = lax.ppermute(self.part, self.axis, self.hops.pop(0))  82.1 us
    pallas_call x2, Pallas kernels, normed_grad(): pl.pallas_call(functools.partial(normed_grad_kernel, held=held), grid=(st...  45.4 us
    pallas_call x2, Pallas kernels, attention_both(): pl.pallas_call(functools.partial(attention_kernel, bq=bq, held=held), gri...  45 us
    ppermute x14, waiting for transfers between devices, send(): return lax.ppermute(a, 'tp', [(i, i ^ step) for i in range(self.size)])  44 us
    convert_element_type x14, other arithmetic, fold(): add = lambda a, b: (a.astype(f32) + b.astype(f32)).astype(a.dtype)  42.3 us
    pallas_call x3, Pallas kernels, weight_grad(): pl.pallas_call(weight_grad_kernel, grid=(cols // tile,), in_specs=[pl.Blo...  40.8 us
    pallas_call x2, Pallas kernels, mlp_hidden_of(): pl.pallas_call(functools.partial(chosen_kernel, held=held), grid_spec=plt...  36 us
    ppermute x24, waiting for transfers between devices, send(): self.came = lax.ppermute(self.part, self.axis, self.hops.pop(0))  34.9 us
  transfers between devices with their start and end apart: 46, of which 15 were waited for; matrix products, arithmetic and copies ran while one was open for 10% of the time, Pallas kernels for 55%

profile of v5, /device:TPU:0, one launch (start us, length us, event | category | flops | bytes accessed | tf_op | source)
XLA Modules:
  0.0 637.5 jit_solution(1482133239831992693)
XLA Ops:
  9.8 4.7 norm_halves.1
  14.5 3.0 collective-permute-start.1
  19.7 2.0 copy.39
  22.2 9.8 %rope_tables.1 = (f32[4096,128]{1,0:T(8,128)}, f32[4096,128]{1,0:T(8,128)}) custom-call(s32[4096,1]{1,0:T(8,128)} %bitcast.68, f32[1,128]{1,0:T(1,128)} %fusion.15.frequency_ref), custom_call_target="tpu_custom_call" | custom-call | flops 1 | bytes 1 | tf_op jit(solution)/shard_map/rope_tables/pallas_call | solution.py:99
  32.6 9.1 %collective-permute-done.1.refs_7_ = bf16[256,2048]{1,0:T(8,128)(2,1)S(1)} collective-permute-done((bf16[256,2048]{1,0:T(8,128)(2,1)}, bf16[256,2048]{1,0:T(8,128)(2,1)S(1)}, u32[]{:S(2)}, u32[]{:S(2)}) %collective-permute-start.1) | collective-permute-done | bytes 1048608 | tf_op jit(solution)/shard_map/ppermute | solution.py:640
  41.7 2.0 collective-permute-done.refs_4_
  43.7 22.2 %collective-permute-done.3.refs_5_ = bf16[256,2048]{1,0:T(8,128)(2,1)} collective-permute-done((bf16[256,2048]{1,0:T(8,128)(2,1)}, bf16[256,2048]{1,0:T(8,128)(2,1)}, u32[]{:S(2)}, u32[]{:S(2)}) %collective-permute-start.3) | collective-permute-done | bytes 1048608 | tf_op jit(solution)/shard_map/ppermute | solution.py:640
  67.3 2.1 collective-permute-done.6.refs_8_
  73.5 13.1 %place_pieces.2.refs_0_ = bf16[2,8,256,2048]{3,2,1,0:T(8,128)(2,1)} custom-call(s32[1]{0:T(128)} %bitcast.3.me_ref, bf16[256,2048]{1,0:T(8,128)(2,1)} %get-tuple-element.212.refs_0_, bf16[256,2048]{1,0:T(8,128)(2,1)} %get-tuple-element.213.refs_1_, bf16[256,2048]{1,0:T(8,128)(2,1)} %collective-permute-done.2.refs_2_, ...), custom_call_target="tpu_custom_call" | custom-call | flops 1 | bytes 1 | tf_op jit(solution)/shard_map/place_pieces/pallas_call | solution.py:701
  86.6 23.6 %mlp_hidden_of.2 = (bf16[2,8,256,1024]{3,2,1,0:T(8,128)(2,1)}, bf16[2,8,256,1024]{3,2,1,0:T(8,128)(2,1)}) custom-call(s32[1]{0:T(128)} %bitcast.3.me_ref, bf16[2,8,256,2048]{3,2,1,0:T(8,128)(2,1)} %place_pieces.2.refs_0_, bf16[2048,1024]{1,0:T(8,128)(2,1)} %refs_3_.1, f32[1,1024]{1,0:T(1,128)} %bitcast.78), custom_call_target="tpu_custom_call" | custom-call | flops 1 | bytes 1 | tf_op jit(solution)/shard_map/mlp_hidden_of/pallas_call | solution.py:180
  110.3 3.7 collective-permute-done.11.refs_2_
  114.5 3.6 collective-permute-done.12.refs_3_
  120.1 4.8 place_pieces.3.refs_2_
  124.8 12.4 %mlp_hidden_of.3 = (bf16[2,8,256,1024]{3,2,1,0:T(8,128)(2,1)}, bf16[2,8,256,1024]{3,2,1,0:T(8,128)(2,1)}) custom-call(s32[1]{0:T(128)} %bitcast.3.me_ref, bf16[2,8,256,1024]{3,2,1,0:T(8,128)(2,1)} %get-tuple-element.236.refs_0_, bf16[2,8,256,1024]{3,2,1,0:T(8,128)(2,1)} %get-tuple-element.237.refs_1_, ...), custom_call_target="tpu_custom_call", output_to_operand_aliasing={{0}: (1, {}), {1}: (2, {})} | custom-call | flops 1 | bytes 1 | tf_op jit(solution)/shard_map/mlp_hidden_of/pallas_call | solution.py:180
  138.1 20.0 %qkv_rope.1.refs_1_.refs_2_.refs_3_.refs_4_.refs_5_.refs_6_ = bf16[3,4096,256]{2,1,0:T(8,128)(2,1)} custom-call(bf16[4096,2048]{1,0:T(8,128)(2,1)} %bitcast.45, bf16[3,2048,256]{2,1,0:T(8,128)(2,1)} %bitcast.63, f32[3,256]{1,0:T(4,128)} %convert_element_type.170.b_ref, f32[4096,128]{1,0:T(8,128)} %get-tuple-element.287.c_ref.refs_5_.refs_8_, ...), custom_call_target="tpu_custom_call" | custom-call | flops 1 | bytes 1 | tf_op jit(solution)/shard_map/qkv_rope/pallas_call | solution.py:131
  158.1 15.4 %all-gather.3.cloned.1.call-done = bf16[2,2048,2048]{2,1,0:T(8,128)(2,1)} async-done(((bf16[2,256,2048]{2,1,0:T(8,128)(2,1)}), bf16[2,2048,2048]{2,1,0:T(8,128)(2,1)}) %all-gather.3.cloned.1.call-update) | async-done | bytes 16777232 | tf_op jit(solution)/shard_map/all_gather | solution.py:784
  173.6 14.2 %weight_grad.3 = bf16[512,2048]{1,0:T(8,128)(2,1)} custom-call(bf16[4096,1024]{1,0:T(8,128)(2,1)} %bitcast.55, bf16[4096,2048]{1,0:T(8,128)(2,1)} %bitcast.50), custom_call_target="tpu_custom_call" | custom-call | flops 1 | bytes 1 | tf_op jit(solution)/shard_map/weight_grad/pallas_call | solution.py:279
  187.8 3.5 collective-permute-start.14
  191.4 13.8 %weight_grad.4 = bf16[512,2048]{1,0:T(8,128)(2,1)} custom-call(bf16[4096,1024]{1,0:T(8,128)(2,1)} %bitcast.56, bf16[4096,2048]{1,0:T(8,128)(2,1)} %bitcast.51), custom_call_target="tpu_custom_call" | custom-call | flops 1 | bytes 1 | tf_op jit(solution)/shard_map/weight_grad/pallas_call | solution.py:279
  206.6 29.6 %grad_in.1 = (bf16[4096,1024]{1,0:T(8,128)(2,1)}, bf16[4096,256]{1,0:T(8,128)(2,1)}, f32[8,1024]{1,0:T(8,128)}) custom-call(bf16[4096,2048]{1,0:T(8,128)(2,1)} %bitcast.52, bf16[1024,2048]{1,0:T(8,128)(2,1)} %w_ref, bf16[256,2048]{1,0:T(8,128)(2,1)} %wd_ref, bf16[4096,1024]{1,0:T(8,128)(2,1)} %bitcast.62), custom_call_target="tpu_custom_call" | custom-call | flops 1 | bytes 1 | tf_op jit(solution)/shard_map/grad_in/pallas_call | solution.py:221
  238.8 2.5 add_convert_fusion.9
  241.3 2.0 collective-permute-start.15
  243.3 24.7 %weight_grad_rows.1 = (bf16[1024,1024]{1,0:T(8,128)(2,1)}, bf16[1024,1024]{1,0:T(8,128)(2,1)}) custom-call(bf16[4096,2048]{1,0:T(8,128)(2,1)} %bitcast.46, bf16[4096,1024]{1,0:T(8,128)(2,1)} %get-tuple-element.314.b_ref.refs_0_.refs_1_), custom_call_target="tpu_custom_call" | custom-call | flops 1 | bytes 1 | tf_op jit(solution)/shard_map/weight_grad_rows/pallas_call | solution.py:313
  268.0 7.4 %collective-permute-start.17 = (bf16[1024,1024]{1,0:T(8,128)(2,1)}, bf16[1024,1024]{1,0:T(8,128)(2,1)}, u32[]{:S(2)}, u32[]{:S(2)}) collective-permute-start(bf16[1024,1024]{1,0:T(8,128)(2,1)} %get-tuple-element.279), channel_id=1, source_target_pairs={{0,8},{24,16},{1,9},{25,17},{2,10},{26,18},{3,11},{27,19},{4,12},{... | collective-permute-start | bytes 6291464 | tf_op jit(solution)/shard_map/ppermute | solution.py:570
  275.4 22.8 %tokens_by_weight.1 = bf16[4096,2048]{1,0:T(8,128)(2,1)} custom-call(bf16[4096,1024]{1,0:T(8,128)(2,1)} %bitcast.57, bf16[1024,2048]{1,0:T(8,128)(2,1)} %w_ref), custom_call_target="tpu_custom_call" | custom-call | flops 1 | bytes 1 | tf_op jit(solution)/shard_map/tokens_by_weight/pallas_call | solution.py:258
  298.2 2.2 add_convert_fusion.8
  300.4 2.0 collective-permute-start.21
  302.4 2.4 add_convert_fusion.7.kept_ref
  306.2 7.3 %collective-permute-start.19 = (bf16[1024,1024]{1,0:T(8,128)(2,1)}, bf16[1024,1024]{1,0:T(8,128)(2,1)}, u32[]{:S(2)}, u32[]{:S(2)}) collective-permute-start(bf16[1024,1024]{1,0:T(8,128)(2,1)} %get-tuple-element.300), channel_id=1, source_target_pairs={{0,8},{24,16},{1,9},{25,17},{2,10},{26,18},{3,11},{27,19},{4,12},{... | collective-permute-start | bytes 6291464 | tf_op jit(solution)/shard_map/ppermute | solution.py:570
  313.5 22.3 %attention_both.2 = (bf16[4096,256]{1,0:T(8,128)(2,1)}, bf16[8,2,256,256]{3,2,1,0:T(8,128)(2,1)}, bf16[3,4096,256]{2,1,0:T(8,128)(2,1)}) custom-call(s32[1,4096]{1,0:T(1,128)} %fusion.11.refs_0_.refs_3_, bf16[3,4096,256]{2,1,0:T(8,128)(2,1)} %qkv_rope.1.refs_1_.refs_2_.refs_3_.refs_4_.refs_5_.refs_6_, ...), custom_call_target="tpu_custom_call" | custom-call | flops 1 | bytes 1 | tf_op jit(solution)/shard_map/attention_both/pallas_call | solution.py:476
  335.8 4.1 add_convert_fusion.6
  339.9 2.2 collective-permute-start.18
  342.1 22.7 %attention_both.3 = (bf16[4096,256]{1,0:T(8,128)(2,1)}, bf16[8,2,256,256]{3,2,1,0:T(8,128)(2,1)}, bf16[3,4096,256]{2,1,0:T(8,128)(2,1)}) custom-call(bf16[4096,256]{1,0:T(8,128)(2,1)} %get-tuple-element.281.refs_0_, bf16[8,2,256,256]{3,2,1,0:T(8,128)(2,1)} %get-tuple-element.282.refs_1_, ...), custom_call_target="tpu_custom_call", output_to_operand_aliasing={{0}: (0, {}), {1}: (1, {}), {2}: (2, {})} | custom-call | flops 1 | bytes 1 | tf_op jit(solution)/shard_map/attention_both/pallas_call | solution.py:476
  364.8 4.6 add_convert_fusion.5.kept_ref
  370.7 19.4 %weight_grad_parts.1 = (bf16[2,2048,256]{2,1,0:T(8,128)(2,1)}, bf16[2048,256]{1,0:T(8,128)(2,1)}) custom-call(bf16[4096,2048]{1,0:T(8,128)(2,1)} %bitcast.47, bf16[3,4096,256]{2,1,0:T(8,128)(2,1)} %get-tuple-element.315.b_ref.refs_1_.refs_2_), custom_call_target="tpu_custom_call" | custom-call | flops 219999993856 | bytes 1 | tf_op jit(solution)/shard_map/weight_grad_parts/pallas_call | solution.py:337
  390.1 3.9 add_convert_fusion.4
  396.0 7.4 %collective-permute-start.24 = (bf16[2,2048,256]{2,1,0:T(8,128)(2,1)}, bf16[2,2048,256]{2,1,0:T(8,128)(2,1)}, u32[]{:S(2)}, u32[]{:S(2)}) collective-permute-start(bf16[2,2048,256]{2,1,0:T(8,128)(2,1)} %get-tuple-element.324), channel_id=1, source_target_pairs={{0,8},{24,16},{1,9},{25,17},{2,10},{26,18},{3,11},{27,19},{4,12},{... | collective-permute-start | bytes 6291464 | tf_op jit(solution)/shard_map/ppermute | solution.py:570
  403.4 3.3 add_convert_fusion.3.kept_ref
  408.3 4.4 all-to-all-start
  415.3 7.0 %collective-permute-start.23 = (bf16[2048,256]{1,0:T(8,128)(2,1)S(1)}, bf16[2048,256]{1,0:T(8,128)(2,1)}, u32[]{:S(2)}, u32[]{:S(2)}) collective-permute-start(bf16[2048,256]{1,0:T(8,128)(2,1)S(1)} %copy-done.13), channel_id=1, source_target_pairs={{0,8},{24,16},{1,9},{25,17},{2,10},{26,18},{3,11},{27,19},{4,12},{... | collective-permute-start | bytes 3145736 | tf_op jit(solution)/shard_map/ppermute | solution.py:570
  422.3 22.7 %normed_grad.2 = (bf16[4096,2048]{1,0:T(8,128)(2,1)}, f32[3,8,256]{2,1,0:T(8,128)}, f32[8,2048]{1,0:T(8,128)}) custom-call(bf16[4096,1024]{1,0:T(8,128)(2,1)} %get-tuple-element.314.b_ref.refs_0_.refs_1_, bf16[3,4096,256]{2,1,0:T(8,128)(2,1)} %get-tuple-element.315.b_ref.refs_1_.refs_2_, bf16[2048,1024]{1,0:T(8,128)(2,1)} %refs_3_.1, ...), custom_call_target="tpu_custom_call" | custom-call | flops 1 | bytes 1 | tf_op jit(solution)/shard_map/normed_grad/pallas_call | solution.py:381
  445.0 22.6 %normed_grad.3 = (bf16[4096,2048]{1,0:T(8,128)(2,1)}, f32[3,8,256]{2,1,0:T(8,128)}, f32[8,2048]{1,0:T(8,128)}) custom-call(bf16[4096,2048]{1,0:T(8,128)(2,1)} %get-tuple-element.313.refs_0_, bf16[4096,1024]{1,0:T(8,128)(2,1)} %get-tuple-element.314.b_ref.refs_0_.refs_1_, ...), custom_call_target="tpu_custom_call", output_to_operand_aliasing={{0}: (0, {})} | custom-call | flops 1 | bytes 1 | tf_op jit(solution)/shard_map/normed_grad/pallas_call | solution.py:381
  469.1 4.5 add_convert_fusion.2.kept_ref
  473.6 4.7 add_convert_fusion.1
  478.3 2.0 collective-permute-start.27
  481.6 12.7 %weight_grad.5 = bf16[256,2048]{1,0:T(8,128)(2,1)} custom-call(bf16[4096,256]{1,0:T(8,128)(2,1)} %get-tuple-element.326.a_ref, bf16[4096,2048]{1,0:T(8,128)(2,1)} %bitcast.53), custom_call_target="tpu_custom_call" | custom-call | flops 1 | bytes 1 | tf_op jit(solution)/shard_map/weight_grad/pallas_call | solution.py:279
  494.3 6.8 %collective-permute-start.29 = (bf16[256,2048]{1,0:T(8,128)(2,1)}, bf16[256,2048]{1,0:T(8,128)(2,1)}, u32[]{:S(2)}, u32[]{:S(2)}) collective-permute-start(bf16[256,2048]{1,0:T(8,128)(2,1)} %weight_grad.5), channel_id=1, source_target_pairs={{0,8},{24,16},{1,9},{25,17},{2,10},{26,18},{3,11},{27,19},{4,12},{... | collective-permute-start | bytes 3145736 | tf_op jit(solution)/shard_map/ppermute | solution.py:570
  501.1 2.5 add_convert_fusion.13
  505.2 3.2 convert_reduce_fusion.1
  508.5 10.5 %project_own.1 = (bf16[512,2048]{1,0:T(8,128)(2,1)}, f32[8,512]{1,0:T(8,128)}) custom-call(bf16[8,2,256,256]{3,2,1,0:T(8,128)(2,1)} %all-to-all-done.x_ref, bf16[2048,2048]{1,0:T(8,128)(2,1)} %all-gather.5.cloned.1.call-done.w_ref, f32[1,2048]{1,0:T(1,128)} %bitcast.84, f32[1,2048]{1,0:T(1,128)} %bitcast.85, bf16[512,2048]{1,0:T(8,128)(2,1)} %bitcast.61, ...), custom_call_target="tpu_custom_call" | custom-call | flops 210000003072 | bytes 1 | tf_op jit(solution)/shard_map/project_own/pallas_call | solution.py:532
  520.0 2.5 collective-permute-done.29
  526.8 2.8 add_convert_fusion
  533.8 17.3 %collective-permute-start.34 = (f32[49,128]{1,0:T(8,128)S(1)}, f32[49,128]{1,0:T(8,128)S(1)}, u32[]{:S(2)}, u32[]{:S(2)}) collective-permute-start(f32[49,128]{1,0:T(8,128)S(1)} %pad_maximum_fusion), channel_id=1, source_target_pairs={{0,8},{24,16},{1,9},{25,17},{2,10},{26,18},{3,11},{27,19},{4,12},{... | collective-permute-start | bytes 75272 | tf_op jit(solution)/shard_map/ppermute | solution.py:570
  553.7 4.6 finish.7.refs_0_
  558.3 4.9 finish.8
  563.2 3.7 finish.9.refs_0_
  572.2 3.7 finish.10
  576.0 8.9 %collective-permute-done.38 = f32[49,128]{1,0:T(8,128)S(1)} collective-permute-done((f32[49,128]{1,0:T(8,128)S(1)}, f32[49,128]{1,0:T(8,128)S(1)}, u32[]{:S(2)}, u32[]{:S(2)}) %collective-permute-start.38) | collective-permute-done | bytes 25120 | tf_op jit(solution)/shard_map/ppermute | solution.py:570
  587.9 6.7 %finish.11.refs_0_ = f32[6144,256]{1,0:T(8,128)} custom-call(s32[1]{0:T(128)} %bitcast.17.inner_ref, bf16[4096,256]{1,0:T(8,128)(2,1)} %bitcast.67, bf16[4096,256]{1,0:T(8,128)(2,1)} %bitcast.22.came_ref), custom_call_target="tpu_custom_call" | custom-call | flops 1 | bytes 1 | tf_op jit(solution)/shard_map/finish/pallas_call | solution.py:629
  597.8 3.2 fusion.8
  601.0 6.5 %collective-permute-done.39.came_ref = bf16[2048,256]{1,0:T(8,128)(2,1)} collective-permute-done((bf16[2048,256]{1,0:T(8,128)(2,1)S(1)}, bf16[2048,256]{1,0:T(8,128)(2,1)}, u32[]{:S(2)}, u32[]{:S(2)}) %collective-permute-start.39) | collective-permute-done | bytes 1048608 | tf_op jit(solution)/shard_map/ppermute | solution.py:570
  607.5 3.8 finish.12
  611.2 15.7 %collective-permute-done.40.came_ref = bf16[256,2048]{1,0:T(8,128)(2,1)} collective-permute-done((bf16[256,2048]{1,0:T(8,128)(2,1)}, bf16[256,2048]{1,0:T(8,128)(2,1)}, u32[]{:S(2)}, u32[]{:S(2)}) %collective-permute-start.40) | collective-permute-done | bytes 1048608 | tf_op jit(solution)/shard_map/ppermute | solution.py:570
  626.9 3.0 finish.13
  (184 shorter events, 56.0 us)
Async XLA Ops:
  7.2 12.4 %copy-start.27 = (s32[2,2048]{1,0:T(2,128)S(1)}, s32[2,2048]{1,0:T(2,128)}, u32[]{:S(2)}) copy-start(s32[2,2048]{1,0:T(2,128)} %param.15) | copy-start | bytes 49156
  7.2 166.4 %all-gather.3.cloned.1.call-start = ((), (), s32[]{:S(2)}) async-start(), calls=%async_computation.3 | async-start | bytes 18874368 | tf_op jit(solution)/shard_map/all_gather | solution.py:784
  14.5 27.2 %collective-permute-start.1 = (bf16[256,2048]{1,0:T(8,128)(2,1)}, bf16[256,2048]{1,0:T(8,128)(2,1)S(1)}, u32[]{:S(2)}, u32[]{:S(2)}) collective-permute-start(bf16[256,2048]{1,0:T(8,128)(2,1)} %get-tuple-element.213.refs_1_), channel_id=1, source_target_pairs={{0,4},{1,5},{2,6},{3,7},{4,0},{5,1},{6,2},{7,3},{8,12},{9,13},{10,... | collective-permute-start | bytes 3145736 | tf_op jit(solution)/shard_map/ppermute | solution.py:640
  17.5 24.2 %collective-permute-start.2 = (bf16[256,2048]{1,0:T(8,128)(2,1)}, bf16[256,2048]{1,0:T(8,128)(2,1)}, u32[]{:S(2)}, u32[]{:S(2)}) collective-permute-start(bf16[256,2048]{1,0:T(8,128)(2,1)} %get-tuple-element.212.refs_0_), channel_id=1, source_target_pairs={{0,1},{1,0},{2,3},{3,2},{4,5},{5,4},{6,7},{7,6},{8,9},{9,8},{10,11... | collective-permute-start | bytes 3145736 | tf_op jit(solution)/shard_map/ppermute | solution.py:640
  17.5 26.2 %collective-permute-start = (bf16[256,2048]{1,0:T(8,128)(2,1)}, bf16[256,2048]{1,0:T(8,128)(2,1)S(1)}, u32[]{:S(2)}, u32[]{:S(2)}) collective-permute-start(bf16[256,2048]{1,0:T(8,128)(2,1)} %get-tuple-element.212.refs_0_), channel_id=1, source_target_pairs={{0,2},{1,3},{2,0},{3,1},{4,6},{5,7},{6,4},{7,5},{8,10},{9,11},{10,... | collective-permute-start | bytes 3145736 | tf_op jit(solution)/shard_map/ppermute | solution.py:640
  19.0 46.9 %collective-permute-start.3 = (bf16[256,2048]{1,0:T(8,128)(2,1)}, bf16[256,2048]{1,0:T(8,128)(2,1)}, u32[]{:S(2)}, u32[]{:S(2)}) collective-permute-start(bf16[256,2048]{1,0:T(8,128)(2,1)} %get-tuple-element.213.refs_1_), channel_id=1, source_target_pairs={{0,2},{1,3},{2,0},{3,1},{4,6},{5,7},{6,4},{7,5},{8,10},{9,11},{10,... | collective-permute-start | bytes 3145736 | tf_op jit(solution)/shard_map/ppermute | solution.py:640
  19.5 46.3 %collective-permute-start.4 = (bf16[256,2048]{1,0:T(8,128)(2,1)}, bf16[256,2048]{1,0:T(8,128)(2,1)}, u32[]{:S(2)}, u32[]{:S(2)}) collective-permute-start(bf16[256,2048]{1,0:T(8,128)(2,1)} %get-tuple-element.212.refs_0_), channel_id=1, source_target_pairs={{0,4},{1,5},{2,6},{3,7},{4,0},{5,1},{6,2},{7,3},{8,12},{9,13},{10,... | collective-permute-start | bytes 3145736 | tf_op jit(solution)/shard_map/ppermute | solution.py:640
  19.6 24.0 %copy-start.15 = (bf16[256,2048]{1,0:T(8,128)(2,1)S(1)}, bf16[256,2048]{1,0:T(8,128)(2,1)}, u32[]{:S(2)}) copy-start(bf16[256,2048]{1,0:T(8,128)(2,1)} %get-tuple-element.213.refs_1_) | copy-start | bytes 3145732
  22.1 49.7 %copy-start.32 = (bf16[1024]{0:T(1024)(128)(2,1)S(1)}, bf16[1024]{0:T(1024)(128)(2,1)}, u32[]{:S(2)}) copy-start(bf16[1024]{0:T(1024)(128)(2,1)} %param.23) | copy-start | bytes 6148
  41.7 31.8 %copy-start.14 = (bf16[256,2048]{1,0:T(8,128)(2,1)}, bf16[256,2048]{1,0:T(8,128)(2,1)S(1)}, u32[]{:S(2)}) copy-start(bf16[256,2048]{1,0:T(8,128)(2,1)S(1)} %collective-permute-done.1.refs_7_) | copy-start | bytes 3145732
  43.7 29.8 %copy-start.16 = (bf16[256,2048]{1,0:T(8,128)(2,1)}, bf16[256,2048]{1,0:T(8,128)(2,1)S(1)}, u32[]{:S(2)}) copy-start(bf16[256,2048]{1,0:T(8,128)(2,1)S(1)} %collective-permute-done.refs_4_) | copy-start | bytes 3145732
  43.7 22.2 %collective-permute-start.5 = (bf16[256,2048]{1,0:T(8,128)(2,1)S(1)}, bf16[256,2048]{1,0:T(8,128)(2,1)}, u32[]{:S(2)}, u32[]{:S(2)}) collective-permute-start(bf16[256,2048]{1,0:T(8,128)(2,1)S(1)} %copy-done.15), channel_id=1, source_target_pairs={{0,1},{1,0},{2,3},{3,2},{4,5},{5,4},{6,7},{7,6},{8,9},{9,8},{10,11... | collective-permute-start | bytes 3145736 | tf_op jit(solution)/shard_map/ppermute | solution.py:640
  65.9 442.5 %all-gather.5.cloned.1.call-start = ((), (), s32[]{:S(2)}) async-start(), calls=%async_computation.4 | async-start | bytes 9437184 | tf_op jit(solution)/shard_map/all_gather | solution.py:805
  66.0 3.4 collective-permute-start.6
  66.0 6.5 %collective-permute-start.7 = (bf16[256,2048]{1,0:T(8,128)(2,1)}, bf16[256,2048]{1,0:T(8,128)(2,1)}, u32[]{:S(2)}, u32[]{:S(2)}) collective-permute-start(bf16[256,2048]{1,0:T(8,128)(2,1)} %collective-permute-done.3.refs_5_), channel_id=1, source_target_pairs={{0,1},{1,0},{2,3},{3,2},{4,5},{5,4},{6,7},{7,6},{8,9},{9,8},{10,11... | collective-permute-start | bytes 3145736 | tf_op jit(solution)/shard_map/ppermute | solution.py:640
  66.5 7.0 %collective-permute-start.8 = (bf16[256,2048]{1,0:T(8,128)(2,1)}, bf16[256,2048]{1,0:T(8,128)(2,1)}, u32[]{:S(2)}, u32[]{:S(2)}) collective-permute-start(bf16[256,2048]{1,0:T(8,128)(2,1)} %collective-permute-done.4.refs_6_), channel_id=1, source_target_pairs={{0,1},{1,0},{2,3},{3,2},{4,5},{5,4},{6,7},{7,6},{8,9},{9,8},{10,11... | collective-permute-start | bytes 3145736 | tf_op jit(solution)/shard_map/ppermute | solution.py:640
  66.6 6.9 %collective-permute-start.9 = (bf16[256,2048]{1,0:T(8,128)(2,1)S(1)}, bf16[256,2048]{1,0:T(8,128)(2,1)}, u32[]{:S(2)}, u32[]{:S(2)}) collective-permute-start(bf16[256,2048]{1,0:T(8,128)(2,1)S(1)} %collective-permute-done.1.refs_7_), channel_id=1, source_target_pairs={{0,1},{1,0},{2,3},{3,2},{4,5},{5,4},{6,7},{7,6},{8,9},{9,8},{10,11... | collective-permute-start | bytes 3145736 | tf_op jit(solution)/shard_map/ppermute | solution.py:640
  67.0 43.2 %collective-permute-start.10 = (bf16[256,2048]{1,0:T(8,128)(2,1)S(1)}, bf16[256,2048]{1,0:T(8,128)(2,1)S(1)}, u32[]{:S(2)}, u32[]{:S(2)}) collective-permute-start(bf16[256,2048]{1,0:T(8,128)(2,1)S(1)} %collective-permute-done.refs_4_), channel_id=1, source_target_pairs={{0,4},{1,5},{2,6},{3,7},{4,0},{5,1},{6,2},{7,3},{8,12},{9,13},{10,... | collective-permute-start | bytes 3145736 | tf_op jit(solution)/shard_map/ppermute | solution.py:640
  70.4 43.6 %collective-permute-start.11 = (bf16[256,2048]{1,0:T(8,128)(2,1)S(1)}, bf16[256,2048]{1,0:T(8,128)(2,1)}, u32[]{:S(2)}, u32[]{:S(2)}) collective-permute-start(bf16[256,2048]{1,0:T(8,128)(2,1)S(1)} %collective-permute-done.1.refs_7_), channel_id=1, source_target_pairs={{0,2},{1,3},{2,0},{3,1},{4,6},{5,7},{6,4},{7,5},{8,10},{9,11},{10,... | collective-permute-start | bytes 3145736 | tf_op jit(solution)/shard_map/ppermute | solution.py:640
  114.0 4.1 collective-permute-start.12
  114.0 4.4 collective-permute-start.13
  124.8 12.7 %copy-start.33 = (bf16[3,256]{1,0:T(4,128)(2,1)S(1)}, bf16[3,256]{1,0:T(4,128)(2,1)}, u32[]{:S(2)}) copy-start(bf16[3,256]{1,0:T(4,128)(2,1)} %param.19) | copy-start | bytes 4612
  137.2 371.2 %reduce-scatter.3.cloned.1.call-start = ((), (), s32[]{:S(2)}) async-start(), calls=%async_computation.5 | async-start | bytes 18874368 | tf_op jit(solution)/shard_map/reduce_scatter | solution.py:813
  187.8 49.7 %collective-permute-start.14 = (bf16[512,2048]{1,0:T(8,128)(2,1)}, bf16[512,2048]{1,0:T(8,128)(2,1)S(1)}, u32[]{:S(2)}, u32[]{:S(2)}) collective-permute-start(bf16[512,2048]{1,0:T(8,128)(2,1)} %weight_grad.3), channel_id=1, source_target_pairs={{0,8},{24,16},{1,9},{25,17},{2,10},{26,18},{3,11},{27,19},{4,12},{... | collective-permute-start | bytes 6291464 | tf_op jit(solution)/shard_map/ppermute | solution.py:570
  205.2 93.0 %collective-permute-start.16 = (bf16[512,2048]{1,0:T(8,128)(2,1)}, bf16[512,2048]{1,0:T(8,128)(2,1)S(1)}, u32[]{:S(2)}, u32[]{:S(2)}) collective-permute-start(bf16[512,2048]{1,0:T(8,128)(2,1)} %weight_grad.4), channel_id=1, source_target_pairs={{0,8},{24,16},{1,9},{25,17},{2,10},{26,18},{3,11},{27,19},{4,12},{... | collective-permute-start | bytes 6291464 | tf_op jit(solution)/shard_map/ppermute | solution.py:570
  206.6 32.2 %copy-start.7 = (bf16[512,2048]{1,0:T(8,128)(2,1)S(1)}, bf16[512,2048]{1,0:T(8,128)(2,1)}, u32[]{:S(2)}) copy-start(bf16[512,2048]{1,0:T(8,128)(2,1)} %weight_grad.3) | copy-start | bytes 6291460
  241.3 61.1 %collective-permute-start.15 = (bf16[512,2048]{1,0:T(8,128)(2,1)S(1)}, bf16[512,2048]{1,0:T(8,128)(2,1)}, u32[]{:S(2)}, u32[]{:S(2)}) collective-permute-start(bf16[512,2048]{1,0:T(8,128)(2,1)S(1)} %add_convert_fusion.9), channel_id=1, source_target_pairs={{8,16},{16,8},{9,17},{17,9},{10,18},{18,10},{11,19},{19,11},{12,20... | collective-permute-start | bytes 6291464 | tf_op jit(solution)/shard_map/ppermute | solution.py:570
  268.0 67.8 %collective-permute-start.17 = (bf16[1024,1024]{1,0:T(8,128)(2,1)}, bf16[1024,1024]{1,0:T(8,128)(2,1)}, u32[]{:S(2)}, u32[]{:S(2)}) collective-permute-start(bf16[1024,1024]{1,0:T(8,128)(2,1)} %get-tuple-element.279), channel_id=1, source_target_pairs={{0,8},{24,16},{1,9},{25,17},{2,10},{26,18},{3,11},{27,19},{4,12},{... | collective-permute-start | bytes 6291464 | tf_op jit(solution)/shard_map/ppermute | solution.py:570
  275.4 22.8 %copy-start.6 = (bf16[512,2048]{1,0:T(8,128)(2,1)S(1)}, bf16[512,2048]{1,0:T(8,128)(2,1)}, u32[]{:S(2)}) copy-start(bf16[512,2048]{1,0:T(8,128)(2,1)} %weight_grad.4) | copy-start | bytes 6291460
  300.4 64.4 %collective-permute-start.21 = (bf16[512,2048]{1,0:T(8,128)(2,1)}, bf16[512,2048]{1,0:T(8,128)(2,1)}, u32[]{:S(2)}, u32[]{:S(2)}) collective-permute-start(bf16[512,2048]{1,0:T(8,128)(2,1)} %add_convert_fusion.8), channel_id=1, source_target_pairs={{8,16},{16,8},{9,17},{17,9},{10,18},{18,10},{11,19},{19,11},{12,20... | collective-permute-start | bytes 6291464 | tf_op jit(solution)/shard_map/ppermute | solution.py:570
  304.8 65.9 %collective-permute-start.20 = (bf16[512,2048]{1,0:T(8,128)(2,1)S(1)}, bf16[512,2048]{1,0:T(8,128)(2,1)}, u32[]{:S(2)}, u32[]{:S(2)}) collective-permute-start(bf16[512,2048]{1,0:T(8,128)(2,1)S(1)} %add_convert_fusion.7.kept_ref), channel_id=1, source_target_pairs={{8,0},{16,24},{9,1},{17,25},{10,2},{18,26},{11,3},{19,27},{12,4},{... | collective-permute-start | bytes 6291464 | tf_op jit(solution)/shard_map/ppermute | solution.py:570
  306.2 29.7 %copy-start.11 = (bf16[1024,1024]{1,0:T(8,128)(2,1)S(1)}, bf16[1024,1024]{1,0:T(8,128)(2,1)}, u32[]{:S(2)}) copy-start(bf16[1024,1024]{1,0:T(8,128)(2,1)} %get-tuple-element.279) | copy-start | bytes 6291460
  306.2 84.0 %collective-permute-start.19 = (bf16[1024,1024]{1,0:T(8,128)(2,1)}, bf16[1024,1024]{1,0:T(8,128)(2,1)}, u32[]{:S(2)}, u32[]{:S(2)}) collective-permute-start(bf16[1024,1024]{1,0:T(8,128)(2,1)} %get-tuple-element.300), channel_id=1, source_target_pairs={{0,8},{24,16},{1,9},{25,17},{2,10},{26,18},{3,11},{27,19},{4,12},{... | collective-permute-start | bytes 6291464 | tf_op jit(solution)/shard_map/ppermute | solution.py:570
  339.9 63.5 %collective-permute-start.18 = (bf16[1024,1024]{1,0:T(8,128)(2,1)}, bf16[1024,1024]{1,0:T(8,128)(2,1)}, u32[]{:S(2)}, u32[]{:S(2)}) collective-permute-start(bf16[1024,1024]{1,0:T(8,128)(2,1)} %add_convert_fusion.6), channel_id=1, source_target_pairs={{8,16},{16,8},{9,17},{17,9},{10,18},{18,10},{11,19},{19,11},{12,20... | collective-permute-start | bytes 6291464 | tf_op jit(solution)/shard_map/ppermute | solution.py:570
  369.4 75.6 %collective-permute-start.26 = (bf16[512,2048]{1,0:T(8,128)(2,1)}, bf16[512,2048]{1,0:T(8,128)(2,1)}, u32[]{:S(2)}, u32[]{:S(2)}) collective-permute-start(bf16[512,2048]{1,0:T(8,128)(2,1)} %add_convert_fusion.5.kept_ref), channel_id=1, source_target_pairs={{8,0},{16,24},{9,1},{17,25},{10,2},{18,26},{11,3},{19,27},{12,4},{... | collective-permute-start | bytes 6291464 | tf_op jit(solution)/shard_map/ppermute | solution.py:570
  370.7 19.4 %copy-start.10 = (bf16[1024,1024]{1,0:T(8,128)(2,1)S(1)}, bf16[1024,1024]{1,0:T(8,128)(2,1)}, u32[]{:S(2)}) copy-start(bf16[1024,1024]{1,0:T(8,128)(2,1)} %get-tuple-element.300) | copy-start | bytes 6291460
  394.0 75.0 %collective-permute-start.25 = (bf16[1024,1024]{1,0:T(8,128)(2,1)}, bf16[1024,1024]{1,0:T(8,128)(2,1)}, u32[]{:S(2)}, u32[]{:S(2)}) collective-permute-start(bf16[1024,1024]{1,0:T(8,128)(2,1)} %add_convert_fusion.4), channel_id=1, source_target_pairs={{8,16},{16,8},{9,17},{17,9},{10,18},{18,10},{11,19},{19,11},{12,20... | collective-permute-start | bytes 6291464 | tf_op jit(solution)/shard_map/ppermute | solution.py:570
  396.0 77.6 %collective-permute-start.24 = (bf16[2,2048,256]{2,1,0:T(8,128)(2,1)}, bf16[2,2048,256]{2,1,0:T(8,128)(2,1)}, u32[]{:S(2)}, u32[]{:S(2)}) collective-permute-start(bf16[2,2048,256]{2,1,0:T(8,128)(2,1)} %get-tuple-element.324), channel_id=1, source_target_pairs={{0,8},{24,16},{1,9},{25,17},{2,10},{26,18},{3,11},{27,19},{4,12},{... | collective-permute-start | bytes 6291464 | tf_op jit(solution)/shard_map/ppermute | solution.py:570
  406.7 8.6 %copy-start.13 = (bf16[2048,256]{1,0:T(8,128)(2,1)S(1)}, bf16[2048,256]{1,0:T(8,128)(2,1)}, u32[]{:S(2)}) copy-start(bf16[2048,256]{1,0:T(8,128)(2,1)} %get-tuple-element.328) | copy-start | bytes 3145732
  406.7 98.5 %collective-permute-start.22 = (bf16[1024,1024]{1,0:T(8,128)(2,1)S(1)}, bf16[1024,1024]{1,0:T(8,128)(2,1)}, u32[]{:S(2)}, u32[]{:S(2)}) collective-permute-start(bf16[1024,1024]{1,0:T(8,128)(2,1)S(1)} %add_convert_fusion.3.kept_ref), channel_id=1, source_target_pairs={{8,0},{16,24},{9,1},{17,25},{10,2},{18,26},{11,3},{19,27},{12,4},{... | collective-permute-start | bytes 6291464 | tf_op jit(solution)/shard_map/ppermute | solution.py:570
  408.3 100.2 %all-to-all-start = ((bf16[8,2,256,256]{3,2,1,0:T(8,128)(2,1)}), bf16[8,2,256,256]{3,2,1,0:T(8,128)(2,1)}, u32[]{:S(2)}, u32[]{:S(2)}) async-start(bf16[8,2,256,256]{3,2,1,0:T(8,128)(2,1)} %get-tuple-element.289), calls=%async_computation | async-start | bytes 4194304 | tf_op jit(solution)/shard_map/all_to_all | solution.py:822
  412.6 182.0 %reduce-scatter.5.cloned.1.call-start = ((), (), s32[]{:S(2)}) async-start(), calls=%async_computation.6 | async-start | bytes 18874368 | tf_op jit(solution)/shard_map/reduce_scatter | solution.py:833
  415.3 85.8 %collective-permute-start.23 = (bf16[2048,256]{1,0:T(8,128)(2,1)S(1)}, bf16[2048,256]{1,0:T(8,128)(2,1)}, u32[]{:S(2)}, u32[]{:S(2)}) collective-permute-start(bf16[2048,256]{1,0:T(8,128)(2,1)S(1)} %copy-done.13), channel_id=1, source_target_pairs={{0,8},{24,16},{1,9},{25,17},{2,10},{26,18},{3,11},{27,19},{4,12},{... | collective-permute-start | bytes 3145736 | tf_op jit(solution)/shard_map/ppermute | solution.py:570
  478.3 48.5 %collective-permute-start.27 = (bf16[2,2048,256]{2,1,0:T(8,128)(2,1)}, bf16[2,2048,256]{2,1,0:T(8,128)(2,1)}, u32[]{:S(2)}, u32[]{:S(2)}) collective-permute-start(bf16[2,2048,256]{2,1,0:T(8,128)(2,1)} %add_convert_fusion.1), channel_id=1, source_target_pairs={{8,16},{16,8},{9,17},{17,9},{10,18},{18,10},{11,19},{19,11},{12,20... | collective-permute-start | bytes 6291464 | tf_op jit(solution)/shard_map/ppermute | solution.py:570
  480.3 92.0 %collective-permute-start.31 = (bf16[1024,1024]{1,0:T(8,128)(2,1)}, bf16[1024,1024]{1,0:T(8,128)(2,1)}, u32[]{:S(2)}, u32[]{:S(2)}) collective-permute-start(bf16[1024,1024]{1,0:T(8,128)(2,1)} %add_convert_fusion.2.kept_ref), channel_id=1, source_target_pairs={{8,0},{16,24},{9,1},{17,25},{10,2},{18,26},{11,3},{19,27},{12,4},{... | collective-permute-start | bytes 6291464 | tf_op jit(solution)/shard_map/ppermute | solution.py:570
  494.3 28.2 %collective-permute-start.29 = (bf16[256,2048]{1,0:T(8,128)(2,1)}, bf16[256,2048]{1,0:T(8,128)(2,1)}, u32[]{:S(2)}, u32[]{:S(2)}) collective-permute-start(bf16[256,2048]{1,0:T(8,128)(2,1)} %weight_grad.5), channel_id=1, source_target_pairs={{0,8},{24,16},{1,9},{25,17},{2,10},{26,18},{3,11},{27,19},{4,12},{... | collective-permute-start | bytes 3145736 | tf_op jit(solution)/shard_map/ppermute | solution.py:570
  503.6 30.3 %collective-permute-start.35 = (bf16[2048,256]{1,0:T(8,128)(2,1)}, bf16[2048,256]{1,0:T(8,128)(2,1)}, u32[]{:S(2)}, u32[]{:S(2)}) collective-permute-start(bf16[2048,256]{1,0:T(8,128)(2,1)} %add_convert_fusion.13), channel_id=1, source_target_pairs={{8,16},{16,8},{9,17},{17,9},{10,18},{18,10},{11,19},{19,11},{12,20... | collective-permute-start | bytes 3145736 | tf_op jit(solution)/shard_map/ppermute | solution.py:570
  508.5 10.5 %copy-start.22 = (f32[8,2048]{1,0:T(8,128)S(1)}, f32[8,2048]{1,0:T(8,128)}, u32[]{:S(2)}) copy-start(f32[8,2048]{1,0:T(8,128)} %get-tuple-element.338) | copy-start | bytes 196612
  508.5 10.5 %copy-start.23 = (f32[8,2048]{1,0:T(8,128)S(1)}, f32[8,2048]{1,0:T(8,128)}, u32[]{:S(2)}) copy-start(f32[8,2048]{1,0:T(8,128)} %get-tuple-element.339) | copy-start | bytes 196612
  508.5 11.4 %copy-start.24 = (bf16[2048]{0:T(1024)(128)(2,1)S(1)}, bf16[2048]{0:T(1024)(128)(2,1)}, u32[]{:S(2)}) copy-start(bf16[2048]{0:T(1024)(128)(2,1)} %param.16) | copy-start | bytes 12292
  508.5 14.0 %copy-start.9 = (bf16[256,2048]{1,0:T(8,128)(2,1)S(1)}, bf16[256,2048]{1,0:T(8,128)(2,1)}, u32[]{:S(2)}) copy-start(bf16[256,2048]{1,0:T(8,128)(2,1)} %weight_grad.5) | copy-start | bytes 3145732
  520.0 5.1 collective-permute-start.28
  524.1 42.8 %collective-permute-start.37 = (bf16[256,2048]{1,0:T(8,128)(2,1)S(1)}, bf16[256,2048]{1,0:T(8,128)(2,1)S(1)}, u32[]{:S(2)}, u32[]{:S(2)}) collective-permute-start(bf16[256,2048]{1,0:T(8,128)(2,1)S(1)} %add_convert_fusion.12), channel_id=1, source_target_pairs={{8,16},{16,8},{9,17},{17,9},{10,18},{18,10},{11,19},{19,11},{12,20... | collective-permute-start | bytes 3145736 | tf_op jit(solution)/shard_map/ppermute | solution.py:570
  525.1 4.4 collective-permute-start.32
  529.5 28.8 %copy-start.3 = (bf16[2,2048,256]{2,1,0:T(8,128)(2,1)}, bf16[2,2048,256]{2,1,0:T(8,128)(2,1)S(1)}, u32[]{:S(2)}) copy-start(bf16[2,2048,256]{2,1,0:T(8,128)(2,1)S(1)} %add_convert_fusion) | copy-start | bytes 6291460
  529.6 4.3 collective-permute-start.33
  531.1 56.8 %collective-permute-start.30 = (bf16[2,2048,256]{2,1,0:T(8,128)(2,1)S(1)}, bf16[2,2048,256]{2,1,0:T(8,128)(2,1)}, u32[]{:S(2)}, u32[]{:S(2)}) collective-permute-start(bf16[2,2048,256]{2,1,0:T(8,128)(2,1)S(1)} %add_convert_fusion), channel_id=1, source_target_pairs={{8,0},{16,24},{9,1},{17,25},{10,2},{18,26},{11,3},{19,27},{12,4},{... | collective-permute-start | bytes 6291464 | tf_op jit(solution)/shard_map/ppermute | solution.py:570
  533.8 19.2 %collective-permute-start.34 = (f32[49,128]{1,0:T(8,128)S(1)}, f32[49,128]{1,0:T(8,128)S(1)}, u32[]{:S(2)}, u32[]{:S(2)}) collective-permute-start(f32[49,128]{1,0:T(8,128)S(1)} %pad_maximum_fusion), channel_id=1, source_target_pairs={{0,8},{24,16},{1,9},{25,17},{2,10},{26,18},{3,11},{27,19},{4,12},{... | collective-permute-start | bytes 75272 | tf_op jit(solution)/shard_map/ppermute | solution.py:570
  553.0 16.6 %copy-start.8 = (bf16[2048,256]{1,0:T(8,128)(2,1)}, bf16[2048,256]{1,0:T(8,128)(2,1)S(1)}, u32[]{:S(2)}) copy-start(bf16[2048,256]{1,0:T(8,128)(2,1)S(1)} %add_convert_fusion.11.kept_ref) | copy-start | bytes 3145732
  553.0 15.3 %collective-permute-start.36 = (f32[49,128]{1,0:T(8,128)S(1)}, f32[49,128]{1,0:T(8,128)S(1)}, u32[]{:S(2)}, u32[]{:S(2)}) collective-permute-start(f32[49,128]{1,0:T(8,128)S(1)} %add.146), channel_id=1, source_target_pairs={{8,16},{16,8},{9,17},{17,9},{10,18},{18,10},{11,19},{19,11},{12,20... | collective-permute-start | bytes 75272 | tf_op jit(solution)/shard_map/ppermute | solution.py:570
  568.3 16.6 %collective-permute-start.38 = (f32[49,128]{1,0:T(8,128)S(1)}, f32[49,128]{1,0:T(8,128)S(1)}, u32[]{:S(2)}, u32[]{:S(2)}) collective-permute-start(f32[49,128]{1,0:T(8,128)S(1)} %add.148), channel_id=1, source_target_pairs={{8,0},{16,24},{9,1},{17,25},{10,2},{18,26},{11,3},{19,27},{12,4},{... | collective-permute-start | bytes 75272 | tf_op jit(solution)/shard_map/ppermute | solution.py:570
  569.6 37.8 %collective-permute-start.39 = (bf16[2048,256]{1,0:T(8,128)(2,1)S(1)}, bf16[2048,256]{1,0:T(8,128)(2,1)}, u32[]{:S(2)}, u32[]{:S(2)}) collective-permute-start(bf16[2048,256]{1,0:T(8,128)(2,1)S(1)} %add_convert_fusion.11.kept_ref), channel_id=1, source_target_pairs={{8,0},{16,24},{9,1},{17,25},{10,2},{18,26},{11,3},{19,27},{12,4},{... | collective-permute-start | bytes 3145736 | tf_op jit(solution)/shard_map/ppermute | solution.py:570
  570.9 56.0 %collective-permute-start.40 = (bf16[256,2048]{1,0:T(8,128)(2,1)}, bf16[256,2048]{1,0:T(8,128)(2,1)}, u32[]{:S(2)}, u32[]{:S(2)}) collective-permute-start(bf16[256,2048]{1,0:T(8,128)(2,1)} %add_convert_fusion.10.kept_ref), channel_id=1, source_target_pairs={{8,0},{16,24},{9,1},{17,25},{10,2},{18,26},{11,3},{19,27},{12,4},{... | collective-permute-start | bytes 3145736 | tf_op jit(solution)/shard_map/ppermute | solution.py:570
  584.9 45.0 %copy-start.31 = (f32[256]{0:T(256)}, f32[256]{0:T(256)S(1)}, u32[]{:S(2)}) copy-start(f32[256]{0:T(256)S(1)} %slice_bitcast_fusion.3) | copy-start | bytes 3076
  (16 other events, 57.1 us)
Sparse Core Ops, SparseCore 0:
  66.0 107.4 all-gather.2
  175.5 54.3 all-gather.4
  306.2 122.3 reduce-scatter.2
  469.2 116.9 reduce-scatter.4

commit v6 on v5

--- a/solution.py
+++ b/solution.py
@@ -15,7 +15,7 @@
 f32 = jnp.float32
 bf16 = jnp.bfloat16
 VMEM_LIMIT = 56 << 20
-ORDER_WEIGHT = int(2.1e11)
+ORDER_WEIGHT = int(2.15e11)
 EARLY_WEIGHT = int(2.2e11)
 
 
@@ -603,7 +603,7 @@
         o_ref[...] = came_ref[...].astype(f32)
 
 
-def finish(total, order, high, first=0, before=None, tile=512):
+def finish(total, order, high, first=0, before=None, tile=512, weight=1):
     flat = lambda a: a.reshape(-1, a.shape[-1])
     rows, cols = flat(total.part).shape
     if not line_ok(total.size):
@@ -623,7 +623,7 @@
         out_shape=jax.ShapeDtypeStruct((high, cols), f32),
         input_output_aliases={3: 0} if held else {},
         compiler_params=params(),
-        cost_estimate=SMALL,
+        cost_estimate=pl.CostEstimate(flops=int(weight), bytes_accessed=1, transcendentals=0),
         name="finish",
     )
     return order(lambda *a: call(inner, *a), flat(total.part), flat(total.came), *held)
@@ -829,12 +829,12 @@
     i0.fold(order)
     part, bias_a, norm_a = order(back(0), hidden_grad, dqkv, inward_weight, w3, normed)
     o1.settle(order)
+    i1.fold(order)
+    qs.fold(order)
     part, bias_b, norm_b = order(back(1), hidden_grad, dqkv, inward_weight, w3, normed, part)
     back_tok = lax.psum_scatter(part.reshape(seqs, length, width), "tp", scatter_dimension=1, tiled=True)
-    i1.fold(order)
-    qs.fold(order)
+    vs.fold(order)
     (ds,) = row_sum([order(weight_grad, attended, grad)])
-    vs.fold(order)
     i0.settle(order)
 
     cols = width // tp
@@ -846,7 +846,7 @@
     out_bias = order(column_sums, grad)
     rows_of = lambda a: a.reshape(seqs * here, width)
     bias_rows = (b_dense.astype(f32)[None], b_out.astype(f32)[None])
-    own = lambda x, w, t, *m: project_own(x, w, *bias_rows, rows_of(t), m, weight=ORDER_WEIGHT)
+    own = lambda x, w, t, *m: project_own(x, w, *bias_rows, rows_of(t), m)
     layer_out, squares = order(own, mine, dense_full, tokens, mlp_tok)
     layer_out = layer_out.reshape(tokens.shape)
 
@@ -856,6 +856,7 @@
         pad = jnp.zeros((124,), f32)
         return jnp.concatenate([norm_sums[0] / gain, norm_sums[1], squares, pad]).reshape(-1, 128)
 
+    i1.settle(order)
     packed = TpSum(order(pack, norm_a, norm_b, squares), tp)
     ds.fold(order)
     packed.fold(order)
@@ -866,10 +867,10 @@
     small = RowSum(jnp.concatenate([packed.result(order), small]), rows)
     vs.fold(order)
     small.fold(order)
-    out_grad = finish(o0, order, units)
+    ds.fold(order)
+    out_grad = finish(o0, order, units, weight=ORDER_WEIGHT)
     out_grad = finish(o1, order, units, units // 2, out_grad)
     in_grad = finish(i0, order, width)
-    ds.fold(order)
     small.fold(order)
     in_grad = finish(i1, order, width, width // 2, in_grad)
     qkv_grad = finish(qs, order, 3 * width)

time: 647 us -> 645 us (level)
  waiting for transfers between devices: 95.8 us -> 104 us
  transfers between devices with their start and end apart: 46 -> 46, of which waited for: 15 -> 16; matrix products, arithmetic and copies ran while one was open for 10% -> 9% of each run, Pallas kernels for 55% -> 55%
where the time goes in v6:
time: 645 us; the launch traced here: 636 us
  Pallas kernels  356 us (55%)
  waiting for transfers between devices  104 us (16%)
  starting transfers between devices  94.2 us (15%)
  other arithmetic  57.4 us (9%)
  between operations  14.8 us (2%)
  local copies, waits for them, and re-layouts  9.65 us (1%)
    ppermute x24, starting transfers between devices, send(): self.came = lax.ppermute(self.part, self.axis, self.hops.pop(0))  77.5 us
    pallas_call x2, Pallas kernels, normed_grad(): pl.pallas_call(functools.partial(normed_grad_kernel, held=held), grid=(st...  45.7 us
    pallas_call x2, Pallas kernels, attention_both(): pl.pallas_call(functools.partial(attention_kernel, bq=bq, held=held), gri...  44.4 us
    ppermute x14, waiting for transfers between devices, send(): return lax.ppermute(a, 'tp', [(i, i ^ step) for i in range(self.size)])  44 us
    convert_element_type x14, other arithmetic, fold(): add = lambda a, b: (a.astype(f32) + b.astype(f32)).astype(a.dtype)  39.8 us
    pallas_call x3, Pallas kernels, weight_grad(): pl.pallas_call(weight_grad_kernel, grid=(cols // tile,), in_specs=[pl.Blo...  39.5 us
    ppermute x24, waiting for transfers between devices, send(): self.came = lax.ppermute(self.part, self.axis, self.hops.pop(0))  37.4 us
    pallas_call x2, Pallas kernels, mlp_hidden_of(): pl.pallas_call(functools.partial(chosen_kernel, held=held), grid_spec=plt...  36 us
  transfers between devices with their start and end apart: 46, of which 16 were waited for; matrix products, arithmetic and copies ran while one was open for 9% of the time, Pallas kernels for 55%

profile of v6, /device:TPU:0, one launch (start us, length us, event | category | flops | bytes accessed | tf_op | source)
XLA Modules:
  0.0 635.5 jit_solution(13495071293361887052)
XLA Ops:
  9.8 4.7 norm_halves.1
  14.6 3.0 collective-permute-start.1
  19.7 2.0 copy.39
  22.2 9.8 %rope_tables.1 = (f32[4096,128]{1,0:T(8,128)}, f32[4096,128]{1,0:T(8,128)}) custom-call(s32[4096,1]{1,0:T(8,128)} %bitcast.67, f32[1,128]{1,0:T(1,128)} %fusion.15.frequency_ref), custom_call_target="tpu_custom_call" | custom-call | flops 1 | bytes 1 | tf_op jit(solution)/shard_map/rope_tables/pallas_call | solution.py:99
  32.6 9.1 %collective-permute-done.1.refs_7_ = bf16[256,2048]{1,0:T(8,128)(2,1)S(1)} collective-permute-done((bf16[256,2048]{1,0:T(8,128)(2,1)}, bf16[256,2048]{1,0:T(8,128)(2,1)S(1)}, u32[]{:S(2)}, u32[]{:S(2)}) %collective-permute-start.1) | collective-permute-done | bytes 1048608 | tf_op jit(solution)/shard_map/ppermute | solution.py:640
  41.7 2.0 collective-permute-done.refs_4_
  43.7 22.2 %collective-permute-done.3.refs_5_ = bf16[256,2048]{1,0:T(8,128)(2,1)} collective-permute-done((bf16[256,2048]{1,0:T(8,128)(2,1)}, bf16[256,2048]{1,0:T(8,128)(2,1)}, u32[]{:S(2)}, u32[]{:S(2)}) %collective-permute-start.3) | collective-permute-done | bytes 1048608 | tf_op jit(solution)/shard_map/ppermute | solution.py:640
  67.3 2.1 collective-permute-done.6.refs_8_
  73.5 13.1 %place_pieces.2.refs_0_ = bf16[2,8,256,2048]{3,2,1,0:T(8,128)(2,1)} custom-call(s32[1]{0:T(128)} %bitcast.3.me_ref, bf16[256,2048]{1,0:T(8,128)(2,1)} %get-tuple-element.213.refs_0_, bf16[256,2048]{1,0:T(8,128)(2,1)} %get-tuple-element.214.refs_1_, bf16[256,2048]{1,0:T(8,128)(2,1)} %collective-permute-done.2.refs_2_, ...), custom_call_target="tpu_custom_call" | custom-call | flops 1 | bytes 1 | tf_op jit(solution)/shard_map/place_pieces/pallas_call | solution.py:701
  86.6 23.6 %mlp_hidden_of.2 = (bf16[2,8,256,1024]{3,2,1,0:T(8,128)(2,1)}, bf16[2,8,256,1024]{3,2,1,0:T(8,128)(2,1)}) custom-call(s32[1]{0:T(128)} %bitcast.3.me_ref, bf16[2,8,256,2048]{3,2,1,0:T(8,128)(2,1)} %place_pieces.2.refs_0_, bf16[2048,1024]{1,0:T(8,128)(2,1)} %refs_3_.1, f32[1,1024]{1,0:T(1,128)} %bitcast.78), custom_call_target="tpu_custom_call" | custom-call | flops 1 | bytes 1 | tf_op jit(solution)/shard_map/mlp_hidden_of/pallas_call | solution.py:180
  110.3 3.7 collective-permute-done.11.refs_2_
  114.5 3.6 collective-permute-done.12.refs_3_
  120.1 4.7 place_pieces.3.refs_2_
  124.9 12.4 %mlp_hidden_of.3 = (bf16[2,8,256,1024]{3,2,1,0:T(8,128)(2,1)}, bf16[2,8,256,1024]{3,2,1,0:T(8,128)(2,1)}) custom-call(s32[1]{0:T(128)} %bitcast.3.me_ref, bf16[2,8,256,1024]{3,2,1,0:T(8,128)(2,1)} %get-tuple-element.237.refs_0_, bf16[2,8,256,1024]{3,2,1,0:T(8,128)(2,1)} %get-tuple-element.238.refs_1_, ...), custom_call_target="tpu_custom_call", output_to_operand_aliasing={{0}: (1, {}), {1}: (2, {})} | custom-call | flops 1 | bytes 1 | tf_op jit(solution)/shard_map/mlp_hidden_of/pallas_call | solution.py:180
  138.1 20.0 %qkv_rope.1.refs_1_.refs_2_.refs_3_.refs_4_.refs_5_.refs_6_ = bf16[3,4096,256]{2,1,0:T(8,128)(2,1)} custom-call(bf16[4096,2048]{1,0:T(8,128)(2,1)} %bitcast.45, bf16[3,2048,256]{2,1,0:T(8,128)(2,1)} %bitcast.63, f32[3,256]{1,0:T(4,128)} %convert_element_type.170.b_ref, f32[4096,128]{1,0:T(8,128)} %get-tuple-element.288.c_ref.refs_5_.refs_8_, ...), custom_call_target="tpu_custom_call" | custom-call | flops 1 | bytes 1 | tf_op jit(solution)/shard_map/qkv_rope/pallas_call | solution.py:131
  158.1 15.4 %all-gather.3.cloned.1.call-done = bf16[2,2048,2048]{2,1,0:T(8,128)(2,1)} async-done(((bf16[2,256,2048]{2,1,0:T(8,128)(2,1)}), bf16[2,2048,2048]{2,1,0:T(8,128)(2,1)}) %all-gather.3.cloned.1.call-update) | async-done | bytes 16777232 | tf_op jit(solution)/shard_map/all_gather | solution.py:784
  173.6 14.2 %weight_grad.3 = bf16[512,2048]{1,0:T(8,128)(2,1)} custom-call(bf16[4096,1024]{1,0:T(8,128)(2,1)} %bitcast.55, bf16[4096,2048]{1,0:T(8,128)(2,1)} %bitcast.50), custom_call_target="tpu_custom_call" | custom-call | flops 1 | bytes 1 | tf_op jit(solution)/shard_map/weight_grad/pallas_call | solution.py:279
  187.8 3.5 collective-permute-start.14
  191.3 13.8 %weight_grad.4 = bf16[512,2048]{1,0:T(8,128)(2,1)} custom-call(bf16[4096,1024]{1,0:T(8,128)(2,1)} %bitcast.56, bf16[4096,2048]{1,0:T(8,128)(2,1)} %bitcast.51), custom_call_target="tpu_custom_call" | custom-call | flops 1 | bytes 1 | tf_op jit(solution)/shard_map/weight_grad/pallas_call | solution.py:279
  205.1 2.6 collective-permute-start.16
  207.8 29.6 %grad_in.1 = (bf16[4096,1024]{1,0:T(8,128)(2,1)}, bf16[4096,256]{1,0:T(8,128)(2,1)}, f32[8,1024]{1,0:T(8,128)}) custom-call(bf16[4096,2048]{1,0:T(8,128)(2,1)} %bitcast.52, bf16[1024,2048]{1,0:T(8,128)(2,1)} %w_ref, bf16[256,2048]{1,0:T(8,128)(2,1)} %wd_ref, bf16[4096,1024]{1,0:T(8,128)(2,1)} %bitcast.62), custom_call_target="tpu_custom_call" | custom-call | flops 1 | bytes 1 | tf_op jit(solution)/shard_map/grad_in/pallas_call | solution.py:221
  238.4 2.0 collective-permute-start.15
  240.4 24.6 %weight_grad_rows.1 = (bf16[1024,1024]{1,0:T(8,128)(2,1)}, bf16[1024,1024]{1,0:T(8,128)(2,1)}) custom-call(bf16[4096,2048]{1,0:T(8,128)(2,1)} %bitcast.46, bf16[4096,1024]{1,0:T(8,128)(2,1)} %get-tuple-element.319.b_ref.refs_0_.refs_1_), custom_call_target="tpu_custom_call" | custom-call | flops 1 | bytes 1 | tf_op jit(solution)/shard_map/weight_grad_rows/pallas_call | solution.py:313
  265.0 7.4 %collective-permute-start.17 = (bf16[1024,1024]{1,0:T(8,128)(2,1)}, bf16[1024,1024]{1,0:T(8,128)(2,1)}, u32[]{:S(2)}, u32[]{:S(2)}) collective-permute-start(bf16[1024,1024]{1,0:T(8,128)(2,1)} %get-tuple-element.280), channel_id=1, source_target_pairs={{0,8},{24,16},{1,9},{25,17},{2,10},{26,18},{3,11},{27,19},{4,12},{... | collective-permute-start | bytes 6291464 | tf_op jit(solution)/shard_map/ppermute | solution.py:570
  272.4 22.8 %tokens_by_weight.1 = bf16[4096,2048]{1,0:T(8,128)(2,1)} custom-call(bf16[4096,1024]{1,0:T(8,128)(2,1)} %bitcast.57, bf16[1024,2048]{1,0:T(8,128)(2,1)} %w_ref), custom_call_target="tpu_custom_call" | custom-call | flops 1 | bytes 1 | tf_op jit(solution)/shard_map/tokens_by_weight/pallas_call | solution.py:258
  295.2 2.4 add_convert_fusion.8
  297.6 2.1 collective-permute-start.21
  299.6 3.9 add_convert_fusion.7.kept_ref
  304.8 7.4 %collective-permute-start.19 = (bf16[1024,1024]{1,0:T(8,128)(2,1)}, bf16[1024,1024]{1,0:T(8,128)(2,1)}, u32[]{:S(2)}, u32[]{:S(2)}) collective-permute-start(bf16[1024,1024]{1,0:T(8,128)(2,1)} %get-tuple-element.301), channel_id=1, source_target_pairs={{0,8},{24,16},{1,9},{25,17},{2,10},{26,18},{3,11},{27,19},{4,12},{... | collective-permute-start | bytes 6291464 | tf_op jit(solution)/shard_map/ppermute | solution.py:570
  312.2 22.2 %attention_both.2 = (bf16[4096,256]{1,0:T(8,128)(2,1)}, bf16[8,2,256,256]{3,2,1,0:T(8,128)(2,1)}, bf16[3,4096,256]{2,1,0:T(8,128)(2,1)}) custom-call(s32[1,4096]{1,0:T(1,128)} %fusion.11.refs_0_.refs_3_, bf16[3,4096,256]{2,1,0:T(8,128)(2,1)} %qkv_rope.1.refs_1_.refs_2_.refs_3_.refs_4_.refs_5_.refs_6_, ...), custom_call_target="tpu_custom_call" | custom-call | flops 1 | bytes 1 | tf_op jit(solution)/shard_map/attention_both/pallas_call | solution.py:476
  334.4 4.4 add_convert_fusion.6
  338.8 2.1 collective-permute-start.18
  340.9 22.1 %attention_both.3 = (bf16[4096,256]{1,0:T(8,128)(2,1)}, bf16[8,2,256,256]{3,2,1,0:T(8,128)(2,1)}, bf16[3,4096,256]{2,1,0:T(8,128)(2,1)}) custom-call(bf16[4096,256]{1,0:T(8,128)(2,1)} %get-tuple-element.282.refs_0_, bf16[8,2,256,256]{3,2,1,0:T(8,128)(2,1)} %get-tuple-element.283.refs_1_, ...), custom_call_target="tpu_custom_call", output_to_operand_aliasing={{0}: (0, {}), {1}: (1, {}), {2}: (2, {})} | custom-call | flops 1 | bytes 1 | tf_op jit(solution)/shard_map/attention_both/pallas_call | solution.py:476
  363.1 3.8 add_convert_fusion.5.kept_ref
  368.2 19.2 %weight_grad_parts.1 = (bf16[2,2048,256]{2,1,0:T(8,128)(2,1)}, bf16[2048,256]{1,0:T(8,128)(2,1)}) custom-call(bf16[4096,2048]{1,0:T(8,128)(2,1)} %bitcast.47, bf16[3,4096,256]{2,1,0:T(8,128)(2,1)} %get-tuple-element.320.b_ref.refs_1_.refs_2_), custom_call_target="tpu_custom_call" | custom-call | flops 219999993856 | bytes 1 | tf_op jit(solution)/shard_map/weight_grad_parts/pallas_call | solution.py:337
  387.4 3.2 add_convert_fusion.4
  391.4 9.0 %collective-permute-start.24 = (bf16[2,2048,256]{2,1,0:T(8,128)(2,1)}, bf16[2,2048,256]{2,1,0:T(8,128)(2,1)}, u32[]{:S(2)}, u32[]{:S(2)}) collective-permute-start(bf16[2,2048,256]{2,1,0:T(8,128)(2,1)} %get-tuple-element.316), channel_id=1, source_target_pairs={{0,8},{24,16},{1,9},{25,17},{2,10},{26,18},{3,11},{27,19},{4,12},{... | collective-permute-start | bytes 6291464 | tf_op jit(solution)/shard_map/ppermute | solution.py:570
  400.3 4.6 add_convert_fusion.3.kept_ref
  406.4 23.1 %normed_grad.2 = (bf16[4096,2048]{1,0:T(8,128)(2,1)}, f32[3,8,256]{2,1,0:T(8,128)}, f32[8,2048]{1,0:T(8,128)}) custom-call(bf16[4096,1024]{1,0:T(8,128)(2,1)} %get-tuple-element.319.b_ref.refs_0_.refs_1_, bf16[3,4096,256]{2,1,0:T(8,128)(2,1)} %get-tuple-element.320.b_ref.refs_1_.refs_2_, bf16[2048,1024]{1,0:T(8,128)(2,1)} %refs_3_.1, ...), custom_call_target="tpu_custom_call" | custom-call | flops 1 | bytes 1 | tf_op jit(solution)/shard_map/normed_grad/pallas_call | solution.py:381
  431.8 16.1 %collective-permute-start.23 = (bf16[2048,256]{1,0:T(8,128)(2,1)S(1)}, bf16[2048,256]{1,0:T(8,128)(2,1)}, u32[]{:S(2)}, u32[]{:S(2)}) collective-permute-start(bf16[2048,256]{1,0:T(8,128)(2,1)S(1)} %copy-done.11), channel_id=1, source_target_pairs={{0,8},{24,16},{1,9},{25,17},{2,10},{26,18},{3,11},{27,19},{4,12},{... | collective-permute-start | bytes 3145736 | tf_op jit(solution)/shard_map/ppermute | solution.py:570
  447.9 4.4 all-to-all-start
  452.3 4.1 add_convert_fusion.1
  456.4 2.0 collective-permute-start.27
  458.4 22.6 %normed_grad.3 = (bf16[4096,2048]{1,0:T(8,128)(2,1)}, f32[3,8,256]{2,1,0:T(8,128)}, f32[8,2048]{1,0:T(8,128)}) custom-call(bf16[4096,2048]{1,0:T(8,128)(2,1)} %get-tuple-element.318.refs_0_, bf16[4096,1024]{1,0:T(8,128)(2,1)} %get-tuple-element.319.b_ref.refs_0_.refs_1_, ...), custom_call_target="tpu_custom_call", output_to_operand_aliasing={{0}: (0, {})} | custom-call | flops 1 | bytes 1 | tf_op jit(solution)/shard_map/normed_grad/pallas_call | solution.py:381
  482.8 11.5 %weight_grad.5 = bf16[256,2048]{1,0:T(8,128)(2,1)} custom-call(bf16[4096,256]{1,0:T(8,128)(2,1)} %get-tuple-element.329.a_ref, bf16[4096,2048]{1,0:T(8,128)(2,1)} %bitcast.53), custom_call_target="tpu_custom_call" | custom-call | flops 1 | bytes 1 | tf_op jit(solution)/shard_map/weight_grad/pallas_call | solution.py:279
  494.3 2.3 collective-permute-start.30
  501.3 2.5 convert_reduce_fusion.1
  503.9 11.2 %project_own.1 = (bf16[512,2048]{1,0:T(8,128)(2,1)}, f32[8,512]{1,0:T(8,128)}) custom-call(bf16[8,2,256,256]{3,2,1,0:T(8,128)(2,1)} %all-to-all-done.x_ref, bf16[2048,2048]{1,0:T(8,128)(2,1)} %all-gather.5.cloned.1.call-done.w_ref, f32[1,2048]{1,0:T(1,128)} %bitcast.80, f32[1,2048]{1,0:T(1,128)} %bitcast.81, bf16[512,2048]{1,0:T(8,128)(2,1)} %bitcast.59, ...), custom_call_target="tpu_custom_call" | custom-call | flops 1 | bytes 1 | tf_op jit(solution)/shard_map/project_own/pallas_call | solution.py:532
  516.4 2.7 collective-permute-done.30
  519.1 1.9 add_convert_fusion.12
  523.5 4.1 add_convert_fusion
  531.9 5.9 collective-permute-start.35
  537.9 2.5 add_convert_fusion.11.kept_ref
  543.6 4.5 finish.7.refs_0_
  548.1 4.8 finish.8
  552.8 3.9 finish.9.refs_0_
  561.4 3.7 finish.10
  565.2 16.6 %collective-permute-done.38 = f32[49,128]{1,0:T(8,128)S(1)} collective-permute-done((f32[49,128]{1,0:T(8,128)S(1)}, f32[49,128]{1,0:T(8,128)S(1)}, u32[]{:S(2)}, u32[]{:S(2)}) %collective-permute-start.38) | collective-permute-done | bytes 25120 | tf_op jit(solution)/shard_map/ppermute | solution.py:570
  584.8 6.7 %finish.11.refs_0_ = f32[6144,256]{1,0:T(8,128)} custom-call(s32[1]{0:T(128)} %bitcast.17.inner_ref, bf16[4096,256]{1,0:T(8,128)(2,1)} %bitcast.21.kept_ref, bf16[4096,256]{1,0:T(8,128)(2,1)} %bitcast.22.came_ref), custom_call_target="tpu_custom_call" | custom-call | flops 1 | bytes 1 | tf_op jit(solution)/shard_map/finish/pallas_call | solution.py:629
  591.5 5.4 reduce-scatter.5.cloned.1.call-done
  600.2 3.2 fusion.8
  604.3 3.8 finish.12
  608.1 16.9 %collective-permute-done.40.came_ref = bf16[256,2048]{1,0:T(8,128)(2,1)} collective-permute-done((bf16[256,2048]{1,0:T(8,128)(2,1)}, bf16[256,2048]{1,0:T(8,128)(2,1)}, u32[]{:S(2)}, u32[]{:S(2)}) %collective-permute-start.40) | collective-permute-done | bytes 1048608 | tf_op jit(solution)/shard_map/ppermute | solution.py:570
  625.0 3.0 finish.13
  (168 shorter events, 53.1 us)
Async XLA Ops:
  7.2 12.4 %copy-start.20 = (s32[2,2048]{1,0:T(2,128)S(1)}, s32[2,2048]{1,0:T(2,128)}, u32[]{:S(2)}) copy-start(s32[2,2048]{1,0:T(2,128)} %param.15) | copy-start | bytes 49156
  7.2 166.4 %all-gather.3.cloned.1.call-start = ((), (), s32[]{:S(2)}) async-start(), calls=%async_computation.3 | async-start | bytes 18874368 | tf_op jit(solution)/shard_map/all_gather | solution.py:784
  14.6 27.2 %collective-permute-start.1 = (bf16[256,2048]{1,0:T(8,128)(2,1)}, bf16[256,2048]{1,0:T(8,128)(2,1)S(1)}, u32[]{:S(2)}, u32[]{:S(2)}) collective-permute-start(bf16[256,2048]{1,0:T(8,128)(2,1)} %get-tuple-element.214.refs_1_), channel_id=1, source_target_pairs={{0,4},{1,5},{2,6},{3,7},{4,0},{5,1},{6,2},{7,3},{8,12},{9,13},{10,... | collective-permute-start | bytes 3145736 | tf_op jit(solution)/shard_map/ppermute | solution.py:640
  17.5 24.2 %collective-permute-start.2 = (bf16[256,2048]{1,0:T(8,128)(2,1)}, bf16[256,2048]{1,0:T(8,128)(2,1)}, u32[]{:S(2)}, u32[]{:S(2)}) collective-permute-start(bf16[256,2048]{1,0:T(8,128)(2,1)} %get-tuple-element.213.refs_0_), channel_id=1, source_target_pairs={{0,1},{1,0},{2,3},{3,2},{4,5},{5,4},{6,7},{7,6},{8,9},{9,8},{10,11... | collective-permute-start | bytes 3145736 | tf_op jit(solution)/shard_map/ppermute | solution.py:640
  17.5 26.2 %collective-permute-start = (bf16[256,2048]{1,0:T(8,128)(2,1)}, bf16[256,2048]{1,0:T(8,128)(2,1)S(1)}, u32[]{:S(2)}, u32[]{:S(2)}) collective-permute-start(bf16[256,2048]{1,0:T(8,128)(2,1)} %get-tuple-element.213.refs_0_), channel_id=1, source_target_pairs={{0,2},{1,3},{2,0},{3,1},{4,6},{5,7},{6,4},{7,5},{8,10},{9,11},{10,... | collective-permute-start | bytes 3145736 | tf_op jit(solution)/shard_map/ppermute | solution.py:640
  19.0 46.9 %collective-permute-start.3 = (bf16[256,2048]{1,0:T(8,128)(2,1)}, bf16[256,2048]{1,0:T(8,128)(2,1)}, u32[]{:S(2)}, u32[]{:S(2)}) collective-permute-start(bf16[256,2048]{1,0:T(8,128)(2,1)} %get-tuple-element.214.refs_1_), channel_id=1, source_target_pairs={{0,2},{1,3},{2,0},{3,1},{4,6},{5,7},{6,4},{7,5},{8,10},{9,11},{10,... | collective-permute-start | bytes 3145736 | tf_op jit(solution)/shard_map/ppermute | solution.py:640
  19.5 46.3 %collective-permute-start.4 = (bf16[256,2048]{1,0:T(8,128)(2,1)}, bf16[256,2048]{1,0:T(8,128)(2,1)}, u32[]{:S(2)}, u32[]{:S(2)}) collective-permute-start(bf16[256,2048]{1,0:T(8,128)(2,1)} %get-tuple-element.213.refs_0_), channel_id=1, source_target_pairs={{0,4},{1,5},{2,6},{3,7},{4,0},{5,1},{6,2},{7,3},{8,12},{9,13},{10,... | collective-permute-start | bytes 3145736 | tf_op jit(solution)/shard_map/ppermute | solution.py:640
  19.6 24.0 %copy-start.9 = (bf16[256,2048]{1,0:T(8,128)(2,1)S(1)}, bf16[256,2048]{1,0:T(8,128)(2,1)}, u32[]{:S(2)}) copy-start(bf16[256,2048]{1,0:T(8,128)(2,1)} %get-tuple-element.214.refs_1_) | copy-start | bytes 3145732
  22.2 49.7 %copy-start.24 = (bf16[1024]{0:T(1024)(128)(2,1)S(1)}, bf16[1024]{0:T(1024)(128)(2,1)}, u32[]{:S(2)}) copy-start(bf16[1024]{0:T(1024)(128)(2,1)} %param.23) | copy-start | bytes 6148
  41.7 31.8 %copy-start.8 = (bf16[256,2048]{1,0:T(8,128)(2,1)}, bf16[256,2048]{1,0:T(8,128)(2,1)S(1)}, u32[]{:S(2)}) copy-start(bf16[256,2048]{1,0:T(8,128)(2,1)S(1)} %collective-permute-done.1.refs_7_) | copy-start | bytes 3145732
  43.7 29.8 %copy-start.10 = (bf16[256,2048]{1,0:T(8,128)(2,1)}, bf16[256,2048]{1,0:T(8,128)(2,1)S(1)}, u32[]{:S(2)}) copy-start(bf16[256,2048]{1,0:T(8,128)(2,1)S(1)} %collective-permute-done.refs_4_) | copy-start | bytes 3145732
  43.7 22.2 %collective-permute-start.5 = (bf16[256,2048]{1,0:T(8,128)(2,1)S(1)}, bf16[256,2048]{1,0:T(8,128)(2,1)}, u32[]{:S(2)}, u32[]{:S(2)}) collective-permute-start(bf16[256,2048]{1,0:T(8,128)(2,1)S(1)} %copy-done.9), channel_id=1, source_target_pairs={{0,1},{1,0},{2,3},{3,2},{4,5},{5,4},{6,7},{7,6},{8,9},{9,8},{10,11... | collective-permute-start | bytes 3145736 | tf_op jit(solution)/shard_map/ppermute | solution.py:640
  65.9 437.9 %all-gather.5.cloned.1.call-start = ((), (), s32[]{:S(2)}) async-start(), calls=%async_computation.4 | async-start | bytes 9437184 | tf_op jit(solution)/shard_map/all_gather | solution.py:805
  66.0 3.4 collective-permute-start.6
  66.0 6.4 %collective-permute-start.7 = (bf16[256,2048]{1,0:T(8,128)(2,1)}, bf16[256,2048]{1,0:T(8,128)(2,1)}, u32[]{:S(2)}, u32[]{:S(2)}) collective-permute-start(bf16[256,2048]{1,0:T(8,128)(2,1)} %collective-permute-done.3.refs_5_), channel_id=1, source_target_pairs={{0,1},{1,0},{2,3},{3,2},{4,5},{5,4},{6,7},{7,6},{8,9},{9,8},{10,11... | collective-permute-start | bytes 3145736 | tf_op jit(solution)/shard_map/ppermute | solution.py:640
  66.5 7.0 %collective-permute-start.8 = (bf16[256,2048]{1,0:T(8,128)(2,1)}, bf16[256,2048]{1,0:T(8,128)(2,1)}, u32[]{:S(2)}, u32[]{:S(2)}) collective-permute-start(bf16[256,2048]{1,0:T(8,128)(2,1)} %collective-permute-done.4.refs_6_), channel_id=1, source_target_pairs={{0,1},{1,0},{2,3},{3,2},{4,5},{5,4},{6,7},{7,6},{8,9},{9,8},{10,11... | collective-permute-start | bytes 3145736 | tf_op jit(solution)/shard_map/ppermute | solution.py:640
  66.6 6.9 %collective-permute-start.9 = (bf16[256,2048]{1,0:T(8,128)(2,1)S(1)}, bf16[256,2048]{1,0:T(8,128)(2,1)}, u32[]{:S(2)}, u32[]{:S(2)}) collective-permute-start(bf16[256,2048]{1,0:T(8,128)(2,1)S(1)} %collective-permute-done.1.refs_7_), channel_id=1, source_target_pairs={{0,1},{1,0},{2,3},{3,2},{4,5},{5,4},{6,7},{7,6},{8,9},{9,8},{10,11... | collective-permute-start | bytes 3145736 | tf_op jit(solution)/shard_map/ppermute | solution.py:640
  67.0 43.2 %collective-permute-start.10 = (bf16[256,2048]{1,0:T(8,128)(2,1)S(1)}, bf16[256,2048]{1,0:T(8,128)(2,1)S(1)}, u32[]{:S(2)}, u32[]{:S(2)}) collective-permute-start(bf16[256,2048]{1,0:T(8,128)(2,1)S(1)} %collective-permute-done.refs_4_), channel_id=1, source_target_pairs={{0,4},{1,5},{2,6},{3,7},{4,0},{5,1},{6,2},{7,3},{8,12},{9,13},{10,... | collective-permute-start | bytes 3145736 | tf_op jit(solution)/shard_map/ppermute | solution.py:640
  70.4 43.6 %collective-permute-start.11 = (bf16[256,2048]{1,0:T(8,128)(2,1)S(1)}, bf16[256,2048]{1,0:T(8,128)(2,1)}, u32[]{:S(2)}, u32[]{:S(2)}) collective-permute-start(bf16[256,2048]{1,0:T(8,128)(2,1)S(1)} %collective-permute-done.1.refs_7_), channel_id=1, source_target_pairs={{0,2},{1,3},{2,0},{3,1},{4,6},{5,7},{6,4},{7,5},{8,10},{9,11},{10,... | collective-permute-start | bytes 3145736 | tf_op jit(solution)/shard_map/ppermute | solution.py:640
  110.2 8.1 %copy-start.12 = (bf16[256,2048]{1,0:T(8,128)(2,1)}, bf16[256,2048]{1,0:T(8,128)(2,1)S(1)}, u32[]{:S(2)}) copy-start(bf16[256,2048]{1,0:T(8,128)(2,1)S(1)} %collective-permute-done.10.refs_1_) | copy-start | bytes 3145732
  114.0 4.1 collective-permute-start.12
  114.0 4.4 collective-permute-start.13
  124.8 12.6 %copy-start.25 = (bf16[3,256]{1,0:T(4,128)(2,1)S(1)}, bf16[3,256]{1,0:T(4,128)(2,1)}, u32[]{:S(2)}) copy-start(bf16[3,256]{1,0:T(4,128)(2,1)} %param.19) | copy-start | bytes 4612
  137.2 366.6 %reduce-scatter.3.cloned.1.call-start = ((), (), s32[]{:S(2)}) async-start(), calls=%async_computation.5 | async-start | bytes 18874368 | tf_op jit(solution)/shard_map/reduce_scatter | solution.py:813
  187.8 49.7 %collective-permute-start.14 = (bf16[512,2048]{1,0:T(8,128)(2,1)}, bf16[512,2048]{1,0:T(8,128)(2,1)S(1)}, u32[]{:S(2)}, u32[]{:S(2)}) collective-permute-start(bf16[512,2048]{1,0:T(8,128)(2,1)} %weight_grad.3), channel_id=1, source_target_pairs={{0,8},{24,16},{1,9},{25,17},{2,10},{26,18},{3,11},{27,19},{4,12},{... | collective-permute-start | bytes 6291464 | tf_op jit(solution)/shard_map/ppermute | solution.py:570
  205.1 90.0 %collective-permute-start.16 = (bf16[512,2048]{1,0:T(8,128)(2,1)}, bf16[512,2048]{1,0:T(8,128)(2,1)}, u32[]{:S(2)}, u32[]{:S(2)}) collective-permute-start(bf16[512,2048]{1,0:T(8,128)(2,1)} %weight_grad.4), channel_id=1, source_target_pairs={{0,8},{24,16},{1,9},{25,17},{2,10},{26,18},{3,11},{27,19},{4,12},{... | collective-permute-start | bytes 6291464 | tf_op jit(solution)/shard_map/ppermute | solution.py:570
  207.8 29.7 %copy-start.5 = (bf16[512,2048]{1,0:T(8,128)(2,1)S(1)}, bf16[512,2048]{1,0:T(8,128)(2,1)}, u32[]{:S(2)}) copy-start(bf16[512,2048]{1,0:T(8,128)(2,1)} %weight_grad.3) | copy-start | bytes 6291460
  238.4 61.2 %collective-permute-start.15 = (bf16[512,2048]{1,0:T(8,128)(2,1)S(1)}, bf16[512,2048]{1,0:T(8,128)(2,1)}, u32[]{:S(2)}, u32[]{:S(2)}) collective-permute-start(bf16[512,2048]{1,0:T(8,128)(2,1)S(1)} %add_convert_fusion.9), channel_id=1, source_target_pairs={{8,16},{16,8},{9,17},{17,9},{10,18},{18,10},{11,19},{19,11},{12,20... | collective-permute-start | bytes 6291464 | tf_op jit(solution)/shard_map/ppermute | solution.py:570
  265.0 69.4 %collective-permute-start.17 = (bf16[1024,1024]{1,0:T(8,128)(2,1)}, bf16[1024,1024]{1,0:T(8,128)(2,1)}, u32[]{:S(2)}, u32[]{:S(2)}) collective-permute-start(bf16[1024,1024]{1,0:T(8,128)(2,1)} %get-tuple-element.280), channel_id=1, source_target_pairs={{0,8},{24,16},{1,9},{25,17},{2,10},{26,18},{3,11},{27,19},{4,12},{... | collective-permute-start | bytes 6291464 | tf_op jit(solution)/shard_map/ppermute | solution.py:570
  272.4 22.8 %copy-start.4 = (bf16[512,2048]{1,0:T(8,128)(2,1)S(1)}, bf16[512,2048]{1,0:T(8,128)(2,1)}, u32[]{:S(2)}) copy-start(bf16[512,2048]{1,0:T(8,128)(2,1)} %weight_grad.4) | copy-start | bytes 6291460
  297.6 65.5 %collective-permute-start.21 = (bf16[512,2048]{1,0:T(8,128)(2,1)S(1)}, bf16[512,2048]{1,0:T(8,128)(2,1)}, u32[]{:S(2)}, u32[]{:S(2)}) collective-permute-start(bf16[512,2048]{1,0:T(8,128)(2,1)S(1)} %add_convert_fusion.8), channel_id=1, source_target_pairs={{8,16},{16,8},{9,17},{17,9},{10,18},{18,10},{11,19},{19,11},{12,20... | collective-permute-start | bytes 6291464 | tf_op jit(solution)/shard_map/ppermute | solution.py:570
  303.5 64.7 %collective-permute-start.20 = (bf16[512,2048]{1,0:T(8,128)(2,1)}, bf16[512,2048]{1,0:T(8,128)(2,1)}, u32[]{:S(2)}, u32[]{:S(2)}) collective-permute-start(bf16[512,2048]{1,0:T(8,128)(2,1)} %add_convert_fusion.7.kept_ref), channel_id=1, source_target_pairs={{8,0},{16,24},{9,1},{17,25},{10,2},{18,26},{11,3},{19,27},{12,4},{... | collective-permute-start | bytes 6291464 | tf_op jit(solution)/shard_map/ppermute | solution.py:570
  304.8 82.6 %collective-permute-start.19 = (bf16[1024,1024]{1,0:T(8,128)(2,1)}, bf16[1024,1024]{1,0:T(8,128)(2,1)}, u32[]{:S(2)}, u32[]{:S(2)}) collective-permute-start(bf16[1024,1024]{1,0:T(8,128)(2,1)} %get-tuple-element.301), channel_id=1, source_target_pairs={{0,8},{24,16},{1,9},{25,17},{2,10},{26,18},{3,11},{27,19},{4,12},{... | collective-permute-start | bytes 6291464 | tf_op jit(solution)/shard_map/ppermute | solution.py:570
  312.2 22.2 %copy-start.7 = (bf16[1024,1024]{1,0:T(8,128)(2,1)S(1)}, bf16[1024,1024]{1,0:T(8,128)(2,1)}, u32[]{:S(2)}) copy-start(bf16[1024,1024]{1,0:T(8,128)(2,1)} %get-tuple-element.280) | copy-start | bytes 6291460
  338.8 61.5 %collective-permute-start.18 = (bf16[1024,1024]{1,0:T(8,128)(2,1)}, bf16[1024,1024]{1,0:T(8,128)(2,1)}, u32[]{:S(2)}, u32[]{:S(2)}) collective-permute-start(bf16[1024,1024]{1,0:T(8,128)(2,1)} %add_convert_fusion.6), channel_id=1, source_target_pairs={{8,16},{16,8},{9,17},{17,9},{10,18},{18,10},{11,19},{19,11},{12,20... | collective-permute-start | bytes 6291464 | tf_op jit(solution)/shard_map/ppermute | solution.py:570
  366.9 62.6 %collective-permute-start.26 = (bf16[512,2048]{1,0:T(8,128)(2,1)}, bf16[512,2048]{1,0:T(8,128)(2,1)}, u32[]{:S(2)}, u32[]{:S(2)}) collective-permute-start(bf16[512,2048]{1,0:T(8,128)(2,1)} %add_convert_fusion.5.kept_ref), channel_id=1, source_target_pairs={{8,0},{16,24},{9,1},{17,25},{10,2},{18,26},{11,3},{19,27},{12,4},{... | collective-permute-start | bytes 6291464 | tf_op jit(solution)/shard_map/ppermute | solution.py:570
  390.5 39.0 %collective-permute-start.25 = (bf16[1024,1024]{1,0:T(8,128)(2,1)S(1)}, bf16[1024,1024]{1,0:T(8,128)(2,1)S(1)}, u32[]{:S(2)}, u32[]{:S(2)}) collective-permute-start(bf16[1024,1024]{1,0:T(8,128)(2,1)S(1)} %add_convert_fusion.4), channel_id=1, source_target_pairs={{8,16},{16,8},{9,17},{17,9},{10,18},{18,10},{11,19},{19,11},{12,20... | collective-permute-start | bytes 6291464 | tf_op jit(solution)/shard_map/ppermute | solution.py:570
  391.4 61.0 %collective-permute-start.24 = (bf16[2,2048,256]{2,1,0:T(8,128)(2,1)}, bf16[2,2048,256]{2,1,0:T(8,128)(2,1)}, u32[]{:S(2)}, u32[]{:S(2)}) collective-permute-start(bf16[2,2048,256]{2,1,0:T(8,128)(2,1)} %get-tuple-element.316), channel_id=1, source_target_pairs={{0,8},{24,16},{1,9},{25,17},{2,10},{26,18},{3,11},{27,19},{4,12},{... | collective-permute-start | bytes 6291464 | tf_op jit(solution)/shard_map/ppermute | solution.py:570
  404.9 96.3 %collective-permute-start.22 = (bf16[1024,1024]{1,0:T(8,128)(2,1)}, bf16[1024,1024]{1,0:T(8,128)(2,1)}, u32[]{:S(2)}, u32[]{:S(2)}) collective-permute-start(bf16[1024,1024]{1,0:T(8,128)(2,1)} %add_convert_fusion.3.kept_ref), channel_id=1, source_target_pairs={{8,0},{16,24},{9,1},{17,25},{10,2},{18,26},{11,3},{19,27},{12,4},{... | collective-permute-start | bytes 6291464 | tf_op jit(solution)/shard_map/ppermute | solution.py:570
  430.5 17.4 %copy-start.1 = (bf16[1024,1024]{1,0:T(8,128)(2,1)}, bf16[1024,1024]{1,0:T(8,128)(2,1)S(1)}, u32[]{:S(2)}) copy-start(bf16[1024,1024]{1,0:T(8,128)(2,1)S(1)} %add_convert_fusion.2.kept_ref) | copy-start | bytes 6291460
  430.5 84.6 %collective-permute-start.28 = (bf16[1024,1024]{1,0:T(8,128)(2,1)S(1)}, bf16[1024,1024]{1,0:T(8,128)(2,1)}, u32[]{:S(2)}, u32[]{:S(2)}) collective-permute-start(bf16[1024,1024]{1,0:T(8,128)(2,1)S(1)} %add_convert_fusion.2.kept_ref), channel_id=1, source_target_pairs={{8,0},{16,24},{9,1},{17,25},{10,2},{18,26},{11,3},{19,27},{12,4},{... | collective-permute-start | bytes 6291464 | tf_op jit(solution)/shard_map/ppermute | solution.py:570
  431.8 49.1 %collective-permute-start.23 = (bf16[2048,256]{1,0:T(8,128)(2,1)S(1)}, bf16[2048,256]{1,0:T(8,128)(2,1)}, u32[]{:S(2)}, u32[]{:S(2)}) collective-permute-start(bf16[2048,256]{1,0:T(8,128)(2,1)S(1)} %copy-done.11), channel_id=1, source_target_pairs={{0,8},{24,16},{1,9},{25,17},{2,10},{26,18},{3,11},{27,19},{4,12},{... | collective-permute-start | bytes 3145736 | tf_op jit(solution)/shard_map/ppermute | solution.py:570
  447.9 55.9 %all-to-all-start = ((bf16[8,2,256,256]{3,2,1,0:T(8,128)(2,1)}), bf16[8,2,256,256]{3,2,1,0:T(8,128)(2,1)}, u32[]{:S(2)}, u32[]{:S(2)}) async-start(bf16[8,2,256,256]{3,2,1,0:T(8,128)(2,1)} %get-tuple-element.290), calls=%async_computation | async-start | bytes 4194304 | tf_op jit(solution)/shard_map/all_to_all | solution.py:822
  452.3 144.7 %reduce-scatter.5.cloned.1.call-start = ((), (), s32[]{:S(2)}) async-start(), calls=%async_computation.6 | async-start | bytes 18874368 | tf_op jit(solution)/shard_map/reduce_scatter | solution.py:835
  456.4 67.1 %collective-permute-start.27 = (bf16[2,2048,256]{2,1,0:T(8,128)(2,1)}, bf16[2,2048,256]{2,1,0:T(8,128)(2,1)}, u32[]{:S(2)}, u32[]{:S(2)}) collective-permute-start(bf16[2,2048,256]{2,1,0:T(8,128)(2,1)} %add_convert_fusion.1), channel_id=1, source_target_pairs={{8,16},{16,8},{9,17},{17,9},{10,18},{18,10},{11,19},{19,11},{12,20... | collective-permute-start | bytes 6291464 | tf_op jit(solution)/shard_map/ppermute | solution.py:570
  482.8 13.8 %copy-start.21 = (bf16[2048]{0:T(1024)(128)(2,1)S(1)}, bf16[2048]{0:T(1024)(128)(2,1)}, u32[]{:S(2)}) copy-start(bf16[2048]{0:T(1024)(128)(2,1)} %param.21) | copy-start | bytes 12292
  482.8 14.4 %copy-start.22 = (bf16[2048]{0:T(1024)(128)(2,1)S(1)}, bf16[2048]{0:T(1024)(128)(2,1)}, u32[]{:S(2)}) copy-start(bf16[2048]{0:T(1024)(128)(2,1)} %param.25) | copy-start | bytes 12292
  494.3 24.8 %collective-permute-start.30 = (bf16[256,2048]{1,0:T(8,128)(2,1)}, bf16[256,2048]{1,0:T(8,128)(2,1)}, u32[]{:S(2)}, u32[]{:S(2)}) collective-permute-start(bf16[256,2048]{1,0:T(8,128)(2,1)} %weight_grad.5), channel_id=1, source_target_pairs={{0,8},{24,16},{1,9},{25,17},{2,10},{26,18},{3,11},{27,19},{4,12},{... | collective-permute-start | bytes 3145736 | tf_op jit(solution)/shard_map/ppermute | solution.py:570
  498.6 33.3 %collective-permute-start.36 = (bf16[2048,256]{1,0:T(8,128)(2,1)S(1)}, bf16[2048,256]{1,0:T(8,128)(2,1)}, u32[]{:S(2)}, u32[]{:S(2)}) collective-permute-start(bf16[2048,256]{1,0:T(8,128)(2,1)S(1)} %add_convert_fusion.13), channel_id=1, source_target_pairs={{8,16},{16,8},{9,17},{17,9},{10,18},{18,10},{11,19},{19,11},{12,20... | collective-permute-start | bytes 3145736 | tf_op jit(solution)/shard_map/ppermute | solution.py:570
  503.9 11.2 %copy-start.17 = (f32[8,2048]{1,0:T(8,128)S(1)}, f32[8,2048]{1,0:T(8,128)}, u32[]{:S(2)}) copy-start(f32[8,2048]{1,0:T(8,128)} %get-tuple-element.340) | copy-start | bytes 196612
  503.9 11.2 %copy-start.18 = (f32[8,2048]{1,0:T(8,128)S(1)}, f32[8,2048]{1,0:T(8,128)}, u32[]{:S(2)}) copy-start(f32[8,2048]{1,0:T(8,128)} %get-tuple-element.341) | copy-start | bytes 196612
  503.9 12.1 %copy-start.19 = (bf16[2048]{0:T(1024)(128)(2,1)S(1)}, bf16[2048]{0:T(1024)(128)(2,1)}, u32[]{:S(2)}) copy-start(bf16[2048]{0:T(1024)(128)(2,1)} %param.16) | copy-start | bytes 12292
  516.1 5.7 collective-permute-start.29
  521.1 21.1 %collective-permute-start.32 = (bf16[256,2048]{1,0:T(8,128)(2,1)S(1)}, bf16[256,2048]{1,0:T(8,128)(2,1)S(1)}, u32[]{:S(2)}, u32[]{:S(2)}) collective-permute-start(bf16[256,2048]{1,0:T(8,128)(2,1)S(1)} %add_convert_fusion.12), channel_id=1, source_target_pairs={{8,16},{16,8},{9,17},{17,9},{10,18},{18,10},{11,19},{19,11},{12,20... | collective-permute-start | bytes 3145736 | tf_op jit(solution)/shard_map/ppermute | solution.py:570
  521.8 5.8 collective-permute-start.33
  527.6 4.3 collective-permute-start.34
  529.2 55.6 %collective-permute-start.31 = (bf16[2,2048,256]{2,1,0:T(8,128)(2,1)}, bf16[2,2048,256]{2,1,0:T(8,128)(2,1)}, u32[]{:S(2)}, u32[]{:S(2)}) collective-permute-start(bf16[2,2048,256]{2,1,0:T(8,128)(2,1)} %add_convert_fusion), channel_id=1, source_target_pairs={{8,0},{16,24},{9,1},{17,25},{10,2},{18,26},{11,3},{19,27},{12,4},{... | collective-permute-start | bytes 6291464 | tf_op jit(solution)/shard_map/ppermute | solution.py:570
  531.9 8.4 %collective-permute-start.35 = (f32[49,128]{1,0:T(8,128)S(1)}, f32[49,128]{1,0:T(8,128)S(1)}, u32[]{:S(2)}, u32[]{:S(2)}) collective-permute-start(f32[49,128]{1,0:T(8,128)S(1)} %pad_maximum_fusion), channel_id=1, source_target_pairs={{0,8},{24,16},{1,9},{25,17},{2,10},{26,18},{3,11},{27,19},{4,12},{... | collective-permute-start | bytes 75272 | tf_op jit(solution)/shard_map/ppermute | solution.py:570
  540.9 15.8 %collective-permute-start.37 = (f32[49,128]{1,0:T(8,128)}, f32[49,128]{1,0:T(8,128)}, u32[]{:S(2)}, u32[]{:S(2)}) collective-permute-start(f32[49,128]{1,0:T(8,128)} %add.146), channel_id=1, source_target_pairs={{8,16},{16,8},{9,17},{17,9},{10,18},{18,10},{11,19},{19,11},{12,20... | collective-permute-start | bytes 75272 | tf_op jit(solution)/shard_map/ppermute | solution.py:570
  557.6 24.2 %collective-permute-start.38 = (f32[49,128]{1,0:T(8,128)S(1)}, f32[49,128]{1,0:T(8,128)S(1)}, u32[]{:S(2)}, u32[]{:S(2)}) collective-permute-start(f32[49,128]{1,0:T(8,128)S(1)} %add.148), channel_id=1, source_target_pairs={{8,0},{16,24},{9,1},{17,25},{10,2},{18,26},{11,3},{19,27},{12,4},{... | collective-permute-start | bytes 75272 | tf_op jit(solution)/shard_map/ppermute | solution.py:570
  558.8 45.5 %collective-permute-start.39 = (bf16[2048,256]{1,0:T(8,128)(2,1)S(1)}, bf16[2048,256]{1,0:T(8,128)(2,1)}, u32[]{:S(2)}, u32[]{:S(2)}) collective-permute-start(bf16[2048,256]{1,0:T(8,128)(2,1)S(1)} %copy-done.6), channel_id=1, source_target_pairs={{8,0},{16,24},{9,1},{17,25},{10,2},{18,26},{11,3},{19,27},{12,4},{... | collective-permute-start | bytes 3145736 | tf_op jit(solution)/shard_map/ppermute | solution.py:570
  560.1 64.8 %collective-permute-start.40 = (bf16[256,2048]{1,0:T(8,128)(2,1)}, bf16[256,2048]{1,0:T(8,128)(2,1)}, u32[]{:S(2)}, u32[]{:S(2)}) collective-permute-start(bf16[256,2048]{1,0:T(8,128)(2,1)} %add_convert_fusion.10.kept_ref), channel_id=1, source_target_pairs={{8,0},{16,24},{9,1},{17,25},{10,2},{18,26},{11,3},{19,27},{12,4},{... | collective-permute-start | bytes 3145736 | tf_op jit(solution)/shard_map/ppermute | solution.py:570
  581.8 46.2 %copy-start.23 = (f32[256]{0:T(256)}, f32[256]{0:T(256)S(1)}, u32[]{:S(2)}) copy-start(f32[256]{0:T(256)S(1)} %slice_bitcast_fusion.3) | copy-start | bytes 3076
  584.8 12.2 %copy-start = (bf16[2,256,2048]{2,1,0:T(8,128)(2,1)S(1)}, bf16[2,256,2048]{2,1,0:T(8,128)(2,1)}, u32[]{:S(2)}) copy-start(bf16[2,256,2048]{2,1,0:T(8,128)(2,1)} %param.14) | copy-start | bytes 6291460
  (8 other events, 21.0 us)
Sparse Core Ops, SparseCore 0:
  66.0 107.4 all-gather.2
  175.4 54.3 all-gather.4
  312.3 114.0 reduce-scatter.2
  481.1 115.8 reduce-scatter.4

commit v7 on v6

--- a/solution.py
+++ b/solution.py
@@ -243,28 +243,32 @@
     )(g, wo, wd, slope)
 
 
-def tokens_kernel(x_ref, w_ref, o_ref):
+def tokens_kernel(*refs, held):
+    x_ref, w_ref, o_ref = refs[held:]
     width = w_ref.shape[1]
     step = min(512, width)
     for at in range(0, width, step):
         o_ref[:, at : at + step] = dot(x_ref[...], w_ref[:, at : at + step], 1, 0).astype(o_ref.dtype)
 
 
-def tokens_by_weight(x, w, share, shares, tm=512):
+def tokens_by_weight(x, w, share, shares, before=(), tm=512):
     n, depth = x.shape
-    n //= shares
+    held = len(before)
+    steps = n // shares // tm
     width = w.shape[1]
-    first = share * (n // tm)
-    return pl.pallas_call(
-        tokens_kernel,
-        grid=(n // tm,),
-        in_specs=[pl.BlockSpec((tm, depth), lambda i: (first + i, 0)), pl.BlockSpec((depth, width), lambda i: (0, 0))],
-        out_specs=pl.BlockSpec((tm, width), lambda i: (i, 0)),
+    first = share * steps
+    return pl.pallas_call(
+        functools.partial(tokens_kernel, held=held),
+        grid=(steps,),
+        in_specs=[pl.BlockSpec(memory_space=pl.ANY)] * held
+        + [pl.BlockSpec((tm, depth), lambda i: (first + i, 0)), pl.BlockSpec((depth, width), lambda i: (0, 0))],
+        out_specs=pl.BlockSpec((tm, width), lambda i: (first + i, 0)),
         out_shape=jax.ShapeDtypeStruct((n, width), bf16),
+        input_output_aliases={i: i for i in range(held)},
         compiler_params=params(),
         cost_estimate=SMALL,
         name="tokens_by_weight",
-    )(x, w)
+    )(*before, x, w)
 
 
 def weight_grad_kernel(a_ref, b_ref, o_ref):
@@ -801,6 +805,7 @@
         act, slope = order(hidden_of, normed_full, inward_weight, in_bias_row)
     normed, act, slope = token_rows(normed_full), token_rows(act), token_rows(slope)
     qkv = order(project_qkv, normed, w3, b_qkv.astype(f32), cosine, sine)
+    mlp_half = order(lambda *a: tokens_by_weight(*a, 0, 2), act, outward_weight)
     dense_ready, _ = lax.optimization_barrier((dense_weight, act))
     dense_full = lax.all_gather(dense_ready, "tp", axis=0, tiled=True)
     o0 = RowSum(order(lambda *a: weight_grad(*a, 0, 2), act, grad), rows)
@@ -809,7 +814,8 @@
     hidden_grad, attended_grad, in_bias = order(grad_in, grad, outward_weight, dense_weight, slope)
     o0.fold(order)
     i0, i1 = row_sum(order(lambda a, b: weight_grad_rows(a, b, (1, 1)), normed, hidden_grad))
-    mlp_part = order(lambda *a: tokens_by_weight(*a, 0, 1), act, outward_weight).reshape(seqs, length, width)
+    mlp_part = order(lambda x, w, *kept: tokens_by_weight(x, w, 1, 2, kept), act, outward_weight, mlp_half)
+    mlp_part = mlp_part.reshape(seqs, length, width)
     mlp_tok = lax.psum_scatter(mlp_part, "tp", scatter_dimension=1, tiled=True).reshape(seqs * here, width)
     o1.fold(order)
     o0.fold(order)
@@ -844,6 +850,7 @@
         return jnp.sum(mine.astype(f32), axis=0)
 
     out_bias = order(column_sums, grad)
+    qs.fold(order)
     rows_of = lambda a: a.reshape(seqs * here, width)
     bias_rows = (b_dense.astype(f32)[None], b_out.astype(f32)[None])
     own = lambda x, w, t, *m: project_own(x, w, *bias_rows, rows_of(t), m)
@@ -860,7 +867,6 @@
     packed = TpSum(order(pack, norm_a, norm_b, squares), tp)
     ds.fold(order)
     packed.fold(order)
-    qs.fold(order)
     packed.fold(order)
     qkv_bias = bias_a + bias_b
     small = jnp.concatenate([in_bias[0], qkv_bias[:, 0].reshape(-1), out_bias]).reshape(-1, 128)
@@ -868,6 +874,7 @@
     vs.fold(order)
     small.fold(order)
     ds.fold(order)
+    qs.settle(order)
     out_grad = finish(o0, order, units, weight=ORDER_WEIGHT)
     out_grad = finish(o1, order, units, units // 2, out_grad)
     in_grad = finish(i0, order, width)

time: 645 us -> 644 us (level)
  waiting for transfers between devices: 104 us -> 97.1 us
    all_gather x1, waiting for transfers between devices: 15.4 us -> 2.03 us  [body(): lax.all_gather(order(lambda b: b, a), 'tp', axis=1, tiled=True)]
    pallas_call x1 -> x2, Pallas kernels: 22.8 us -> 26.6 us  [tokens_by_weight(): pl.pallas_call(functools.partial(tokens_kernel, held=held), grid=(steps,)...]
  transfers between devices with their start and end apart: 46 -> 46, of which waited for: 16 -> 19; matrix products, arithmetic and copies ran while one was open for 9% -> 10% of each run, Pallas kernels for 55% -> 55%
where the time goes in v7:
time: 644 us; the launch traced here: 634 us
  Pallas kernels  358 us (56%)
  waiting for transfers between devices  97.1 us (15%)
  starting transfers between devices  95.3 us (15%)
  other arithmetic  59 us (9%)
  between operations  14.5 us (2%)
  local copies, waits for them, and re-layouts  9.62 us (1%)
    ppermute x24, starting transfers between devices, send(): self.came = lax.ppermute(self.part, self.axis, self.hops.pop(0))  77.7 us
    pallas_call x2, Pallas kernels, normed_grad(): pl.pallas_call(functools.partial(normed_grad_kernel, held=held), grid=(st...  45.5 us
    pallas_call x2, Pallas kernels, attention_both(): pl.pallas_call(functools.partial(attention_kernel, bq=bq, held=held), gri...  44.3 us
    ppermute x14, waiting for transfers between devices, send(): return lax.ppermute(a, 'tp', [(i, i ^ step) for i in range(self.size)])  44 us
    convert_element_type x14, other arithmetic, fold(): add = lambda a, b: (a.astype(f32) + b.astype(f32)).astype(a.dtype)  41.3 us
    ppermute x24, waiting for transfers between devices, send(): self.came = lax.ppermute(self.part, self.axis, self.hops.pop(0))  40.1 us
    pallas_call x3, Pallas kernels, weight_grad(): pl.pallas_call(weight_grad_kernel, grid=(cols // tile,), in_specs=[pl.Blo...  39 us
    pallas_call x2, Pallas kernels, mlp_hidden_of(): pl.pallas_call(functools.partial(chosen_kernel, held=held), grid_spec=plt...  36 us
  transfers between devices with their start and end apart: 46, of which 19 were waited for; matrix products, arithmetic and copies ran while one was open for 10% of the time, Pallas kernels for 55%

profile of v7, /device:TPU:0, one launch (start us, length us, event | category | flops | bytes accessed | tf_op | source)
XLA Modules:
  0.0 633.8 jit_solution(5680794663347567021)
XLA Ops:
  9.8 4.7 norm_halves.1
  14.6 3.0 collective-permute-start.1
  22.2 9.8 %rope_tables.1 = (f32[4096,128]{1,0:T(8,128)}, f32[4096,128]{1,0:T(8,128)}) custom-call(s32[4096,1]{1,0:T(8,128)} %bitcast.68, f32[1,128]{1,0:T(1,128)} %fusion.15.frequency_ref), custom_call_target="tpu_custom_call" | custom-call | flops 1 | bytes 1 | tf_op jit(solution)/shard_map/rope_tables/pallas_call | solution.py:99
  32.6 9.1 %collective-permute-done.1.refs_7_ = bf16[256,2048]{1,0:T(8,128)(2,1)S(1)} collective-permute-done((bf16[256,2048]{1,0:T(8,128)(2,1)}, bf16[256,2048]{1,0:T(8,128)(2,1)S(1)}, u32[]{:S(2)}, u32[]{:S(2)}) %collective-permute-start.1) | collective-permute-done | bytes 1048608 | tf_op jit(solution)/shard_map/ppermute | solution.py:644
  43.7 22.2 %collective-permute-done.3.refs_5_ = bf16[256,2048]{1,0:T(8,128)(2,1)} collective-permute-done((bf16[256,2048]{1,0:T(8,128)(2,1)}, bf16[256,2048]{1,0:T(8,128)(2,1)}, u32[]{:S(2)}, u32[]{:S(2)}) %collective-permute-start.3) | collective-permute-done | bytes 1048608 | tf_op jit(solution)/shard_map/ppermute | solution.py:644
  67.3 2.1 collective-permute-done.6.refs_8_
  73.5 13.1 %place_pieces.2.refs_0_ = bf16[2,8,256,2048]{3,2,1,0:T(8,128)(2,1)} custom-call(s32[1]{0:T(128)} %bitcast.3.me_ref, bf16[256,2048]{1,0:T(8,128)(2,1)} %get-tuple-element.217.refs_0_, bf16[256,2048]{1,0:T(8,128)(2,1)} %get-tuple-element.218.refs_1_, bf16[256,2048]{1,0:T(8,128)(2,1)} %collective-permute-done.2.refs_2_, ...), custom_call_target="tpu_custom_call" | custom-call | flops 1 | bytes 1 | tf_op jit(solution)/shard_map/place_pieces/pallas_call | solution.py:705
  86.6 23.6 %mlp_hidden_of.2 = (bf16[2,8,256,1024]{3,2,1,0:T(8,128)(2,1)}, bf16[2,8,256,1024]{3,2,1,0:T(8,128)(2,1)}) custom-call(s32[1]{0:T(128)} %bitcast.3.me_ref, bf16[2,8,256,2048]{3,2,1,0:T(8,128)(2,1)} %place_pieces.2.refs_0_, bf16[2048,1024]{1,0:T(8,128)(2,1)} %refs_3_.1, f32[1,1024]{1,0:T(1,128)} %bitcast.79), custom_call_target="tpu_custom_call" | custom-call | flops 1 | bytes 1 | tf_op jit(solution)/shard_map/mlp_hidden_of/pallas_call | solution.py:180
  110.3 3.7 collective-permute-done.11.refs_2_
  114.5 3.6 collective-permute-done.12.refs_3_
  120.1 4.7 place_pieces.3.refs_2_
  124.8 12.4 %mlp_hidden_of.3 = (bf16[2,8,256,1024]{3,2,1,0:T(8,128)(2,1)}, bf16[2,8,256,1024]{3,2,1,0:T(8,128)(2,1)}) custom-call(s32[1]{0:T(128)} %bitcast.3.me_ref, bf16[2,8,256,1024]{3,2,1,0:T(8,128)(2,1)} %get-tuple-element.241.refs_0_, bf16[2,8,256,1024]{3,2,1,0:T(8,128)(2,1)} %get-tuple-element.242.refs_1_, ...), custom_call_target="tpu_custom_call", output_to_operand_aliasing={{0}: (1, {}), {1}: (2, {})} | custom-call | flops 1 | bytes 1 | tf_op jit(solution)/shard_map/mlp_hidden_of/pallas_call | solution.py:180
  138.4 19.9 %qkv_rope.1.refs_1_.refs_2_.refs_3_.refs_4_.refs_5_.refs_6_ = bf16[3,4096,256]{2,1,0:T(8,128)(2,1)} custom-call(bf16[4096,2048]{1,0:T(8,128)(2,1)} %bitcast.45, bf16[3,2048,256]{2,1,0:T(8,128)(2,1)} %bitcast.64, f32[3,256]{1,0:T(4,128)} %convert_element_type.170.b_ref, f32[4096,128]{1,0:T(8,128)} %get-tuple-element.295.c_ref.refs_5_.refs_8_, ...), custom_call_target="tpu_custom_call" | custom-call | flops 1 | bytes 1 | tf_op jit(solution)/shard_map/qkv_rope/pallas_call | solution.py:131
  158.3 13.3 %tokens_by_weight.2.refs_0_ = bf16[4096,2048]{1,0:T(8,128)(2,1)} custom-call(bf16[4096,1024]{1,0:T(8,128)(2,1)} %bitcast.55, bf16[1024,2048]{1,0:T(8,128)(2,1)} %refs_2_), custom_call_target="tpu_custom_call" | custom-call | flops 1 | bytes 1 | tf_op jit(solution)/shard_map/tokens_by_weight/pallas_call | solution.py:260
  171.5 2.0 all-gather.3.cloned.1.call-done
  173.6 14.2 %weight_grad.3 = bf16[512,2048]{1,0:T(8,128)(2,1)} custom-call(bf16[4096,1024]{1,0:T(8,128)(2,1)} %bitcast.56, bf16[4096,2048]{1,0:T(8,128)(2,1)} %bitcast.50), custom_call_target="tpu_custom_call" | custom-call | flops 1 | bytes 1 | tf_op jit(solution)/shard_map/weight_grad/pallas_call | solution.py:283
  187.8 3.5 collective-permute-start.14
  191.3 13.8 %weight_grad.4 = bf16[512,2048]{1,0:T(8,128)(2,1)} custom-call(bf16[4096,1024]{1,0:T(8,128)(2,1)} %bitcast.57, bf16[4096,2048]{1,0:T(8,128)(2,1)} %bitcast.51), custom_call_target="tpu_custom_call" | custom-call | flops 1 | bytes 1 | tf_op jit(solution)/shard_map/weight_grad/pallas_call | solution.py:283
  205.1 2.7 collective-permute-start.16
  207.8 29.6 %grad_in.1 = (bf16[4096,1024]{1,0:T(8,128)(2,1)}, bf16[4096,256]{1,0:T(8,128)(2,1)}, f32[8,1024]{1,0:T(8,128)}) custom-call(bf16[4096,2048]{1,0:T(8,128)(2,1)} %bitcast.52, bf16[1024,2048]{1,0:T(8,128)(2,1)} %refs_2_, bf16[256,2048]{1,0:T(8,128)(2,1)} %wd_ref, bf16[4096,1024]{1,0:T(8,128)(2,1)} %bitcast.63), custom_call_target="tpu_custom_call" | custom-call | flops 1 | bytes 1 | tf_op jit(solution)/shard_map/grad_in/pallas_call | solution.py:221
  238.4 2.0 collective-permute-start.15
  240.4 24.6 %weight_grad_rows.1 = (bf16[1024,1024]{1,0:T(8,128)(2,1)}, bf16[1024,1024]{1,0:T(8,128)(2,1)}) custom-call(bf16[4096,2048]{1,0:T(8,128)(2,1)} %bitcast.46, bf16[4096,1024]{1,0:T(8,128)(2,1)} %get-tuple-element.326.b_ref.refs_0_.refs_1_), custom_call_target="tpu_custom_call" | custom-call | flops 1 | bytes 1 | tf_op jit(solution)/shard_map/weight_grad_rows/pallas_call | solution.py:317
  265.0 7.1 %collective-permute-start.17 = (bf16[1024,1024]{1,0:T(8,128)(2,1)}, bf16[1024,1024]{1,0:T(8,128)(2,1)}, u32[]{:S(2)}, u32[]{:S(2)}) collective-permute-start(bf16[1024,1024]{1,0:T(8,128)(2,1)} %get-tuple-element.287), channel_id=1, source_target_pairs={{0,8},{24,16},{1,9},{25,17},{2,10},{26,18},{3,11},{27,19},{4,12},{... | collective-permute-start | bytes 6291464 | tf_op jit(solution)/shard_map/ppermute | solution.py:574
  272.1 13.4 %tokens_by_weight.3 = bf16[4096,2048]{1,0:T(8,128)(2,1)} custom-call(bf16[4096,2048]{1,0:T(8,128)(2,1)} %tokens_by_weight.2.refs_0_, bf16[4096,1024]{1,0:T(8,128)(2,1)} %bitcast.58, bf16[1024,2048]{1,0:T(8,128)(2,1)} %refs_2_), custom_call_target="tpu_custom_call", output_to_operand_aliasing={{}: (0, {})} | custom-call | flops 1 | bytes 1 | tf_op jit(solution)/shard_map/tokens_by_weight/pallas_call | solution.py:260
  285.4 2.4 add_convert_fusion.8
  287.8 2.0 collective-permute-start.19
  289.9 3.8 add_convert_fusion.7.kept_ref
  295.0 7.4 %collective-permute-start.21 = (bf16[1024,1024]{1,0:T(8,128)(2,1)}, bf16[1024,1024]{1,0:T(8,128)(2,1)}, u32[]{:S(2)}, u32[]{:S(2)}) collective-permute-start(bf16[1024,1024]{1,0:T(8,128)(2,1)} %get-tuple-element.308), channel_id=1, source_target_pairs={{0,8},{24,16},{1,9},{25,17},{2,10},{26,18},{3,11},{27,19},{4,12},{... | collective-permute-start | bytes 6291464 | tf_op jit(solution)/shard_map/ppermute | solution.py:574
  302.4 22.2 %attention_both.2 = (bf16[4096,256]{1,0:T(8,128)(2,1)}, bf16[8,2,256,256]{3,2,1,0:T(8,128)(2,1)}, bf16[3,4096,256]{2,1,0:T(8,128)(2,1)}) custom-call(s32[1,4096]{1,0:T(1,128)} %fusion.11.refs_0_.refs_3_, bf16[3,4096,256]{2,1,0:T(8,128)(2,1)} %qkv_rope.1.refs_1_.refs_2_.refs_3_.refs_4_.refs_5_.refs_6_, ...), custom_call_target="tpu_custom_call" | custom-call | flops 1 | bytes 1 | tf_op jit(solution)/shard_map/attention_both/pallas_call | solution.py:480
  324.7 2.7 collective-permute-done.17
  327.4 4.0 add_convert_fusion.6
  333.4 22.1 %attention_both.3 = (bf16[4096,256]{1,0:T(8,128)(2,1)}, bf16[8,2,256,256]{3,2,1,0:T(8,128)(2,1)}, bf16[3,4096,256]{2,1,0:T(8,128)(2,1)}) custom-call(bf16[4096,256]{1,0:T(8,128)(2,1)} %get-tuple-element.289.refs_0_, bf16[8,2,256,256]{3,2,1,0:T(8,128)(2,1)} %get-tuple-element.290.refs_1_, ...), custom_call_target="tpu_custom_call", output_to_operand_aliasing={{0}: (0, {}), {1}: (1, {}), {2}: (2, {})} | custom-call | flops 1 | bytes 1 | tf_op jit(solution)/shard_map/attention_both/pallas_call | solution.py:480
  355.5 3.7 add_convert_fusion.5.kept_ref
  360.7 19.2 %weight_grad_parts.1 = (bf16[2,2048,256]{2,1,0:T(8,128)(2,1)}, bf16[2048,256]{1,0:T(8,128)(2,1)}) custom-call(bf16[4096,2048]{1,0:T(8,128)(2,1)} %bitcast.47, bf16[3,4096,256]{2,1,0:T(8,128)(2,1)} %get-tuple-element.327.b_ref.refs_1_.refs_2_), custom_call_target="tpu_custom_call" | custom-call | flops 219999993856 | bytes 1 | tf_op jit(solution)/shard_map/weight_grad_parts/pallas_call | solution.py:341
  379.9 3.3 add_convert_fusion.4
  385.2 9.1 %collective-permute-start.20 = (bf16[2,2048,256]{2,1,0:T(8,128)(2,1)S(1)}, bf16[2,2048,256]{2,1,0:T(8,128)(2,1)}, u32[]{:S(2)}, u32[]{:S(2)}) collective-permute-start(bf16[2,2048,256]{2,1,0:T(8,128)(2,1)S(1)} %copy-done.8), channel_id=1, source_target_pairs={{0,8},{24,16},{1,9},{25,17},{2,10},{26,18},{3,11},{27,19},{4,12},{... | collective-permute-start | bytes 6291464 | tf_op jit(solution)/shard_map/ppermute | solution.py:574
  394.3 4.5 add_convert_fusion.3.kept_ref
  400.1 22.9 %normed_grad.2 = (bf16[4096,2048]{1,0:T(8,128)(2,1)}, f32[3,8,256]{2,1,0:T(8,128)}, f32[8,2048]{1,0:T(8,128)}) custom-call(bf16[4096,1024]{1,0:T(8,128)(2,1)} %get-tuple-element.326.b_ref.refs_0_.refs_1_, bf16[3,4096,256]{2,1,0:T(8,128)(2,1)} %get-tuple-element.327.b_ref.refs_1_.refs_2_, bf16[2048,1024]{1,0:T(8,128)(2,1)} %refs_3_.1, ...), custom_call_target="tpu_custom_call" | custom-call | flops 1 | bytes 1 | tf_op jit(solution)/shard_map/normed_grad/pallas_call | solution.py:385
  423.1 2.6 add_convert_fusion.2.kept_ref
  425.6 10.8 %collective-permute-done.20 = bf16[2,2048,256]{2,1,0:T(8,128)(2,1)} collective-permute-done((bf16[2,2048,256]{2,1,0:T(8,128)(2,1)S(1)}, bf16[2,2048,256]{2,1,0:T(8,128)(2,1)}, u32[]{:S(2)}, u32[]{:S(2)}) %collective-permute-start.20) | collective-permute-done | bytes 2097184 | tf_op jit(solution)/shard_map/ppermute | solution.py:574
  436.4 3.4 add_convert_fusion.1
  439.9 2.1 collective-permute-start.25
  442.0 7.5 %collective-permute-start.27 = (bf16[2048,256]{1,0:T(8,128)(2,1)S(1)}, bf16[2048,256]{1,0:T(8,128)(2,1)}, u32[]{:S(2)}, u32[]{:S(2)}) collective-permute-start(bf16[2048,256]{1,0:T(8,128)(2,1)S(1)} %copy-done.12), channel_id=1, source_target_pairs={{0,8},{24,16},{1,9},{25,17},{2,10},{26,18},{3,11},{27,19},{4,12},{... | collective-permute-start | bytes 3145736 | tf_op jit(solution)/shard_map/ppermute | solution.py:574
  450.7 4.4 all-to-all-start
  456.8 22.6 %normed_grad.3 = (bf16[4096,2048]{1,0:T(8,128)(2,1)}, f32[3,8,256]{2,1,0:T(8,128)}, f32[8,2048]{1,0:T(8,128)}) custom-call(bf16[4096,2048]{1,0:T(8,128)(2,1)} %get-tuple-element.325.refs_0_, bf16[4096,1024]{1,0:T(8,128)(2,1)} %get-tuple-element.326.b_ref.refs_0_.refs_1_, ...), custom_call_target="tpu_custom_call", output_to_operand_aliasing={{0}: (0, {})} | custom-call | flops 1 | bytes 1 | tf_op jit(solution)/shard_map/normed_grad/pallas_call | solution.py:385
  482.8 11.0 %weight_grad.5 = bf16[256,2048]{1,0:T(8,128)(2,1)} custom-call(bf16[4096,256]{1,0:T(8,128)(2,1)} %get-tuple-element.336.a_ref, bf16[4096,2048]{1,0:T(8,128)(2,1)} %bitcast.53), custom_call_target="tpu_custom_call" | custom-call | flops 1 | bytes 1 | tf_op jit(solution)/shard_map/weight_grad/pallas_call | solution.py:283
  493.8 9.6 %collective-permute-start.29 = (bf16[256,2048]{1,0:T(8,128)(2,1)}, bf16[256,2048]{1,0:T(8,128)(2,1)}, u32[]{:S(2)}, u32[]{:S(2)}) collective-permute-start(bf16[256,2048]{1,0:T(8,128)(2,1)} %weight_grad.5), channel_id=1, source_target_pairs={{0,8},{24,16},{1,9},{25,17},{2,10},{26,18},{3,11},{27,19},{4,12},{... | collective-permute-start | bytes 3145736 | tf_op jit(solution)/shard_map/ppermute | solution.py:574
  503.4 2.5 convert_reduce_fusion.1
  506.0 4.8 add_convert_fusion
  512.2 10.7 %project_own.1 = (bf16[512,2048]{1,0:T(8,128)(2,1)}, f32[8,512]{1,0:T(8,128)}) custom-call(bf16[8,2,256,256]{3,2,1,0:T(8,128)(2,1)} %all-to-all-done.x_ref, bf16[2048,2048]{1,0:T(8,128)(2,1)} %all-gather.5.cloned.1.call-done.w_ref, f32[1,2048]{1,0:T(1,128)} %bitcast.81, f32[1,2048]{1,0:T(1,128)} %bitcast.82, bf16[512,2048]{1,0:T(8,128)(2,1)} %bitcast.61, ...), custom_call_target="tpu_custom_call" | custom-call | flops 1 | bytes 1 | tf_op jit(solution)/shard_map/project_own/pallas_call | solution.py:536
  535.1 2.3 collective-permute-done.34
  537.5 6.5 %collective-permute-start.35 = (f32[49,128]{1,0:T(8,128)S(1)}, f32[49,128]{1,0:T(8,128)S(1)}, u32[]{:S(2)}, u32[]{:S(2)}) collective-permute-start(f32[49,128]{1,0:T(8,128)S(1)} %pad_maximum_fusion), channel_id=1, source_target_pairs={{0,8},{24,16},{1,9},{25,17},{2,10},{26,18},{3,11},{27,19},{4,12},{... | collective-permute-start | bytes 75272 | tf_op jit(solution)/shard_map/ppermute | solution.py:574
  544.0 2.7 add_convert_fusion.11.kept_ref
  550.0 10.1 %collective-permute-done.28 = bf16[2,2048,256]{2,1,0:T(8,128)(2,1)} collective-permute-done((bf16[2,2048,256]{2,1,0:T(8,128)(2,1)}, bf16[2,2048,256]{2,1,0:T(8,128)(2,1)}, u32[]{:S(2)}, u32[]{:S(2)}) %collective-permute-start.28) | collective-permute-done | bytes 2097184 | tf_op jit(solution)/shard_map/ppermute | solution.py:574
  560.1 4.6 finish.7.refs_0_
  564.7 4.5 finish.8
  569.2 3.9 finish.9.refs_0_
  577.9 4.0 finish.10
  581.9 6.8 %finish.11.refs_0_ = f32[6144,256]{1,0:T(8,128)} custom-call(s32[1]{0:T(128)} %bitcast.17.inner_ref, bf16[4096,256]{1,0:T(8,128)(2,1)} %bitcast.18.kept_ref, bf16[4096,256]{1,0:T(8,128)(2,1)} %bitcast.24.came_ref), custom_call_target="tpu_custom_call" | custom-call | flops 1 | bytes 1 | tf_op jit(solution)/shard_map/finish/pallas_call | solution.py:633
  591.7 6.7 %reduce-scatter.5.cloned.1.call-done = bf16[2,256,2048]{2,1,0:T(8,128)(2,1)} async-done(((bf16[2,2048,2048]{2,1,0:T(8,128)(2,1)}), bf16[2,256,2048]{2,1,0:T(8,128)(2,1)}) %reduce-scatter.5.cloned.1.call-update) | async-done | bytes 2097168 | tf_op jit(solution)/shard_map/reduce_scatter | solution.py:841
  601.6 3.2 fusion.8
  604.8 3.8 finish.12
  608.5 15.0 %collective-permute-done.40.came_ref = bf16[256,2048]{1,0:T(8,128)(2,1)} collective-permute-done((bf16[256,2048]{1,0:T(8,128)(2,1)}, bf16[256,2048]{1,0:T(8,128)(2,1)}, u32[]{:S(2)}, u32[]{:S(2)}) %collective-permute-start.40) | collective-permute-done | bytes 1048608 | tf_op jit(solution)/shard_map/ppermute | solution.py:574
  623.5 3.0 finish.13
  (171 shorter events, 62.9 us)
Async XLA Ops:
  7.2 12.5 %copy-start.21 = (s32[2,2048]{1,0:T(2,128)S(1)}, s32[2,2048]{1,0:T(2,128)}, u32[]{:S(2)}) copy-start(s32[2,2048]{1,0:T(2,128)} %param.15) | copy-start | bytes 49156
  7.2 166.4 %all-gather.3.cloned.1.call-start = ((), (), s32[]{:S(2)}) async-start(), calls=%async_computation.3 | async-start | bytes 18874368 | tf_op jit(solution)/shard_map/all_gather | solution.py:788
  14.6 27.2 %collective-permute-start.1 = (bf16[256,2048]{1,0:T(8,128)(2,1)}, bf16[256,2048]{1,0:T(8,128)(2,1)S(1)}, u32[]{:S(2)}, u32[]{:S(2)}) collective-permute-start(bf16[256,2048]{1,0:T(8,128)(2,1)} %get-tuple-element.218.refs_1_), channel_id=1, source_target_pairs={{0,4},{1,5},{2,6},{3,7},{4,0},{5,1},{6,2},{7,3},{8,12},{9,13},{10,... | collective-permute-start | bytes 3145736 | tf_op jit(solution)/shard_map/ppermute | solution.py:644
  17.5 24.2 %collective-permute-start.2 = (bf16[256,2048]{1,0:T(8,128)(2,1)}, bf16[256,2048]{1,0:T(8,128)(2,1)}, u32[]{:S(2)}, u32[]{:S(2)}) collective-permute-start(bf16[256,2048]{1,0:T(8,128)(2,1)} %get-tuple-element.217.refs_0_), channel_id=1, source_target_pairs={{0,1},{1,0},{2,3},{3,2},{4,5},{5,4},{6,7},{7,6},{8,9},{9,8},{10,11... | collective-permute-start | bytes 3145736 | tf_op jit(solution)/shard_map/ppermute | solution.py:644
  17.5 26.2 %collective-permute-start = (bf16[256,2048]{1,0:T(8,128)(2,1)}, bf16[256,2048]{1,0:T(8,128)(2,1)S(1)}, u32[]{:S(2)}, u32[]{:S(2)}) collective-permute-start(bf16[256,2048]{1,0:T(8,128)(2,1)} %get-tuple-element.217.refs_0_), channel_id=1, source_target_pairs={{0,2},{1,3},{2,0},{3,1},{4,6},{5,7},{6,4},{7,5},{8,10},{9,11},{10,... | collective-permute-start | bytes 3145736 | tf_op jit(solution)/shard_map/ppermute | solution.py:644
  19.0 46.9 %collective-permute-start.3 = (bf16[256,2048]{1,0:T(8,128)(2,1)}, bf16[256,2048]{1,0:T(8,128)(2,1)}, u32[]{:S(2)}, u32[]{:S(2)}) collective-permute-start(bf16[256,2048]{1,0:T(8,128)(2,1)} %get-tuple-element.218.refs_1_), channel_id=1, source_target_pairs={{0,2},{1,3},{2,0},{3,1},{4,6},{5,7},{6,4},{7,5},{8,10},{9,11},{10,... | collective-permute-start | bytes 3145736 | tf_op jit(solution)/shard_map/ppermute | solution.py:644
  19.6 46.3 %collective-permute-start.4 = (bf16[256,2048]{1,0:T(8,128)(2,1)}, bf16[256,2048]{1,0:T(8,128)(2,1)}, u32[]{:S(2)}, u32[]{:S(2)}) collective-permute-start(bf16[256,2048]{1,0:T(8,128)(2,1)} %get-tuple-element.217.refs_0_), channel_id=1, source_target_pairs={{0,4},{1,5},{2,6},{3,7},{4,0},{5,1},{6,2},{7,3},{8,12},{9,13},{10,... | collective-permute-start | bytes 3145736 | tf_op jit(solution)/shard_map/ppermute | solution.py:644
  19.7 24.0 %copy-start.10 = (bf16[256,2048]{1,0:T(8,128)(2,1)S(1)}, bf16[256,2048]{1,0:T(8,128)(2,1)}, u32[]{:S(2)}) copy-start(bf16[256,2048]{1,0:T(8,128)(2,1)} %get-tuple-element.218.refs_1_) | copy-start | bytes 3145732
  22.2 49.7 %copy-start.25 = (bf16[1024]{0:T(1024)(128)(2,1)S(1)}, bf16[1024]{0:T(1024)(128)(2,1)}, u32[]{:S(2)}) copy-start(bf16[1024]{0:T(1024)(128)(2,1)} %param.23) | copy-start | bytes 6148
  41.7 31.8 %copy-start.9 = (bf16[256,2048]{1,0:T(8,128)(2,1)}, bf16[256,2048]{1,0:T(8,128)(2,1)S(1)}, u32[]{:S(2)}) copy-start(bf16[256,2048]{1,0:T(8,128)(2,1)S(1)} %collective-permute-done.1.refs_7_) | copy-start | bytes 3145732
  43.7 29.8 %copy-start.11 = (bf16[256,2048]{1,0:T(8,128)(2,1)}, bf16[256,2048]{1,0:T(8,128)(2,1)S(1)}, u32[]{:S(2)}) copy-start(bf16[256,2048]{1,0:T(8,128)(2,1)S(1)} %collective-permute-done.refs_4_) | copy-start | bytes 3145732
  43.7 22.2 %collective-permute-start.5 = (bf16[256,2048]{1,0:T(8,128)(2,1)S(1)}, bf16[256,2048]{1,0:T(8,128)(2,1)}, u32[]{:S(2)}, u32[]{:S(2)}) collective-permute-start(bf16[256,2048]{1,0:T(8,128)(2,1)S(1)} %copy-done.10), channel_id=1, source_target_pairs={{0,1},{1,0},{2,3},{3,2},{4,5},{5,4},{6,7},{7,6},{8,9},{9,8},{10,11... | collective-permute-start | bytes 3145736 | tf_op jit(solution)/shard_map/ppermute | solution.py:644
  65.9 446.2 %all-gather.5.cloned.1.call-start = ((), (), s32[]{:S(2)}) async-start(), calls=%async_computation.4 | async-start | bytes 9437184 | tf_op jit(solution)/shard_map/all_gather | solution.py:810
  66.0 3.4 collective-permute-start.6
  66.0 6.4 %collective-permute-start.7 = (bf16[256,2048]{1,0:T(8,128)(2,1)}, bf16[256,2048]{1,0:T(8,128)(2,1)}, u32[]{:S(2)}, u32[]{:S(2)}) collective-permute-start(bf16[256,2048]{1,0:T(8,128)(2,1)} %collective-permute-done.3.refs_5_), channel_id=1, source_target_pairs={{0,1},{1,0},{2,3},{3,2},{4,5},{5,4},{6,7},{7,6},{8,9},{9,8},{10,11... | collective-permute-start | bytes 3145736 | tf_op jit(solution)/shard_map/ppermute | solution.py:644
  66.5 7.0 %collective-permute-start.8 = (bf16[256,2048]{1,0:T(8,128)(2,1)}, bf16[256,2048]{1,0:T(8,128)(2,1)}, u32[]{:S(2)}, u32[]{:S(2)}) collective-permute-start(bf16[256,2048]{1,0:T(8,128)(2,1)} %collective-permute-done.4.refs_6_), channel_id=1, source_target_pairs={{0,1},{1,0},{2,3},{3,2},{4,5},{5,4},{6,7},{7,6},{8,9},{9,8},{10,11... | collective-permute-start | bytes 3145736 | tf_op jit(solution)/shard_map/ppermute | solution.py:644
  66.6 6.9 %collective-permute-start.9 = (bf16[256,2048]{1,0:T(8,128)(2,1)S(1)}, bf16[256,2048]{1,0:T(8,128)(2,1)}, u32[]{:S(2)}, u32[]{:S(2)}) collective-permute-start(bf16[256,2048]{1,0:T(8,128)(2,1)S(1)} %collective-permute-done.1.refs_7_), channel_id=1, source_target_pairs={{0,1},{1,0},{2,3},{3,2},{4,5},{5,4},{6,7},{7,6},{8,9},{9,8},{10,11... | collective-permute-start | bytes 3145736 | tf_op jit(solution)/shard_map/ppermute | solution.py:644
  67.1 43.2 %collective-permute-start.10 = (bf16[256,2048]{1,0:T(8,128)(2,1)S(1)}, bf16[256,2048]{1,0:T(8,128)(2,1)S(1)}, u32[]{:S(2)}, u32[]{:S(2)}) collective-permute-start(bf16[256,2048]{1,0:T(8,128)(2,1)S(1)} %collective-permute-done.refs_4_), channel_id=1, source_target_pairs={{0,4},{1,5},{2,6},{3,7},{4,0},{5,1},{6,2},{7,3},{8,12},{9,13},{10,... | collective-permute-start | bytes 3145736 | tf_op jit(solution)/shard_map/ppermute | solution.py:644
  70.4 43.6 %collective-permute-start.11 = (bf16[256,2048]{1,0:T(8,128)(2,1)S(1)}, bf16[256,2048]{1,0:T(8,128)(2,1)}, u32[]{:S(2)}, u32[]{:S(2)}) collective-permute-start(bf16[256,2048]{1,0:T(8,128)(2,1)S(1)} %collective-permute-done.1.refs_7_), channel_id=1, source_target_pairs={{0,2},{1,3},{2,0},{3,1},{4,6},{5,7},{6,4},{7,5},{8,10},{9,11},{10,... | collective-permute-start | bytes 3145736 | tf_op jit(solution)/shard_map/ppermute | solution.py:644
  114.0 4.1 collective-permute-start.12
  114.0 4.4 collective-permute-start.13
  124.8 12.9 %copy-start.26 = (bf16[3,256]{1,0:T(4,128)(2,1)S(1)}, bf16[3,256]{1,0:T(4,128)(2,1)}, u32[]{:S(2)}) copy-start(bf16[3,256]{1,0:T(4,128)(2,1)} %param.19) | copy-start | bytes 4612
  137.2 374.9 %reduce-scatter.3.cloned.1.call-start = ((), (), s32[]{:S(2)}) async-start(), calls=%async_computation.5 | async-start | bytes 18874368 | tf_op jit(solution)/shard_map/reduce_scatter | solution.py:819
  187.8 49.7 %collective-permute-start.14 = (bf16[512,2048]{1,0:T(8,128)(2,1)}, bf16[512,2048]{1,0:T(8,128)(2,1)S(1)}, u32[]{:S(2)}, u32[]{:S(2)}) collective-permute-start(bf16[512,2048]{1,0:T(8,128)(2,1)} %weight_grad.3), channel_id=1, source_target_pairs={{0,8},{24,16},{1,9},{25,17},{2,10},{26,18},{3,11},{27,19},{4,12},{... | collective-permute-start | bytes 6291464 | tf_op jit(solution)/shard_map/ppermute | solution.py:574
  205.1 80.3 %collective-permute-start.16 = (bf16[512,2048]{1,0:T(8,128)(2,1)}, bf16[512,2048]{1,0:T(8,128)(2,1)}, u32[]{:S(2)}, u32[]{:S(2)}) collective-permute-start(bf16[512,2048]{1,0:T(8,128)(2,1)} %weight_grad.4), channel_id=1, source_target_pairs={{0,8},{24,16},{1,9},{25,17},{2,10},{26,18},{3,11},{27,19},{4,12},{... | collective-permute-start | bytes 6291464 | tf_op jit(solution)/shard_map/ppermute | solution.py:574
  207.8 29.7 %copy-start.5 = (bf16[512,2048]{1,0:T(8,128)(2,1)S(1)}, bf16[512,2048]{1,0:T(8,128)(2,1)}, u32[]{:S(2)}) copy-start(bf16[512,2048]{1,0:T(8,128)(2,1)} %weight_grad.3) | copy-start | bytes 6291460
  238.4 51.5 %collective-permute-start.15 = (bf16[512,2048]{1,0:T(8,128)(2,1)S(1)}, bf16[512,2048]{1,0:T(8,128)(2,1)}, u32[]{:S(2)}, u32[]{:S(2)}) collective-permute-start(bf16[512,2048]{1,0:T(8,128)(2,1)S(1)} %add_convert_fusion.9), channel_id=1, source_target_pairs={{8,16},{16,8},{9,17},{17,9},{10,18},{18,10},{11,19},{19,11},{12,20... | collective-permute-start | bytes 6291464 | tf_op jit(solution)/shard_map/ppermute | solution.py:574
  265.0 62.4 %collective-permute-start.17 = (bf16[1024,1024]{1,0:T(8,128)(2,1)}, bf16[1024,1024]{1,0:T(8,128)(2,1)}, u32[]{:S(2)}, u32[]{:S(2)}) collective-permute-start(bf16[1024,1024]{1,0:T(8,128)(2,1)} %get-tuple-element.287), channel_id=1, source_target_pairs={{0,8},{24,16},{1,9},{25,17},{2,10},{26,18},{3,11},{27,19},{4,12},{... | collective-permute-start | bytes 6291464 | tf_op jit(solution)/shard_map/ppermute | solution.py:574
  272.1 13.4 %copy-start.4 = (bf16[512,2048]{1,0:T(8,128)(2,1)S(1)}, bf16[512,2048]{1,0:T(8,128)(2,1)}, u32[]{:S(2)}) copy-start(bf16[512,2048]{1,0:T(8,128)(2,1)} %weight_grad.4) | copy-start | bytes 6291460
  287.8 67.7 %collective-permute-start.19 = (bf16[512,2048]{1,0:T(8,128)(2,1)S(1)}, bf16[512,2048]{1,0:T(8,128)(2,1)}, u32[]{:S(2)}, u32[]{:S(2)}) collective-permute-start(bf16[512,2048]{1,0:T(8,128)(2,1)S(1)} %add_convert_fusion.8), channel_id=1, source_target_pairs={{8,16},{16,8},{9,17},{17,9},{10,18},{18,10},{11,19},{19,11},{12,20... | collective-permute-start | bytes 6291464 | tf_op jit(solution)/shard_map/ppermute | solution.py:574
  293.7 67.0 %collective-permute-start.18 = (bf16[512,2048]{1,0:T(8,128)(2,1)}, bf16[512,2048]{1,0:T(8,128)(2,1)}, u32[]{:S(2)}, u32[]{:S(2)}) collective-permute-start(bf16[512,2048]{1,0:T(8,128)(2,1)} %add_convert_fusion.7.kept_ref), channel_id=1, source_target_pairs={{8,0},{16,24},{9,1},{17,25},{10,2},{18,26},{11,3},{19,27},{12,4},{... | collective-permute-start | bytes 6291464 | tf_op jit(solution)/shard_map/ppermute | solution.py:574
  295.0 84.9 %collective-permute-start.21 = (bf16[1024,1024]{1,0:T(8,128)(2,1)}, bf16[1024,1024]{1,0:T(8,128)(2,1)}, u32[]{:S(2)}, u32[]{:S(2)}) collective-permute-start(bf16[1024,1024]{1,0:T(8,128)(2,1)} %get-tuple-element.308), channel_id=1, source_target_pairs={{0,8},{24,16},{1,9},{25,17},{2,10},{26,18},{3,11},{27,19},{4,12},{... | collective-permute-start | bytes 6291464 | tf_op jit(solution)/shard_map/ppermute | solution.py:574
  302.4 25.0 %copy-start.7 = (bf16[1024,1024]{1,0:T(8,128)(2,1)S(1)}, bf16[1024,1024]{1,0:T(8,128)(2,1)}, u32[]{:S(2)}) copy-start(bf16[1024,1024]{1,0:T(8,128)(2,1)} %get-tuple-element.287) | copy-start | bytes 6291460
  331.4 62.9 %collective-permute-start.24 = (bf16[1024,1024]{1,0:T(8,128)(2,1)}, bf16[1024,1024]{1,0:T(8,128)(2,1)}, u32[]{:S(2)}, u32[]{:S(2)}) collective-permute-start(bf16[1024,1024]{1,0:T(8,128)(2,1)} %add_convert_fusion.6), channel_id=1, source_target_pairs={{8,16},{16,8},{9,17},{17,9},{10,18},{18,10},{11,19},{19,11},{12,20... | collective-permute-start | bytes 6291464 | tf_op jit(solution)/shard_map/ppermute | solution.py:574
  359.2 63.9 %collective-permute-start.23 = (bf16[512,2048]{1,0:T(8,128)(2,1)}, bf16[512,2048]{1,0:T(8,128)(2,1)}, u32[]{:S(2)}, u32[]{:S(2)}) collective-permute-start(bf16[512,2048]{1,0:T(8,128)(2,1)} %add_convert_fusion.5.kept_ref), channel_id=1, source_target_pairs={{8,0},{16,24},{9,1},{17,25},{10,2},{18,26},{11,3},{19,27},{12,4},{... | collective-permute-start | bytes 6291464 | tf_op jit(solution)/shard_map/ppermute | solution.py:574
  383.2 39.8 %collective-permute-start.22 = (bf16[1024,1024]{1,0:T(8,128)(2,1)S(1)}, bf16[1024,1024]{1,0:T(8,128)(2,1)}, u32[]{:S(2)}, u32[]{:S(2)}) collective-permute-start(bf16[1024,1024]{1,0:T(8,128)(2,1)S(1)} %add_convert_fusion.4), channel_id=1, source_target_pairs={{8,16},{16,8},{9,17},{17,9},{10,18},{18,10},{11,19},{19,11},{12,20... | collective-permute-start | bytes 6291464 | tf_op jit(solution)/shard_map/ppermute | solution.py:574
  385.2 51.2 %collective-permute-start.20 = (bf16[2,2048,256]{2,1,0:T(8,128)(2,1)S(1)}, bf16[2,2048,256]{2,1,0:T(8,128)(2,1)}, u32[]{:S(2)}, u32[]{:S(2)}) collective-permute-start(bf16[2,2048,256]{2,1,0:T(8,128)(2,1)S(1)} %copy-done.8), channel_id=1, source_target_pairs={{0,8},{24,16},{1,9},{25,17},{2,10},{26,18},{3,11},{27,19},{4,12},{... | collective-permute-start | bytes 6291464 | tf_op jit(solution)/shard_map/ppermute | solution.py:574
  398.8 104.6 %collective-permute-start.26 = (bf16[1024,1024]{1,0:T(8,128)(2,1)}, bf16[1024,1024]{1,0:T(8,128)(2,1)}, u32[]{:S(2)}, u32[]{:S(2)}) collective-permute-start(bf16[1024,1024]{1,0:T(8,128)(2,1)} %add_convert_fusion.3.kept_ref), channel_id=1, source_target_pairs={{8,0},{16,24},{9,1},{17,25},{10,2},{18,26},{11,3},{19,27},{12,4},{... | collective-permute-start | bytes 6291464 | tf_op jit(solution)/shard_map/ppermute | solution.py:574
  425.6 23.8 %copy-start.1 = (bf16[1024,1024]{1,0:T(8,128)(2,1)}, bf16[1024,1024]{1,0:T(8,128)(2,1)S(1)}, u32[]{:S(2)}) copy-start(bf16[1024,1024]{1,0:T(8,128)(2,1)S(1)} %add_convert_fusion.2.kept_ref) | copy-start | bytes 6291460
  425.6 16.4 %copy-start.12 = (bf16[2048,256]{1,0:T(8,128)(2,1)S(1)}, bf16[2048,256]{1,0:T(8,128)(2,1)}, u32[]{:S(2)}) copy-start(bf16[2048,256]{1,0:T(8,128)(2,1)} %get-tuple-element.334) | copy-start | bytes 3145732
  439.9 15.7 %copy-start.22 = (bf16[2048]{0:T(1024)(128)(2,1)S(1)}, bf16[2048]{0:T(1024)(128)(2,1)}, u32[]{:S(2)}) copy-start(bf16[2048]{0:T(1024)(128)(2,1)} %param.21) | copy-start | bytes 12292
  439.9 16.3 %copy-start.23 = (bf16[2048]{0:T(1024)(128)(2,1)S(1)}, bf16[2048]{0:T(1024)(128)(2,1)}, u32[]{:S(2)}) copy-start(bf16[2048]{0:T(1024)(128)(2,1)} %param.25) | copy-start | bytes 12292
  439.9 66.1 %collective-permute-start.25 = (bf16[2,2048,256]{2,1,0:T(8,128)(2,1)}, bf16[2,2048,256]{2,1,0:T(8,128)(2,1)}, u32[]{:S(2)}, u32[]{:S(2)}) collective-permute-start(bf16[2,2048,256]{2,1,0:T(8,128)(2,1)} %add_convert_fusion.1), channel_id=1, source_target_pairs={{8,16},{16,8},{9,17},{17,9},{10,18},{18,10},{11,19},{19,11},{12,20... | collective-permute-start | bytes 6291464 | tf_op jit(solution)/shard_map/ppermute | solution.py:574
  442.0 37.4 %collective-permute-start.27 = (bf16[2048,256]{1,0:T(8,128)(2,1)S(1)}, bf16[2048,256]{1,0:T(8,128)(2,1)}, u32[]{:S(2)}, u32[]{:S(2)}) collective-permute-start(bf16[2048,256]{1,0:T(8,128)(2,1)S(1)} %copy-done.12), channel_id=1, source_target_pairs={{0,8},{24,16},{1,9},{25,17},{2,10},{26,18},{3,11},{27,19},{4,12},{... | collective-permute-start | bytes 3145736 | tf_op jit(solution)/shard_map/ppermute | solution.py:574
  449.5 73.4 %collective-permute-start.30 = (bf16[1024,1024]{1,0:T(8,128)(2,1)S(1)}, bf16[1024,1024]{1,0:T(8,128)(2,1)}, u32[]{:S(2)}, u32[]{:S(2)}) collective-permute-start(bf16[1024,1024]{1,0:T(8,128)(2,1)S(1)} %add_convert_fusion.2.kept_ref), channel_id=1, source_target_pairs={{8,0},{16,24},{9,1},{17,25},{10,2},{18,26},{11,3},{19,27},{12,4},{... | collective-permute-start | bytes 6291464 | tf_op jit(solution)/shard_map/ppermute | solution.py:574
  450.7 61.4 %all-to-all-start = ((bf16[8,2,256,256]{3,2,1,0:T(8,128)(2,1)}), bf16[8,2,256,256]{3,2,1,0:T(8,128)(2,1)}, u32[]{:S(2)}, u32[]{:S(2)}) async-start(bf16[8,2,256,256]{3,2,1,0:T(8,128)(2,1)} %get-tuple-element.297), calls=%async_computation | async-start | bytes 4194304 | tf_op jit(solution)/shard_map/all_to_all | solution.py:828
  455.1 143.3 %reduce-scatter.5.cloned.1.call-start = ((), (), s32[]{:S(2)}) async-start(), calls=%async_computation.6 | async-start | bytes 18874368 | tf_op jit(solution)/shard_map/reduce_scatter | solution.py:841
  481.2 56.3 %collective-permute-start.36 = (bf16[2048,256]{1,0:T(8,128)(2,1)S(1)}, bf16[2048,256]{1,0:T(8,128)(2,1)}, u32[]{:S(2)}, u32[]{:S(2)}) collective-permute-start(bf16[2048,256]{1,0:T(8,128)(2,1)S(1)} %add_convert_fusion.13), channel_id=1, source_target_pairs={{8,16},{16,8},{9,17},{17,9},{10,18},{18,10},{11,19},{19,11},{12,20... | collective-permute-start | bytes 3145736 | tf_op jit(solution)/shard_map/ppermute | solution.py:574
  493.8 31.3 %collective-permute-start.29 = (bf16[256,2048]{1,0:T(8,128)(2,1)}, bf16[256,2048]{1,0:T(8,128)(2,1)}, u32[]{:S(2)}, u32[]{:S(2)}) collective-permute-start(bf16[256,2048]{1,0:T(8,128)(2,1)} %weight_grad.5), channel_id=1, source_target_pairs={{0,8},{24,16},{1,9},{25,17},{2,10},{26,18},{3,11},{27,19},{4,12},{... | collective-permute-start | bytes 3145736 | tf_op jit(solution)/shard_map/ppermute | solution.py:574
  510.8 49.3 %collective-permute-start.28 = (bf16[2,2048,256]{2,1,0:T(8,128)(2,1)}, bf16[2,2048,256]{2,1,0:T(8,128)(2,1)}, u32[]{:S(2)}, u32[]{:S(2)}) collective-permute-start(bf16[2,2048,256]{2,1,0:T(8,128)(2,1)} %add_convert_fusion), channel_id=1, source_target_pairs={{8,0},{16,24},{9,1},{17,25},{10,2},{18,26},{11,3},{19,27},{12,4},{... | collective-permute-start | bytes 6291464 | tf_op jit(solution)/shard_map/ppermute | solution.py:574
  512.1 10.7 %copy-start.18 = (f32[8,2048]{1,0:T(8,128)S(1)}, f32[8,2048]{1,0:T(8,128)}, u32[]{:S(2)}) copy-start(f32[8,2048]{1,0:T(8,128)} %get-tuple-element.349) | copy-start | bytes 196612
  512.2 10.7 %copy-start.19 = (f32[8,2048]{1,0:T(8,128)S(1)}, f32[8,2048]{1,0:T(8,128)}, u32[]{:S(2)}) copy-start(f32[8,2048]{1,0:T(8,128)} %get-tuple-element.350) | copy-start | bytes 196612
  512.2 10.8 %copy-start.20 = (bf16[2048]{0:T(1024)(128)(2,1)S(1)}, bf16[2048]{0:T(1024)(128)(2,1)}, u32[]{:S(2)}) copy-start(bf16[2048]{0:T(1024)(128)(2,1)} %param.16) | copy-start | bytes 12292
  527.1 21.5 %collective-permute-start.31 = (bf16[256,2048]{1,0:T(8,128)(2,1)S(1)}, bf16[256,2048]{1,0:T(8,128)(2,1)S(1)}, u32[]{:S(2)}, u32[]{:S(2)}) collective-permute-start(bf16[256,2048]{1,0:T(8,128)(2,1)S(1)} %add_convert_fusion.12), channel_id=1, source_target_pairs={{8,16},{16,8},{9,17},{17,9},{10,18},{18,10},{11,19},{19,11},{12,20... | collective-permute-start | bytes 3145736 | tf_op jit(solution)/shard_map/ppermute | solution.py:574
  527.8 1.3 collective-permute-start.32
  529.1 4.2 collective-permute-start.33
  533.3 4.2 collective-permute-start.34
  537.5 9.2 %collective-permute-start.35 = (f32[49,128]{1,0:T(8,128)S(1)}, f32[49,128]{1,0:T(8,128)S(1)}, u32[]{:S(2)}, u32[]{:S(2)}) collective-permute-start(f32[49,128]{1,0:T(8,128)S(1)} %pad_maximum_fusion), channel_id=1, source_target_pairs={{0,8},{24,16},{1,9},{25,17},{2,10},{26,18},{3,11},{27,19},{4,12},{... | collective-permute-start | bytes 75272 | tf_op jit(solution)/shard_map/ppermute | solution.py:574
  547.3 25.8 %collective-permute-start.37 = (f32[49,128]{1,0:T(8,128)}, f32[49,128]{1,0:T(8,128)}, u32[]{:S(2)}, u32[]{:S(2)}) collective-permute-start(f32[49,128]{1,0:T(8,128)} %add.146), channel_id=1, source_target_pairs={{8,16},{16,8},{9,17},{17,9},{10,18},{18,10},{11,19},{19,11},{12,20... | collective-permute-start | bytes 75272 | tf_op jit(solution)/shard_map/ppermute | solution.py:574
  573.9 14.8 %collective-permute-start.38 = (f32[49,128]{1,0:T(8,128)S(1)}, f32[49,128]{1,0:T(8,128)S(1)}, u32[]{:S(2)}, u32[]{:S(2)}) collective-permute-start(f32[49,128]{1,0:T(8,128)S(1)} %add.148), channel_id=1, source_target_pairs={{8,0},{16,24},{9,1},{17,25},{10,2},{18,26},{11,3},{19,27},{12,4},{... | collective-permute-start | bytes 75272 | tf_op jit(solution)/shard_map/ppermute | solution.py:574
  575.1 29.6 %collective-permute-start.39 = (bf16[2048,256]{1,0:T(8,128)(2,1)S(1)}, bf16[2048,256]{1,0:T(8,128)(2,1)}, u32[]{:S(2)}, u32[]{:S(2)}) collective-permute-start(bf16[2048,256]{1,0:T(8,128)(2,1)S(1)} %copy-done.6), channel_id=1, source_target_pairs={{8,0},{16,24},{9,1},{17,25},{10,2},{18,26},{11,3},{19,27},{12,4},{... | collective-permute-start | bytes 3145736 | tf_op jit(solution)/shard_map/ppermute | solution.py:574
  576.4 47.1 %collective-permute-start.40 = (bf16[256,2048]{1,0:T(8,128)(2,1)}, bf16[256,2048]{1,0:T(8,128)(2,1)}, u32[]{:S(2)}, u32[]{:S(2)}) collective-permute-start(bf16[256,2048]{1,0:T(8,128)(2,1)} %add_convert_fusion.10.kept_ref), channel_id=1, source_target_pairs={{8,0},{16,24},{9,1},{17,25},{10,2},{18,26},{11,3},{19,27},{12,4},{... | collective-permute-start | bytes 3145736 | tf_op jit(solution)/shard_map/ppermute | solution.py:574
  581.9 16.5 %copy-start = (bf16[2,256,2048]{2,1,0:T(8,128)(2,1)S(1)}, bf16[2,256,2048]{2,1,0:T(8,128)(2,1)}, u32[]{:S(2)}) copy-start(bf16[2,256,2048]{2,1,0:T(8,128)(2,1)} %param.14) | copy-start | bytes 6291460
  588.7 37.8 %copy-start.24 = (f32[256]{0:T(256)}, f32[256]{0:T(256)S(1)}, u32[]{:S(2)}) copy-start(f32[256]{0:T(256)S(1)} %slice_bitcast_fusion.3) | copy-start | bytes 3076
  (9 other events, 33.2 us)
Sparse Core Ops, SparseCore 0:
  66.0 107.4 all-gather.2
  175.5 54.3 all-gather.4
  302.5 114.0 reduce-scatter.2
  479.5 118.8 reduce-scatter.4

commit v8 on v7

--- a/solution.py
+++ b/solution.py
@@ -81,6 +81,33 @@
         cost_estimate=SMALL,
         name="norm_halves",
     )(x, gain[None], shift[None])
+
+
+def norm_back_kernel(back_ref, x_ref, g_ref, gain_ref, o_ref):
+    x = x_ref[...].astype(f32)
+    center = x - jnp.mean(x, axis=-1, keepdims=True)
+    inverse = lax.rsqrt(jnp.mean(center * center, axis=-1, keepdims=True) + epsilon)
+    unit = center * inverse
+    unit_grad = back_ref[...].astype(f32) * gain_ref[...]
+    mean_grad = jnp.mean(unit_grad, axis=-1, keepdims=True)
+    mean_both = jnp.mean(unit_grad * unit, axis=-1, keepdims=True)
+    value_grad = (unit_grad - mean_grad - unit * mean_both) * inverse
+    o_ref[...] = (g_ref[...].astype(f32) + value_grad).astype(bf16)
+
+
+def norm_back(back, x, g, gain, tm=128):
+    n, width = x.shape
+    block = pl.BlockSpec((tm, width), lambda i: (i, 0))
+    return pl.pallas_call(
+        norm_back_kernel,
+        grid=(n // tm,),
+        in_specs=[block, block, block, pl.BlockSpec((1, width), lambda i: (0, 0))],
+        out_specs=block,
+        out_shape=jax.ShapeDtypeStruct((n, width), bf16),
+        compiler_params=params(),
+        cost_estimate=SMALL,
+        name="norm_back",
+    )(back, x, g, gain[None])
 
 
 def table_kernel(place_ref, frequency_ref, c_ref, s_ref):
@@ -882,21 +909,12 @@
     in_grad = finish(i1, order, width, width // 2, in_grad)
     qkv_grad = finish(qs, order, 3 * width)
 
-    def norm_back(back_tok, tokens, cotangent):
-        values = tokens.astype(f32)
-        center = values - jnp.mean(values, axis=-1, keepdims=True)
-        inverse = lax.rsqrt(jnp.mean(center * center, axis=-1, keepdims=True) + epsilon)
-        unit = center * inverse
-        unit_grad = back_tok.astype(f32) * gain
-        mean_grad = jnp.mean(unit_grad, axis=-1, keepdims=True)
-        mean_both = jnp.mean(unit_grad * unit, axis=-1, keepdims=True)
-        value_grad = (unit_grad - mean_grad - unit * mean_both) * inverse
-        return (cotangent.astype(f32) + value_grad).astype(bf16)
-
-    input_grad = order(norm_back, back_tok, tokens, cotangent)
+    token_back = lambda b, t, c: norm_back(rows_of(b), rows_of(t), rows_of(c), gain).reshape(tokens.shape)
+    input_grad = order(token_back, back_tok, tokens, cotangent)
     qkv_grad = finish(vs, order, 3 * width, 2 * width, qkv_grad)
     qkv_grad = jnp.transpose(qkv_grad.reshape(3, width, local), (1, 0, 2))
     dense_grad = finish(ds, order, local)
+    small.settle(order)
     small = small.result().reshape(-1)
     slice_at = lambda a: lax.dynamic_slice_in_dim(a, lax.axis_index("tp") * cols, cols, 0)
     gain_grad, shift_grad = slice_at(small[:width]), slice_at(small[width : 2 * width])

time: 644 us -> 631 us (0.980)
  waiting for transfers between devices: 97.1 us -> 75.8 us
  Pallas kernels: 358 us -> 367 us
    ppermute x24, waiting for transfers between devices: 40.1 us -> 18 us  [send(): self.came = lax.ppermute(self.part, self.axis, self.hops.pop(0))]
    reduce_scatter x1, starting transfers between devices: 0.45 us -> 8.52 us  [body(): lax.psum_scatter(part.reshape(seqs, length, width), 'tp', scatter_dimensi...]
  transfers between devices with their start and end apart: 46 -> 46, of which waited for: 19 -> 18; matrix products, arithmetic and copies ran while one was open for 10% -> 9% of each run, Pallas kernels for 55% -> 58%
where the time goes in v8:
time: 631 us; the launch traced here: 621 us
  Pallas kernels  367 us (58%)
  starting transfers between devices  100 us (16%)
  waiting for transfers between devices  75.8 us (12%)
  other arithmetic  53.8 us (9%)
  between operations  14.7 us (2%)
  local copies, waits for them, and re-layouts  8.71 us (1%)
    ppermute x24, starting transfers between devices, send(): self.came = lax.ppermute(self.part, self.axis, self.hops.pop(0))  75.5 us
    pallas_call x2, Pallas kernels, normed_grad(): pl.pallas_call(functools.partial(normed_grad_kernel, held=held), grid=(st...  45.6 us
    pallas_call x2, Pallas kernels, attention_both(): pl.pallas_call(functools.partial(attention_kernel, bq=bq, held=held), gri...  44.7 us
    ppermute x14, waiting for transfers between devices, send(): return lax.ppermute(a, 'tp', [(i, i ^ step) for i in range(self.size)])  44 us
    convert_element_type x14, other arithmetic, fold(): add = lambda a, b: (a.astype(f32) + b.astype(f32)).astype(a.dtype)  42 us
    pallas_call x3, Pallas kernels, weight_grad(): pl.pallas_call(weight_grad_kernel, grid=(cols // tile,), in_specs=[pl.Blo...  40.7 us
    pallas_call x2, Pallas kernels, mlp_hidden_of(): pl.pallas_call(functools.partial(chosen_kernel, held=held), grid_spec=plt...  36 us
    pallas_call x7, Pallas kernels, finish(): call(inner, *a)  30.4 us
  transfers between devices with their start and end apart: 46, of which 18 were waited for; matrix products, arithmetic and copies ran while one was open for 9% of the time, Pallas kernels for 58%

profile of v8, /device:TPU:0, one launch (start us, length us, event | category | flops | bytes accessed | tf_op | source)
XLA Modules:
  0.0 620.7 jit_solution(1825017224167675610)
XLA Ops:
  9.8 4.7 norm_halves.1
  14.6 3.0 collective-permute-start.1
  22.2 9.8 %rope_tables.1 = (f32[4096,128]{1,0:T(8,128)}, f32[4096,128]{1,0:T(8,128)}) custom-call(s32[4096,1]{1,0:T(8,128)} %bitcast.75, f32[1,128]{1,0:T(1,128)} %fusion.4.frequency_ref), custom_call_target="tpu_custom_call" | custom-call | flops 1 | bytes 1 | tf_op jit(solution)/shard_map/rope_tables/pallas_call | solution.py:126
  32.6 9.1 %collective-permute-done.1.refs_7_ = bf16[256,2048]{1,0:T(8,128)(2,1)S(1)} collective-permute-done((bf16[256,2048]{1,0:T(8,128)(2,1)}, bf16[256,2048]{1,0:T(8,128)(2,1)S(1)}, u32[]{:S(2)}, u32[]{:S(2)}) %collective-permute-start.1) | collective-permute-done | bytes 1048608 | tf_op jit(solution)/shard_map/ppermute | solution.py:671
  43.7 22.2 %collective-permute-done.3.refs_5_ = bf16[256,2048]{1,0:T(8,128)(2,1)} collective-permute-done((bf16[256,2048]{1,0:T(8,128)(2,1)}, bf16[256,2048]{1,0:T(8,128)(2,1)}, u32[]{:S(2)}, u32[]{:S(2)}) %collective-permute-start.3) | collective-permute-done | bytes 1048608 | tf_op jit(solution)/shard_map/ppermute | solution.py:671
  67.3 2.1 collective-permute-done.6.refs_8_
  73.5 13.1 %place_pieces.2.refs_0_ = bf16[2,8,256,2048]{3,2,1,0:T(8,128)(2,1)} custom-call(s32[1]{0:T(128)} %bitcast.3.me_ref, bf16[256,2048]{1,0:T(8,128)(2,1)} %get-tuple-element.218.refs_0_, bf16[256,2048]{1,0:T(8,128)(2,1)} %get-tuple-element.219.refs_1_, bf16[256,2048]{1,0:T(8,128)(2,1)} %collective-permute-done.2.refs_2_, ...), custom_call_target="tpu_custom_call" | custom-call | flops 1 | bytes 1 | tf_op jit(solution)/shard_map/place_pieces/pallas_call | solution.py:732
  86.6 23.6 %mlp_hidden_of.2 = (bf16[2,8,256,1024]{3,2,1,0:T(8,128)(2,1)}, bf16[2,8,256,1024]{3,2,1,0:T(8,128)(2,1)}) custom-call(s32[1]{0:T(128)} %bitcast.3.me_ref, bf16[2,8,256,2048]{3,2,1,0:T(8,128)(2,1)} %place_pieces.2.refs_0_, bf16[2048,1024]{1,0:T(8,128)(2,1)} %refs_3_.1, f32[1,1024]{1,0:T(1,128)} %bitcast.89), custom_call_target="tpu_custom_call" | custom-call | flops 1 | bytes 1 | tf_op jit(solution)/shard_map/mlp_hidden_of/pallas_call | solution.py:207
  110.2 3.7 collective-permute-done.11.refs_2_
  114.5 3.6 collective-permute-done.12.refs_3_
  120.1 4.8 place_pieces.3.refs_2_
  124.8 12.4 %mlp_hidden_of.3 = (bf16[2,8,256,1024]{3,2,1,0:T(8,128)(2,1)}, bf16[2,8,256,1024]{3,2,1,0:T(8,128)(2,1)}) custom-call(s32[1]{0:T(128)} %bitcast.3.me_ref, bf16[2,8,256,1024]{3,2,1,0:T(8,128)(2,1)} %get-tuple-element.242.refs_0_, bf16[2,8,256,1024]{3,2,1,0:T(8,128)(2,1)} %get-tuple-element.243.refs_1_, ...), custom_call_target="tpu_custom_call", output_to_operand_aliasing={{0}: (1, {}), {1}: (2, {})} | custom-call | flops 1 | bytes 1 | tf_op jit(solution)/shard_map/mlp_hidden_of/pallas_call | solution.py:207
  138.1 20.0 %qkv_rope.1.refs_1_.refs_2_.refs_3_.refs_4_.refs_5_.refs_6_ = bf16[3,4096,256]{2,1,0:T(8,128)(2,1)} custom-call(bf16[4096,2048]{1,0:T(8,128)(2,1)} %bitcast.49, bf16[3,2048,256]{2,1,0:T(8,128)(2,1)} %bitcast.66, f32[3,256]{1,0:T(4,128)} %convert_element_type.158.b_ref, f32[4096,128]{1,0:T(8,128)} %get-tuple-element.296.c_ref.refs_5_.refs_8_, ...), custom_call_target="tpu_custom_call" | custom-call | flops 1 | bytes 1 | tf_op jit(solution)/shard_map/qkv_rope/pallas_call | solution.py:158
  158.2 13.3 %tokens_by_weight.2.refs_0_ = bf16[4096,2048]{1,0:T(8,128)(2,1)} custom-call(bf16[4096,1024]{1,0:T(8,128)(2,1)} %bitcast.59, bf16[1024,2048]{1,0:T(8,128)(2,1)} %refs_2_), custom_call_target="tpu_custom_call" | custom-call | flops 1 | bytes 1 | tf_op jit(solution)/shard_map/tokens_by_weight/pallas_call | solution.py:287
  171.4 2.2 all-gather.3.cloned.1.call-done
  173.6 14.2 %weight_grad.3 = bf16[512,2048]{1,0:T(8,128)(2,1)} custom-call(bf16[4096,1024]{1,0:T(8,128)(2,1)} %bitcast.60, bf16[4096,2048]{1,0:T(8,128)(2,1)} %bitcast.54), custom_call_target="tpu_custom_call" | custom-call | flops 1 | bytes 1 | tf_op jit(solution)/shard_map/weight_grad/pallas_call | solution.py:310
  187.8 3.5 collective-permute-start.14
  191.3 13.8 %weight_grad.4 = bf16[512,2048]{1,0:T(8,128)(2,1)} custom-call(bf16[4096,1024]{1,0:T(8,128)(2,1)} %bitcast.61, bf16[4096,2048]{1,0:T(8,128)(2,1)} %bitcast.55), custom_call_target="tpu_custom_call" | custom-call | flops 1 | bytes 1 | tf_op jit(solution)/shard_map/weight_grad/pallas_call | solution.py:310
  205.1 2.7 collective-permute-start.16
  207.8 29.6 %grad_in.1 = (bf16[4096,1024]{1,0:T(8,128)(2,1)}, bf16[4096,256]{1,0:T(8,128)(2,1)}, f32[8,1024]{1,0:T(8,128)}) custom-call(bf16[4096,2048]{1,0:T(8,128)(2,1)} %bitcast.56, bf16[1024,2048]{1,0:T(8,128)(2,1)} %refs_2_, bf16[256,2048]{1,0:T(8,128)(2,1)} %wd_ref, bf16[4096,1024]{1,0:T(8,128)(2,1)} %bitcast.65), custom_call_target="tpu_custom_call" | custom-call | flops 1 | bytes 1 | tf_op jit(solution)/shard_map/grad_in/pallas_call | solution.py:248
  240.4 24.6 %weight_grad_rows.1 = (bf16[1024,1024]{1,0:T(8,128)(2,1)}, bf16[1024,1024]{1,0:T(8,128)(2,1)}) custom-call(bf16[4096,2048]{1,0:T(8,128)(2,1)} %bitcast.50, bf16[4096,1024]{1,0:T(8,128)(2,1)} %get-tuple-element.327.b_ref.refs_0_.refs_1_), custom_call_target="tpu_custom_call" | custom-call | flops 1 | bytes 1 | tf_op jit(solution)/shard_map/weight_grad_rows/pallas_call | solution.py:344
  265.0 7.0 %collective-permute-start.17 = (bf16[1024,1024]{1,0:T(8,128)(2,1)}, bf16[1024,1024]{1,0:T(8,128)(2,1)}, u32[]{:S(2)}, u32[]{:S(2)}) collective-permute-start(bf16[1024,1024]{1,0:T(8,128)(2,1)} %get-tuple-element.288), channel_id=1, source_target_pairs={{0,8},{24,16},{1,9},{25,17},{2,10},{26,18},{3,11},{27,19},{4,12},{... | collective-permute-start | bytes 6291464 | tf_op jit(solution)/shard_map/ppermute | solution.py:601
  272.0 13.4 %tokens_by_weight.3 = bf16[4096,2048]{1,0:T(8,128)(2,1)} custom-call(bf16[4096,2048]{1,0:T(8,128)(2,1)} %tokens_by_weight.2.refs_0_, bf16[4096,1024]{1,0:T(8,128)(2,1)} %bitcast.62, bf16[1024,2048]{1,0:T(8,128)(2,1)} %refs_2_), custom_call_target="tpu_custom_call", output_to_operand_aliasing={{}: (0, {})} | custom-call | flops 1 | bytes 1 | tf_op jit(solution)/shard_map/tokens_by_weight/pallas_call | solution.py:287
  285.4 2.4 add_convert_fusion.8
  287.8 2.1 collective-permute-start.19
  289.9 3.8 add_convert_fusion.7.kept_ref
  295.0 7.2 %collective-permute-start.21 = (bf16[1024,1024]{1,0:T(8,128)(2,1)}, bf16[1024,1024]{1,0:T(8,128)(2,1)}, u32[]{:S(2)}, u32[]{:S(2)}) collective-permute-start(bf16[1024,1024]{1,0:T(8,128)(2,1)} %get-tuple-element.309), channel_id=1, source_target_pairs={{0,8},{24,16},{1,9},{25,17},{2,10},{26,18},{3,11},{27,19},{4,12},{... | collective-permute-start | bytes 6291464 | tf_op jit(solution)/shard_map/ppermute | solution.py:601
  302.2 8.5 %reduce-scatter.5.cloned.1.call-start = ((), (), s32[]{:S(2)}) async-start(), calls=%async_computation.6 | async-start | bytes 18874368 | tf_op jit(solution)/shard_map/reduce_scatter | solution.py:868
  310.8 22.6 %attention_both.2 = (bf16[4096,256]{1,0:T(8,128)(2,1)}, bf16[8,2,256,256]{3,2,1,0:T(8,128)(2,1)}, bf16[3,4096,256]{2,1,0:T(8,128)(2,1)}) custom-call(s32[1,4096]{1,0:T(1,128)} %fusion.refs_0_.refs_3_, bf16[3,4096,256]{2,1,0:T(8,128)(2,1)} %qkv_rope.1.refs_1_.refs_2_.refs_3_.refs_4_.refs_5_.refs_6_, ...), custom_call_target="tpu_custom_call" | custom-call | flops 1 | bytes 1 | tf_op jit(solution)/shard_map/attention_both/pallas_call | solution.py:507
  333.4 3.9 add_convert_fusion.6
  339.4 22.1 %attention_both.3 = (bf16[4096,256]{1,0:T(8,128)(2,1)}, bf16[8,2,256,256]{3,2,1,0:T(8,128)(2,1)}, bf16[3,4096,256]{2,1,0:T(8,128)(2,1)}) custom-call(bf16[4096,256]{1,0:T(8,128)(2,1)} %get-tuple-element.290.refs_0_, bf16[8,2,256,256]{3,2,1,0:T(8,128)(2,1)} %get-tuple-element.291.refs_1_, ...), custom_call_target="tpu_custom_call", output_to_operand_aliasing={{0}: (0, {}), {1}: (1, {}), {2}: (2, {})} | custom-call | flops 1 | bytes 1 | tf_op jit(solution)/shard_map/attention_both/pallas_call | solution.py:507
  361.5 3.7 add_convert_fusion.5.kept_ref
  366.7 19.2 %weight_grad_parts.1 = (bf16[2,2048,256]{2,1,0:T(8,128)(2,1)}, bf16[2048,256]{1,0:T(8,128)(2,1)}) custom-call(bf16[4096,2048]{1,0:T(8,128)(2,1)} %bitcast.51, bf16[3,4096,256]{2,1,0:T(8,128)(2,1)} %get-tuple-element.328.b_ref.refs_1_.refs_2_), custom_call_target="tpu_custom_call" | custom-call | flops 219999993856 | bytes 1 | tf_op jit(solution)/shard_map/weight_grad_parts/pallas_call | solution.py:368
  385.9 3.3 add_convert_fusion.4
  391.2 7.9 %collective-permute-start.20 = (bf16[2,2048,256]{2,1,0:T(8,128)(2,1)S(1)}, bf16[2,2048,256]{2,1,0:T(8,128)(2,1)}, u32[]{:S(2)}, u32[]{:S(2)}) collective-permute-start(bf16[2,2048,256]{2,1,0:T(8,128)(2,1)S(1)} %copy-done.5), channel_id=1, source_target_pairs={{0,8},{24,16},{1,9},{25,17},{2,10},{26,18},{3,11},{27,19},{4,12},{... | collective-permute-start | bytes 6291464 | tf_op jit(solution)/shard_map/ppermute | solution.py:601
  399.1 3.4 add_convert_fusion.3.kept_ref
  403.9 23.0 %normed_grad.2 = (bf16[4096,2048]{1,0:T(8,128)(2,1)}, f32[3,8,256]{2,1,0:T(8,128)}, f32[8,2048]{1,0:T(8,128)}) custom-call(bf16[4096,1024]{1,0:T(8,128)(2,1)} %get-tuple-element.327.b_ref.refs_0_.refs_1_, bf16[3,4096,256]{2,1,0:T(8,128)(2,1)} %get-tuple-element.328.b_ref.refs_1_.refs_2_, bf16[2048,1024]{1,0:T(8,128)(2,1)} %refs_3_.1, ...), custom_call_target="tpu_custom_call" | custom-call | flops 1 | bytes 1 | tf_op jit(solution)/shard_map/normed_grad/pallas_call | solution.py:412
  426.9 3.9 add_convert_fusion.2.kept_ref
  430.7 9.0 %collective-permute-done.20 = bf16[2,2048,256]{2,1,0:T(8,128)(2,1)} collective-permute-done((bf16[2,2048,256]{2,1,0:T(8,128)(2,1)S(1)}, bf16[2,2048,256]{2,1,0:T(8,128)(2,1)}, u32[]{:S(2)}, u32[]{:S(2)}) %collective-permute-start.20) | collective-permute-done | bytes 2097184 | tf_op jit(solution)/shard_map/ppermute | solution.py:601
  439.7 3.4 add_convert_fusion.1
  445.1 7.8 %collective-permute-start.27 = (bf16[2048,256]{1,0:T(8,128)(2,1)S(1)}, bf16[2048,256]{1,0:T(8,128)(2,1)}, u32[]{:S(2)}, u32[]{:S(2)}) collective-permute-start(bf16[2048,256]{1,0:T(8,128)(2,1)S(1)} %copy-done.9), channel_id=1, source_target_pairs={{0,8},{24,16},{1,9},{25,17},{2,10},{26,18},{3,11},{27,19},{4,12},{... | collective-permute-start | bytes 3145736 | tf_op jit(solution)/shard_map/ppermute | solution.py:601
  454.5 22.6 %normed_grad.3 = (bf16[4096,2048]{1,0:T(8,128)(2,1)}, f32[3,8,256]{2,1,0:T(8,128)}, f32[8,2048]{1,0:T(8,128)}) custom-call(bf16[4096,2048]{1,0:T(8,128)(2,1)} %get-tuple-element.326.refs_0_, bf16[4096,1024]{1,0:T(8,128)(2,1)} %get-tuple-element.327.b_ref.refs_0_.refs_1_, ...), custom_call_target="tpu_custom_call", output_to_operand_aliasing={{0}: (0, {})} | custom-call | flops 1 | bytes 1 | tf_op jit(solution)/shard_map/normed_grad/pallas_call | solution.py:412
  477.1 4.4 all-to-all-start
  486.2 12.7 %weight_grad.5 = bf16[256,2048]{1,0:T(8,128)(2,1)} custom-call(bf16[4096,256]{1,0:T(8,128)(2,1)} %get-tuple-element.337.a_ref, bf16[4096,2048]{1,0:T(8,128)(2,1)} %bitcast.57), custom_call_target="tpu_custom_call" | custom-call | flops 1 | bytes 1 | tf_op jit(solution)/shard_map/weight_grad/pallas_call | solution.py:310
  498.9 8.8 %collective-permute-start.29 = (bf16[256,2048]{1,0:T(8,128)(2,1)}, bf16[256,2048]{1,0:T(8,128)(2,1)}, u32[]{:S(2)}, u32[]{:S(2)}) collective-permute-start(bf16[256,2048]{1,0:T(8,128)(2,1)} %weight_grad.5), channel_id=1, source_target_pairs={{0,8},{24,16},{1,9},{25,17},{2,10},{26,18},{3,11},{27,19},{4,12},{... | collective-permute-start | bytes 3145736 | tf_op jit(solution)/shard_map/ppermute | solution.py:601
  507.7 2.1 convert_reduce_fusion
  509.9 2.8 add_convert_fusion
  514.0 11.2 %project_own.1 = (bf16[512,2048]{1,0:T(8,128)(2,1)}, f32[8,512]{1,0:T(8,128)}) custom-call(bf16[8,2,256,256]{3,2,1,0:T(8,128)(2,1)} %all-to-all-done.x_ref, bf16[2048,2048]{1,0:T(8,128)(2,1)} %all-gather.5.cloned.1.call-done.w_ref, f32[1,2048]{1,0:T(1,128)} %bitcast.91, f32[1,2048]{1,0:T(1,128)} %bitcast.92, bf16[512,2048]{1,0:T(8,128)(2,1)} %bitcast.71, ...), custom_call_target="tpu_custom_call" | custom-call | flops 1 | bytes 1 | tf_op jit(solution)/shard_map/project_own/pallas_call | solution.py:563
  526.2 3.4 collective-permute-done.29
  529.6 3.1 add_convert_fusion.12
  541.3 2.6 collective-permute-done.34
  543.9 5.2 collective-permute-start.35
  549.1 2.5 add_convert_fusion.11.kept_ref
  554.7 3.1 add_convert_fusion.10.kept_ref
  559.1 4.1 collective-permute-done.28
  563.2 4.6 finish.7.refs_0_
  567.8 4.9 finish.8
  572.7 3.7 finish.9.refs_0_
  578.5 3.9 finish.10
  582.3 6.6 %finish.11.refs_0_ = f32[6144,256]{1,0:T(8,128)} custom-call(s32[1]{0:T(128)} %bitcast.17.inner_ref, bf16[4096,256]{1,0:T(8,128)(2,1)} %bitcast.74, bf16[4096,256]{1,0:T(8,128)(2,1)} %bitcast.24.came_ref), custom_call_target="tpu_custom_call" | custom-call | flops 1 | bytes 1 | tf_op jit(solution)/shard_map/finish/pallas_call | solution.py:660
  588.9 6.7 %reduce-scatter.5.cloned.1.call-done = bf16[2,256,2048]{2,1,0:T(8,128)(2,1)} async-done(((bf16[2,2048,2048]{2,1,0:T(8,128)(2,1)}), bf16[2,256,2048]{2,1,0:T(8,128)(2,1)}) %reduce-scatter.5.cloned.1.call-update) | async-done | bytes 2097168 | tf_op jit(solution)/shard_map/reduce_scatter | solution.py:868
  595.6 6.3 %norm_back.1 = bf16[512,2048]{1,0:T(8,128)(2,1)} custom-call(bf16[512,2048]{1,0:T(8,128)(2,1)} %bitcast.76, bf16[512,2048]{1,0:T(8,128)(2,1)} %bitcast.72, bf16[512,2048]{1,0:T(8,128)(2,1)} %bitcast.73, f32[1,2048]{1,0:T(1,128)} %bitcast.88), custom_call_target="tpu_custom_call" | custom-call | flops 1 | bytes 1 | tf_op jit(solution)/shard_map/norm_back/pallas_call | solution.py:101
  601.9 3.8 finish.12
  607.1 3.0 finish.13
  (157 shorter events, 60.5 us)
Async XLA Ops:
  7.2 12.4 %copy-start.17 = (s32[2,2048]{1,0:T(2,128)S(1)}, s32[2,2048]{1,0:T(2,128)}, u32[]{:S(2)}) copy-start(s32[2,2048]{1,0:T(2,128)} %param.15) | copy-start | bytes 49156
  7.2 166.4 %all-gather.3.cloned.1.call-start = ((), (), s32[]{:S(2)}) async-start(), calls=%async_computation.3 | async-start | bytes 18874368 | tf_op jit(solution)/shard_map/all_gather | solution.py:815
  14.6 27.2 %collective-permute-start.1 = (bf16[256,2048]{1,0:T(8,128)(2,1)}, bf16[256,2048]{1,0:T(8,128)(2,1)S(1)}, u32[]{:S(2)}, u32[]{:S(2)}) collective-permute-start(bf16[256,2048]{1,0:T(8,128)(2,1)} %get-tuple-element.219.refs_1_), channel_id=1, source_target_pairs={{0,4},{1,5},{2,6},{3,7},{4,0},{5,1},{6,2},{7,3},{8,12},{9,13},{10,... | collective-permute-start | bytes 3145736 | tf_op jit(solution)/shard_map/ppermute | solution.py:671
  17.5 24.2 %collective-permute-start.2 = (bf16[256,2048]{1,0:T(8,128)(2,1)}, bf16[256,2048]{1,0:T(8,128)(2,1)}, u32[]{:S(2)}, u32[]{:S(2)}) collective-permute-start(bf16[256,2048]{1,0:T(8,128)(2,1)} %get-tuple-element.218.refs_0_), channel_id=1, source_target_pairs={{0,1},{1,0},{2,3},{3,2},{4,5},{5,4},{6,7},{7,6},{8,9},{9,8},{10,11... | collective-permute-start | bytes 3145736 | tf_op jit(solution)/shard_map/ppermute | solution.py:671
  17.5 26.2 %collective-permute-start = (bf16[256,2048]{1,0:T(8,128)(2,1)}, bf16[256,2048]{1,0:T(8,128)(2,1)S(1)}, u32[]{:S(2)}, u32[]{:S(2)}) collective-permute-start(bf16[256,2048]{1,0:T(8,128)(2,1)} %get-tuple-element.218.refs_0_), channel_id=1, source_target_pairs={{0,2},{1,3},{2,0},{3,1},{4,6},{5,7},{6,4},{7,5},{8,10},{9,11},{10,... | collective-permute-start | bytes 3145736 | tf_op jit(solution)/shard_map/ppermute | solution.py:671
  19.0 46.9 %collective-permute-start.3 = (bf16[256,2048]{1,0:T(8,128)(2,1)}, bf16[256,2048]{1,0:T(8,128)(2,1)}, u32[]{:S(2)}, u32[]{:S(2)}) collective-permute-start(bf16[256,2048]{1,0:T(8,128)(2,1)} %get-tuple-element.219.refs_1_), channel_id=1, source_target_pairs={{0,2},{1,3},{2,0},{3,1},{4,6},{5,7},{6,4},{7,5},{8,10},{9,11},{10,... | collective-permute-start | bytes 3145736 | tf_op jit(solution)/shard_map/ppermute | solution.py:671
  19.5 46.3 %collective-permute-start.4 = (bf16[256,2048]{1,0:T(8,128)(2,1)}, bf16[256,2048]{1,0:T(8,128)(2,1)}, u32[]{:S(2)}, u32[]{:S(2)}) collective-permute-start(bf16[256,2048]{1,0:T(8,128)(2,1)} %get-tuple-element.218.refs_0_), channel_id=1, source_target_pairs={{0,4},{1,5},{2,6},{3,7},{4,0},{5,1},{6,2},{7,3},{8,12},{9,13},{10,... | collective-permute-start | bytes 3145736 | tf_op jit(solution)/shard_map/ppermute | solution.py:671
  19.6 24.0 %copy-start.7 = (bf16[256,2048]{1,0:T(8,128)(2,1)S(1)}, bf16[256,2048]{1,0:T(8,128)(2,1)}, u32[]{:S(2)}) copy-start(bf16[256,2048]{1,0:T(8,128)(2,1)} %get-tuple-element.219.refs_1_) | copy-start | bytes 3145732
  22.2 49.7 %copy-start.21 = (bf16[1024]{0:T(1024)(128)(2,1)S(1)}, bf16[1024]{0:T(1024)(128)(2,1)}, u32[]{:S(2)}) copy-start(bf16[1024]{0:T(1024)(128)(2,1)} %param.23) | copy-start | bytes 6148
  41.7 31.8 %copy-start.6 = (bf16[256,2048]{1,0:T(8,128)(2,1)}, bf16[256,2048]{1,0:T(8,128)(2,1)S(1)}, u32[]{:S(2)}) copy-start(bf16[256,2048]{1,0:T(8,128)(2,1)S(1)} %collective-permute-done.1.refs_7_) | copy-start | bytes 3145732
  43.7 29.8 %copy-start.8 = (bf16[256,2048]{1,0:T(8,128)(2,1)}, bf16[256,2048]{1,0:T(8,128)(2,1)S(1)}, u32[]{:S(2)}) copy-start(bf16[256,2048]{1,0:T(8,128)(2,1)S(1)} %collective-permute-done.refs_4_) | copy-start | bytes 3145732
  43.7 22.2 %collective-permute-start.5 = (bf16[256,2048]{1,0:T(8,128)(2,1)S(1)}, bf16[256,2048]{1,0:T(8,128)(2,1)}, u32[]{:S(2)}, u32[]{:S(2)}) collective-permute-start(bf16[256,2048]{1,0:T(8,128)(2,1)S(1)} %copy-done.7), channel_id=1, source_target_pairs={{0,1},{1,0},{2,3},{3,2},{4,5},{5,4},{6,7},{7,6},{8,9},{9,8},{10,11... | collective-permute-start | bytes 3145736 | tf_op jit(solution)/shard_map/ppermute | solution.py:671
  65.9 448.0 %all-gather.5.cloned.1.call-start = ((), (), s32[]{:S(2)}) async-start(), calls=%async_computation.4 | async-start | bytes 9437184 | tf_op jit(solution)/shard_map/all_gather | solution.py:837
  66.0 3.4 collective-permute-start.6
  66.0 6.4 %collective-permute-start.7 = (bf16[256,2048]{1,0:T(8,128)(2,1)}, bf16[256,2048]{1,0:T(8,128)(2,1)}, u32[]{:S(2)}, u32[]{:S(2)}) collective-permute-start(bf16[256,2048]{1,0:T(8,128)(2,1)} %collective-permute-done.3.refs_5_), channel_id=1, source_target_pairs={{0,1},{1,0},{2,3},{3,2},{4,5},{5,4},{6,7},{7,6},{8,9},{9,8},{10,11... | collective-permute-start | bytes 3145736 | tf_op jit(solution)/shard_map/ppermute | solution.py:671
  66.5 7.0 %collective-permute-start.8 = (bf16[256,2048]{1,0:T(8,128)(2,1)}, bf16[256,2048]{1,0:T(8,128)(2,1)}, u32[]{:S(2)}, u32[]{:S(2)}) collective-permute-start(bf16[256,2048]{1,0:T(8,128)(2,1)} %collective-permute-done.4.refs_6_), channel_id=1, source_target_pairs={{0,1},{1,0},{2,3},{3,2},{4,5},{5,4},{6,7},{7,6},{8,9},{9,8},{10,11... | collective-permute-start | bytes 3145736 | tf_op jit(solution)/shard_map/ppermute | solution.py:671
  66.6 6.9 %collective-permute-start.9 = (bf16[256,2048]{1,0:T(8,128)(2,1)S(1)}, bf16[256,2048]{1,0:T(8,128)(2,1)}, u32[]{:S(2)}, u32[]{:S(2)}) collective-permute-start(bf16[256,2048]{1,0:T(8,128)(2,1)S(1)} %collective-permute-done.1.refs_7_), channel_id=1, source_target_pairs={{0,1},{1,0},{2,3},{3,2},{4,5},{5,4},{6,7},{7,6},{8,9},{9,8},{10,11... | collective-permute-start | bytes 3145736 | tf_op jit(solution)/shard_map/ppermute | solution.py:671
  67.1 43.2 %collective-permute-start.10 = (bf16[256,2048]{1,0:T(8,128)(2,1)S(1)}, bf16[256,2048]{1,0:T(8,128)(2,1)S(1)}, u32[]{:S(2)}, u32[]{:S(2)}) collective-permute-start(bf16[256,2048]{1,0:T(8,128)(2,1)S(1)} %collective-permute-done.refs_4_), channel_id=1, source_target_pairs={{0,4},{1,5},{2,6},{3,7},{4,0},{5,1},{6,2},{7,3},{8,12},{9,13},{10,... | collective-permute-start | bytes 3145736 | tf_op jit(solution)/shard_map/ppermute | solution.py:671
  70.4 43.6 %collective-permute-start.11 = (bf16[256,2048]{1,0:T(8,128)(2,1)S(1)}, bf16[256,2048]{1,0:T(8,128)(2,1)}, u32[]{:S(2)}, u32[]{:S(2)}) collective-permute-start(bf16[256,2048]{1,0:T(8,128)(2,1)S(1)} %collective-permute-done.1.refs_7_), channel_id=1, source_target_pairs={{0,2},{1,3},{2,0},{3,1},{4,6},{5,7},{6,4},{7,5},{8,10},{9,11},{10,... | collective-permute-start | bytes 3145736 | tf_op jit(solution)/shard_map/ppermute | solution.py:671
  110.2 8.1 %copy-start.10 = (bf16[256,2048]{1,0:T(8,128)(2,1)}, bf16[256,2048]{1,0:T(8,128)(2,1)S(1)}, u32[]{:S(2)}) copy-start(bf16[256,2048]{1,0:T(8,128)(2,1)S(1)} %collective-permute-done.10.refs_1_) | copy-start | bytes 3145732
  114.0 4.1 collective-permute-start.12
  114.0 4.4 collective-permute-start.13
  124.8 12.7 %copy-start.22 = (bf16[3,256]{1,0:T(4,128)(2,1)S(1)}, bf16[3,256]{1,0:T(4,128)(2,1)}, u32[]{:S(2)}) copy-start(bf16[3,256]{1,0:T(4,128)(2,1)} %param.19) | copy-start | bytes 4612
  137.2 376.8 %reduce-scatter.3.cloned.1.call-start = ((), (), s32[]{:S(2)}) async-start(), calls=%async_computation.5 | async-start | bytes 18874368 | tf_op jit(solution)/shard_map/reduce_scatter | solution.py:846
  187.8 49.7 %collective-permute-start.14 = (bf16[512,2048]{1,0:T(8,128)(2,1)}, bf16[512,2048]{1,0:T(8,128)(2,1)S(1)}, u32[]{:S(2)}, u32[]{:S(2)}) collective-permute-start(bf16[512,2048]{1,0:T(8,128)(2,1)} %weight_grad.3), channel_id=1, source_target_pairs={{0,8},{24,16},{1,9},{25,17},{2,10},{26,18},{3,11},{27,19},{4,12},{... | collective-permute-start | bytes 6291464 | tf_op jit(solution)/shard_map/ppermute | solution.py:601
  205.1 80.3 %collective-permute-start.16 = (bf16[512,2048]{1,0:T(8,128)(2,1)}, bf16[512,2048]{1,0:T(8,128)(2,1)}, u32[]{:S(2)}, u32[]{:S(2)}) collective-permute-start(bf16[512,2048]{1,0:T(8,128)(2,1)} %weight_grad.4), channel_id=1, source_target_pairs={{0,8},{24,16},{1,9},{25,17},{2,10},{26,18},{3,11},{27,19},{4,12},{... | collective-permute-start | bytes 6291464 | tf_op jit(solution)/shard_map/ppermute | solution.py:601
  207.8 29.7 %copy-start.3 = (bf16[512,2048]{1,0:T(8,128)(2,1)S(1)}, bf16[512,2048]{1,0:T(8,128)(2,1)}, u32[]{:S(2)}) copy-start(bf16[512,2048]{1,0:T(8,128)(2,1)} %weight_grad.3) | copy-start | bytes 6291460
  238.4 51.5 %collective-permute-start.15 = (bf16[512,2048]{1,0:T(8,128)(2,1)S(1)}, bf16[512,2048]{1,0:T(8,128)(2,1)}, u32[]{:S(2)}, u32[]{:S(2)}) collective-permute-start(bf16[512,2048]{1,0:T(8,128)(2,1)S(1)} %add_convert_fusion.9), channel_id=1, source_target_pairs={{8,16},{16,8},{9,17},{17,9},{10,18},{18,10},{11,19},{19,11},{12,20... | collective-permute-start | bytes 6291464 | tf_op jit(solution)/shard_map/ppermute | solution.py:601
  265.0 68.4 %collective-permute-start.17 = (bf16[1024,1024]{1,0:T(8,128)(2,1)}, bf16[1024,1024]{1,0:T(8,128)(2,1)}, u32[]{:S(2)}, u32[]{:S(2)}) collective-permute-start(bf16[1024,1024]{1,0:T(8,128)(2,1)} %get-tuple-element.288), channel_id=1, source_target_pairs={{0,8},{24,16},{1,9},{25,17},{2,10},{26,18},{3,11},{27,19},{4,12},{... | collective-permute-start | bytes 6291464 | tf_op jit(solution)/shard_map/ppermute | solution.py:601
  272.0 13.4 %copy-start.2 = (bf16[512,2048]{1,0:T(8,128)(2,1)S(1)}, bf16[512,2048]{1,0:T(8,128)(2,1)}, u32[]{:S(2)}) copy-start(bf16[512,2048]{1,0:T(8,128)(2,1)} %weight_grad.4) | copy-start | bytes 6291460
  287.8 73.7 %collective-permute-start.19 = (bf16[512,2048]{1,0:T(8,128)(2,1)S(1)}, bf16[512,2048]{1,0:T(8,128)(2,1)}, u32[]{:S(2)}, u32[]{:S(2)}) collective-permute-start(bf16[512,2048]{1,0:T(8,128)(2,1)S(1)} %add_convert_fusion.8), channel_id=1, source_target_pairs={{8,16},{16,8},{9,17},{17,9},{10,18},{18,10},{11,19},{19,11},{12,20... | collective-permute-start | bytes 6291464 | tf_op jit(solution)/shard_map/ppermute | solution.py:601
  293.7 73.0 %collective-permute-start.18 = (bf16[512,2048]{1,0:T(8,128)(2,1)}, bf16[512,2048]{1,0:T(8,128)(2,1)}, u32[]{:S(2)}, u32[]{:S(2)}) collective-permute-start(bf16[512,2048]{1,0:T(8,128)(2,1)} %add_convert_fusion.7.kept_ref), channel_id=1, source_target_pairs={{8,0},{16,24},{9,1},{17,25},{10,2},{18,26},{11,3},{19,27},{12,4},{... | collective-permute-start | bytes 6291464 | tf_op jit(solution)/shard_map/ppermute | solution.py:601
  295.0 90.9 %collective-permute-start.21 = (bf16[1024,1024]{1,0:T(8,128)(2,1)}, bf16[1024,1024]{1,0:T(8,128)(2,1)}, u32[]{:S(2)}, u32[]{:S(2)}) collective-permute-start(bf16[1024,1024]{1,0:T(8,128)(2,1)} %get-tuple-element.309), channel_id=1, source_target_pairs={{0,8},{24,16},{1,9},{25,17},{2,10},{26,18},{3,11},{27,19},{4,12},{... | collective-permute-start | bytes 6291464 | tf_op jit(solution)/shard_map/ppermute | solution.py:601
  302.2 293.4 %reduce-scatter.5.cloned.1.call-start = ((), (), s32[]{:S(2)}) async-start(), calls=%async_computation.6 | async-start | bytes 18874368 | tf_op jit(solution)/shard_map/reduce_scatter | solution.py:868
  310.8 22.7 %copy-start.4 = (bf16[1024,1024]{1,0:T(8,128)(2,1)S(1)}, bf16[1024,1024]{1,0:T(8,128)(2,1)}, u32[]{:S(2)}) copy-start(bf16[1024,1024]{1,0:T(8,128)(2,1)} %get-tuple-element.288) | copy-start | bytes 6291460
  337.3 61.8 %collective-permute-start.24 = (bf16[1024,1024]{1,0:T(8,128)(2,1)}, bf16[1024,1024]{1,0:T(8,128)(2,1)}, u32[]{:S(2)}, u32[]{:S(2)}) collective-permute-start(bf16[1024,1024]{1,0:T(8,128)(2,1)} %add_convert_fusion.6), channel_id=1, source_target_pairs={{8,16},{16,8},{9,17},{17,9},{10,18},{18,10},{11,19},{19,11},{12,20... | collective-permute-start | bytes 6291464 | tf_op jit(solution)/shard_map/ppermute | solution.py:601
  365.2 61.7 %collective-permute-start.23 = (bf16[512,2048]{1,0:T(8,128)(2,1)}, bf16[512,2048]{1,0:T(8,128)(2,1)}, u32[]{:S(2)}, u32[]{:S(2)}) collective-permute-start(bf16[512,2048]{1,0:T(8,128)(2,1)} %add_convert_fusion.5.kept_ref), channel_id=1, source_target_pairs={{8,0},{16,24},{9,1},{17,25},{10,2},{18,26},{11,3},{19,27},{12,4},{... | collective-permute-start | bytes 6291464 | tf_op jit(solution)/shard_map/ppermute | solution.py:601
  385.9 5.3 copy-start.5
  389.2 37.6 %collective-permute-start.22 = (bf16[1024,1024]{1,0:T(8,128)(2,1)S(1)}, bf16[1024,1024]{1,0:T(8,128)(2,1)}, u32[]{:S(2)}, u32[]{:S(2)}) collective-permute-start(bf16[1024,1024]{1,0:T(8,128)(2,1)S(1)} %add_convert_fusion.4), channel_id=1, source_target_pairs={{8,16},{16,8},{9,17},{17,9},{10,18},{18,10},{11,19},{19,11},{12,20... | collective-permute-start | bytes 6291464 | tf_op jit(solution)/shard_map/ppermute | solution.py:601
  391.2 48.5 %collective-permute-start.20 = (bf16[2,2048,256]{2,1,0:T(8,128)(2,1)S(1)}, bf16[2,2048,256]{2,1,0:T(8,128)(2,1)}, u32[]{:S(2)}, u32[]{:S(2)}) collective-permute-start(bf16[2,2048,256]{2,1,0:T(8,128)(2,1)S(1)} %copy-done.5), channel_id=1, source_target_pairs={{0,8},{24,16},{1,9},{25,17},{2,10},{26,18},{3,11},{27,19},{4,12},{... | collective-permute-start | bytes 6291464 | tf_op jit(solution)/shard_map/ppermute | solution.py:601
  402.5 24.3 %copy-start = (bf16[1024,1024]{1,0:T(8,128)(2,1)}, bf16[1024,1024]{1,0:T(8,128)(2,1)S(1)}, u32[]{:S(2)}) copy-start(bf16[1024,1024]{1,0:T(8,128)(2,1)S(1)} %add_convert_fusion.3.kept_ref) | copy-start | bytes 6291460
  402.6 105.2 %collective-permute-start.26 = (bf16[1024,1024]{1,0:T(8,128)(2,1)S(1)}, bf16[1024,1024]{1,0:T(8,128)(2,1)}, u32[]{:S(2)}, u32[]{:S(2)}) collective-permute-start(bf16[1024,1024]{1,0:T(8,128)(2,1)S(1)} %add_convert_fusion.3.kept_ref), channel_id=1, source_target_pairs={{8,0},{16,24},{9,1},{17,25},{10,2},{18,26},{11,3},{19,27},{12,4},{... | collective-permute-start | bytes 6291464 | tf_op jit(solution)/shard_map/ppermute | solution.py:601
  430.7 14.4 %copy-start.9 = (bf16[2048,256]{1,0:T(8,128)(2,1)S(1)}, bf16[2048,256]{1,0:T(8,128)(2,1)}, u32[]{:S(2)}) copy-start(bf16[2048,256]{1,0:T(8,128)(2,1)} %get-tuple-element.335) | copy-start | bytes 3145732
  443.2 66.7 %collective-permute-start.25 = (bf16[2,2048,256]{2,1,0:T(8,128)(2,1)}, bf16[2,2048,256]{2,1,0:T(8,128)(2,1)}, u32[]{:S(2)}, u32[]{:S(2)}) collective-permute-start(bf16[2,2048,256]{2,1,0:T(8,128)(2,1)} %add_convert_fusion.1), channel_id=1, source_target_pairs={{8,16},{16,8},{9,17},{17,9},{10,18},{18,10},{11,19},{19,11},{12,20... | collective-permute-start | bytes 6291464 | tf_op jit(solution)/shard_map/ppermute | solution.py:601
  445.1 37.6 %collective-permute-start.27 = (bf16[2048,256]{1,0:T(8,128)(2,1)S(1)}, bf16[2048,256]{1,0:T(8,128)(2,1)}, u32[]{:S(2)}, u32[]{:S(2)}) collective-permute-start(bf16[2048,256]{1,0:T(8,128)(2,1)S(1)} %copy-done.9), channel_id=1, source_target_pairs={{0,8},{24,16},{1,9},{25,17},{2,10},{26,18},{3,11},{27,19},{4,12},{... | collective-permute-start | bytes 3145736 | tf_op jit(solution)/shard_map/ppermute | solution.py:601
  452.9 72.3 %collective-permute-start.30 = (bf16[1024,1024]{1,0:T(8,128)(2,1)}, bf16[1024,1024]{1,0:T(8,128)(2,1)}, u32[]{:S(2)}, u32[]{:S(2)}) collective-permute-start(bf16[1024,1024]{1,0:T(8,128)(2,1)} %add_convert_fusion.2.kept_ref), channel_id=1, source_target_pairs={{8,0},{16,24},{9,1},{17,25},{10,2},{18,26},{11,3},{19,27},{12,4},{... | collective-permute-start | bytes 6291464 | tf_op jit(solution)/shard_map/ppermute | solution.py:601
  477.1 5.0 copy-start.19
  477.1 36.8 %all-to-all-start = ((bf16[8,2,256,256]{3,2,1,0:T(8,128)(2,1)}), bf16[8,2,256,256]{3,2,1,0:T(8,128)(2,1)}, u32[]{:S(2)}, u32[]{:S(2)}) async-start(bf16[8,2,256,256]{3,2,1,0:T(8,128)(2,1)} %get-tuple-element.298), calls=%async_computation | async-start | bytes 4194304 | tf_op jit(solution)/shard_map/all_to_all | solution.py:855
  484.5 59.4 %collective-permute-start.36 = (bf16[2048,256]{1,0:T(8,128)(2,1)S(1)}, bf16[2048,256]{1,0:T(8,128)(2,1)}, u32[]{:S(2)}, u32[]{:S(2)}) collective-permute-start(bf16[2048,256]{1,0:T(8,128)(2,1)S(1)} %add_convert_fusion.13), channel_id=1, source_target_pairs={{8,16},{16,8},{9,17},{17,9},{10,18},{18,10},{11,19},{19,11},{12,20... | collective-permute-start | bytes 3145736 | tf_op jit(solution)/shard_map/ppermute | solution.py:601
  498.9 30.7 %collective-permute-start.29 = (bf16[256,2048]{1,0:T(8,128)(2,1)}, bf16[256,2048]{1,0:T(8,128)(2,1)}, u32[]{:S(2)}, u32[]{:S(2)}) collective-permute-start(bf16[256,2048]{1,0:T(8,128)(2,1)} %weight_grad.5), channel_id=1, source_target_pairs={{0,8},{24,16},{1,9},{25,17},{2,10},{26,18},{3,11},{27,19},{4,12},{... | collective-permute-start | bytes 3145736 | tf_op jit(solution)/shard_map/ppermute | solution.py:601
  512.6 12.6 %copy-start.1 = (bf16[2,2048,256]{2,1,0:T(8,128)(2,1)}, bf16[2,2048,256]{2,1,0:T(8,128)(2,1)S(1)}, u32[]{:S(2)}) copy-start(bf16[2,2048,256]{2,1,0:T(8,128)(2,1)S(1)} %add_convert_fusion) | copy-start | bytes 6291460
  512.6 50.5 %collective-permute-start.28 = (bf16[2,2048,256]{2,1,0:T(8,128)(2,1)S(1)}, bf16[2,2048,256]{2,1,0:T(8,128)(2,1)}, u32[]{:S(2)}, u32[]{:S(2)}) collective-permute-start(bf16[2,2048,256]{2,1,0:T(8,128)(2,1)S(1)} %add_convert_fusion), channel_id=1, source_target_pairs={{8,0},{16,24},{9,1},{17,25},{10,2},{18,26},{11,3},{19,27},{12,4},{... | collective-permute-start | bytes 6291464 | tf_op jit(solution)/shard_map/ppermute | solution.py:601
  514.0 11.2 %copy-start.14 = (f32[8,2048]{1,0:T(8,128)S(1)}, f32[8,2048]{1,0:T(8,128)}, u32[]{:S(2)}) copy-start(f32[8,2048]{1,0:T(8,128)} %get-tuple-element.350) | copy-start | bytes 196612
  514.0 11.2 %copy-start.15 = (f32[8,2048]{1,0:T(8,128)S(1)}, f32[8,2048]{1,0:T(8,128)}, u32[]{:S(2)}) copy-start(f32[8,2048]{1,0:T(8,128)} %get-tuple-element.351) | copy-start | bytes 196612
  514.0 11.3 %copy-start.16 = (bf16[2048]{0:T(1024)(128)(2,1)S(1)}, bf16[2048]{0:T(1024)(128)(2,1)}, u32[]{:S(2)}) copy-start(bf16[2048]{0:T(1024)(128)(2,1)} %param.16) | copy-start | bytes 12292
  532.7 22.0 %collective-permute-start.31 = (bf16[256,2048]{1,0:T(8,128)(2,1)}, bf16[256,2048]{1,0:T(8,128)(2,1)}, u32[]{:S(2)}, u32[]{:S(2)}) collective-permute-start(bf16[256,2048]{1,0:T(8,128)(2,1)} %add_convert_fusion.12), channel_id=1, source_target_pairs={{8,16},{16,8},{9,17},{17,9},{10,18},{18,10},{11,19},{19,11},{12,20... | collective-permute-start | bytes 3145736 | tf_op jit(solution)/shard_map/ppermute | solution.py:601
  534.3 1.2 collective-permute-start.32
  535.5 4.2 collective-permute-start.33
  539.7 4.2 collective-permute-start.34
  543.9 9.0 %collective-permute-start.35 = (f32[49,128]{1,0:T(8,128)S(1)}, f32[49,128]{1,0:T(8,128)S(1)}, u32[]{:S(2)}, u32[]{:S(2)}) collective-permute-start(f32[49,128]{1,0:T(8,128)S(1)} %pad_maximum_fusion), channel_id=1, source_target_pairs={{0,8},{24,16},{1,9},{25,17},{2,10},{26,18},{3,11},{27,19},{4,12},{... | collective-permute-start | bytes 75272 | tf_op jit(solution)/shard_map/ppermute | solution.py:601
  551.6 50.3 %collective-permute-start.40 = (bf16[2048,256]{1,0:T(8,128)(2,1)}, bf16[2048,256]{1,0:T(8,128)(2,1)}, u32[]{:S(2)}, u32[]{:S(2)}) collective-permute-start(bf16[2048,256]{1,0:T(8,128)(2,1)} %add_convert_fusion.11.kept_ref), channel_id=1, source_target_pairs={{8,0},{16,24},{9,1},{17,25},{10,2},{18,26},{11,3},{19,27},{12,4},{... | collective-permute-start | bytes 3145736 | tf_op jit(solution)/shard_map/ppermute | solution.py:601
  553.5 22.9 %collective-permute-start.37 = (f32[49,128]{1,0:T(8,128)}, f32[49,128]{1,0:T(8,128)}, u32[]{:S(2)}, u32[]{:S(2)}) collective-permute-start(f32[49,128]{1,0:T(8,128)} %add.132), channel_id=1, source_target_pairs={{8,16},{16,8},{9,17},{17,9},{10,18},{18,10},{11,19},{19,11},{12,20... | collective-permute-start | bytes 75272 | tf_op jit(solution)/shard_map/ppermute | solution.py:601
  557.8 49.3 %collective-permute-start.39 = (bf16[256,2048]{1,0:T(8,128)(2,1)}, bf16[256,2048]{1,0:T(8,128)(2,1)}, u32[]{:S(2)}, u32[]{:S(2)}) collective-permute-start(bf16[256,2048]{1,0:T(8,128)(2,1)} %add_convert_fusion.10.kept_ref), channel_id=1, source_target_pairs={{8,0},{16,24},{9,1},{17,25},{10,2},{18,26},{11,3},{19,27},{12,4},{... | collective-permute-start | bytes 3145736 | tf_op jit(solution)/shard_map/ppermute | solution.py:601
  577.2 32.9 %collective-permute-start.38 = (f32[49,128]{1,0:T(8,128)S(1)}, f32[49,128]{1,0:T(8,128)S(1)}, u32[]{:S(2)}, u32[]{:S(2)}) collective-permute-start(f32[49,128]{1,0:T(8,128)S(1)} %add.134), channel_id=1, source_target_pairs={{8,0},{16,24},{9,1},{17,25},{10,2},{18,26},{11,3},{19,27},{12,4},{... | collective-permute-start | bytes 75272 | tf_op jit(solution)/shard_map/ppermute | solution.py:601
  (5 other events, 10.9 us)
Sparse Core Ops, SparseCore 0:
  66.0 107.4 all-gather.2
  175.4 54.3 all-gather.4
  302.4 114.1 reduce-scatter.2
  477.2 118.3 reduce-scatter.4

commit v9 on v8

--- a/solution.py
+++ b/solution.py
@@ -15,7 +15,7 @@
 f32 = jnp.float32
 bf16 = jnp.bfloat16
 VMEM_LIMIT = 56 << 20
-ORDER_WEIGHT = int(2.15e11)
+ORDER_WEIGHT = int(2.2e11)
 EARLY_WEIGHT = int(2.2e11)
 
 
@@ -862,12 +862,12 @@
     i0.fold(order)
     part, bias_a, norm_a = order(back(0), hidden_grad, dqkv, inward_weight, w3, normed)
     o1.settle(order)
+    (ds,) = row_sum([order(weight_grad, attended, grad)])
     i1.fold(order)
     qs.fold(order)
     part, bias_b, norm_b = order(back(1), hidden_grad, dqkv, inward_weight, w3, normed, part)
     back_tok = lax.psum_scatter(part.reshape(seqs, length, width), "tp", scatter_dimension=1, tiled=True)
     vs.fold(order)
-    (ds,) = row_sum([order(weight_grad, attended, grad)])
     i0.settle(order)
 
     cols = width // tp
@@ -877,7 +877,6 @@
         return jnp.sum(mine.astype(f32), axis=0)
 
     out_bias = order(column_sums, grad)
-    qs.fold(order)
     rows_of = lambda a: a.reshape(seqs * here, width)
     bias_rows = (b_dense.astype(f32)[None], b_out.astype(f32)[None])
     own = lambda x, w, t, *m: project_own(x, w, *bias_rows, rows_of(t), m)
@@ -890,6 +889,7 @@
         pad = jnp.zeros((124,), f32)
         return jnp.concatenate([norm_sums[0] / gain, norm_sums[1], squares, pad]).reshape(-1, 128)
 
+    qs.fold(order)
     i1.settle(order)
     packed = TpSum(order(pack, norm_a, norm_b, squares), tp)
     ds.fold(order)

time: 631 us -> 634 us (level)
    ppermute x24, starting transfers between devices: 75.5 us -> 84.8 us  [send(): self.came = lax.ppermute(self.part, self.axis, self.hops.pop(0))]
    reduce_scatter x1, starting transfers between devices: 8.52 us -> 0.04 us  [body(): lax.psum_scatter(part.reshape(seqs, length, width), 'tp', scatter_dimensi...]
  transfers between devices with their start and end apart: 46 -> 46, of which waited for: 18 -> 17; matrix products, arithmetic and copies ran while one was open for 9% -> 9% of each run, Pallas kernels for 58% -> 58%
where the time goes in v9:
time: 634 us; the launch traced here: 624 us
  Pallas kernels  365 us (58%)
  starting transfers between devices  102 us (16%)
  waiting for transfers between devices  79.1 us (12%)
  other arithmetic  54.5 us (9%)
  between operations  14.7 us (2%)
  local copies, waits for them, and re-layouts  9.37 us (1%)
    ppermute x24, starting transfers between devices, send(): self.came = lax.ppermute(self.part, self.axis, self.hops.pop(0))  84.8 us
    pallas_call x2, Pallas kernels, normed_grad(): pl.pallas_call(functools.partial(normed_grad_kernel, held=held), grid=(st...  45.6 us
    pallas_call x2, Pallas kernels, attention_both(): pl.pallas_call(functools.partial(attention_kernel, bq=bq, held=held), gri...  44.3 us
    convert_element_type x14, other arithmetic, fold(): add = lambda a, b: (a.astype(f32) + b.astype(f32)).astype(a.dtype)  43.1 us
    ppermute x14, waiting for transfers between devices, send(): return lax.ppermute(a, 'tp', [(i, i ^ step) for i in range(self.size)])  42.8 us
    pallas_call x3, Pallas kernels, weight_grad(): pl.pallas_call(weight_grad_kernel, grid=(cols // tile,), in_specs=[pl.Blo...  38.1 us
    pallas_call x2, Pallas kernels, mlp_hidden_of(): pl.pallas_call(functools.partial(chosen_kernel, held=held), grid_spec=plt...  36.1 us
    pallas_call x7, Pallas kernels, finish(): call(inner, *a)  30 us
  transfers between devices with their start and end apart: 46, of which 17 were waited for; matrix products, arithmetic and copies ran while one was open for 9% of the time, Pallas kernels for 58%

profile of v9, /device:TPU:0, one launch (start us, length us, event | category | flops | bytes accessed | tf_op | source)
XLA Modules:
  0.0 624.4 jit_solution(6047928925463117627)
XLA Ops:
  9.8 4.7 norm_halves.1
  14.6 2.9 collective-permute-start
  22.1 9.8 %rope_tables.1 = (f32[4096,128]{1,0:T(8,128)}, f32[4096,128]{1,0:T(8,128)}) custom-call(s32[4096,1]{1,0:T(8,128)} %bitcast.75, f32[1,128]{1,0:T(1,128)} %fusion.4.frequency_ref), custom_call_target="tpu_custom_call" | custom-call | flops 1 | bytes 1 | tf_op jit(solution)/shard_map/rope_tables/pallas_call | solution.py:126
  32.5 9.2 %collective-permute-done.refs_4_ = bf16[256,2048]{1,0:T(8,128)(2,1)S(1)} collective-permute-done((bf16[256,2048]{1,0:T(8,128)(2,1)}, bf16[256,2048]{1,0:T(8,128)(2,1)S(1)}, u32[]{:S(2)}, u32[]{:S(2)}) %collective-permute-start) | collective-permute-done | bytes 1048608 | tf_op jit(solution)/shard_map/ppermute | solution.py:671
  41.7 2.1 collective-permute-done.1.refs_7_
  43.9 19.6 %collective-permute-done.3.refs_5_ = bf16[256,2048]{1,0:T(8,128)(2,1)} collective-permute-done((bf16[256,2048]{1,0:T(8,128)(2,1)}, bf16[256,2048]{1,0:T(8,128)(2,1)}, u32[]{:S(2)}, u32[]{:S(2)}) %collective-permute-start.3) | collective-permute-done | bytes 1048608 | tf_op jit(solution)/shard_map/ppermute | solution.py:671
  72.6 13.1 %place_pieces.2.refs_0_ = bf16[2,8,256,2048]{3,2,1,0:T(8,128)(2,1)} custom-call(s32[1]{0:T(128)} %bitcast.3.me_ref, bf16[256,2048]{1,0:T(8,128)(2,1)} %get-tuple-element.218.refs_0_, bf16[256,2048]{1,0:T(8,128)(2,1)} %get-tuple-element.219.refs_1_, bf16[256,2048]{1,0:T(8,128)(2,1)} %collective-permute-done.2.refs_2_, ...), custom_call_target="tpu_custom_call" | custom-call | flops 1 | bytes 1 | tf_op jit(solution)/shard_map/place_pieces/pallas_call | solution.py:732
  85.6 23.6 %mlp_hidden_of.2 = (bf16[2,8,256,1024]{3,2,1,0:T(8,128)(2,1)}, bf16[2,8,256,1024]{3,2,1,0:T(8,128)(2,1)}) custom-call(s32[1]{0:T(128)} %bitcast.3.me_ref, bf16[2,8,256,2048]{3,2,1,0:T(8,128)(2,1)} %place_pieces.2.refs_0_, bf16[2048,1024]{1,0:T(8,128)(2,1)} %refs_3_.1, f32[1,1024]{1,0:T(1,128)} %bitcast.89), custom_call_target="tpu_custom_call" | custom-call | flops 1 | bytes 1 | tf_op jit(solution)/shard_map/mlp_hidden_of/pallas_call | solution.py:207
  109.3 3.6 collective-permute-done.11.refs_2_
  113.4 3.6 collective-permute-done.12.refs_3_
  119.0 4.8 place_pieces.3.refs_2_
  123.7 12.4 %mlp_hidden_of.3 = (bf16[2,8,256,1024]{3,2,1,0:T(8,128)(2,1)}, bf16[2,8,256,1024]{3,2,1,0:T(8,128)(2,1)}) custom-call(s32[1]{0:T(128)} %bitcast.3.me_ref, bf16[2,8,256,1024]{3,2,1,0:T(8,128)(2,1)} %get-tuple-element.242.refs_0_, bf16[2,8,256,1024]{3,2,1,0:T(8,128)(2,1)} %get-tuple-element.243.refs_1_, ...), custom_call_target="tpu_custom_call", output_to_operand_aliasing={{0}: (1, {}), {1}: (2, {})} | custom-call | flops 1 | bytes 1 | tf_op jit(solution)/shard_map/mlp_hidden_of/pallas_call | solution.py:207
  137.1 20.1 %qkv_rope.1.refs_1_.refs_2_.refs_3_.refs_4_.refs_5_.refs_6_ = bf16[3,4096,256]{2,1,0:T(8,128)(2,1)} custom-call(bf16[4096,2048]{1,0:T(8,128)(2,1)} %bitcast.49, bf16[3,2048,256]{2,1,0:T(8,128)(2,1)} %bitcast.66, f32[3,256]{1,0:T(4,128)} %convert_element_type.158.b_ref, f32[4096,128]{1,0:T(8,128)} %get-tuple-element.296.c_ref.refs_5_.refs_8_, ...), custom_call_target="tpu_custom_call" | custom-call | flops 1 | bytes 1 | tf_op jit(solution)/shard_map/qkv_rope/pallas_call | solution.py:158
  157.2 13.3 %tokens_by_weight.2.refs_0_ = bf16[4096,2048]{1,0:T(8,128)(2,1)} custom-call(bf16[4096,1024]{1,0:T(8,128)(2,1)} %bitcast.59, bf16[1024,2048]{1,0:T(8,128)(2,1)} %refs_2_), custom_call_target="tpu_custom_call" | custom-call | flops 1 | bytes 1 | tf_op jit(solution)/shard_map/tokens_by_weight/pallas_call | solution.py:287
  170.4 2.2 all-gather.3.cloned.1.call-done
  172.6 14.2 %weight_grad.3 = bf16[512,2048]{1,0:T(8,128)(2,1)} custom-call(bf16[4096,1024]{1,0:T(8,128)(2,1)} %bitcast.60, bf16[4096,2048]{1,0:T(8,128)(2,1)} %bitcast.54), custom_call_target="tpu_custom_call" | custom-call | flops 1 | bytes 1 | tf_op jit(solution)/shard_map/weight_grad/pallas_call | solution.py:310
  186.9 3.5 collective-permute-start.14
  190.4 13.8 %weight_grad.4 = bf16[512,2048]{1,0:T(8,128)(2,1)} custom-call(bf16[4096,1024]{1,0:T(8,128)(2,1)} %bitcast.61, bf16[4096,2048]{1,0:T(8,128)(2,1)} %bitcast.55), custom_call_target="tpu_custom_call" | custom-call | flops 1 | bytes 1 | tf_op jit(solution)/shard_map/weight_grad/pallas_call | solution.py:310
  204.2 2.7 collective-permute-start.16
  206.9 29.6 %grad_in.1 = (bf16[4096,1024]{1,0:T(8,128)(2,1)}, bf16[4096,256]{1,0:T(8,128)(2,1)}, f32[8,1024]{1,0:T(8,128)}) custom-call(bf16[4096,2048]{1,0:T(8,128)(2,1)} %bitcast.56, bf16[1024,2048]{1,0:T(8,128)(2,1)} %refs_2_, bf16[256,2048]{1,0:T(8,128)(2,1)} %wd_ref, bf16[4096,1024]{1,0:T(8,128)(2,1)} %bitcast.65), custom_call_target="tpu_custom_call" | custom-call | flops 1 | bytes 1 | tf_op jit(solution)/shard_map/grad_in/pallas_call | solution.py:248
  239.5 24.6 %weight_grad_rows.1 = (bf16[1024,1024]{1,0:T(8,128)(2,1)}, bf16[1024,1024]{1,0:T(8,128)(2,1)}) custom-call(bf16[4096,2048]{1,0:T(8,128)(2,1)} %bitcast.50, bf16[4096,1024]{1,0:T(8,128)(2,1)} %get-tuple-element.329.b_ref.refs_0_.refs_1_), custom_call_target="tpu_custom_call" | custom-call | flops 1 | bytes 1 | tf_op jit(solution)/shard_map/weight_grad_rows/pallas_call | solution.py:344
  264.1 7.1 %collective-permute-start.17 = (bf16[1024,1024]{1,0:T(8,128)(2,1)}, bf16[1024,1024]{1,0:T(8,128)(2,1)}, u32[]{:S(2)}, u32[]{:S(2)}) collective-permute-start(bf16[1024,1024]{1,0:T(8,128)(2,1)} %get-tuple-element.288), channel_id=1, source_target_pairs={{0,8},{24,16},{1,9},{25,17},{2,10},{26,18},{3,11},{27,19},{4,12},{... | collective-permute-start | bytes 6291464 | tf_op jit(solution)/shard_map/ppermute | solution.py:601
  271.1 13.4 %tokens_by_weight.3 = bf16[4096,2048]{1,0:T(8,128)(2,1)} custom-call(bf16[4096,2048]{1,0:T(8,128)(2,1)} %tokens_by_weight.2.refs_0_, bf16[4096,1024]{1,0:T(8,128)(2,1)} %bitcast.62, bf16[1024,2048]{1,0:T(8,128)(2,1)} %refs_2_), custom_call_target="tpu_custom_call", output_to_operand_aliasing={{}: (0, {})} | custom-call | flops 1 | bytes 1 | tf_op jit(solution)/shard_map/tokens_by_weight/pallas_call | solution.py:287
  284.5 2.4 add_convert_fusion.8
  286.9 2.1 collective-permute-start.21
  288.9 3.9 add_convert_fusion.7.kept_ref
  294.1 15.4 %collective-permute-start.19 = (bf16[1024,1024]{1,0:T(8,128)(2,1)}, bf16[1024,1024]{1,0:T(8,128)(2,1)}, u32[]{:S(2)}, u32[]{:S(2)}) collective-permute-start(bf16[1024,1024]{1,0:T(8,128)(2,1)} %get-tuple-element.309), channel_id=1, source_target_pairs={{0,8},{24,16},{1,9},{25,17},{2,10},{26,18},{3,11},{27,19},{4,12},{... | collective-permute-start | bytes 6291464 | tf_op jit(solution)/shard_map/ppermute | solution.py:601
  309.6 22.2 %attention_both.2 = (bf16[4096,256]{1,0:T(8,128)(2,1)}, bf16[8,2,256,256]{3,2,1,0:T(8,128)(2,1)}, bf16[3,4096,256]{2,1,0:T(8,128)(2,1)}) custom-call(s32[1,4096]{1,0:T(1,128)} %fusion.refs_0_.refs_3_, bf16[3,4096,256]{2,1,0:T(8,128)(2,1)} %qkv_rope.1.refs_1_.refs_2_.refs_3_.refs_4_.refs_5_.refs_6_, ...), custom_call_target="tpu_custom_call" | custom-call | flops 1 | bytes 1 | tf_op jit(solution)/shard_map/attention_both/pallas_call | solution.py:507
  331.8 4.4 add_convert_fusion.6
  336.2 2.0 collective-permute-start.18
  338.2 22.1 %attention_both.3 = (bf16[4096,256]{1,0:T(8,128)(2,1)}, bf16[8,2,256,256]{3,2,1,0:T(8,128)(2,1)}, bf16[3,4096,256]{2,1,0:T(8,128)(2,1)}) custom-call(bf16[4096,256]{1,0:T(8,128)(2,1)} %get-tuple-element.290.refs_0_, bf16[8,2,256,256]{3,2,1,0:T(8,128)(2,1)} %get-tuple-element.291.refs_1_, ...), custom_call_target="tpu_custom_call", output_to_operand_aliasing={{0}: (0, {}), {1}: (1, {}), {2}: (2, {})} | custom-call | flops 1 | bytes 1 | tf_op jit(solution)/shard_map/attention_both/pallas_call | solution.py:507
  360.3 3.7 add_convert_fusion.5.kept_ref
  365.6 19.2 %weight_grad_parts.1 = (bf16[2,2048,256]{2,1,0:T(8,128)(2,1)}, bf16[2048,256]{1,0:T(8,128)(2,1)}) custom-call(bf16[4096,2048]{1,0:T(8,128)(2,1)} %bitcast.51, bf16[3,4096,256]{2,1,0:T(8,128)(2,1)} %get-tuple-element.330.b_ref.refs_1_.refs_2_), custom_call_target="tpu_custom_call" | custom-call | flops 219999993856 | bytes 1 | tf_op jit(solution)/shard_map/weight_grad_parts/pallas_call | solution.py:368
  384.8 3.4 add_convert_fusion.4
  390.1 7.8 %collective-permute-start.24 = (bf16[2,2048,256]{2,1,0:T(8,128)(2,1)S(1)}, bf16[2,2048,256]{2,1,0:T(8,128)(2,1)}, u32[]{:S(2)}, u32[]{:S(2)}) collective-permute-start(bf16[2,2048,256]{2,1,0:T(8,128)(2,1)S(1)} %copy-done.5), channel_id=1, source_target_pairs={{0,8},{24,16},{1,9},{25,17},{2,10},{26,18},{3,11},{27,19},{4,12},{... | collective-permute-start | bytes 6291464 | tf_op jit(solution)/shard_map/ppermute | solution.py:601
  397.9 3.3 add_convert_fusion.3.kept_ref
  402.5 23.0 %normed_grad.2 = (bf16[4096,2048]{1,0:T(8,128)(2,1)}, f32[3,8,256]{2,1,0:T(8,128)}, f32[8,2048]{1,0:T(8,128)}) custom-call(bf16[4096,1024]{1,0:T(8,128)(2,1)} %get-tuple-element.329.b_ref.refs_0_.refs_1_, bf16[3,4096,256]{2,1,0:T(8,128)(2,1)} %get-tuple-element.330.b_ref.refs_1_.refs_2_, bf16[2048,1024]{1,0:T(8,128)(2,1)} %refs_3_.1, ...), custom_call_target="tpu_custom_call" | custom-call | flops 1 | bytes 1 | tf_op jit(solution)/shard_map/normed_grad/pallas_call | solution.py:412
  425.5 10.1 %weight_grad.5 = bf16[256,2048]{1,0:T(8,128)(2,1)} custom-call(bf16[4096,256]{1,0:T(8,128)(2,1)} %get-tuple-element.322.a_ref, bf16[4096,2048]{1,0:T(8,128)(2,1)} %bitcast.57), custom_call_target="tpu_custom_call" | custom-call | flops 1 | bytes 1 | tf_op jit(solution)/shard_map/weight_grad/pallas_call | solution.py:310
  435.6 3.9 add_convert_fusion.2.kept_ref
  439.5 3.4 add_convert_fusion.1
  442.9 2.1 collective-permute-start.27
  445.0 4.3 all-to-all-start
  449.4 8.7 %collective-permute-start.23 = (bf16[2048,256]{1,0:T(8,128)(2,1)S(1)}, bf16[2048,256]{1,0:T(8,128)(2,1)}, u32[]{:S(2)}, u32[]{:S(2)}) collective-permute-start(bf16[2048,256]{1,0:T(8,128)(2,1)S(1)} %copy-done.9), channel_id=1, source_target_pairs={{0,8},{24,16},{1,9},{25,17},{2,10},{26,18},{3,11},{27,19},{4,12},{... | collective-permute-start | bytes 3145736 | tf_op jit(solution)/shard_map/ppermute | solution.py:601
  459.7 22.6 %normed_grad.3 = (bf16[4096,2048]{1,0:T(8,128)(2,1)}, f32[3,8,256]{2,1,0:T(8,128)}, f32[8,2048]{1,0:T(8,128)}) custom-call(bf16[4096,2048]{1,0:T(8,128)(2,1)} %get-tuple-element.328.refs_0_, bf16[4096,1024]{1,0:T(8,128)(2,1)} %get-tuple-element.329.b_ref.refs_0_.refs_1_, ...), custom_call_target="tpu_custom_call", output_to_operand_aliasing={{0}: (0, {})} | custom-call | flops 1 | bytes 1 | tf_op jit(solution)/shard_map/normed_grad/pallas_call | solution.py:412
  484.2 6.9 %collective-permute-start.29 = (bf16[256,2048]{1,0:T(8,128)(2,1)}, bf16[256,2048]{1,0:T(8,128)(2,1)}, u32[]{:S(2)}, u32[]{:S(2)}) collective-permute-start(bf16[256,2048]{1,0:T(8,128)(2,1)} %weight_grad.5), channel_id=1, source_target_pairs={{0,8},{24,16},{1,9},{25,17},{2,10},{26,18},{3,11},{27,19},{4,12},{... | collective-permute-start | bytes 3145736 | tf_op jit(solution)/shard_map/ppermute | solution.py:601
  491.1 2.1 add_convert_fusion.13
  495.0 2.5 convert_reduce_fusion
  497.5 12.0 %project_own.1 = (bf16[512,2048]{1,0:T(8,128)(2,1)}, f32[8,512]{1,0:T(8,128)}) custom-call(bf16[8,2,256,256]{3,2,1,0:T(8,128)(2,1)} %all-to-all-done.x_ref, bf16[2048,2048]{1,0:T(8,128)(2,1)} %all-gather.5.cloned.1.call-done.w_ref, f32[1,2048]{1,0:T(1,128)} %bitcast.91, f32[1,2048]{1,0:T(1,128)} %bitcast.92, bf16[512,2048]{1,0:T(8,128)(2,1)} %bitcast.71, ...), custom_call_target="tpu_custom_call" | custom-call | flops 1 | bytes 1 | tf_op jit(solution)/shard_map/project_own/pallas_call | solution.py:563
  509.6 3.2 add_convert_fusion
  514.5 2.9 add_convert_fusion.12
  526.2 2.2 collective-permute-done.34
  528.4 7.1 %collective-permute-start.35 = (f32[49,128]{1,0:T(8,128)S(1)}, f32[49,128]{1,0:T(8,128)S(1)}, u32[]{:S(2)}, u32[]{:S(2)}) collective-permute-start(f32[49,128]{1,0:T(8,128)S(1)} %pad_maximum_fusion), channel_id=1, source_target_pairs={{0,8},{24,16},{1,9},{25,17},{2,10},{26,18},{3,11},{27,19},{4,12},{... | collective-permute-start | bytes 75272 | tf_op jit(solution)/shard_map/ppermute | solution.py:601
  535.5 2.7 add_convert_fusion.11.kept_ref
  541.3 3.0 add_convert_fusion.10.kept_ref
  545.6 17.8 %collective-permute-done.28 = bf16[2,2048,256]{2,1,0:T(8,128)(2,1)} collective-permute-done((bf16[2,2048,256]{2,1,0:T(8,128)(2,1)S(1)}, bf16[2,2048,256]{2,1,0:T(8,128)(2,1)}, u32[]{:S(2)}, u32[]{:S(2)}) %collective-permute-start.28) | collective-permute-done | bytes 2097184 | tf_op jit(solution)/shard_map/ppermute | solution.py:601
  563.4 4.6 finish.7.refs_0_
  568.0 4.6 finish.8
  572.6 3.7 finish.9.refs_0_
  578.3 3.7 finish.10
  582.0 6.7 %finish.11.refs_0_ = f32[6144,256]{1,0:T(8,128)} custom-call(s32[1]{0:T(128)} %bitcast.17.inner_ref, bf16[4096,256]{1,0:T(8,128)(2,1)} %bitcast.74, bf16[4096,256]{1,0:T(8,128)(2,1)} %bitcast.24.came_ref), custom_call_target="tpu_custom_call" | custom-call | flops 1 | bytes 1 | tf_op jit(solution)/shard_map/finish/pallas_call | solution.py:660
  588.7 12.1 %reduce-scatter.5.cloned.1.call-done = bf16[2,256,2048]{2,1,0:T(8,128)(2,1)} async-done(((bf16[2,2048,2048]{2,1,0:T(8,128)(2,1)}), bf16[2,256,2048]{2,1,0:T(8,128)(2,1)}) %reduce-scatter.5.cloned.1.call-update) | async-done | bytes 2097168 | tf_op jit(solution)/shard_map/reduce_scatter | solution.py:869
  600.8 6.3 %norm_back.1 = bf16[512,2048]{1,0:T(8,128)(2,1)} custom-call(bf16[512,2048]{1,0:T(8,128)(2,1)} %bitcast.76, bf16[512,2048]{1,0:T(8,128)(2,1)} %bitcast.72, bf16[512,2048]{1,0:T(8,128)(2,1)} %bitcast.73, f32[1,2048]{1,0:T(1,128)} %bitcast.88), custom_call_target="tpu_custom_call" | custom-call | flops 1 | bytes 1 | tf_op jit(solution)/shard_map/norm_back/pallas_call | solution.py:101
  607.1 3.8 finish.12
  610.8 3.0 finish.13
  (159 shorter events, 55.1 us)
Async XLA Ops:
  7.2 12.4 %copy-start.17 = (s32[2,2048]{1,0:T(2,128)S(1)}, s32[2,2048]{1,0:T(2,128)}, u32[]{:S(2)}) copy-start(s32[2,2048]{1,0:T(2,128)} %param.15) | copy-start | bytes 49156
  7.2 165.4 %all-gather.3.cloned.1.call-start = ((), (), s32[]{:S(2)}) async-start(), calls=%async_computation.3 | async-start | bytes 18874368 | tf_op jit(solution)/shard_map/all_gather | solution.py:815
  14.6 27.1 %collective-permute-start = (bf16[256,2048]{1,0:T(8,128)(2,1)}, bf16[256,2048]{1,0:T(8,128)(2,1)S(1)}, u32[]{:S(2)}, u32[]{:S(2)}) collective-permute-start(bf16[256,2048]{1,0:T(8,128)(2,1)} %get-tuple-element.218.refs_0_), channel_id=1, source_target_pairs={{0,2},{1,3},{2,0},{3,1},{4,6},{5,7},{6,4},{7,5},{8,10},{9,11},{10,... | collective-permute-start | bytes 3145736 | tf_op jit(solution)/shard_map/ppermute | solution.py:671
  17.5 26.3 %collective-permute-start.1 = (bf16[256,2048]{1,0:T(8,128)(2,1)}, bf16[256,2048]{1,0:T(8,128)(2,1)S(1)}, u32[]{:S(2)}, u32[]{:S(2)}) collective-permute-start(bf16[256,2048]{1,0:T(8,128)(2,1)} %get-tuple-element.219.refs_1_), channel_id=1, source_target_pairs={{0,4},{1,5},{2,6},{3,7},{4,0},{5,1},{6,2},{7,3},{8,12},{9,13},{10,... | collective-permute-start | bytes 3145736 | tf_op jit(solution)/shard_map/ppermute | solution.py:671
  19.0 24.8 %collective-permute-start.2 = (bf16[256,2048]{1,0:T(8,128)(2,1)}, bf16[256,2048]{1,0:T(8,128)(2,1)}, u32[]{:S(2)}, u32[]{:S(2)}) collective-permute-start(bf16[256,2048]{1,0:T(8,128)(2,1)} %get-tuple-element.218.refs_0_), channel_id=1, source_target_pairs={{0,1},{1,0},{2,3},{3,2},{4,5},{5,4},{6,7},{7,6},{8,9},{9,8},{10,11... | collective-permute-start | bytes 3145736 | tf_op jit(solution)/shard_map/ppermute | solution.py:671
  19.0 44.4 %collective-permute-start.3 = (bf16[256,2048]{1,0:T(8,128)(2,1)}, bf16[256,2048]{1,0:T(8,128)(2,1)}, u32[]{:S(2)}, u32[]{:S(2)}) collective-permute-start(bf16[256,2048]{1,0:T(8,128)(2,1)} %get-tuple-element.219.refs_1_), channel_id=1, source_target_pairs={{0,2},{1,3},{2,0},{3,1},{4,6},{5,7},{6,4},{7,5},{8,10},{9,11},{10,... | collective-permute-start | bytes 3145736 | tf_op jit(solution)/shard_map/ppermute | solution.py:671
  19.5 45.3 %collective-permute-start.4 = (bf16[256,2048]{1,0:T(8,128)(2,1)}, bf16[256,2048]{1,0:T(8,128)(2,1)}, u32[]{:S(2)}, u32[]{:S(2)}) collective-permute-start(bf16[256,2048]{1,0:T(8,128)(2,1)} %get-tuple-element.218.refs_0_), channel_id=1, source_target_pairs={{0,4},{1,5},{2,6},{3,7},{4,0},{5,1},{6,2},{7,3},{8,12},{9,13},{10,... | collective-permute-start | bytes 3145736 | tf_op jit(solution)/shard_map/ppermute | solution.py:671
  19.6 24.2 %copy-start.8 = (bf16[256,2048]{1,0:T(8,128)(2,1)S(1)}, bf16[256,2048]{1,0:T(8,128)(2,1)}, u32[]{:S(2)}) copy-start(bf16[256,2048]{1,0:T(8,128)(2,1)} %get-tuple-element.219.refs_1_) | copy-start | bytes 3145732
  22.1 47.7 %copy-start.22 = (bf16[1024]{0:T(1024)(128)(2,1)S(1)}, bf16[1024]{0:T(1024)(128)(2,1)}, u32[]{:S(2)}) copy-start(bf16[1024]{0:T(1024)(128)(2,1)} %param.23) | copy-start | bytes 6148
  41.7 30.9 %copy-start.6 = (bf16[256,2048]{1,0:T(8,128)(2,1)}, bf16[256,2048]{1,0:T(8,128)(2,1)S(1)}, u32[]{:S(2)}) copy-start(bf16[256,2048]{1,0:T(8,128)(2,1)S(1)} %collective-permute-done.refs_4_) | copy-start | bytes 3145732
  43.8 28.8 %copy-start.7 = (bf16[256,2048]{1,0:T(8,128)(2,1)}, bf16[256,2048]{1,0:T(8,128)(2,1)S(1)}, u32[]{:S(2)}) copy-start(bf16[256,2048]{1,0:T(8,128)(2,1)S(1)} %collective-permute-done.1.refs_7_) | copy-start | bytes 3145732
  43.8 21.1 %collective-permute-start.5 = (bf16[256,2048]{1,0:T(8,128)(2,1)S(1)}, bf16[256,2048]{1,0:T(8,128)(2,1)}, u32[]{:S(2)}, u32[]{:S(2)}) collective-permute-start(bf16[256,2048]{1,0:T(8,128)(2,1)S(1)} %copy-done.8), channel_id=1, source_target_pairs={{0,1},{1,0},{2,3},{3,2},{4,5},{5,4},{6,7},{7,6},{8,9},{9,8},{10,11... | collective-permute-start | bytes 3145736 | tf_op jit(solution)/shard_map/ppermute | solution.py:671
  64.9 432.6 %all-gather.5.cloned.1.call-start = ((), (), s32[]{:S(2)}) async-start(), calls=%async_computation.4 | async-start | bytes 9437184 | tf_op jit(solution)/shard_map/all_gather | solution.py:837
  65.0 3.4 collective-permute-start.6
  65.1 5.6 collective-permute-start.7
  65.5 7.0 %collective-permute-start.8 = (bf16[256,2048]{1,0:T(8,128)(2,1)}, bf16[256,2048]{1,0:T(8,128)(2,1)}, u32[]{:S(2)}, u32[]{:S(2)}) collective-permute-start(bf16[256,2048]{1,0:T(8,128)(2,1)} %collective-permute-done.4.refs_6_), channel_id=1, source_target_pairs={{0,1},{1,0},{2,3},{3,2},{4,5},{5,4},{6,7},{7,6},{8,9},{9,8},{10,11... | collective-permute-start | bytes 3145736 | tf_op jit(solution)/shard_map/ppermute | solution.py:671
  65.6 6.9 %collective-permute-start.9 = (bf16[256,2048]{1,0:T(8,128)(2,1)S(1)}, bf16[256,2048]{1,0:T(8,128)(2,1)}, u32[]{:S(2)}, u32[]{:S(2)}) collective-permute-start(bf16[256,2048]{1,0:T(8,128)(2,1)S(1)} %collective-permute-done.1.refs_7_), channel_id=1, source_target_pairs={{0,1},{1,0},{2,3},{3,2},{4,5},{5,4},{6,7},{7,6},{8,9},{9,8},{10,11... | collective-permute-start | bytes 3145736 | tf_op jit(solution)/shard_map/ppermute | solution.py:671
  66.1 43.2 %collective-permute-start.10 = (bf16[256,2048]{1,0:T(8,128)(2,1)S(1)}, bf16[256,2048]{1,0:T(8,128)(2,1)S(1)}, u32[]{:S(2)}, u32[]{:S(2)}) collective-permute-start(bf16[256,2048]{1,0:T(8,128)(2,1)S(1)} %collective-permute-done.refs_4_), channel_id=1, source_target_pairs={{0,4},{1,5},{2,6},{3,7},{4,0},{5,1},{6,2},{7,3},{8,12},{9,13},{10,... | collective-permute-start | bytes 3145736 | tf_op jit(solution)/shard_map/ppermute | solution.py:671
  69.4 43.5 %collective-permute-start.11 = (bf16[256,2048]{1,0:T(8,128)(2,1)S(1)}, bf16[256,2048]{1,0:T(8,128)(2,1)}, u32[]{:S(2)}, u32[]{:S(2)}) collective-permute-start(bf16[256,2048]{1,0:T(8,128)(2,1)S(1)} %collective-permute-done.1.refs_7_), channel_id=1, source_target_pairs={{0,2},{1,3},{2,0},{3,1},{4,6},{5,7},{6,4},{7,5},{8,10},{9,11},{10,... | collective-permute-start | bytes 3145736 | tf_op jit(solution)/shard_map/ppermute | solution.py:671
  109.3 8.0 %copy-start.10 = (bf16[256,2048]{1,0:T(8,128)(2,1)}, bf16[256,2048]{1,0:T(8,128)(2,1)S(1)}, u32[]{:S(2)}) copy-start(bf16[256,2048]{1,0:T(8,128)(2,1)S(1)} %collective-permute-done.10.refs_1_) | copy-start | bytes 3145732
  112.9 4.1 collective-permute-start.12
  112.9 4.4 collective-permute-start.13
  123.7 12.8 %copy-start.23 = (bf16[3,256]{1,0:T(4,128)(2,1)S(1)}, bf16[3,256]{1,0:T(4,128)(2,1)}, u32[]{:S(2)}) copy-start(bf16[3,256]{1,0:T(4,128)(2,1)} %param.19) | copy-start | bytes 4612
  136.2 361.3 %reduce-scatter.3.cloned.1.call-start = ((), (), s32[]{:S(2)}) async-start(), calls=%async_computation.5 | async-start | bytes 18874368 | tf_op jit(solution)/shard_map/reduce_scatter | solution.py:846
  186.9 49.7 %collective-permute-start.14 = (bf16[512,2048]{1,0:T(8,128)(2,1)}, bf16[512,2048]{1,0:T(8,128)(2,1)S(1)}, u32[]{:S(2)}, u32[]{:S(2)}) collective-permute-start(bf16[512,2048]{1,0:T(8,128)(2,1)} %weight_grad.3), channel_id=1, source_target_pairs={{0,8},{24,16},{1,9},{25,17},{2,10},{26,18},{3,11},{27,19},{4,12},{... | collective-permute-start | bytes 6291464 | tf_op jit(solution)/shard_map/ppermute | solution.py:601
  204.2 80.3 %collective-permute-start.16 = (bf16[512,2048]{1,0:T(8,128)(2,1)}, bf16[512,2048]{1,0:T(8,128)(2,1)}, u32[]{:S(2)}, u32[]{:S(2)}) collective-permute-start(bf16[512,2048]{1,0:T(8,128)(2,1)} %weight_grad.4), channel_id=1, source_target_pairs={{0,8},{24,16},{1,9},{25,17},{2,10},{26,18},{3,11},{27,19},{4,12},{... | collective-permute-start | bytes 6291464 | tf_op jit(solution)/shard_map/ppermute | solution.py:601
  206.9 29.7 %copy-start.3 = (bf16[512,2048]{1,0:T(8,128)(2,1)S(1)}, bf16[512,2048]{1,0:T(8,128)(2,1)}, u32[]{:S(2)}) copy-start(bf16[512,2048]{1,0:T(8,128)(2,1)} %weight_grad.3) | copy-start | bytes 6291460
  237.5 51.5 %collective-permute-start.15 = (bf16[512,2048]{1,0:T(8,128)(2,1)S(1)}, bf16[512,2048]{1,0:T(8,128)(2,1)}, u32[]{:S(2)}, u32[]{:S(2)}) collective-permute-start(bf16[512,2048]{1,0:T(8,128)(2,1)S(1)} %add_convert_fusion.9), channel_id=1, source_target_pairs={{8,16},{16,8},{9,17},{17,9},{10,18},{18,10},{11,19},{19,11},{12,20... | collective-permute-start | bytes 6291464 | tf_op jit(solution)/shard_map/ppermute | solution.py:601
  264.1 67.7 %collective-permute-start.17 = (bf16[1024,1024]{1,0:T(8,128)(2,1)}, bf16[1024,1024]{1,0:T(8,128)(2,1)}, u32[]{:S(2)}, u32[]{:S(2)}) collective-permute-start(bf16[1024,1024]{1,0:T(8,128)(2,1)} %get-tuple-element.288), channel_id=1, source_target_pairs={{0,8},{24,16},{1,9},{25,17},{2,10},{26,18},{3,11},{27,19},{4,12},{... | collective-permute-start | bytes 6291464 | tf_op jit(solution)/shard_map/ppermute | solution.py:601
  271.1 13.4 %copy-start.2 = (bf16[512,2048]{1,0:T(8,128)(2,1)S(1)}, bf16[512,2048]{1,0:T(8,128)(2,1)}, u32[]{:S(2)}) copy-start(bf16[512,2048]{1,0:T(8,128)(2,1)} %weight_grad.4) | copy-start | bytes 6291460
  286.9 73.5 %collective-permute-start.21 = (bf16[512,2048]{1,0:T(8,128)(2,1)S(1)}, bf16[512,2048]{1,0:T(8,128)(2,1)}, u32[]{:S(2)}, u32[]{:S(2)}) collective-permute-start(bf16[512,2048]{1,0:T(8,128)(2,1)S(1)} %add_convert_fusion.8), channel_id=1, source_target_pairs={{8,16},{16,8},{9,17},{17,9},{10,18},{18,10},{11,19},{19,11},{12,20... | collective-permute-start | bytes 6291464 | tf_op jit(solution)/shard_map/ppermute | solution.py:601
  292.8 72.8 %collective-permute-start.20 = (bf16[512,2048]{1,0:T(8,128)(2,1)}, bf16[512,2048]{1,0:T(8,128)(2,1)}, u32[]{:S(2)}, u32[]{:S(2)}) collective-permute-start(bf16[512,2048]{1,0:T(8,128)(2,1)} %add_convert_fusion.7.kept_ref), channel_id=1, source_target_pairs={{8,0},{16,24},{9,1},{17,25},{10,2},{18,26},{11,3},{19,27},{12,4},{... | collective-permute-start | bytes 6291464 | tf_op jit(solution)/shard_map/ppermute | solution.py:601
  294.1 90.7 %collective-permute-start.19 = (bf16[1024,1024]{1,0:T(8,128)(2,1)}, bf16[1024,1024]{1,0:T(8,128)(2,1)}, u32[]{:S(2)}, u32[]{:S(2)}) collective-permute-start(bf16[1024,1024]{1,0:T(8,128)(2,1)} %get-tuple-element.309), channel_id=1, source_target_pairs={{0,8},{24,16},{1,9},{25,17},{2,10},{26,18},{3,11},{27,19},{4,12},{... | collective-permute-start | bytes 6291464 | tf_op jit(solution)/shard_map/ppermute | solution.py:601
  309.6 22.2 %copy-start.4 = (bf16[1024,1024]{1,0:T(8,128)(2,1)S(1)}, bf16[1024,1024]{1,0:T(8,128)(2,1)}, u32[]{:S(2)}) copy-start(bf16[1024,1024]{1,0:T(8,128)(2,1)} %get-tuple-element.288) | copy-start | bytes 6291460
  336.2 61.8 %collective-permute-start.18 = (bf16[1024,1024]{1,0:T(8,128)(2,1)}, bf16[1024,1024]{1,0:T(8,128)(2,1)}, u32[]{:S(2)}, u32[]{:S(2)}) collective-permute-start(bf16[1024,1024]{1,0:T(8,128)(2,1)} %add_convert_fusion.6), channel_id=1, source_target_pairs={{8,16},{16,8},{9,17},{17,9},{10,18},{18,10},{11,19},{19,11},{12,20... | collective-permute-start | bytes 6291464 | tf_op jit(solution)/shard_map/ppermute | solution.py:601
  364.1 61.4 %collective-permute-start.26 = (bf16[512,2048]{1,0:T(8,128)(2,1)}, bf16[512,2048]{1,0:T(8,128)(2,1)}, u32[]{:S(2)}, u32[]{:S(2)}) collective-permute-start(bf16[512,2048]{1,0:T(8,128)(2,1)} %add_convert_fusion.5.kept_ref), channel_id=1, source_target_pairs={{8,0},{16,24},{9,1},{17,25},{10,2},{18,26},{11,3},{19,27},{12,4},{... | collective-permute-start | bytes 6291464 | tf_op jit(solution)/shard_map/ppermute | solution.py:601
  384.8 5.3 copy-start.5
  388.1 47.5 %collective-permute-start.25 = (bf16[1024,1024]{1,0:T(8,128)(2,1)S(1)}, bf16[1024,1024]{1,0:T(8,128)(2,1)}, u32[]{:S(2)}, u32[]{:S(2)}) collective-permute-start(bf16[1024,1024]{1,0:T(8,128)(2,1)S(1)} %add_convert_fusion.4), channel_id=1, source_target_pairs={{8,16},{16,8},{9,17},{17,9},{10,18},{18,10},{11,19},{19,11},{12,20... | collective-permute-start | bytes 6291464 | tf_op jit(solution)/shard_map/ppermute | solution.py:601
  390.1 49.4 %collective-permute-start.24 = (bf16[2,2048,256]{2,1,0:T(8,128)(2,1)S(1)}, bf16[2,2048,256]{2,1,0:T(8,128)(2,1)}, u32[]{:S(2)}, u32[]{:S(2)}) collective-permute-start(bf16[2,2048,256]{2,1,0:T(8,128)(2,1)S(1)} %copy-done.5), channel_id=1, source_target_pairs={{0,8},{24,16},{1,9},{25,17},{2,10},{26,18},{3,11},{27,19},{4,12},{... | collective-permute-start | bytes 6291464 | tf_op jit(solution)/shard_map/ppermute | solution.py:601
  401.2 24.3 %copy-start = (bf16[1024,1024]{1,0:T(8,128)(2,1)}, bf16[1024,1024]{1,0:T(8,128)(2,1)S(1)}, u32[]{:S(2)}) copy-start(bf16[1024,1024]{1,0:T(8,128)(2,1)S(1)} %add_convert_fusion.3.kept_ref) | copy-start | bytes 6291460
  401.2 93.7 %collective-permute-start.22 = (bf16[1024,1024]{1,0:T(8,128)(2,1)S(1)}, bf16[1024,1024]{1,0:T(8,128)(2,1)}, u32[]{:S(2)}, u32[]{:S(2)}) collective-permute-start(bf16[1024,1024]{1,0:T(8,128)(2,1)S(1)} %add_convert_fusion.3.kept_ref), channel_id=1, source_target_pairs={{8,0},{16,24},{9,1},{17,25},{10,2},{18,26},{11,3},{19,27},{12,4},{... | collective-permute-start | bytes 6291464 | tf_op jit(solution)/shard_map/ppermute | solution.py:601
  442.9 6.5 %copy-start.9 = (bf16[2048,256]{1,0:T(8,128)(2,1)S(1)}, bf16[2048,256]{1,0:T(8,128)(2,1)}, u32[]{:S(2)}) copy-start(bf16[2048,256]{1,0:T(8,128)(2,1)} %get-tuple-element.337) | copy-start | bytes 3145732
  442.9 66.6 %collective-permute-start.27 = (bf16[2,2048,256]{2,1,0:T(8,128)(2,1)}, bf16[2,2048,256]{2,1,0:T(8,128)(2,1)}, u32[]{:S(2)}, u32[]{:S(2)}) collective-permute-start(bf16[2,2048,256]{2,1,0:T(8,128)(2,1)} %add_convert_fusion.1), channel_id=1, source_target_pairs={{8,16},{16,8},{9,17},{17,9},{10,18},{18,10},{11,19},{19,11},{12,20... | collective-permute-start | bytes 6291464 | tf_op jit(solution)/shard_map/ppermute | solution.py:601
  445.0 52.5 %all-to-all-start = ((bf16[8,2,256,256]{3,2,1,0:T(8,128)(2,1)}), bf16[8,2,256,256]{3,2,1,0:T(8,128)(2,1)}, u32[]{:S(2)}, u32[]{:S(2)}) async-start(bf16[8,2,256,256]{3,2,1,0:T(8,128)(2,1)} %get-tuple-element.298), calls=%async_computation | async-start | bytes 4194304 | tf_op jit(solution)/shard_map/all_to_all | solution.py:855
  449.4 151.4 %reduce-scatter.5.cloned.1.call-start = ((), (), s32[]{:S(2)}) async-start(), calls=%async_computation.6 | async-start | bytes 18874368 | tf_op jit(solution)/shard_map/reduce_scatter | solution.py:869
  449.4 41.6 %collective-permute-start.23 = (bf16[2048,256]{1,0:T(8,128)(2,1)S(1)}, bf16[2048,256]{1,0:T(8,128)(2,1)}, u32[]{:S(2)}, u32[]{:S(2)}) collective-permute-start(bf16[2048,256]{1,0:T(8,128)(2,1)S(1)} %copy-done.9), channel_id=1, source_target_pairs={{0,8},{24,16},{1,9},{25,17},{2,10},{26,18},{3,11},{27,19},{4,12},{... | collective-permute-start | bytes 3145736 | tf_op jit(solution)/shard_map/ppermute | solution.py:601
  458.2 56.0 %collective-permute-start.30 = (bf16[1024,1024]{1,0:T(8,128)(2,1)}, bf16[1024,1024]{1,0:T(8,128)(2,1)}, u32[]{:S(2)}, u32[]{:S(2)}) collective-permute-start(bf16[1024,1024]{1,0:T(8,128)(2,1)} %add_convert_fusion.2.kept_ref), channel_id=1, source_target_pairs={{8,0},{16,24},{9,1},{17,25},{10,2},{18,26},{11,3},{19,27},{12,4},{... | collective-permute-start | bytes 6291464 | tf_op jit(solution)/shard_map/ppermute | solution.py:601
  484.2 30.3 %collective-permute-start.29 = (bf16[256,2048]{1,0:T(8,128)(2,1)}, bf16[256,2048]{1,0:T(8,128)(2,1)}, u32[]{:S(2)}, u32[]{:S(2)}) collective-permute-start(bf16[256,2048]{1,0:T(8,128)(2,1)} %weight_grad.5), channel_id=1, source_target_pairs={{0,8},{24,16},{1,9},{25,17},{2,10},{26,18},{3,11},{27,19},{4,12},{... | collective-permute-start | bytes 3145736 | tf_op jit(solution)/shard_map/ppermute | solution.py:601
  493.2 42.3 %collective-permute-start.36 = (bf16[2048,256]{1,0:T(8,128)(2,1)S(1)}, bf16[2048,256]{1,0:T(8,128)(2,1)}, u32[]{:S(2)}, u32[]{:S(2)}) collective-permute-start(bf16[2048,256]{1,0:T(8,128)(2,1)S(1)} %add_convert_fusion.13), channel_id=1, source_target_pairs={{8,16},{16,8},{9,17},{17,9},{10,18},{18,10},{11,19},{19,11},{12,20... | collective-permute-start | bytes 3145736 | tf_op jit(solution)/shard_map/ppermute | solution.py:601
  509.6 4.6 copy-start.14
  509.6 4.6 copy-start.15
  509.6 4.6 copy-start.16
  509.6 4.6 copy-start.20
  512.8 25.3 %copy-start.1 = (bf16[2,2048,256]{2,1,0:T(8,128)(2,1)}, bf16[2,2048,256]{2,1,0:T(8,128)(2,1)S(1)}, u32[]{:S(2)}) copy-start(bf16[2,2048,256]{2,1,0:T(8,128)(2,1)S(1)} %add_convert_fusion) | copy-start | bytes 6291460
  512.8 50.6 %collective-permute-start.28 = (bf16[2,2048,256]{2,1,0:T(8,128)(2,1)S(1)}, bf16[2,2048,256]{2,1,0:T(8,128)(2,1)}, u32[]{:S(2)}, u32[]{:S(2)}) collective-permute-start(bf16[2,2048,256]{2,1,0:T(8,128)(2,1)S(1)} %add_convert_fusion), channel_id=1, source_target_pairs={{8,0},{16,24},{9,1},{17,25},{10,2},{18,26},{11,3},{19,27},{12,4},{... | collective-permute-start | bytes 6291464 | tf_op jit(solution)/shard_map/ppermute | solution.py:601
  517.4 24.0 %collective-permute-start.31 = (bf16[256,2048]{1,0:T(8,128)(2,1)}, bf16[256,2048]{1,0:T(8,128)(2,1)}, u32[]{:S(2)}, u32[]{:S(2)}) collective-permute-start(bf16[256,2048]{1,0:T(8,128)(2,1)} %add_convert_fusion.12), channel_id=1, source_target_pairs={{8,16},{16,8},{9,17},{17,9},{10,18},{18,10},{11,19},{19,11},{12,20... | collective-permute-start | bytes 3145736 | tf_op jit(solution)/shard_map/ppermute | solution.py:601
  519.0 1.2 collective-permute-start.32
  520.2 4.0 collective-permute-start.33
  524.2 4.2 collective-permute-start.34
  528.4 11.1 %collective-permute-start.35 = (f32[49,128]{1,0:T(8,128)S(1)}, f32[49,128]{1,0:T(8,128)S(1)}, u32[]{:S(2)}, u32[]{:S(2)}) collective-permute-start(f32[49,128]{1,0:T(8,128)S(1)} %pad_maximum_fusion), channel_id=1, source_target_pairs={{0,8},{24,16},{1,9},{25,17},{2,10},{26,18},{3,11},{27,19},{4,12},{... | collective-permute-start | bytes 75272 | tf_op jit(solution)/shard_map/ppermute | solution.py:601
  538.2 68.9 %collective-permute-start.40 = (bf16[2048,256]{1,0:T(8,128)(2,1)}, bf16[2048,256]{1,0:T(8,128)(2,1)}, u32[]{:S(2)}, u32[]{:S(2)}) collective-permute-start(bf16[2048,256]{1,0:T(8,128)(2,1)} %add_convert_fusion.11.kept_ref), channel_id=1, source_target_pairs={{8,0},{16,24},{9,1},{17,25},{10,2},{18,26},{11,3},{19,27},{12,4},{... | collective-permute-start | bytes 3145736 | tf_op jit(solution)/shard_map/ppermute | solution.py:601
  540.1 36.2 %collective-permute-start.37 = (f32[49,128]{1,0:T(8,128)}, f32[49,128]{1,0:T(8,128)}, u32[]{:S(2)}, u32[]{:S(2)}) collective-permute-start(f32[49,128]{1,0:T(8,128)} %add.132), channel_id=1, source_target_pairs={{8,16},{16,8},{9,17},{17,9},{10,18},{18,10},{11,19},{19,11},{12,20... | collective-permute-start | bytes 75272 | tf_op jit(solution)/shard_map/ppermute | solution.py:601
  544.3 66.5 %collective-permute-start.39 = (bf16[256,2048]{1,0:T(8,128)(2,1)}, bf16[256,2048]{1,0:T(8,128)(2,1)}, u32[]{:S(2)}, u32[]{:S(2)}) collective-permute-start(bf16[256,2048]{1,0:T(8,128)(2,1)} %add_convert_fusion.10.kept_ref), channel_id=1, source_target_pairs={{8,0},{16,24},{9,1},{17,25},{10,2},{18,26},{11,3},{19,27},{12,4},{... | collective-permute-start | bytes 3145736 | tf_op jit(solution)/shard_map/ppermute | solution.py:601
  577.0 36.8 %collective-permute-start.38 = (f32[49,128]{1,0:T(8,128)S(1)}, f32[49,128]{1,0:T(8,128)S(1)}, u32[]{:S(2)}, u32[]{:S(2)}) collective-permute-start(f32[49,128]{1,0:T(8,128)S(1)} %add.134), channel_id=1, source_target_pairs={{8,0},{16,24},{9,1},{17,25},{10,2},{18,26},{11,3},{19,27},{12,4},{... | collective-permute-start | bytes 75272 | tf_op jit(solution)/shard_map/ppermute | solution.py:601
  (6 other events, 8.5 us)
Sparse Core Ops, SparseCore 0:
  65.0 107.5 all-gather.2
  174.5 54.3 all-gather.4
  309.7 114.0 reduce-scatter.2
  482.5 118.2 reduce-scatter.4

commit v10 on v9

--- a/solution.py
+++ b/solution.py
@@ -909,11 +909,11 @@
     in_grad = finish(i1, order, width, width // 2, in_grad)
     qkv_grad = finish(qs, order, 3 * width)
 
-    token_back = lambda b, t, c: norm_back(rows_of(b), rows_of(t), rows_of(c), gain).reshape(tokens.shape)
-    input_grad = order(token_back, back_tok, tokens, cotangent)
     qkv_grad = finish(vs, order, 3 * width, 2 * width, qkv_grad)
     qkv_grad = jnp.transpose(qkv_grad.reshape(3, width, local), (1, 0, 2))
     dense_grad = finish(ds, order, local)
+    token_back = lambda b, t, c: norm_back(rows_of(b), rows_of(t), rows_of(c), gain).reshape(tokens.shape)
+    input_grad = order(token_back, back_tok, tokens, cotangent)
     small.settle(order)
     small = small.result().reshape(-1)
     slice_at = lambda a: lax.dynamic_slice_in_dim(a, lax.axis_index("tp") * cols, cols, 0)

time: 634 us -> 637 us (level)
    ppermute x24, waiting for transfers between devices: 17.9 us -> 32.6 us  [send(): self.came = lax.ppermute(self.part, self.axis, self.hops.pop(0))]
    reduce_scatter x1, waiting for transfers between devices: 12.1 us -> 0.01 us  [body(): lax.psum_scatter(part.reshape(seqs, length, width), 'tp', scatter_dimensi...]
  transfers between devices with their start and end apart: 46 -> 46, of which waited for: 17 -> 17; matrix products, arithmetic and copies ran while one was open for 9% -> 9% of each run, Pallas kernels for 58% -> 57%
where the time goes in v10:
time: 637 us; the launch traced here: 627 us
  Pallas kernels  365 us (57%)
  starting transfers between devices  102 us (16%)
  waiting for transfers between devices  81.6 us (13%)
  other arithmetic  54.5 us (9%)
  between operations  14.7 us (2%)
  local copies, waits for them, and re-layouts  9.37 us (1%)
    ppermute x24, starting transfers between devices, send(): self.came = lax.ppermute(self.part, self.axis, self.hops.pop(0))  84.8 us
    pallas_call x2, Pallas kernels, normed_grad(): pl.pallas_call(functools.partial(normed_grad_kernel, held=held), grid=(st...  45.6 us
    pallas_call x2, Pallas kernels, attention_both(): pl.pallas_call(functools.partial(attention_kernel, bq=bq, held=held), gri...  44.3 us
    convert_element_type x14, other arithmetic, fold(): add = lambda a, b: (a.astype(f32) + b.astype(f32)).astype(a.dtype)  43.1 us
    ppermute x14, waiting for transfers between devices, send(): return lax.ppermute(a, 'tp', [(i, i ^ step) for i in range(self.size)])  42.8 us
    pallas_call x3, Pallas kernels, weight_grad(): pl.pallas_call(weight_grad_kernel, grid=(cols // tile,), in_specs=[pl.Blo...  38.1 us
    pallas_call x2, Pallas kernels, mlp_hidden_of(): pl.pallas_call(functools.partial(chosen_kernel, held=held), grid_spec=plt...  36.1 us
    ppermute x24, waiting for transfers between devices, send(): self.came = lax.ppermute(self.part, self.axis, self.hops.pop(0))  32.6 us
  transfers between devices with their start and end apart: 46, of which 17 were waited for; matrix products, arithmetic and copies ran while one was open for 9% of the time, Pallas kernels for 57%

profile of v10, /device:TPU:0, one launch (start us, length us, event | category | flops | bytes accessed | tf_op | source)
XLA Modules:
  0.0 627.0 jit_solution(5646751820900330616)
XLA Ops:
  9.8 4.7 norm_halves.1
  14.6 2.9 collective-permute-start
  22.1 9.8 %rope_tables.1 = (f32[4096,128]{1,0:T(8,128)}, f32[4096,128]{1,0:T(8,128)}) custom-call(s32[4096,1]{1,0:T(8,128)} %bitcast.75, f32[1,128]{1,0:T(1,128)} %fusion.4.frequency_ref), custom_call_target="tpu_custom_call" | custom-call | flops 1 | bytes 1 | tf_op jit(solution)/shard_map/rope_tables/pallas_call | solution.py:126
  32.5 9.2 %collective-permute-done.refs_4_ = bf16[256,2048]{1,0:T(8,128)(2,1)S(1)} collective-permute-done((bf16[256,2048]{1,0:T(8,128)(2,1)}, bf16[256,2048]{1,0:T(8,128)(2,1)S(1)}, u32[]{:S(2)}, u32[]{:S(2)}) %collective-permute-start) | collective-permute-done | bytes 1048608 | tf_op jit(solution)/shard_map/ppermute | solution.py:671
  41.7 2.1 collective-permute-done.1.refs_7_
  43.9 19.6 %collective-permute-done.3.refs_5_ = bf16[256,2048]{1,0:T(8,128)(2,1)} collective-permute-done((bf16[256,2048]{1,0:T(8,128)(2,1)}, bf16[256,2048]{1,0:T(8,128)(2,1)}, u32[]{:S(2)}, u32[]{:S(2)}) %collective-permute-start.3) | collective-permute-done | bytes 1048608 | tf_op jit(solution)/shard_map/ppermute | solution.py:671
  72.6 13.1 %place_pieces.2.refs_0_ = bf16[2,8,256,2048]{3,2,1,0:T(8,128)(2,1)} custom-call(s32[1]{0:T(128)} %bitcast.3.me_ref, bf16[256,2048]{1,0:T(8,128)(2,1)} %get-tuple-element.218.refs_0_, bf16[256,2048]{1,0:T(8,128)(2,1)} %get-tuple-element.219.refs_1_, bf16[256,2048]{1,0:T(8,128)(2,1)} %collective-permute-done.2.refs_2_, ...), custom_call_target="tpu_custom_call" | custom-call | flops 1 | bytes 1 | tf_op jit(solution)/shard_map/place_pieces/pallas_call | solution.py:732
  85.6 23.6 %mlp_hidden_of.2 = (bf16[2,8,256,1024]{3,2,1,0:T(8,128)(2,1)}, bf16[2,8,256,1024]{3,2,1,0:T(8,128)(2,1)}) custom-call(s32[1]{0:T(128)} %bitcast.3.me_ref, bf16[2,8,256,2048]{3,2,1,0:T(8,128)(2,1)} %place_pieces.2.refs_0_, bf16[2048,1024]{1,0:T(8,128)(2,1)} %refs_3_.1, f32[1,1024]{1,0:T(1,128)} %bitcast.89), custom_call_target="tpu_custom_call" | custom-call | flops 1 | bytes 1 | tf_op jit(solution)/shard_map/mlp_hidden_of/pallas_call | solution.py:207
  109.3 3.6 collective-permute-done.11.refs_2_
  113.4 3.6 collective-permute-done.12.refs_3_
  119.0 4.8 place_pieces.3.refs_2_
  123.7 12.4 %mlp_hidden_of.3 = (bf16[2,8,256,1024]{3,2,1,0:T(8,128)(2,1)}, bf16[2,8,256,1024]{3,2,1,0:T(8,128)(2,1)}) custom-call(s32[1]{0:T(128)} %bitcast.3.me_ref, bf16[2,8,256,1024]{3,2,1,0:T(8,128)(2,1)} %get-tuple-element.242.refs_0_, bf16[2,8,256,1024]{3,2,1,0:T(8,128)(2,1)} %get-tuple-element.243.refs_1_, ...), custom_call_target="tpu_custom_call", output_to_operand_aliasing={{0}: (1, {}), {1}: (2, {})} | custom-call | flops 1 | bytes 1 | tf_op jit(solution)/shard_map/mlp_hidden_of/pallas_call | solution.py:207
  137.1 20.1 %qkv_rope.1.refs_1_.refs_2_.refs_3_.refs_4_.refs_5_.refs_6_ = bf16[3,4096,256]{2,1,0:T(8,128)(2,1)} custom-call(bf16[4096,2048]{1,0:T(8,128)(2,1)} %bitcast.49, bf16[3,2048,256]{2,1,0:T(8,128)(2,1)} %bitcast.66, f32[3,256]{1,0:T(4,128)} %convert_element_type.158.b_ref, f32[4096,128]{1,0:T(8,128)} %get-tuple-element.296.c_ref.refs_5_.refs_8_, ...), custom_call_target="tpu_custom_call" | custom-call | flops 1 | bytes 1 | tf_op jit(solution)/shard_map/qkv_rope/pallas_call | solution.py:158
  157.2 13.3 %tokens_by_weight.2.refs_0_ = bf16[4096,2048]{1,0:T(8,128)(2,1)} custom-call(bf16[4096,1024]{1,0:T(8,128)(2,1)} %bitcast.59, bf16[1024,2048]{1,0:T(8,128)(2,1)} %refs_2_), custom_call_target="tpu_custom_call" | custom-call | flops 1 | bytes 1 | tf_op jit(solution)/shard_map/tokens_by_weight/pallas_call | solution.py:287
  170.4 2.2 all-gather.3.cloned.1.call-done
  172.6 14.2 %weight_grad.3 = bf16[512,2048]{1,0:T(8,128)(2,1)} custom-call(bf16[4096,1024]{1,0:T(8,128)(2,1)} %bitcast.60, bf16[4096,2048]{1,0:T(8,128)(2,1)} %bitcast.54), custom_call_target="tpu_custom_call" | custom-call | flops 1 | bytes 1 | tf_op jit(solution)/shard_map/weight_grad/pallas_call | solution.py:310
  186.9 3.5 collective-permute-start.14
  190.4 13.8 %weight_grad.4 = bf16[512,2048]{1,0:T(8,128)(2,1)} custom-call(bf16[4096,1024]{1,0:T(8,128)(2,1)} %bitcast.61, bf16[4096,2048]{1,0:T(8,128)(2,1)} %bitcast.55), custom_call_target="tpu_custom_call" | custom-call | flops 1 | bytes 1 | tf_op jit(solution)/shard_map/weight_grad/pallas_call | solution.py:310
  204.2 2.7 collective-permute-start.16
  206.9 29.6 %grad_in.1 = (bf16[4096,1024]{1,0:T(8,128)(2,1)}, bf16[4096,256]{1,0:T(8,128)(2,1)}, f32[8,1024]{1,0:T(8,128)}) custom-call(bf16[4096,2048]{1,0:T(8,128)(2,1)} %bitcast.56, bf16[1024,2048]{1,0:T(8,128)(2,1)} %refs_2_, bf16[256,2048]{1,0:T(8,128)(2,1)} %wd_ref, bf16[4096,1024]{1,0:T(8,128)(2,1)} %bitcast.65), custom_call_target="tpu_custom_call" | custom-call | flops 1 | bytes 1 | tf_op jit(solution)/shard_map/grad_in/pallas_call | solution.py:248
  239.5 24.6 %weight_grad_rows.1 = (bf16[1024,1024]{1,0:T(8,128)(2,1)}, bf16[1024,1024]{1,0:T(8,128)(2,1)}) custom-call(bf16[4096,2048]{1,0:T(8,128)(2,1)} %bitcast.50, bf16[4096,1024]{1,0:T(8,128)(2,1)} %get-tuple-element.329.b_ref.refs_0_.refs_1_), custom_call_target="tpu_custom_call" | custom-call | flops 1 | bytes 1 | tf_op jit(solution)/shard_map/weight_grad_rows/pallas_call | solution.py:344
  264.1 7.1 %collective-permute-start.17 = (bf16[1024,1024]{1,0:T(8,128)(2,1)}, bf16[1024,1024]{1,0:T(8,128)(2,1)}, u32[]{:S(2)}, u32[]{:S(2)}) collective-permute-start(bf16[1024,1024]{1,0:T(8,128)(2,1)} %get-tuple-element.288), channel_id=1, source_target_pairs={{0,8},{24,16},{1,9},{25,17},{2,10},{26,18},{3,11},{27,19},{4,12},{... | collective-permute-start | bytes 6291464 | tf_op jit(solution)/shard_map/ppermute | solution.py:601
  271.1 13.4 %tokens_by_weight.3 = bf16[4096,2048]{1,0:T(8,128)(2,1)} custom-call(bf16[4096,2048]{1,0:T(8,128)(2,1)} %tokens_by_weight.2.refs_0_, bf16[4096,1024]{1,0:T(8,128)(2,1)} %bitcast.62, bf16[1024,2048]{1,0:T(8,128)(2,1)} %refs_2_), custom_call_target="tpu_custom_call", output_to_operand_aliasing={{}: (0, {})} | custom-call | flops 1 | bytes 1 | tf_op jit(solution)/shard_map/tokens_by_weight/pallas_call | solution.py:287
  284.5 2.4 add_convert_fusion.8
  286.9 2.1 collective-permute-start.21
  288.9 3.9 add_convert_fusion.7.kept_ref
  294.1 15.4 %collective-permute-start.19 = (bf16[1024,1024]{1,0:T(8,128)(2,1)}, bf16[1024,1024]{1,0:T(8,128)(2,1)}, u32[]{:S(2)}, u32[]{:S(2)}) collective-permute-start(bf16[1024,1024]{1,0:T(8,128)(2,1)} %get-tuple-element.309), channel_id=1, source_target_pairs={{0,8},{24,16},{1,9},{25,17},{2,10},{26,18},{3,11},{27,19},{4,12},{... | collective-permute-start | bytes 6291464 | tf_op jit(solution)/shard_map/ppermute | solution.py:601
  309.6 22.2 %attention_both.2 = (bf16[4096,256]{1,0:T(8,128)(2,1)}, bf16[8,2,256,256]{3,2,1,0:T(8,128)(2,1)}, bf16[3,4096,256]{2,1,0:T(8,128)(2,1)}) custom-call(s32[1,4096]{1,0:T(1,128)} %fusion.refs_0_.refs_3_, bf16[3,4096,256]{2,1,0:T(8,128)(2,1)} %qkv_rope.1.refs_1_.refs_2_.refs_3_.refs_4_.refs_5_.refs_6_, ...), custom_call_target="tpu_custom_call" | custom-call | flops 1 | bytes 1 | tf_op jit(solution)/shard_map/attention_both/pallas_call | solution.py:507
  331.8 4.4 add_convert_fusion.6
  336.2 2.0 collective-permute-start.18
  338.2 22.1 %attention_both.3 = (bf16[4096,256]{1,0:T(8,128)(2,1)}, bf16[8,2,256,256]{3,2,1,0:T(8,128)(2,1)}, bf16[3,4096,256]{2,1,0:T(8,128)(2,1)}) custom-call(bf16[4096,256]{1,0:T(8,128)(2,1)} %get-tuple-element.290.refs_0_, bf16[8,2,256,256]{3,2,1,0:T(8,128)(2,1)} %get-tuple-element.291.refs_1_, ...), custom_call_target="tpu_custom_call", output_to_operand_aliasing={{0}: (0, {}), {1}: (1, {}), {2}: (2, {})} | custom-call | flops 1 | bytes 1 | tf_op jit(solution)/shard_map/attention_both/pallas_call | solution.py:507
  360.3 3.7 add_convert_fusion.5.kept_ref
  365.6 19.2 %weight_grad_parts.1 = (bf16[2,2048,256]{2,1,0:T(8,128)(2,1)}, bf16[2048,256]{1,0:T(8,128)(2,1)}) custom-call(bf16[4096,2048]{1,0:T(8,128)(2,1)} %bitcast.51, bf16[3,4096,256]{2,1,0:T(8,128)(2,1)} %get-tuple-element.330.b_ref.refs_1_.refs_2_), custom_call_target="tpu_custom_call" | custom-call | flops 219999993856 | bytes 1 | tf_op jit(solution)/shard_map/weight_grad_parts/pallas_call | solution.py:368
  384.8 3.4 add_convert_fusion.4
  390.1 7.8 %collective-permute-start.24 = (bf16[2,2048,256]{2,1,0:T(8,128)(2,1)S(1)}, bf16[2,2048,256]{2,1,0:T(8,128)(2,1)}, u32[]{:S(2)}, u32[]{:S(2)}) collective-permute-start(bf16[2,2048,256]{2,1,0:T(8,128)(2,1)S(1)} %copy-done.5), channel_id=1, source_target_pairs={{0,8},{24,16},{1,9},{25,17},{2,10},{26,18},{3,11},{27,19},{4,12},{... | collective-permute-start | bytes 6291464 | tf_op jit(solution)/shard_map/ppermute | solution.py:601
  397.9 3.3 add_convert_fusion.3.kept_ref
  402.5 23.0 %normed_grad.2 = (bf16[4096,2048]{1,0:T(8,128)(2,1)}, f32[3,8,256]{2,1,0:T(8,128)}, f32[8,2048]{1,0:T(8,128)}) custom-call(bf16[4096,1024]{1,0:T(8,128)(2,1)} %get-tuple-element.329.b_ref.refs_0_.refs_1_, bf16[3,4096,256]{2,1,0:T(8,128)(2,1)} %get-tuple-element.330.b_ref.refs_1_.refs_2_, bf16[2048,1024]{1,0:T(8,128)(2,1)} %refs_3_.1, ...), custom_call_target="tpu_custom_call" | custom-call | flops 1 | bytes 1 | tf_op jit(solution)/shard_map/normed_grad/pallas_call | solution.py:412
  425.5 10.1 %weight_grad.5 = bf16[256,2048]{1,0:T(8,128)(2,1)} custom-call(bf16[4096,256]{1,0:T(8,128)(2,1)} %get-tuple-element.322.a_ref, bf16[4096,2048]{1,0:T(8,128)(2,1)} %bitcast.57), custom_call_target="tpu_custom_call" | custom-call | flops 1 | bytes 1 | tf_op jit(solution)/shard_map/weight_grad/pallas_call | solution.py:310
  435.6 3.9 add_convert_fusion.2.kept_ref
  439.5 3.4 add_convert_fusion.1
  442.9 2.1 collective-permute-start.29
  445.0 4.3 all-to-all-start
  449.4 8.7 %collective-permute-start.23 = (bf16[2048,256]{1,0:T(8,128)(2,1)S(1)}, bf16[2048,256]{1,0:T(8,128)(2,1)}, u32[]{:S(2)}, u32[]{:S(2)}) collective-permute-start(bf16[2048,256]{1,0:T(8,128)(2,1)S(1)} %copy-done.9), channel_id=1, source_target_pairs={{0,8},{24,16},{1,9},{25,17},{2,10},{26,18},{3,11},{27,19},{4,12},{... | collective-permute-start | bytes 3145736 | tf_op jit(solution)/shard_map/ppermute | solution.py:601
  459.7 22.6 %normed_grad.3 = (bf16[4096,2048]{1,0:T(8,128)(2,1)}, f32[3,8,256]{2,1,0:T(8,128)}, f32[8,2048]{1,0:T(8,128)}) custom-call(bf16[4096,2048]{1,0:T(8,128)(2,1)} %get-tuple-element.328.refs_0_, bf16[4096,1024]{1,0:T(8,128)(2,1)} %get-tuple-element.329.b_ref.refs_0_.refs_1_, ...), custom_call_target="tpu_custom_call", output_to_operand_aliasing={{0}: (0, {})} | custom-call | flops 1 | bytes 1 | tf_op jit(solution)/shard_map/normed_grad/pallas_call | solution.py:412
  484.2 6.9 %collective-permute-start.27 = (bf16[256,2048]{1,0:T(8,128)(2,1)}, bf16[256,2048]{1,0:T(8,128)(2,1)}, u32[]{:S(2)}, u32[]{:S(2)}) collective-permute-start(bf16[256,2048]{1,0:T(8,128)(2,1)} %weight_grad.5), channel_id=1, source_target_pairs={{0,8},{24,16},{1,9},{25,17},{2,10},{26,18},{3,11},{27,19},{4,12},{... | collective-permute-start | bytes 3145736 | tf_op jit(solution)/shard_map/ppermute | solution.py:601
  491.1 2.1 add_convert_fusion.13
  495.0 2.5 convert_reduce_fusion
  497.5 12.0 %project_own.1 = (bf16[512,2048]{1,0:T(8,128)(2,1)}, f32[8,512]{1,0:T(8,128)}) custom-call(bf16[8,2,256,256]{3,2,1,0:T(8,128)(2,1)} %all-to-all-done.x_ref, bf16[2048,2048]{1,0:T(8,128)(2,1)} %all-gather.5.cloned.1.call-done.w_ref, f32[1,2048]{1,0:T(1,128)} %bitcast.91, f32[1,2048]{1,0:T(1,128)} %bitcast.92, bf16[512,2048]{1,0:T(8,128)(2,1)} %bitcast.71, ...), custom_call_target="tpu_custom_call" | custom-call | flops 1 | bytes 1 | tf_op jit(solution)/shard_map/project_own/pallas_call | solution.py:563
  509.6 3.2 add_convert_fusion
  514.5 2.9 add_convert_fusion.12
  526.2 2.2 collective-permute-done.33
  528.4 7.1 %collective-permute-start.34 = (f32[49,128]{1,0:T(8,128)S(1)}, f32[49,128]{1,0:T(8,128)S(1)}, u32[]{:S(2)}, u32[]{:S(2)}) collective-permute-start(f32[49,128]{1,0:T(8,128)S(1)} %pad_maximum_fusion), channel_id=1, source_target_pairs={{0,8},{24,16},{1,9},{25,17},{2,10},{26,18},{3,11},{27,19},{4,12},{... | collective-permute-start | bytes 75272 | tf_op jit(solution)/shard_map/ppermute | solution.py:601
  535.5 2.7 add_convert_fusion.11.kept_ref
  541.4 3.0 add_convert_fusion.10.kept_ref
  545.6 17.8 %collective-permute-done.38 = bf16[2,2048,256]{2,1,0:T(8,128)(2,1)} collective-permute-done((bf16[2,2048,256]{2,1,0:T(8,128)(2,1)S(1)}, bf16[2,2048,256]{2,1,0:T(8,128)(2,1)}, u32[]{:S(2)}, u32[]{:S(2)}) %collective-permute-start.38) | collective-permute-done | bytes 2097184 | tf_op jit(solution)/shard_map/ppermute | solution.py:601
  563.4 4.6 finish.7.refs_0_
  568.0 4.6 finish.8
  572.6 3.7 finish.9.refs_0_
  578.3 3.7 finish.10
  582.0 6.7 %finish.11.refs_0_ = f32[6144,256]{1,0:T(8,128)} custom-call(s32[1]{0:T(128)} %bitcast.17.inner_ref, bf16[4096,256]{1,0:T(8,128)(2,1)} %bitcast.74, bf16[4096,256]{1,0:T(8,128)(2,1)} %bitcast.24.came_ref), custom_call_target="tpu_custom_call" | custom-call | flops 1 | bytes 1 | tf_op jit(solution)/shard_map/finish/pallas_call | solution.py:660
  588.7 3.8 finish.12
  592.5 14.7 %collective-permute-done.36.came_ref = bf16[256,2048]{1,0:T(8,128)(2,1)} collective-permute-done((bf16[256,2048]{1,0:T(8,128)(2,1)}, bf16[256,2048]{1,0:T(8,128)(2,1)}, u32[]{:S(2)}, u32[]{:S(2)}) %collective-permute-start.36) | collective-permute-done | bytes 1048608 | tf_op jit(solution)/shard_map/ppermute | solution.py:601
  607.2 3.0 finish.13
  610.2 6.3 norm_back.1
  (159 shorter events, 55.1 us)
Async XLA Ops:
  7.2 12.4 %copy-start.17 = (s32[2,2048]{1,0:T(2,128)S(1)}, s32[2,2048]{1,0:T(2,128)}, u32[]{:S(2)}) copy-start(s32[2,2048]{1,0:T(2,128)} %param.15) | copy-start | bytes 49156
  7.2 165.4 %all-gather.3.cloned.1.call-start = ((), (), s32[]{:S(2)}) async-start(), calls=%async_computation.3 | async-start | bytes 18874368 | tf_op jit(solution)/shard_map/all_gather | solution.py:815
  14.6 27.1 %collective-permute-start = (bf16[256,2048]{1,0:T(8,128)(2,1)}, bf16[256,2048]{1,0:T(8,128)(2,1)S(1)}, u32[]{:S(2)}, u32[]{:S(2)}) collective-permute-start(bf16[256,2048]{1,0:T(8,128)(2,1)} %get-tuple-element.218.refs_0_), channel_id=1, source_target_pairs={{0,2},{1,3},{2,0},{3,1},{4,6},{5,7},{6,4},{7,5},{8,10},{9,11},{10,... | collective-permute-start | bytes 3145736 | tf_op jit(solution)/shard_map/ppermute | solution.py:671
  17.5 26.3 %collective-permute-start.1 = (bf16[256,2048]{1,0:T(8,128)(2,1)}, bf16[256,2048]{1,0:T(8,128)(2,1)S(1)}, u32[]{:S(2)}, u32[]{:S(2)}) collective-permute-start(bf16[256,2048]{1,0:T(8,128)(2,1)} %get-tuple-element.219.refs_1_), channel_id=1, source_target_pairs={{0,4},{1,5},{2,6},{3,7},{4,0},{5,1},{6,2},{7,3},{8,12},{9,13},{10,... | collective-permute-start | bytes 3145736 | tf_op jit(solution)/shard_map/ppermute | solution.py:671
  19.0 24.8 %collective-permute-start.2 = (bf16[256,2048]{1,0:T(8,128)(2,1)}, bf16[256,2048]{1,0:T(8,128)(2,1)}, u32[]{:S(2)}, u32[]{:S(2)}) collective-permute-start(bf16[256,2048]{1,0:T(8,128)(2,1)} %get-tuple-element.218.refs_0_), channel_id=1, source_target_pairs={{0,1},{1,0},{2,3},{3,2},{4,5},{5,4},{6,7},{7,6},{8,9},{9,8},{10,11... | collective-permute-start | bytes 3145736 | tf_op jit(solution)/shard_map/ppermute | solution.py:671
  19.0 44.4 %collective-permute-start.3 = (bf16[256,2048]{1,0:T(8,128)(2,1)}, bf16[256,2048]{1,0:T(8,128)(2,1)}, u32[]{:S(2)}, u32[]{:S(2)}) collective-permute-start(bf16[256,2048]{1,0:T(8,128)(2,1)} %get-tuple-element.219.refs_1_), channel_id=1, source_target_pairs={{0,2},{1,3},{2,0},{3,1},{4,6},{5,7},{6,4},{7,5},{8,10},{9,11},{10,... | collective-permute-start | bytes 3145736 | tf_op jit(solution)/shard_map/ppermute | solution.py:671
  19.5 45.3 %collective-permute-start.4 = (bf16[256,2048]{1,0:T(8,128)(2,1)}, bf16[256,2048]{1,0:T(8,128)(2,1)}, u32[]{:S(2)}, u32[]{:S(2)}) collective-permute-start(bf16[256,2048]{1,0:T(8,128)(2,1)} %get-tuple-element.218.refs_0_), channel_id=1, source_target_pairs={{0,4},{1,5},{2,6},{3,7},{4,0},{5,1},{6,2},{7,3},{8,12},{9,13},{10,... | collective-permute-start | bytes 3145736 | tf_op jit(solution)/shard_map/ppermute | solution.py:671
  19.6 24.2 %copy-start.8 = (bf16[256,2048]{1,0:T(8,128)(2,1)S(1)}, bf16[256,2048]{1,0:T(8,128)(2,1)}, u32[]{:S(2)}) copy-start(bf16[256,2048]{1,0:T(8,128)(2,1)} %get-tuple-element.219.refs_1_) | copy-start | bytes 3145732
  22.1 47.7 %copy-start.22 = (bf16[1024]{0:T(1024)(128)(2,1)S(1)}, bf16[1024]{0:T(1024)(128)(2,1)}, u32[]{:S(2)}) copy-start(bf16[1024]{0:T(1024)(128)(2,1)} %param.23) | copy-start | bytes 6148
  41.7 30.9 %copy-start.6 = (bf16[256,2048]{1,0:T(8,128)(2,1)}, bf16[256,2048]{1,0:T(8,128)(2,1)S(1)}, u32[]{:S(2)}) copy-start(bf16[256,2048]{1,0:T(8,128)(2,1)S(1)} %collective-permute-done.refs_4_) | copy-start | bytes 3145732
  43.8 28.8 %copy-start.7 = (bf16[256,2048]{1,0:T(8,128)(2,1)}, bf16[256,2048]{1,0:T(8,128)(2,1)S(1)}, u32[]{:S(2)}) copy-start(bf16[256,2048]{1,0:T(8,128)(2,1)S(1)} %collective-permute-done.1.refs_7_) | copy-start | bytes 3145732
  43.8 21.1 %collective-permute-start.5 = (bf16[256,2048]{1,0:T(8,128)(2,1)S(1)}, bf16[256,2048]{1,0:T(8,128)(2,1)}, u32[]{:S(2)}, u32[]{:S(2)}) collective-permute-start(bf16[256,2048]{1,0:T(8,128)(2,1)S(1)} %copy-done.8), channel_id=1, source_target_pairs={{0,1},{1,0},{2,3},{3,2},{4,5},{5,4},{6,7},{7,6},{8,9},{9,8},{10,11... | collective-permute-start | bytes 3145736 | tf_op jit(solution)/shard_map/ppermute | solution.py:671
  64.9 432.6 %all-gather.5.cloned.1.call-start = ((), (), s32[]{:S(2)}) async-start(), calls=%async_computation.4 | async-start | bytes 9437184 | tf_op jit(solution)/shard_map/all_gather | solution.py:837
  65.0 3.4 collective-permute-start.6
  65.1 5.6 collective-permute-start.7
  65.5 7.0 %collective-permute-start.8 = (bf16[256,2048]{1,0:T(8,128)(2,1)}, bf16[256,2048]{1,0:T(8,128)(2,1)}, u32[]{:S(2)}, u32[]{:S(2)}) collective-permute-start(bf16[256,2048]{1,0:T(8,128)(2,1)} %collective-permute-done.4.refs_6_), channel_id=1, source_target_pairs={{0,1},{1,0},{2,3},{3,2},{4,5},{5,4},{6,7},{7,6},{8,9},{9,8},{10,11... | collective-permute-start | bytes 3145736 | tf_op jit(solution)/shard_map/ppermute | solution.py:671
  65.6 6.9 %collective-permute-start.9 = (bf16[256,2048]{1,0:T(8,128)(2,1)S(1)}, bf16[256,2048]{1,0:T(8,128)(2,1)}, u32[]{:S(2)}, u32[]{:S(2)}) collective-permute-start(bf16[256,2048]{1,0:T(8,128)(2,1)S(1)} %collective-permute-done.1.refs_7_), channel_id=1, source_target_pairs={{0,1},{1,0},{2,3},{3,2},{4,5},{5,4},{6,7},{7,6},{8,9},{9,8},{10,11... | collective-permute-start | bytes 3145736 | tf_op jit(solution)/shard_map/ppermute | solution.py:671
  66.1 43.2 %collective-permute-start.10 = (bf16[256,2048]{1,0:T(8,128)(2,1)S(1)}, bf16[256,2048]{1,0:T(8,128)(2,1)S(1)}, u32[]{:S(2)}, u32[]{:S(2)}) collective-permute-start(bf16[256,2048]{1,0:T(8,128)(2,1)S(1)} %collective-permute-done.refs_4_), channel_id=1, source_target_pairs={{0,4},{1,5},{2,6},{3,7},{4,0},{5,1},{6,2},{7,3},{8,12},{9,13},{10,... | collective-permute-start | bytes 3145736 | tf_op jit(solution)/shard_map/ppermute | solution.py:671
  69.4 43.5 %collective-permute-start.11 = (bf16[256,2048]{1,0:T(8,128)(2,1)S(1)}, bf16[256,2048]{1,0:T(8,128)(2,1)}, u32[]{:S(2)}, u32[]{:S(2)}) collective-permute-start(bf16[256,2048]{1,0:T(8,128)(2,1)S(1)} %collective-permute-done.1.refs_7_), channel_id=1, source_target_pairs={{0,2},{1,3},{2,0},{3,1},{4,6},{5,7},{6,4},{7,5},{8,10},{9,11},{10,... | collective-permute-start | bytes 3145736 | tf_op jit(solution)/shard_map/ppermute | solution.py:671
  109.3 8.0 %copy-start.10 = (bf16[256,2048]{1,0:T(8,128)(2,1)}, bf16[256,2048]{1,0:T(8,128)(2,1)S(1)}, u32[]{:S(2)}) copy-start(bf16[256,2048]{1,0:T(8,128)(2,1)S(1)} %collective-permute-done.10.refs_1_) | copy-start | bytes 3145732
  112.9 4.1 collective-permute-start.12
  112.9 4.4 collective-permute-start.13
  123.7 12.8 %copy-start.23 = (bf16[3,256]{1,0:T(4,128)(2,1)S(1)}, bf16[3,256]{1,0:T(4,128)(2,1)}, u32[]{:S(2)}) copy-start(bf16[3,256]{1,0:T(4,128)(2,1)} %param.19) | copy-start | bytes 4612
  136.2 361.3 %reduce-scatter.3.cloned.1.call-start = ((), (), s32[]{:S(2)}) async-start(), calls=%async_computation.5 | async-start | bytes 18874368 | tf_op jit(solution)/shard_map/reduce_scatter | solution.py:846
  186.9 49.7 %collective-permute-start.14 = (bf16[512,2048]{1,0:T(8,128)(2,1)}, bf16[512,2048]{1,0:T(8,128)(2,1)S(1)}, u32[]{:S(2)}, u32[]{:S(2)}) collective-permute-start(bf16[512,2048]{1,0:T(8,128)(2,1)} %weight_grad.3), channel_id=1, source_target_pairs={{0,8},{24,16},{1,9},{25,17},{2,10},{26,18},{3,11},{27,19},{4,12},{... | collective-permute-start | bytes 6291464 | tf_op jit(solution)/shard_map/ppermute | solution.py:601
  204.2 80.3 %collective-permute-start.16 = (bf16[512,2048]{1,0:T(8,128)(2,1)}, bf16[512,2048]{1,0:T(8,128)(2,1)}, u32[]{:S(2)}, u32[]{:S(2)}) collective-permute-start(bf16[512,2048]{1,0:T(8,128)(2,1)} %weight_grad.4), channel_id=1, source_target_pairs={{0,8},{24,16},{1,9},{25,17},{2,10},{26,18},{3,11},{27,19},{4,12},{... | collective-permute-start | bytes 6291464 | tf_op jit(solution)/shard_map/ppermute | solution.py:601
  206.9 29.7 %copy-start.3 = (bf16[512,2048]{1,0:T(8,128)(2,1)S(1)}, bf16[512,2048]{1,0:T(8,128)(2,1)}, u32[]{:S(2)}) copy-start(bf16[512,2048]{1,0:T(8,128)(2,1)} %weight_grad.3) | copy-start | bytes 6291460
  237.5 51.5 %collective-permute-start.15 = (bf16[512,2048]{1,0:T(8,128)(2,1)S(1)}, bf16[512,2048]{1,0:T(8,128)(2,1)}, u32[]{:S(2)}, u32[]{:S(2)}) collective-permute-start(bf16[512,2048]{1,0:T(8,128)(2,1)S(1)} %add_convert_fusion.9), channel_id=1, source_target_pairs={{8,16},{16,8},{9,17},{17,9},{10,18},{18,10},{11,19},{19,11},{12,20... | collective-permute-start | bytes 6291464 | tf_op jit(solution)/shard_map/ppermute | solution.py:601
  264.1 67.7 %collective-permute-start.17 = (bf16[1024,1024]{1,0:T(8,128)(2,1)}, bf16[1024,1024]{1,0:T(8,128)(2,1)}, u32[]{:S(2)}, u32[]{:S(2)}) collective-permute-start(bf16[1024,1024]{1,0:T(8,128)(2,1)} %get-tuple-element.288), channel_id=1, source_target_pairs={{0,8},{24,16},{1,9},{25,17},{2,10},{26,18},{3,11},{27,19},{4,12},{... | collective-permute-start | bytes 6291464 | tf_op jit(solution)/shard_map/ppermute | solution.py:601
  271.1 13.4 %copy-start.2 = (bf16[512,2048]{1,0:T(8,128)(2,1)S(1)}, bf16[512,2048]{1,0:T(8,128)(2,1)}, u32[]{:S(2)}) copy-start(bf16[512,2048]{1,0:T(8,128)(2,1)} %weight_grad.4) | copy-start | bytes 6291460
  286.9 73.5 %collective-permute-start.21 = (bf16[512,2048]{1,0:T(8,128)(2,1)S(1)}, bf16[512,2048]{1,0:T(8,128)(2,1)}, u32[]{:S(2)}, u32[]{:S(2)}) collective-permute-start(bf16[512,2048]{1,0:T(8,128)(2,1)S(1)} %add_convert_fusion.8), channel_id=1, source_target_pairs={{8,16},{16,8},{9,17},{17,9},{10,18},{18,10},{11,19},{19,11},{12,20... | collective-permute-start | bytes 6291464 | tf_op jit(solution)/shard_map/ppermute | solution.py:601
  292.8 72.8 %collective-permute-start.20 = (bf16[512,2048]{1,0:T(8,128)(2,1)}, bf16[512,2048]{1,0:T(8,128)(2,1)}, u32[]{:S(2)}, u32[]{:S(2)}) collective-permute-start(bf16[512,2048]{1,0:T(8,128)(2,1)} %add_convert_fusion.7.kept_ref), channel_id=1, source_target_pairs={{8,0},{16,24},{9,1},{17,25},{10,2},{18,26},{11,3},{19,27},{12,4},{... | collective-permute-start | bytes 6291464 | tf_op jit(solution)/shard_map/ppermute | solution.py:601
  294.1 90.7 %collective-permute-start.19 = (bf16[1024,1024]{1,0:T(8,128)(2,1)}, bf16[1024,1024]{1,0:T(8,128)(2,1)}, u32[]{:S(2)}, u32[]{:S(2)}) collective-permute-start(bf16[1024,1024]{1,0:T(8,128)(2,1)} %get-tuple-element.309), channel_id=1, source_target_pairs={{0,8},{24,16},{1,9},{25,17},{2,10},{26,18},{3,11},{27,19},{4,12},{... | collective-permute-start | bytes 6291464 | tf_op jit(solution)/shard_map/ppermute | solution.py:601
  309.6 22.2 %copy-start.4 = (bf16[1024,1024]{1,0:T(8,128)(2,1)S(1)}, bf16[1024,1024]{1,0:T(8,128)(2,1)}, u32[]{:S(2)}) copy-start(bf16[1024,1024]{1,0:T(8,128)(2,1)} %get-tuple-element.288) | copy-start | bytes 6291460
  336.2 61.8 %collective-permute-start.18 = (bf16[1024,1024]{1,0:T(8,128)(2,1)}, bf16[1024,1024]{1,0:T(8,128)(2,1)}, u32[]{:S(2)}, u32[]{:S(2)}) collective-permute-start(bf16[1024,1024]{1,0:T(8,128)(2,1)} %add_convert_fusion.6), channel_id=1, source_target_pairs={{8,16},{16,8},{9,17},{17,9},{10,18},{18,10},{11,19},{19,11},{12,20... | collective-permute-start | bytes 6291464 | tf_op jit(solution)/shard_map/ppermute | solution.py:601
  364.1 61.4 %collective-permute-start.26 = (bf16[512,2048]{1,0:T(8,128)(2,1)}, bf16[512,2048]{1,0:T(8,128)(2,1)}, u32[]{:S(2)}, u32[]{:S(2)}) collective-permute-start(bf16[512,2048]{1,0:T(8,128)(2,1)} %add_convert_fusion.5.kept_ref), channel_id=1, source_target_pairs={{8,0},{16,24},{9,1},{17,25},{10,2},{18,26},{11,3},{19,27},{12,4},{... | collective-permute-start | bytes 6291464 | tf_op jit(solution)/shard_map/ppermute | solution.py:601
  384.8 5.3 copy-start.5
  388.1 47.5 %collective-permute-start.25 = (bf16[1024,1024]{1,0:T(8,128)(2,1)S(1)}, bf16[1024,1024]{1,0:T(8,128)(2,1)}, u32[]{:S(2)}, u32[]{:S(2)}) collective-permute-start(bf16[1024,1024]{1,0:T(8,128)(2,1)S(1)} %add_convert_fusion.4), channel_id=1, source_target_pairs={{8,16},{16,8},{9,17},{17,9},{10,18},{18,10},{11,19},{19,11},{12,20... | collective-permute-start | bytes 6291464 | tf_op jit(solution)/shard_map/ppermute | solution.py:601
  390.1 49.4 %collective-permute-start.24 = (bf16[2,2048,256]{2,1,0:T(8,128)(2,1)S(1)}, bf16[2,2048,256]{2,1,0:T(8,128)(2,1)}, u32[]{:S(2)}, u32[]{:S(2)}) collective-permute-start(bf16[2,2048,256]{2,1,0:T(8,128)(2,1)S(1)} %copy-done.5), channel_id=1, source_target_pairs={{0,8},{24,16},{1,9},{25,17},{2,10},{26,18},{3,11},{27,19},{4,12},{... | collective-permute-start | bytes 6291464 | tf_op jit(solution)/shard_map/ppermute | solution.py:601
  401.2 24.3 %copy-start = (bf16[1024,1024]{1,0:T(8,128)(2,1)}, bf16[1024,1024]{1,0:T(8,128)(2,1)S(1)}, u32[]{:S(2)}) copy-start(bf16[1024,1024]{1,0:T(8,128)(2,1)S(1)} %add_convert_fusion.3.kept_ref) | copy-start | bytes 6291460
  401.2 93.7 %collective-permute-start.22 = (bf16[1024,1024]{1,0:T(8,128)(2,1)S(1)}, bf16[1024,1024]{1,0:T(8,128)(2,1)}, u32[]{:S(2)}, u32[]{:S(2)}) collective-permute-start(bf16[1024,1024]{1,0:T(8,128)(2,1)S(1)} %add_convert_fusion.3.kept_ref), channel_id=1, source_target_pairs={{8,0},{16,24},{9,1},{17,25},{10,2},{18,26},{11,3},{19,27},{12,4},{... | collective-permute-start | bytes 6291464 | tf_op jit(solution)/shard_map/ppermute | solution.py:601
  442.9 6.5 %copy-start.9 = (bf16[2048,256]{1,0:T(8,128)(2,1)S(1)}, bf16[2048,256]{1,0:T(8,128)(2,1)}, u32[]{:S(2)}) copy-start(bf16[2048,256]{1,0:T(8,128)(2,1)} %get-tuple-element.337) | copy-start | bytes 3145732
  442.9 66.6 %collective-permute-start.29 = (bf16[2,2048,256]{2,1,0:T(8,128)(2,1)}, bf16[2,2048,256]{2,1,0:T(8,128)(2,1)}, u32[]{:S(2)}, u32[]{:S(2)}) collective-permute-start(bf16[2,2048,256]{2,1,0:T(8,128)(2,1)} %add_convert_fusion.1), channel_id=1, source_target_pairs={{8,16},{16,8},{9,17},{17,9},{10,18},{18,10},{11,19},{19,11},{12,20... | collective-permute-start | bytes 6291464 | tf_op jit(solution)/shard_map/ppermute | solution.py:601
  445.0 52.5 %all-to-all-start = ((bf16[8,2,256,256]{3,2,1,0:T(8,128)(2,1)}), bf16[8,2,256,256]{3,2,1,0:T(8,128)(2,1)}, u32[]{:S(2)}, u32[]{:S(2)}) async-start(bf16[8,2,256,256]{3,2,1,0:T(8,128)(2,1)} %get-tuple-element.298), calls=%async_computation | async-start | bytes 4194304 | tf_op jit(solution)/shard_map/all_to_all | solution.py:855
  449.4 160.8 %reduce-scatter.5.cloned.1.call-start = ((), (), s32[]{:S(2)}) async-start(), calls=%async_computation.6 | async-start | bytes 18874368 | tf_op jit(solution)/shard_map/reduce_scatter | solution.py:869
  449.4 41.7 %collective-permute-start.23 = (bf16[2048,256]{1,0:T(8,128)(2,1)S(1)}, bf16[2048,256]{1,0:T(8,128)(2,1)}, u32[]{:S(2)}, u32[]{:S(2)}) collective-permute-start(bf16[2048,256]{1,0:T(8,128)(2,1)S(1)} %copy-done.9), channel_id=1, source_target_pairs={{0,8},{24,16},{1,9},{25,17},{2,10},{26,18},{3,11},{27,19},{4,12},{... | collective-permute-start | bytes 3145736 | tf_op jit(solution)/shard_map/ppermute | solution.py:601
  458.2 56.0 %collective-permute-start.28 = (bf16[1024,1024]{1,0:T(8,128)(2,1)}, bf16[1024,1024]{1,0:T(8,128)(2,1)}, u32[]{:S(2)}, u32[]{:S(2)}) collective-permute-start(bf16[1024,1024]{1,0:T(8,128)(2,1)} %add_convert_fusion.2.kept_ref), channel_id=1, source_target_pairs={{8,0},{16,24},{9,1},{17,25},{10,2},{18,26},{11,3},{19,27},{12,4},{... | collective-permute-start | bytes 6291464 | tf_op jit(solution)/shard_map/ppermute | solution.py:601
  484.2 30.3 %collective-permute-start.27 = (bf16[256,2048]{1,0:T(8,128)(2,1)}, bf16[256,2048]{1,0:T(8,128)(2,1)}, u32[]{:S(2)}, u32[]{:S(2)}) collective-permute-start(bf16[256,2048]{1,0:T(8,128)(2,1)} %weight_grad.5), channel_id=1, source_target_pairs={{0,8},{24,16},{1,9},{25,17},{2,10},{26,18},{3,11},{27,19},{4,12},{... | collective-permute-start | bytes 3145736 | tf_op jit(solution)/shard_map/ppermute | solution.py:601
  493.3 42.3 %collective-permute-start.35 = (bf16[2048,256]{1,0:T(8,128)(2,1)S(1)}, bf16[2048,256]{1,0:T(8,128)(2,1)}, u32[]{:S(2)}, u32[]{:S(2)}) collective-permute-start(bf16[2048,256]{1,0:T(8,128)(2,1)S(1)} %add_convert_fusion.13), channel_id=1, source_target_pairs={{8,16},{16,8},{9,17},{17,9},{10,18},{18,10},{11,19},{19,11},{12,20... | collective-permute-start | bytes 3145736 | tf_op jit(solution)/shard_map/ppermute | solution.py:601
  509.6 4.6 copy-start.14
  509.6 4.6 copy-start.15
  509.6 4.6 copy-start.16
  509.6 4.6 copy-start.20
  512.8 25.4 %copy-start.1 = (bf16[2,2048,256]{2,1,0:T(8,128)(2,1)}, bf16[2,2048,256]{2,1,0:T(8,128)(2,1)S(1)}, u32[]{:S(2)}) copy-start(bf16[2,2048,256]{2,1,0:T(8,128)(2,1)S(1)} %add_convert_fusion) | copy-start | bytes 6291460
  512.8 50.6 %collective-permute-start.38 = (bf16[2,2048,256]{2,1,0:T(8,128)(2,1)S(1)}, bf16[2,2048,256]{2,1,0:T(8,128)(2,1)}, u32[]{:S(2)}, u32[]{:S(2)}) collective-permute-start(bf16[2,2048,256]{2,1,0:T(8,128)(2,1)S(1)} %add_convert_fusion), channel_id=1, source_target_pairs={{8,0},{16,24},{9,1},{17,25},{10,2},{18,26},{11,3},{19,27},{12,4},{... | collective-permute-start | bytes 6291464 | tf_op jit(solution)/shard_map/ppermute | solution.py:601
  517.4 24.0 %collective-permute-start.30 = (bf16[256,2048]{1,0:T(8,128)(2,1)}, bf16[256,2048]{1,0:T(8,128)(2,1)}, u32[]{:S(2)}, u32[]{:S(2)}) collective-permute-start(bf16[256,2048]{1,0:T(8,128)(2,1)} %add_convert_fusion.12), channel_id=1, source_target_pairs={{8,16},{16,8},{9,17},{17,9},{10,18},{18,10},{11,19},{19,11},{12,20... | collective-permute-start | bytes 3145736 | tf_op jit(solution)/shard_map/ppermute | solution.py:601
  519.0 1.2 collective-permute-start.31
  520.2 4.0 collective-permute-start.32
  524.2 4.2 collective-permute-start.33
  528.4 11.1 %collective-permute-start.34 = (f32[49,128]{1,0:T(8,128)S(1)}, f32[49,128]{1,0:T(8,128)S(1)}, u32[]{:S(2)}, u32[]{:S(2)}) collective-permute-start(f32[49,128]{1,0:T(8,128)S(1)} %pad_maximum_fusion), channel_id=1, source_target_pairs={{0,8},{24,16},{1,9},{25,17},{2,10},{26,18},{3,11},{27,19},{4,12},{... | collective-permute-start | bytes 75272 | tf_op jit(solution)/shard_map/ppermute | solution.py:601
  538.2 50.5 %collective-permute-start.37 = (bf16[2048,256]{1,0:T(8,128)(2,1)}, bf16[2048,256]{1,0:T(8,128)(2,1)}, u32[]{:S(2)}, u32[]{:S(2)}) collective-permute-start(bf16[2048,256]{1,0:T(8,128)(2,1)} %add_convert_fusion.11.kept_ref), channel_id=1, source_target_pairs={{8,0},{16,24},{9,1},{17,25},{10,2},{18,26},{11,3},{19,27},{12,4},{... | collective-permute-start | bytes 3145736 | tf_op jit(solution)/shard_map/ppermute | solution.py:601
  540.1 36.1 %collective-permute-start.39 = (f32[49,128]{1,0:T(8,128)}, f32[49,128]{1,0:T(8,128)}, u32[]{:S(2)}, u32[]{:S(2)}) collective-permute-start(f32[49,128]{1,0:T(8,128)} %add.132), channel_id=1, source_target_pairs={{8,16},{16,8},{9,17},{17,9},{10,18},{18,10},{11,19},{19,11},{12,20... | collective-permute-start | bytes 75272 | tf_op jit(solution)/shard_map/ppermute | solution.py:601
  544.3 62.9 %collective-permute-start.36 = (bf16[256,2048]{1,0:T(8,128)(2,1)}, bf16[256,2048]{1,0:T(8,128)(2,1)}, u32[]{:S(2)}, u32[]{:S(2)}) collective-permute-start(bf16[256,2048]{1,0:T(8,128)(2,1)} %add_convert_fusion.10.kept_ref), channel_id=1, source_target_pairs={{8,0},{16,24},{9,1},{17,25},{10,2},{18,26},{11,3},{19,27},{12,4},{... | collective-permute-start | bytes 3145736 | tf_op jit(solution)/shard_map/ppermute | solution.py:601
  577.0 39.4 %collective-permute-start.40 = (f32[49,128]{1,0:T(8,128)S(1)}, f32[49,128]{1,0:T(8,128)S(1)}, u32[]{:S(2)}, u32[]{:S(2)}) collective-permute-start(f32[49,128]{1,0:T(8,128)S(1)} %add.134), channel_id=1, source_target_pairs={{8,0},{16,24},{9,1},{17,25},{10,2},{18,26},{11,3},{19,27},{12,4},{... | collective-permute-start | bytes 75272 | tf_op jit(solution)/shard_map/ppermute | solution.py:601
  (6 other events, 8.5 us)
Sparse Core Ops, SparseCore 0:
  65.0 107.5 all-gather.2
  174.5 54.3 all-gather.4
  309.7 114.0 reduce-scatter.2
  482.5 118.2 reduce-scatter.4
